TPU v7x, 32 devices: a whole 2x2x4 slice. The times are simulated.
32 devices in a mesh: field: 2 (over y), expo: 8 (over z, core), strip: 2 (over x).
Axes of the slice: x: 2, y: 2, z: 4, core: 2. Of those that a mesh axis runs over, the one named last changes fastest.
Arguments:
- science: bfloat16 [128, 64, 512], P(('field', 'expo'), 'strip'), parts along dimension 0, may hold values from -6 to 6
- inv_var: bfloat16 [128, 64, 512], P(('field', 'expo'), 'strip'), parts along dimension 0, may hold values from 0.25 to 4
- psf_rows: float32 [128, 9], P(('field', 'expo')), parts along dimension 0, may hold values from 0.2 to 1
- psf_cols: float32 [128, 9], P(('field', 'expo')), parts along dimension 0, may hold values from 0.2 to 1
- row_shift: int32 [128, 8], P(('field', 'expo')), parts along dimension 0, may hold values from 0 to 16
- col_shift: int32 [128, 8], P(('field', 'expo')), parts along dimension 0, may hold values from -16 to 16
- exposure_ok: int32 [128], P(('field', 'expo')), parts along dimension 0, may hold values 0 or 1
Outputs:
- likelihood: float32 [2, 16, 32, 512], P('strip', 'field', 'expo'), parts along dimension 1
There are 2 independent parts, one for each index of `field`. A program takes and returns all parts, laid end to end along the dimension named above; each array names one. Nothing has to cross between parts.
Inputs may be any that keep to these rules, and one draw needn't show every extreme that they name: `row_shift`: every shift lies in 0..16, so S[e, v, r] reads map rows r to r + 16 only, never lower rows.
All inputs are finite; a program needn't handle non-finite values. No bound on the sum of `exposure_ok` on one device may be relied on, other than what follows from the above.
Results may differ from a plain program's by a relative error of at most 0.0017.
Values may be sent and summed in bfloat16 or wider, within the bound.
No kernel may reach another device: no remote copies, remote signals or barrier semaphores. Data moves between devices by JAX's collectives and lax.ppermute only.
A program may use at most 64 MiB of HBM per device.

v0:
```python
import jax
import jax.numpy as jnp
from jax import lax
from jax.sharding import PartitionSpec as P

SHIFT = 16


def extended_2(cells, sides, width):
    for axis, dim in sides:
        count = lax.axis_size(axis)
        ends = count - 1
        head = lax.slice_in_dim(cells, 0, width, axis=dim)
        tail = lax.slice_in_dim(cells, cells.shape[dim] - width, cells.shape[dim], axis=dim)
        cells = jnp.concatenate(
            [
                lax.ppermute(tail, axis, [(i, (i + 1) % count) for i in range(ends)]),
                cells,
                lax.ppermute(head, axis, [((i + 1) % count, i) for i in range(ends)]),
            ],
            axis=dim,
        )
    return cells


def filter_one(picture, row_taps, col_taps, out_rows):
    columns = picture.shape[2]
    tap_count = row_taps.shape[1]
    radius = tap_count // 2
    padded = jnp.pad(picture, ((0, 0), (0, 0), (radius, radius)))
    colpass = col_taps[:, 0, None, None] * padded[:, :, 0:columns]
    for b in range(1, tap_count):
        colpass = colpass + col_taps[:, b, None, None] * padded[:, :, b : b + columns]
    result = row_taps[:, 0, None, None] * colpass[:, 0:out_rows]
    for a in range(1, tap_count):
        result = result + row_taps[:, a, None, None] * colpass[:, a : a + out_rows]
    return result.astype(jnp.bfloat16)


def matched_pair(science, inv_var, psf_rows, psf_cols, out_rows):
    science_f = science.astype(jnp.float32)
    inverse = inv_var.astype(jnp.float32)
    signal_map = filter_one(science_f * inverse, psf_rows, psf_cols, out_rows)
    depth_map = filter_one(inverse, psf_rows * psf_rows, psf_cols * psf_cols, out_rows)
    return (signal_map, depth_map)


def per_device(science, inv_var, psf_rows, psf_cols, row_shift, col_shift, exposure_ok):
    local_rows = science.shape[1]
    columns = science.shape[2]
    vel_count = row_shift.shape[1]
    radius = psf_rows.shape[1] // 2
    stacked = jnp.stack([science, inv_var])
    extended = extended_2(stacked, (("strip", 2),), radius + SHIFT)
    inner_rows = extended[:, :, SHIFT:]
    signal_map, depth_map = matched_pair(
        inner_rows[0], inner_rows[1], psf_rows, psf_cols, local_rows + SHIFT
    )
    row_keep = (lax.iota(jnp.int32, local_rows + SHIFT) < local_rows) | (
        lax.axis_index("strip") < lax.axis_size("strip") - 1
    )
    row_keep = row_keep[None, :, None]
    signal_map = jnp.where(row_keep, signal_map, jnp.zeros_like(signal_map))
    depth_map = jnp.where(row_keep, depth_map, jnp.zeros_like(depth_map))
    pair_maps = jnp.stack([signal_map, depth_map], 1)
    padded = jnp.pad(pair_maps, ((0, 0), (0, 0), (0, 0), (SHIFT, SHIFT)))
    usable = exposure_ok.astype(jnp.float32)[:, None, None, None]

    def cut_one(maps_block, row_at, col_at):
        return lax.dynamic_slice(
            maps_block, (jnp.zeros((), jnp.int32), row_at, col_at + SHIFT), (2, local_rows, columns)
        )

    def cut_all(velocity):
        return jax.vmap(cut_one)(padded, row_shift[:, velocity], col_shift[:, velocity]).astype(
            jnp.float32
        )

    first_sums = jnp.stack(
        [jnp.sum(usable * cut_all(velocity), axis=0) for velocity in range(vel_count)]
    )
    whole_sums = lax.psum((first_sums[:, 0], first_sums[:, 1]), "expo")
    flux_est = whole_sums[0] / (whole_sums[1] + 1.0)
    robust_signal = []
    robust_depth = []
    for velocity in range(vel_count):
        windows_now = cut_all(velocity)
        signal = windows_now[:, 0]
        depth = windows_now[:, 1]
        residual = signal - flux_est[velocity][None] * depth
        weight = usable[:, 0] / (1.0 + residual * residual / (depth + 1.0))
        robust_signal.append(jnp.sum(weight * signal, axis=0))
        robust_depth.append(jnp.sum(weight * depth, axis=0))
    robust = (
        lax.psum_scatter(jnp.stack(robust_signal), "expo", scatter_dimension=1, tiled=True),
        lax.psum_scatter(jnp.stack(robust_depth), "expo", scatter_dimension=1, tiled=True),
    )
    likelihood = robust[0] / jnp.sqrt(robust[1] + 1.0)
    return likelihood[None]


def solution(mesh):
    in_specs = (
        P(("field", "expo"), "strip", None),
        P(("field", "expo"), "strip", None),
        P(("field", "expo"), None),
        P(("field", "expo"), None),
        P(("field", "expo"), None),
        P(("field", "expo"), None),
        P(("field", "expo")),
    )
    out_specs = P("strip", "field", "expo", None)
    return jax.shard_map(
        per_device, mesh=mesh, in_specs=in_specs, out_specs=out_specs, check_vma=False
    )
```

profile of v0, /device:TPU:0, one launch (start us, length us, event | category | flops | bytes accessed | tf_op | source)
XLA Modules:
  0.0 361.9 jit_solution(3347741036529363502)
XLA Ops:
  8.1 4.9 %collective-permute-start = (bf16[2,8,20,512]{3,2,1,0:T(8,128)(2,1)S(1)}, bf16[2,8,20,512]{3,2,1,0:T(8,128)(2,1)S(1)}, u32[]{:S(2)}, u32[]{:S(2)}) collective-permute-start(bf16[2,8,20,512]{3,2,1,0:T(8,128)(2,1)S(1)} %get-tuple-element.229), channel_id=1, source_target_pairs={{0,1},{2,3},{4,5},{6,7},{8,9},{10,11},{12,13},{14,15},{16,17},{18,... | collective-permute-start | bytes 983048 | tf_op jit(solution)/shard_map/ppermute | solution.py:17
  17.2 4.1 %collective-permute-done = bf16[2,8,20,512]{3,2,1,0:T(8,128)(2,1)S(1)} collective-permute-done((bf16[2,8,20,512]{3,2,1,0:T(8,128)(2,1)S(1)}, bf16[2,8,20,512]{3,2,1,0:T(8,128)(2,1)S(1)}, u32[]{:S(2)}, u32[]{:S(2)}) %collective-permute-start) | collective-permute-done | bytes 327712 | tf_op jit(solution)/shard_map/ppermute | solution.py:17
  21.3 4.1 %collective-permute-done.1 = bf16[2,8,20,512]{3,2,1,0:T(8,128)(2,1)S(1)} collective-permute-done((bf16[2,8,20,512]{3,2,1,0:T(8,128)(2,1)S(1)}, bf16[2,8,20,512]{3,2,1,0:T(8,128)(2,1)S(1)}, u32[]{:S(2)}, u32[]{:S(2)}) %collective-permute-start.1) | collective-permute-done | bytes 327712 | tf_op jit(solution)/shard_map/ppermute | solution.py:19
  25.7 2.1 fusion.12
  27.9 2.1 fusion.28
  32.5 21.5 %while.8 = (s32[]{:T(128)}, bf16[8,2,48,544]{3,2,1,0:T(8,128)(2,1)S(1)}, s32[8,4]{0,1:T(4,128)S(1)}, bf16[8,2,32,512]{3,2,0,1:T(8,128)(2,1)S(1)}, s32[]{:T(128)}) while((s32[]{:T(128)}, bf16[8,2,48,544]{3,2,1,0:T(8,128)(2,1)S(1)}, s32[8,4]{0,1:T(4,128)S(1)}, bf16[8,2,32,512]{3,2,0,1:T(8,128)(2,1)S(1)}, s32[]{:T(128)}) %tuple.233), condition=%wide.while_cond, body=%wide.while_body.sunk | while | flops 2 | bytes 131209 | solution.py:70
  33.2 2.0 bitcast_dynamic-update-slice_fusion.22
  38.6 2.0 bitcast_dynamic-update-slice_fusion.22
  44.0 2.0 bitcast_dynamic-update-slice_fusion.22
  46.7 2.0 bitcast_dynamic-update-slice_fusion.22
  49.4 2.0 bitcast_dynamic-update-slice_fusion.22
  52.1 2.0 bitcast_dynamic-update-slice_fusion.22
  54.2 21.0 %while.9 = (s32[]{:T(128)}, bf16[8,2,48,544]{3,2,1,0:T(8,128)(2,1)S(1)}, s32[8,4]{0,1:T(4,128)S(1)}, bf16[8,2,32,512]{3,2,0,1:T(8,128)(2,1)S(1)}, s32[]{:T(128)}) while((s32[]{:T(128)}, bf16[8,2,48,544]{3,2,1,0:T(8,128)(2,1)S(1)}, s32[8,4]{0,1:T(4,128)S(1)}, bf16[8,2,32,512]{3,2,0,1:T(8,128)(2,1)S(1)}, s32[]{:T(128)}) %tuple.246), condition=%wide.while_cond.1, body=%wide.while_body.1.sunk | while | flops 2 | bytes 131209 | solution.py:70
  75.2 20.7 %while.10 = (s32[]{:T(128)}, bf16[8,2,48,544]{3,2,1,0:T(8,128)(2,1)S(1)}, s32[8,4]{0,1:T(4,128)S(1)}, bf16[8,2,32,512]{3,2,0,1:T(8,128)(2,1)S(1)}, s32[]{:T(128)}) while((s32[]{:T(128)}, bf16[8,2,48,544]{3,2,1,0:T(8,128)(2,1)S(1)}, s32[8,4]{0,1:T(4,128)S(1)}, bf16[8,2,32,512]{3,2,0,1:T(8,128)(2,1)S(1)}, s32[]{:T(128)}) %tuple.247), condition=%wide.while_cond.2, body=%wide.while_body.2.sunk | while | flops 2 | bytes 131209 | solution.py:70
  96.9 25.5 %while.11 = (s32[]{:T(128)}, bf16[8,2,48,544]{3,2,1,0:T(8,128)(2,1)S(1)}, s32[8,4]{0,1:T(4,128)S(1)}, bf16[8,2,32,512]{3,2,0,1:T(8,128)(2,1)}, s32[]{:T(128)}) while((s32[]{:T(128)}, bf16[8,2,48,544]{3,2,1,0:T(8,128)(2,1)S(1)}, s32[8,4]{0,1:T(4,128)S(1)}, bf16[8,2,32,512]{3,2,0,1:T(8,128)(2,1)}, s32[]{:T(128)}) %tuple.248), condition=%wide.while_cond.3, body=%wide.while_body.3.sunk | while | flops 2 | bytes 133241 | solution.py:70
  97.5 2.5 bitcast_dynamic-update-slice_fusion.25
  100.7 2.5 bitcast_dynamic-update-slice_fusion.25
  103.9 2.5 bitcast_dynamic-update-slice_fusion.25
  107.1 2.5 bitcast_dynamic-update-slice_fusion.25
  110.3 2.5 bitcast_dynamic-update-slice_fusion.25
  113.5 2.5 bitcast_dynamic-update-slice_fusion.25
  116.7 2.5 bitcast_dynamic-update-slice_fusion.25
  119.8 2.5 bitcast_dynamic-update-slice_fusion.25
  123.2 26.1 %while.12 = (s32[]{:T(128)}, bf16[8,2,48,544]{3,2,1,0:T(8,128)(2,1)S(1)}, s32[8,4]{0,1:T(4,128)S(1)}, bf16[8,2,32,512]{3,2,0,1:T(8,128)(2,1)}, s32[]{:T(128)}) while((s32[]{:T(128)}, bf16[8,2,48,544]{3,2,1,0:T(8,128)(2,1)S(1)}, s32[8,4]{0,1:T(4,128)S(1)}, bf16[8,2,32,512]{3,2,0,1:T(8,128)(2,1)}, s32[]{:T(128)}) %tuple.249), condition=%wide.while_cond.4, body=%wide.while_body.4.sunk | while | flops 2 | bytes 133241 | solution.py:70
  123.9 2.6 bitcast_dynamic-update-slice_fusion.26
  127.2 2.6 bitcast_dynamic-update-slice_fusion.26
  130.4 2.6 bitcast_dynamic-update-slice_fusion.26
  133.7 2.6 bitcast_dynamic-update-slice_fusion.26
  137.0 2.6 bitcast_dynamic-update-slice_fusion.26
  140.2 2.6 bitcast_dynamic-update-slice_fusion.26
  143.5 2.6 bitcast_dynamic-update-slice_fusion.26
  146.8 2.6 bitcast_dynamic-update-slice_fusion.26
  150.2 25.7 %while.13 = (s32[]{:T(128)}, bf16[8,2,48,544]{3,2,1,0:T(8,128)(2,1)S(1)}, s32[8,4]{0,1:T(4,128)S(1)}, bf16[8,2,32,512]{3,2,0,1:T(8,128)(2,1)}, s32[]{:T(128)}) while((s32[]{:T(128)}, bf16[8,2,48,544]{3,2,1,0:T(8,128)(2,1)S(1)}, s32[8,4]{0,1:T(4,128)S(1)}, bf16[8,2,32,512]{3,2,0,1:T(8,128)(2,1)}, s32[]{:T(128)}) %tuple.250), condition=%wide.while_cond.5, body=%wide.while_body.5.sunk | while | flops 2 | bytes 133241 | solution.py:70
  150.9 2.5 bitcast_dynamic-update-slice_fusion.27
  154.1 2.5 bitcast_dynamic-update-slice_fusion.27
  157.3 2.5 bitcast_dynamic-update-slice_fusion.27
  160.5 2.6 bitcast_dynamic-update-slice_fusion.27
  163.7 2.6 bitcast_dynamic-update-slice_fusion.27
  166.9 2.6 bitcast_dynamic-update-slice_fusion.27
  170.1 2.6 bitcast_dynamic-update-slice_fusion.27
  173.4 2.6 bitcast_dynamic-update-slice_fusion.27
  175.9 20.8 %while.15 = (s32[]{:T(128)}, bf16[8,2,48,544]{3,2,1,0:T(8,128)(2,1)S(1)}, s32[8,4]{0,1:T(4,128)S(1)}, bf16[8,2,32,512]{3,2,1,0:T(8,128)(2,1)S(1)}, s32[]{:T(128)}) while((s32[]{:T(128)}, bf16[8,2,48,544]{3,2,1,0:T(8,128)(2,1)S(1)}, s32[8,4]{0,1:T(4,128)S(1)}, bf16[8,2,32,512]{3,2,1,0:T(8,128)(2,1)S(1)}, s32[]{:T(128)}) %tuple.251), condition=%wide.while_cond.7, body=%wide.while_body.7.sunk | while | flops 2 | bytes 131209 | solution.py:70
  196.8 21.5 %while.14 = (s32[]{:T(128)}, bf16[8,2,48,544]{3,2,1,0:T(8,128)(2,1)S(1)}, s32[8,4]{0,1:T(4,128)S(1)}, bf16[8,2,32,512]{3,2,0,1:T(8,128)(2,1)S(1)}, s32[]{:T(128)}) while((s32[]{:T(128)}, bf16[8,2,48,544]{3,2,1,0:T(8,128)(2,1)S(1)}, s32[8,4]{0,1:T(4,128)S(1)}, bf16[8,2,32,512]{3,2,0,1:T(8,128)(2,1)S(1)}, s32[]{:T(128)}) %tuple.252), condition=%wide.while_cond.6, body=%wide.while_body.6.sunk | while | flops 2 | bytes 131209 | solution.py:70
  218.3 2.7 multiply_reduce_fusion
  231.3 50.8 %all-reduce.6.cloned.1.call-done = (f32[8,32,512]{2,1,0:T(8,128)}, f32[8,32,512]{2,1,0:T(8,128)}) async-done(((f32[8,32,512]{2,1,0:T(8,128)}, f32[8,32,512]{2,1,0:T(8,128)}), (f32[8,32,512]{2,1,0:T(8,128)}, f32[8,32,512]{2,1,0:T(8,128)})) %all-reduce.6.cloned.1.call-update) | async-done | bytes 1048592 | tf_op jit(solution)/shard_map/psum | solution.py:82
  284.1 2.1 add_divide_fusion
  293.6 28.5 %reduce-scatter.5.cloned.1.call-done = f32[8,4,512]{2,0,1:T(8,128)} async-done(((f32[8,32,512]{2,0,1:T(8,128)}), f32[8,4,512]{2,0,1:T(8,128)}) %reduce-scatter.5.cloned.1.call-update) | async-done | bytes 65552 | tf_op jit(solution)/shard_map/reduce_scatter | solution.py:96
  322.1 31.7 %reduce-scatter.3.cloned.1.call-done = f32[8,4,512]{2,0,1:T(8,128)} async-done(((f32[8,32,512]{2,0,1:T(8,128)}), f32[8,4,512]{2,0,1:T(8,128)}) %reduce-scatter.3.cloned.1.call-update) | async-done | bytes 65552 | tf_op jit(solution)/shard_map/reduce_scatter | solution.py:95
  (319 shorter events, 140.6 us)
Async XLA Ops:
  6.5 18.9 %copy-start.17 = (bf16[8,32,512]{2,1,0:T(8,128)(2,1)S(1)}, bf16[8,32,512]{2,1,0:T(8,128)(2,1)}, u32[]{:S(2)}) copy-start(bf16[8,32,512]{2,1,0:T(8,128)(2,1)} %param.7) | copy-start | bytes 786436
  6.5 18.9 %copy-start.18 = (bf16[8,32,512]{2,1,0:T(8,128)(2,1)S(1)}, bf16[8,32,512]{2,1,0:T(8,128)(2,1)}, u32[]{:S(2)}) copy-start(bf16[8,32,512]{2,1,0:T(8,128)(2,1)} %param.8) | copy-start | bytes 786436
  6.5 7.7 %copy-start.19 = (f32[8,9]{1,0:T(8,128)S(1)}, f32[8,9]{1,0:T(8,128)}, u32[]{:S(2)}) copy-start(f32[8,9]{1,0:T(8,128)} %param.10) | copy-start | bytes 868
  6.5 8.0 %copy-start.20 = (f32[8,9]{1,0:T(8,128)S(1)}, f32[8,9]{1,0:T(8,128)}, u32[]{:S(2)}) copy-start(f32[8,9]{1,0:T(8,128)} %param.9) | copy-start | bytes 868
  6.5 8.4 %copy-start.21 = (s32[8,8]{1,0:T(8,128)S(1)}, s32[8,8]{1,0:T(8,128)}, u32[]{:S(2)}) copy-start(s32[8,8]{1,0:T(8,128)} %param.11) | copy-start | bytes 772
  6.5 8.5 %copy-start.22 = (s32[8,8]{1,0:T(8,128)S(1)}, s32[8,8]{1,0:T(8,128)}, u32[]{:S(2)}) copy-start(s32[8,8]{1,0:T(8,128)} %param.12) | copy-start | bytes 772
  6.6 9.8 %copy-start.24 = (s32[8]{0:T(128)S(1)}, s32[8]{0:T(128)}, u32[]{:S(2)}) copy-start(s32[8]{0:T(128)} %param.13) | copy-start | bytes 100
  6.6 275.5 %all-reduce.6.cloned.1.call-start = ((), (), s32[]{:S(2)}) async-start(), calls=%async_computation.4 | async-start | bytes 2097152 | tf_op jit(solution)/shard_map/psum | solution.py:82
  8.1 13.2 %collective-permute-start = (bf16[2,8,20,512]{3,2,1,0:T(8,128)(2,1)S(1)}, bf16[2,8,20,512]{3,2,1,0:T(8,128)(2,1)S(1)}, u32[]{:S(2)}, u32[]{:S(2)}) collective-permute-start(bf16[2,8,20,512]{3,2,1,0:T(8,128)(2,1)S(1)} %get-tuple-element.229), channel_id=1, source_target_pairs={{0,1},{2,3},{4,5},{6,7},{8,9},{10,11},{12,13},{14,15},{16,17},{18,... | collective-permute-start | bytes 983048 | tf_op jit(solution)/shard_map/ppermute | solution.py:17
  13.0 12.5 %collective-permute-start.1 = (bf16[2,8,20,512]{3,2,1,0:T(8,128)(2,1)S(1)}, bf16[2,8,20,512]{3,2,1,0:T(8,128)(2,1)S(1)}, u32[]{:S(2)}, u32[]{:S(2)}) collective-permute-start(bf16[2,8,20,512]{3,2,1,0:T(8,128)(2,1)S(1)} %get-tuple-element.230), channel_id=1, source_target_pairs={{1,0},{3,2},{5,4},{7,6},{9,8},{11,10},{13,12},{15,14},{17,16},{19,... | collective-permute-start | bytes 983048 | tf_op jit(solution)/shard_map/ppermute | solution.py:19
  54.1 164.2 %copy-start.9 = (bf16[8,2,32,512]{3,2,0,1:T(8,128)(2,1)}, bf16[8,2,32,512]{3,2,0,1:T(8,128)(2,1)S(1)}, u32[]{:S(2)}) copy-start(bf16[8,2,32,512]{3,2,0,1:T(8,128)(2,1)S(1)} %get-tuple-element.12) | copy-start | bytes 1572868
  95.9 100.8 %copy-start.11 = (bf16[8,2,32,512]{3,2,0,1:T(8,128)(2,1)}, bf16[8,2,32,512]{3,2,0,1:T(8,128)(2,1)S(1)}, u32[]{:S(2)}) copy-start(bf16[8,2,32,512]{3,2,0,1:T(8,128)(2,1)S(1)} %get-tuple-element.28) | copy-start | bytes 1572868
  196.8 24.3 %copy-start.4 = (bf16[8,2,32,512]{3,2,1,0:T(8,128)(2,1)}, bf16[8,2,32,512]{3,2,1,0:T(8,128)(2,1)S(1)}, u32[]{:S(2)}) copy-start(bf16[8,2,32,512]{3,2,1,0:T(8,128)(2,1)S(1)} %get-tuple-element.68) | copy-start | bytes 1572868
  218.3 2.8 copy-start.7
  222.3 99.8 %reduce-scatter.5.cloned.1.call-start = ((), (), s32[]{:S(2)}) async-start(), calls=%async_computation.3 | async-start | bytes 589824 | tf_op jit(solution)/shard_map/reduce_scatter | solution.py:96
  222.5 1.0 copy-start.12
  223.6 1.0 copy-start.13
  224.6 1.0 copy-start.14
  225.7 1.2 copy-start.15
  226.8 1.1 copy-start.5
  227.9 1.1 copy-start.10
  229.1 1.1 copy-start.8
  282.1 1.5 copy-start
  282.1 1.9 copy-start.1
  282.1 2.0 copy-start.6
  284.1 2.1 copy-start.16
  287.7 1.2 copy-start.3
  287.9 1.4 copy-start.2
  290.0 1.8 copy-start.23
  291.6 62.3 %reduce-scatter.3.cloned.1.call-start = ((), (), s32[]{:S(2)}) async-start(), calls=%async_computation.2 | async-start | bytes 589824 | tf_op jit(solution)/shard_map/reduce_scatter | solution.py:95
Sparse Core Ops, SparseCore 0:
  222.4 59.6 all-reduce.5
  291.7 30.3 reduce-scatter.4
  324.4 29.3 reduce-scatter.2
where the time goes:
time: 364 us; the launch traced here: 362 us
  local copies, waits for them, and re-layouts  198 us (54%)
  waiting for transfers between devices  119 us (33%)
  other arithmetic  23.9 us (7%)
  between operations  13.9 us (4%)
  starting transfers between devices  6.49 us (2%)
    gather x192, local copies, waits for them, and re-layouts  182 us
    psum x1, waiting for transfers between devices, per_device(): whole_sums = lax.psum((first_sums[:, 0], first_sums[:, 1]), 'expo')  50.8 us
    reduce_scatter x1, waiting for transfers between devices, per_device(): lax.psum_scatter(jnp.stack(robust_signal), 'expo', scatter_dimension=1, t...  31.7 us
    reduce_scatter x1, waiting for transfers between devices, per_device(): lax.psum_scatter(jnp.stack(robust_depth), 'expo', scatter_dimension=1, ti...  28.5 us
    unnamed x81, local copies, waits for them, and re-layouts  8.68 us
  transfers between devices with their start and end apart: 5, of which 5 were waited for; matrix products, arithmetic and copies ran while one was open for 3% of the time, Pallas kernels for 0%

commit v1 on v0

v1 whole, which is shorter than its diff:
```python
import functools

import jax
import jax.numpy as jnp
from jax import lax
from jax.experimental import pallas as pl
from jax.experimental.pallas import tpu as pltpu
from jax.sharding import PartitionSpec as P

SHIFT = 16
LANES = 128
SUBLANES = 8

SMEM = pl.BlockSpec(memory_space=pltpu.SMEM)
VMEM = pl.BlockSpec(memory_space=pltpu.VMEM)


def partner(index, step, count):
    if count & (count - 1) == 0:
        return index ^ step
    return (index + step) % count


def chunk_pairs(step, chunks, subs):
    return [
        (j * subs + k, partner(j, step, chunks) * subs + k) for j in range(chunks) for k in range(subs)
    ]


def sub_pairs(step, chunks, subs):
    return [
        (j * subs + k, j * subs + partner(k, step, subs)) for j in range(chunks) for k in range(subs)
    ]


def filter_kernel(
    radius, chunks, info, row_taps, col_taps, row_shift, col_shift, usable, science, inv_var, above, below, *rest
):
    sends, (pixels, colpass, maps, edges, params) = rest[:chunks], rest[chunks:]
    exposures, rows, columns = science.shape
    taps = 2 * radius + 1
    halo = above.shape[2]
    reach = rows + SHIFT
    third = reach // 2
    tiles = columns // LANES
    lead = SUBLANES
    span = pixels.shape[1]
    lane = lax.broadcasted_iota(jnp.int32, (SUBLANES, LANES), 1)
    has_above = info[0] > 0
    has_below = info[1] > 0
    own = info[2]
    zero = jnp.zeros((SUBLANES, LANES), jnp.float32)

    params[...] = jnp.zeros_like(params)
    vels = row_shift.shape[1]
    params[:, 0:vels] = row_shift[...].astype(jnp.float32)
    params[:, vels : 2 * vels] = col_shift[...].astype(jnp.float32)
    params[:, 2 * vels : 2 * vels + 1] = usable[...].astype(jnp.float32)

    def one_exposure(e, carry):
        for kind, cells in ((0, science), (1, inv_var)):
            pixels[kind, lead : lead + rows] = cells[e].astype(jnp.float32)
            top = above[kind, e, halo - lead : halo].astype(jnp.float32)
            pixels[kind, 0:lead] = jnp.where(has_above, top, 0.0)
            low = below[kind, e].astype(jnp.float32)
            pixels[kind, lead + rows : lead + rows + halo] = jnp.where(has_below, low, 0.0)
        for g in range(span // SUBLANES):
            at = pl.ds(g * SUBLANES, SUBLANES)
            inverse = pixels[1, at]
            product = pixels[0, at] * inverse
            for m, picture in ((0, product), (1, inverse)):
                cut = [picture[:, t * LANES : (t + 1) * LANES] for t in range(tiles)]
                totals = [None] * tiles
                for b in range(taps):
                    step = b - radius
                    tap = col_taps[e, b]
                    if m == 1:
                        tap = tap * tap
                    if step == 0:
                        moved = cut
                    else:
                        turned = [pltpu.roll(c, (-step) % LANES, 1) for c in cut]
                        if step > 0:
                            turned = turned + [zero]
                            moved = [
                                jnp.where(lane < LANES - step, turned[t], turned[t + 1]) for t in range(tiles)
                            ]
                        else:
                            turned = [zero] + turned
                            moved = [
                                jnp.where(lane >= -step, turned[t + 1], turned[t]) for t in range(tiles)
                            ]
                    for t in range(tiles):
                        term = tap * moved[t]
                        totals[t] = term if totals[t] is None else totals[t] + term
                for t in range(tiles):
                    colpass[m, t, at] = totals[t]

        def padded_group(m, g):
            out = []
            for t in range(tiles):
                total = None
                for a in range(taps):
                    tap = row_taps[e, a]
                    if m == 1:
                        tap = tap * tap
                    term = tap * colpass[m, t, pl.ds(g * SUBLANES + lead - radius + a, SUBLANES)]
                    total = term if total is None else total + term
                if g * SUBLANES >= rows:
                    total = jnp.where(has_below, total, 0.0)
                out.append(pltpu.roll(total, SHIFT, 1))
            out = [zero] + out + [zero]
            return [jnp.where(lane < SHIFT, out[t], out[t + 1]) for t in range(tiles + 1)]

        for g in range(third // SUBLANES):
            parts = [padded_group(m, g + h * (third // SUBLANES)) for m in (0, 1) for h in (0, 1)]
            for t in range(tiles):
                for q, part in enumerate(parts):
                    at = (q // 2) * exposures * reach + e * reach + (q % 2) * third + g * SUBLANES
                    maps[t, pl.ds(pl.multiple_of(at, SUBLANES), SUBLANES)] = part[t]
                packed = parts[0][t + 1]
                for q in range(1, 4):
                    packed = jnp.where(lane < 2 * SHIFT * q, packed, pltpu.roll(parts[q][t + 1], 2 * SHIFT * q, 1))
                at = e * third + g * SUBLANES
                edges[t, pl.ds(pl.multiple_of(at, SUBLANES), SUBLANES)] = packed
        return carry

    lax.fori_loop(0, exposures, one_exposure, 0)
    main = 2 * exposures * reach
    edge = exposures * third
    for step in range(chunks):
        to = partner(own, step, chunks)
        sends[step][0:main] = maps[to].astype(jnp.bfloat16)
        sends[step][main : main + edge] = edges[to].astype(jnp.bfloat16)
        sends[step][main + edge : main + edge + exposures] = params[...].astype(jnp.bfloat16)


def stack_kernel(
    groups, chunks, exposures, rows, vels, share, info, *rest
):
    blocks = rest[:groups]
    outs = rest[groups : groups + chunks]
    main, side, windows, edge, whole_params, scalars, result, sem = rest[groups + chunks :]
    reach = rows + SHIFT
    third = reach // 2
    own = info[0]
    first_vel = info[1]
    main_rows = 2 * exposures * reach
    edge_rows = exposures * third
    total = groups * exposures
    for g in range(groups):
        whole_params[g * exposures : (g + 1) * exposures] = (
            blocks[g][main_rows + edge_rows : main_rows + edge_rows + exposures].astype(jnp.float32).astype(jnp.int32)
        )
    fetch = pltpu.make_async_copy(whole_params, scalars, sem)
    fetch.start()
    fetch.wait()
    for g in range(groups):
        edge[...] = blocks[g][main_rows : main_rows + edge_rows].astype(jnp.float32)

        def unpack(e, carry, g=g):
            at = g * exposures + e
            keep = scalars[at, 2 * vels].astype(jnp.float32)
            for m in (0, 1):
                start = pl.multiple_of(m * exposures * reach + e * reach, reach)
                main[at, m] = blocks[g][pl.ds(start, reach)].astype(jnp.float32) * keep
            packed = edge[pl.ds(pl.multiple_of(e * third, SUBLANES), third)] * keep
            for q in range(4):
                piece = packed if q == 0 else pltpu.roll(packed, LANES - 2 * SHIFT * q, 1)
                side[at, q // 2, (q % 2) * third : (q % 2 + 1) * third] = piece
            return carry

        lax.fori_loop(0, exposures, unpack, 0)

    lane = lax.broadcasted_iota(jnp.int32, (rows, LANES), 1)
    zeros = jnp.zeros((rows, LANES), jnp.float32)

    def one_velocity(v, carry):
        def gather(e, sums):
            row_at = scalars[e, first_vel + v]
            col_at = scalars[e, vels + first_vel + v] + SHIFT
            turn = lax.rem(LANES - col_at, LANES)
            from_side = lane < col_at
            out = []
            for m in (0, 1):
                cells = jnp.where(
                    from_side, side[e, m, pl.ds(row_at, rows)], main[e, m, pl.ds(row_at, rows)]
                )
                cells = pltpu.roll(cells, turn, 1)
                windows[e, m] = cells
                out.append(sums[m] + cells)
            return tuple(out)

        signal_sum, depth_sum = lax.fori_loop(0, total, gather, (zeros, zeros), unroll=2)
        flux = signal_sum / (depth_sum + 1.0)

        def reweigh(e, sums):
            signal = windows[e, 0]
            depth = windows[e, 1]
            residual = signal - flux * depth
            base = depth + 1.0
            weight = base / (base + residual * residual)
            return sums[0] + weight * signal, sums[1] + weight * depth

        robust = lax.fori_loop(0, total, reweigh, (zeros, zeros), unroll=2)
        result[v] = robust[0] / jnp.sqrt(robust[1] + 1.0)
        return carry

    lax.fori_loop(0, share, one_velocity, 0)
    block = rows // chunks
    for step in range(chunks):
        to = partner(own, step, chunks)
        outs[step][...] = result[:, pl.ds(pl.multiple_of(to * block, block), block)]


def columns_kernel(chunks, subs, info, *rest):
    pieces = rest[:chunks]
    outs = rest[chunks : chunks + subs]
    held, wide = rest[chunks + subs :]
    own_chunk, own_sub = info[0], info[1]
    for step in range(chunks):
        held[step] = pieces[step][...]
    rows = wide.shape[2]
    for c in range(chunks):
        piece = held[partner(own_chunk, c, chunks)]
        for k in range(subs):
            wide[k, :, :, c * LANES : (c + 1) * LANES] = piece[:, k * rows : (k + 1) * rows]
    for step in range(subs):
        outs[step][...] = wide[partner(own_sub, step, subs)]


def velocities_kernel(subs, info, *rest):
    pieces = rest[:subs]
    out, held = rest[subs:]
    own_sub = info[1]
    for step in range(subs):
        held[step] = pieces[step][...]
    share = held.shape[1]
    for k in range(subs):
        out[k * share : (k + 1) * share] = held[partner(own_sub, k, subs)]


def per_device(science, inv_var, psf_rows, psf_cols, row_shift, col_shift, exposure_ok):
    exposures, rows, columns = science.shape
    vels = row_shift.shape[1]
    radius = psf_rows.shape[1] // 2
    strips = lax.axis_size("strip")
    members = lax.axis_size("expo")
    chunks = columns // LANES
    subs = members // chunks
    share = vels // subs
    reach = rows + SHIFT
    halo = -(-(radius + SHIFT) // SUBLANES) * SUBLANES
    strip = lax.axis_index("strip")
    me = lax.axis_index("expo")
    own_chunk = me // subs
    own_sub = me % subs

    head = jnp.stack([science[:, :halo], inv_var[:, :halo]])
    tail = jnp.stack([science[:, rows - halo :], inv_var[:, rows - halo :]])
    if strips == 2:
        met = lax.ppermute(jnp.where(strip == 0, tail, head), "strip", [(0, 1), (1, 0)])
        above = below = met
    else:
        above = lax.ppermute(tail, "strip", [(i, i + 1) for i in range(strips - 1)])
        below = lax.ppermute(head, "strip", [(i + 1, i) for i in range(strips - 1)])
    info = jnp.stack([strip > 0, strip < strips - 1, own_chunk]).astype(jnp.int32)

    main_rows = 2 * exposures * reach
    edge_rows = exposures * reach // 2
    sent_rows = main_rows + edge_rows + exposures
    span = rows + halo + SUBLANES
    sent = jax.ShapeDtypeStruct((sent_rows, LANES), jnp.bfloat16)
    sends = pl.pallas_call(
        functools.partial(filter_kernel, radius, chunks),
        out_shape=[sent] * chunks,
        in_specs=[SMEM] * 3 + [VMEM] * 7,
        out_specs=[VMEM] * chunks,
        scratch_shapes=[
            pltpu.VMEM((2, span, columns), jnp.float32),
            pltpu.VMEM((2, chunks, span, LANES), jnp.float32),
            pltpu.VMEM((chunks, main_rows, LANES), jnp.float32),
            pltpu.VMEM((chunks, edge_rows, LANES), jnp.float32),
            pltpu.VMEM((exposures, LANES), jnp.float32),
        ],
        name="filter_maps",
    )(info, psf_rows, psf_cols, row_shift, col_shift, exposure_ok[:, None], science, inv_var, above, below)

    blocks = [sends[0]]
    for step in range(1, chunks):
        blocks.append(lax.ppermute(sends[step], "expo", chunk_pairs(step, chunks, subs)))
    for step in range(1, subs):
        pairs = sub_pairs(step, chunks, subs)
        blocks += [lax.ppermute(block, "expo", pairs) for block in blocks[:chunks]]

    groups = len(blocks)
    block_rows = rows // chunks
    piece = jax.ShapeDtypeStruct((share, block_rows, LANES), jnp.float32)
    where = jnp.stack([own_chunk, own_sub * share]).astype(jnp.int32)
    total = groups * exposures
    pieces = pl.pallas_call(
        functools.partial(stack_kernel, groups, chunks, exposures, rows, vels, share),
        out_shape=[piece] * chunks,
        in_specs=[SMEM] + [VMEM] * groups,
        out_specs=[VMEM] * chunks,
        scratch_shapes=[
            pltpu.VMEM((total, 2, reach, LANES), jnp.float32),
            pltpu.VMEM((total, 2, reach, LANES), jnp.float32),
            pltpu.VMEM((total, 2, rows, LANES), jnp.float32),
            pltpu.VMEM((edge_rows, LANES), jnp.float32),
            pltpu.VMEM((total, LANES), jnp.int32),
            pltpu.SMEM((total, LANES), jnp.int32),
            pltpu.VMEM((share, rows, LANES), jnp.float32),
            pltpu.SemaphoreType.DMA(()),
        ],
        name="stack_twice",
    )(where, *blocks)

    held = [pieces[0]]
    for step in range(1, chunks):
        held.append(lax.ppermute(pieces[step], "expo", chunk_pairs(step, chunks, subs)))
    place = jnp.stack([own_chunk, own_sub]).astype(jnp.int32)
    out_rows = block_rows // subs
    wide = jax.ShapeDtypeStruct((share, out_rows, columns), jnp.float32)
    parts = pl.pallas_call(
        functools.partial(columns_kernel, chunks, subs),
        out_shape=[wide] * subs,
        in_specs=[SMEM] + [VMEM] * chunks,
        out_specs=[VMEM] * subs,
        scratch_shapes=[
            pltpu.VMEM((chunks, share, block_rows, LANES), jnp.float32),
            pltpu.VMEM((subs, share, out_rows, columns), jnp.float32),
        ],
        name="join_columns",
    )(place, *held)
    met = [parts[0]]
    for step in range(1, subs):
        met.append(lax.ppermute(parts[step], "expo", sub_pairs(step, chunks, subs)))
    likelihood = pl.pallas_call(
        functools.partial(velocities_kernel, subs),
        out_shape=jax.ShapeDtypeStruct((vels, out_rows, columns), jnp.float32),
        in_specs=[SMEM] + [VMEM] * subs,
        out_specs=VMEM,
        scratch_shapes=[pltpu.VMEM((subs, share, out_rows, columns), jnp.float32)],
        name="join_velocities",
    )(place, *met)
    return likelihood[None]


def solution(mesh):
    in_specs = (
        P(("field", "expo"), "strip", None),
        P(("field", "expo"), "strip", None),
        P(("field", "expo"), None),
        P(("field", "expo"), None),
        P(("field", "expo"), None),
        P(("field", "expo"), None),
        P(("field", "expo")),
    )
    out_specs = P("strip", "field", "expo", None)
    return jax.shard_map(
        per_device, mesh=mesh, in_specs=in_specs, out_specs=out_specs, check_vma=False
    )
```

time: 364 us -> 85.6 us (0.24)
  local copies, waits for them, and re-layouts: 198 us -> 5.66 us
  waiting for transfers between devices: 119 us -> 31 us
  Pallas kernels: 0 us -> 33.1 us
  other arithmetic: 23.9 us -> 1.93 us
  between operations: 13.9 us -> 0.08 us
  starting transfers between devices: 6.49 us -> 13.5 us
    gather x192 -> x0, local copies, waits for them, and re-layouts: 182 us -> none
    reduce_scatter x2 -> x0, waiting for transfers between devices: 60.2 us -> none  [the longest x1 31.7 us: per_device(): lax.psum_scatter(jnp.stack(robust_signal), 'expo', scatter_dimension=1, t...]
    psum x1 -> x0, waiting for transfers between devices: 50.8 us -> none  [per_device(): whole_sums = lax.psum((first_sums[:, 0], first_sums[:, 1]), 'expo')]
    pallas_call x0 -> x4, Pallas kernels: none -> 33.1 us  [the longest x1 22.4 us: per_device(): pl.pallas_call(functools.partial(stack_kernel, groups, chunks, exposures,...]
    ppermute x2 -> x12, waiting for transfers between devices: 8.27 us -> 31 us  [the longest x3 18 us: per_device(): lax.ppermute(sends[step], 'expo', chunk_pairs(step, chunks, subs))]
    ppermute x2 -> x12, starting transfers between devices: 6.19 us -> 13.5 us  [the longest x3 5.5 us: per_device(): lax.ppermute(pieces[step], 'expo', chunk_pairs(step, chunks, subs))]
    convert_element_type x10 -> x0, other arithmetic: 6.1 us -> none  [the longest x8 5.94 us: cut_all(): jax.vmap(cut_one)(padded, row_shift[:, velocity], col_shift[:, velocity])]
    unnamed x81 -> x26, local copies, waits for them, and re-layouts: 8.68 us -> 3.7 us
  transfers between devices with their start and end apart: 5 -> 12, of which waited for: 5 -> 8; matrix products, arithmetic and copies ran while one was open for 3% -> 3% of each run, Pallas kernels for 0% -> 0%
where the time goes in v1:
time: 85.6 us; the launch traced here: 85.2 us
  Pallas kernels  33.1 us (39%)
  waiting for transfers between devices  31 us (36%)
  starting transfers between devices  13.5 us (16%)
  local copies, waits for them, and re-layouts  5.66 us (7%)
  other arithmetic  1.93 us (2%)
    pallas_call x1, Pallas kernels, per_device(): pl.pallas_call(functools.partial(stack_kernel, groups, chunks, exposures,...  22.4 us
    ppermute x3, waiting for transfers between devices, per_device(): lax.ppermute(sends[step], 'expo', chunk_pairs(step, chunks, subs))  18 us
    pallas_call x1, Pallas kernels, per_device(): pl.pallas_call(functools.partial(filter_kernel, radius, chunks), out_shap...  7.83 us
    ppermute x1, waiting for transfers between devices, per_device(): lax.ppermute(jnp.where(strip == 0, tail, head), 'strip', [(0, 1), (1, 0)])  7.18 us
    ppermute x3, starting transfers between devices, per_device(): lax.ppermute(pieces[step], 'expo', chunk_pairs(step, chunks, subs))  5.5 us
    ppermute x3, starting transfers between devices, per_device(): lax.ppermute(sends[step], 'expo', chunk_pairs(step, chunks, subs))  4.42 us
    unnamed x26, local copies, waits for them, and re-layouts  3.7 us
    ppermute x3, waiting for transfers between devices, per_device(): lax.ppermute(pieces[step], 'expo', chunk_pairs(step, chunks, subs))  3.69 us
  transfers between devices with their start and end apart: 12, of which 8 were waited for; matrix products, arithmetic and copies ran while one was open for 3% of the time, Pallas kernels for 0%

profile of v1, /device:TPU:0, one launch (start us, length us, event | category | flops | bytes accessed | tf_op | source)
XLA Modules:
  0.0 85.2 jit_solution(7575187675182343639)
XLA Ops:
  0.0 1.3 %slice_bitcast_fusion = (bf16[1,8,24,512]{3,2,1,0:T(8,128)(2,1)S(1)}, bf16[1,8,24,512]{3,2,1,0:T(8,128)(2,1)S(1)}, bf16[1,8,24,512]{3,2,1,0:T(8,128)(2,1)S(1)}, bf16[1,8,24,512]{3,2,1,0:T(8,128)(2,1)S(1)}) fusion(bf16[8,32,512]{2,1,0:T(8,128)(2,1)} %inv_var.1, bf16[8,32,512]{2,1,0:T(8,128)(2,1)} %science.1), kind=kLoop, calls=%fused_computation.1 | loop fusion | bytes 1572864 | tf_op jit(solution)/shard_map/stack | solution.py:259
  1.3 0.1 maximum_select_fusion
  1.4 3.0 %collective-permute-start = (bf16[2,8,24,512]{3,2,1,0:T(8,128)(2,1)S(1)}, bf16[2,8,24,512]{3,2,1,0:T(8,128)(2,1)S(1)}, u32[]{:S(2)}, u32[]{:S(2)}) collective-permute-start(bf16[2,8,24,512]{3,2,1,0:T(8,128)(2,1)S(1)} %maximum_select_fusion), channel_id=1, source_target_pairs={{0,1},{1,0},{2,3},{3,2},{4,5},{5,4},{6,7},{7,6},{8,9},{9,8},{10,11... | collective-permute-start | bytes 1179656 | tf_op jit(solution)/shard_map/ppermute | solution.py:262
  4.4 0.7 copy-done.12
  5.1 0.7 copy.8.usable
  5.7 0.6 pad_add_fusion.2.info
  6.3 7.2 %collective-permute-done.above.below = bf16[2,8,24,512]{3,2,1,0:T(8,128)(2,1)S(1)} collective-permute-done((bf16[2,8,24,512]{3,2,1,0:T(8,128)(2,1)S(1)}, bf16[2,8,24,512]{3,2,1,0:T(8,128)(2,1)S(1)}, u32[]{:S(2)}, u32[]{:S(2)}) %collective-permute-start) | collective-permute-done | bytes 393248 | tf_op jit(solution)/shard_map/ppermute | solution.py:262
  13.5 0.7 copy-done
  14.3 7.8 %filter_maps.1 = (bf16[968,128]{1,0:T(8,128)(2,1)}, bf16[968,128]{1,0:T(8,128)(2,1)}, bf16[968,128]{1,0:T(8,128)(2,1)}, bf16[968,128]{1,0:T(8,128)(2,1)}) custom-call(s32[3]{0:T(128)} %pad_add_fusion.2.info, f32[8,9]{1,0:T(8,128)} %row_taps.1, f32[8,9]{1,0:T(8,128)} %col_taps.1, s32[8,8]{1,0:T(8,128)} %row_shift.1, s32[8,8]{1,0:T(8,128)} %col_shift.1, ...), custom_call_target="tpu_custom_call" | custom-call | tf_op jit(solution)/shard_map/filter_maps/pallas_call | solution.py:274
  22.1 1.8 %collective-permute-start.1 = (bf16[968,128]{1,0:T(8,128)(2,1)}, bf16[968,128]{1,0:T(8,128)(2,1)S(1)}, u32[]{:S(2)}, u32[]{:S(2)}) collective-permute-start(bf16[968,128]{1,0:T(8,128)(2,1)} %get-tuple-element.16), channel_id=1, source_target_pairs={{0,4},{2,6},{4,0},{6,2},{8,12},{10,14},{12,8},{14,10},{1,5},{3,7},... | collective-permute-start | bytes 743432 | tf_op jit(solution)/shard_map/ppermute | solution.py:291
  23.9 2.6 %collective-permute-start.2 = (bf16[968,128]{1,0:T(8,128)(2,1)}, bf16[968,128]{1,0:T(8,128)(2,1)S(1)}, u32[]{:S(2)}, u32[]{:S(2)}) collective-permute-start(bf16[968,128]{1,0:T(8,128)(2,1)} %get-tuple-element.17), channel_id=1, source_target_pairs={{0,8},{2,10},{4,12},{6,14},{8,0},{10,2},{12,4},{14,6},{1,9},{3,11}... | collective-permute-start | bytes 743432 | tf_op jit(solution)/shard_map/ppermute | solution.py:291
  26.5 0.0 collective-permute-start.3
  26.5 0.0 collective-permute-start.4
  26.5 7.1 %collective-permute-done.1.rest_1_ = bf16[968,128]{1,0:T(8,128)(2,1)S(1)} collective-permute-done((bf16[968,128]{1,0:T(8,128)(2,1)}, bf16[968,128]{1,0:T(8,128)(2,1)S(1)}, u32[]{:S(2)}, u32[]{:S(2)}) %collective-permute-start.1) | collective-permute-done | bytes 247840 | tf_op jit(solution)/shard_map/ppermute | solution.py:291
  33.6 0.0 collective-permute-start.5
  33.6 10.9 %collective-permute-done.2.rest_2_ = bf16[968,128]{1,0:T(8,128)(2,1)S(1)} collective-permute-done((bf16[968,128]{1,0:T(8,128)(2,1)}, bf16[968,128]{1,0:T(8,128)(2,1)S(1)}, u32[]{:S(2)}, u32[]{:S(2)}) %collective-permute-start.2) | collective-permute-done | bytes 247840 | tf_op jit(solution)/shard_map/ppermute | solution.py:291
  44.5 0.0 collective-permute-start.6
  44.5 0.0 collective-permute-done.3.rest_3_
  44.5 0.0 copy-start.3
  44.5 0.5 collective-permute-start.7
  45.0 0.6 pad_add_fusion.1.info
  45.6 0.0 collective-permute-done.4.rest_4_
  45.6 0.0 collective-permute-done.5.rest_5_
  45.6 0.0 copy-start.5
  45.6 0.4 collective-permute-done.6.rest_6_
  46.0 0.4 collective-permute-done.7.rest_7_
  46.4 0.0 copy-done.1
  46.4 0.0 copy-done.2
  46.4 0.0 copy-done.3
  46.4 0.0 copy-done.4
  46.4 0.0 copy-done.5
  46.4 0.3 copy-done.6
  46.8 0.7 copy-done.7
  47.5 22.4 %stack_twice.1 = (f32[4,8,128]{2,1,0:T(8,128)}, f32[4,8,128]{2,1,0:T(8,128)}, f32[4,8,128]{2,1,0:T(8,128)}, f32[4,8,128]{2,1,0:T(8,128)}) custom-call(s32[2]{0:T(128)} %pad_add_fusion.1.info, bf16[968,128]{1,0:T(8,128)(2,1)} %get-tuple-element.15.rest_0_, bf16[968,128]{1,0:T(8,128)(2,1)} %copy-done.1, bf16[968,128]{1,0:T(8,128)(2,1)} %copy-done.2, ...), custom_call_target="tpu_custom_call" | custom-call | tf_op jit(solution)/shard_map/stack_twice/pallas_call | solution.py:301
  69.9 3.0 %collective-permute-start.8 = (f32[4,8,128]{2,1,0:T(8,128)}, f32[4,8,128]{2,1,0:T(8,128)S(1)}, u32[]{:S(2)}, u32[]{:S(2)}) collective-permute-start(f32[4,8,128]{2,1,0:T(8,128)} %get-tuple-element.20), channel_id=1, source_target_pairs={{0,4},{2,6},{4,0},{6,2},{8,12},{10,14},{12,8},{14,10},{1,5},{3,7},... | collective-permute-start | bytes 49160 | tf_op jit(solution)/shard_map/ppermute | solution.py:321
  72.9 1.1 %collective-permute-start.9 = (f32[4,8,128]{2,1,0:T(8,128)}, f32[4,8,128]{2,1,0:T(8,128)S(1)}, u32[]{:S(2)}, u32[]{:S(2)}) collective-permute-start(f32[4,8,128]{2,1,0:T(8,128)} %get-tuple-element.21), channel_id=1, source_target_pairs={{0,8},{2,10},{4,12},{6,14},{8,0},{10,2},{12,4},{14,6},{1,9},{3,11}... | collective-permute-start | bytes 49160 | tf_op jit(solution)/shard_map/ppermute | solution.py:321
  74.0 1.4 %collective-permute-start.10 = (f32[4,8,128]{2,1,0:T(8,128)}, f32[4,8,128]{2,1,0:T(8,128)S(1)}, u32[]{:S(2)}, u32[]{:S(2)}) collective-permute-start(f32[4,8,128]{2,1,0:T(8,128)} %get-tuple-element.22), channel_id=1, source_target_pairs={{0,12},{2,14},{4,8},{6,10},{8,4},{10,6},{12,0},{14,2},{1,13},{3,15... | collective-permute-start | bytes 49160 | tf_op jit(solution)/shard_map/ppermute | solution.py:321
  75.4 0.7 pad_add_fusion.info
  76.0 0.0 collective-permute-done.8.rest_1_
  76.0 1.7 %collective-permute-done.9.rest_2_ = f32[4,8,128]{2,1,0:T(8,128)S(1)} collective-permute-done((f32[4,8,128]{2,1,0:T(8,128)}, f32[4,8,128]{2,1,0:T(8,128)S(1)}, u32[]{:S(2)}, u32[]{:S(2)}) %collective-permute-start.9) | collective-permute-done | bytes 16416 | tf_op jit(solution)/shard_map/ppermute | solution.py:321
  77.7 2.0 %collective-permute-done.10.rest_3_ = f32[4,8,128]{2,1,0:T(8,128)S(1)} collective-permute-done((f32[4,8,128]{2,1,0:T(8,128)}, f32[4,8,128]{2,1,0:T(8,128)S(1)}, u32[]{:S(2)}, u32[]{:S(2)}) %collective-permute-start.10) | collective-permute-done | bytes 16416 | tf_op jit(solution)/shard_map/ppermute | solution.py:321
  79.7 0.0 copy-done.9
  79.7 0.6 copy-done.11
  80.3 1.4 %join_columns.1 = (f32[4,4,512]{2,1,0:T(4,128)}, f32[4,4,512]{2,1,0:T(4,128)}) custom-call(s32[2]{0:T(128)} %pad_add_fusion.info, f32[4,8,128]{2,1,0:T(8,128)} %get-tuple-element.19.rest_0_, f32[4,8,128]{2,1,0:T(8,128)} %copy-done.9, f32[4,8,128]{2,1,0:T(8,128)} %copy-done.10, f32[4,8,128]{2,1,0:T(8,128)} %copy-done.11), custom_call_target="tpu_custom_call" | custom-call | tf_op jit(solution)/shard_map/join_columns/pallas_call | solution.py:325
  81.8 0.0 collective-permute-start.11
  81.8 1.4 %collective-permute-done.11.rest_1_ = f32[4,4,512]{2,1,0:T(4,128)S(1)} collective-permute-done((f32[4,4,512]{2,1,0:T(4,128)}, f32[4,4,512]{2,1,0:T(4,128)S(1)}, u32[]{:S(2)}, u32[]{:S(2)}) %collective-permute-start.11) | collective-permute-done | bytes 32800 | tf_op jit(solution)/shard_map/ppermute | solution.py:338
  83.2 0.6 copy-done.8
  83.8 1.4 %join_velocities.1 = f32[8,4,512]{2,1,0:T(4,128)} custom-call(s32[2]{0:T(128)} %pad_add_fusion.info, f32[4,4,512]{2,1,0:T(4,128)} %get-tuple-element.23.rest_0_, f32[4,4,512]{2,1,0:T(4,128)} %copy-done.8), custom_call_target="tpu_custom_call" | custom-call | tf_op jit(solution)/shard_map/join_velocities/pallas_call | solution.py:339
  (12 shorter events, 0.0 us)
Async XLA Ops:
  1.4 12.1 %collective-permute-start = (bf16[2,8,24,512]{3,2,1,0:T(8,128)(2,1)S(1)}, bf16[2,8,24,512]{3,2,1,0:T(8,128)(2,1)S(1)}, u32[]{:S(2)}, u32[]{:S(2)}) collective-permute-start(bf16[2,8,24,512]{3,2,1,0:T(8,128)(2,1)S(1)} %maximum_select_fusion), channel_id=1, source_target_pairs={{0,1},{1,0},{2,3},{3,2},{4,5},{5,4},{6,7},{7,6},{8,9},{9,8},{10,11... | collective-permute-start | bytes 1179656 | tf_op jit(solution)/shard_map/ppermute | solution.py:262
  4.4 0.7 copy-start.12
  13.5 0.7 copy-start
  22.1 11.5 %collective-permute-start.1 = (bf16[968,128]{1,0:T(8,128)(2,1)}, bf16[968,128]{1,0:T(8,128)(2,1)S(1)}, u32[]{:S(2)}, u32[]{:S(2)}) collective-permute-start(bf16[968,128]{1,0:T(8,128)(2,1)} %get-tuple-element.16), channel_id=1, source_target_pairs={{0,4},{2,6},{4,0},{6,2},{8,12},{10,14},{12,8},{14,10},{1,5},{3,7},... | collective-permute-start | bytes 743432 | tf_op jit(solution)/shard_map/ppermute | solution.py:291
  23.9 20.6 %collective-permute-start.2 = (bf16[968,128]{1,0:T(8,128)(2,1)}, bf16[968,128]{1,0:T(8,128)(2,1)S(1)}, u32[]{:S(2)}, u32[]{:S(2)}) collective-permute-start(bf16[968,128]{1,0:T(8,128)(2,1)} %get-tuple-element.17), channel_id=1, source_target_pairs={{0,8},{2,10},{4,12},{6,14},{8,0},{10,2},{12,4},{14,6},{1,9},{3,11}... | collective-permute-start | bytes 743432 | tf_op jit(solution)/shard_map/ppermute | solution.py:291
  26.5 18.0 %collective-permute-start.3 = (bf16[968,128]{1,0:T(8,128)(2,1)}, bf16[968,128]{1,0:T(8,128)(2,1)S(1)}, u32[]{:S(2)}, u32[]{:S(2)}) collective-permute-start(bf16[968,128]{1,0:T(8,128)(2,1)} %get-tuple-element.18), channel_id=1, source_target_pairs={{0,12},{2,14},{4,8},{6,10},{8,4},{10,6},{12,0},{14,2},{1,13},{3,15... | collective-permute-start | bytes 743432 | tf_op jit(solution)/shard_map/ppermute | solution.py:291
  26.5 19.1 %collective-permute-start.4 = (bf16[968,128]{1,0:T(8,128)(2,1)}, bf16[968,128]{1,0:T(8,128)(2,1)S(1)}, u32[]{:S(2)}, u32[]{:S(2)}) collective-permute-start(bf16[968,128]{1,0:T(8,128)(2,1)} %get-tuple-element.15.rest_0_), channel_id=1, source_target_pairs={{0,2},{2,0},{4,6},{6,4},{8,10},{10,8},{12,14},{14,12},{1,3},{3,1},... | collective-permute-start | bytes 743432 | tf_op jit(solution)/shard_map/ppermute | solution.py:294
  33.6 12.8 %copy-start.1 = (bf16[968,128]{1,0:T(8,128)(2,1)}, bf16[968,128]{1,0:T(8,128)(2,1)S(1)}, u32[]{:S(2)}) copy-start(bf16[968,128]{1,0:T(8,128)(2,1)S(1)} %collective-permute-done.1.rest_1_) | copy-start | bytes 743428
  33.6 12.0 %collective-permute-start.5 = (bf16[968,128]{1,0:T(8,128)(2,1)S(1)}, bf16[968,128]{1,0:T(8,128)(2,1)S(1)}, u32[]{:S(2)}, u32[]{:S(2)}) collective-permute-start(bf16[968,128]{1,0:T(8,128)(2,1)S(1)} %collective-permute-done.1.rest_1_), channel_id=1, source_target_pairs={{0,2},{2,0},{4,6},{6,4},{8,10},{10,8},{12,14},{14,12},{1,3},{3,1},... | collective-permute-start | bytes 743432 | tf_op jit(solution)/shard_map/ppermute | solution.py:294
  44.5 1.9 %copy-start.2 = (bf16[968,128]{1,0:T(8,128)(2,1)}, bf16[968,128]{1,0:T(8,128)(2,1)S(1)}, u32[]{:S(2)}) copy-start(bf16[968,128]{1,0:T(8,128)(2,1)S(1)} %collective-permute-done.2.rest_2_) | copy-start | bytes 743428
  44.5 1.5 %collective-permute-start.6 = (bf16[968,128]{1,0:T(8,128)(2,1)S(1)}, bf16[968,128]{1,0:T(8,128)(2,1)S(1)}, u32[]{:S(2)}, u32[]{:S(2)}) collective-permute-start(bf16[968,128]{1,0:T(8,128)(2,1)S(1)} %collective-permute-done.2.rest_2_), channel_id=1, source_target_pairs={{0,2},{2,0},{4,6},{6,4},{8,10},{10,8},{12,14},{14,12},{1,3},{3,1},... | collective-permute-start | bytes 743432 | tf_op jit(solution)/shard_map/ppermute | solution.py:294
  44.5 1.9 %copy-start.3 = (bf16[968,128]{1,0:T(8,128)(2,1)}, bf16[968,128]{1,0:T(8,128)(2,1)S(1)}, u32[]{:S(2)}) copy-start(bf16[968,128]{1,0:T(8,128)(2,1)S(1)} %collective-permute-done.3.rest_3_) | copy-start | bytes 743428
  44.5 1.9 %collective-permute-start.7 = (bf16[968,128]{1,0:T(8,128)(2,1)S(1)}, bf16[968,128]{1,0:T(8,128)(2,1)S(1)}, u32[]{:S(2)}, u32[]{:S(2)}) collective-permute-start(bf16[968,128]{1,0:T(8,128)(2,1)S(1)} %collective-permute-done.3.rest_3_), channel_id=1, source_target_pairs={{0,2},{2,0},{4,6},{6,4},{8,10},{10,8},{12,14},{14,12},{1,3},{3,1},... | collective-permute-start | bytes 743432 | tf_op jit(solution)/shard_map/ppermute | solution.py:294
  45.6 0.8 copy-start.4
  45.6 0.8 copy-start.5
  46.0 0.7 copy-start.6
  46.8 0.7 copy-start.7
  69.9 6.2 %collective-permute-start.8 = (f32[4,8,128]{2,1,0:T(8,128)}, f32[4,8,128]{2,1,0:T(8,128)S(1)}, u32[]{:S(2)}, u32[]{:S(2)}) collective-permute-start(f32[4,8,128]{2,1,0:T(8,128)} %get-tuple-element.20), channel_id=1, source_target_pairs={{0,4},{2,6},{4,0},{6,2},{8,12},{10,14},{12,8},{14,10},{1,5},{3,7},... | collective-permute-start | bytes 49160 | tf_op jit(solution)/shard_map/ppermute | solution.py:321
  72.9 4.8 %collective-permute-start.9 = (f32[4,8,128]{2,1,0:T(8,128)}, f32[4,8,128]{2,1,0:T(8,128)S(1)}, u32[]{:S(2)}, u32[]{:S(2)}) collective-permute-start(f32[4,8,128]{2,1,0:T(8,128)} %get-tuple-element.21), channel_id=1, source_target_pairs={{0,8},{2,10},{4,12},{6,14},{8,0},{10,2},{12,4},{14,6},{1,9},{3,11}... | collective-permute-start | bytes 49160 | tf_op jit(solution)/shard_map/ppermute | solution.py:321
  74.0 5.7 %collective-permute-start.10 = (f32[4,8,128]{2,1,0:T(8,128)}, f32[4,8,128]{2,1,0:T(8,128)S(1)}, u32[]{:S(2)}, u32[]{:S(2)}) collective-permute-start(f32[4,8,128]{2,1,0:T(8,128)} %get-tuple-element.22), channel_id=1, source_target_pairs={{0,12},{2,14},{4,8},{6,10},{8,4},{10,6},{12,0},{14,2},{1,13},{3,15... | collective-permute-start | bytes 49160 | tf_op jit(solution)/shard_map/ppermute | solution.py:321
  76.0 3.7 %copy-start.9 = (f32[4,8,128]{2,1,0:T(8,128)}, f32[4,8,128]{2,1,0:T(8,128)S(1)}, u32[]{:S(2)}) copy-start(f32[4,8,128]{2,1,0:T(8,128)S(1)} %collective-permute-done.8.rest_1_) | copy-start | bytes 49156
  77.7 2.0 %copy-start.10 = (f32[4,8,128]{2,1,0:T(8,128)}, f32[4,8,128]{2,1,0:T(8,128)S(1)}, u32[]{:S(2)}) copy-start(f32[4,8,128]{2,1,0:T(8,128)S(1)} %collective-permute-done.9.rest_2_) | copy-start | bytes 49156
  79.7 0.6 copy-start.11
  81.8 1.4 %collective-permute-start.11 = (f32[4,4,512]{2,1,0:T(4,128)}, f32[4,4,512]{2,1,0:T(4,128)S(1)}, u32[]{:S(2)}, u32[]{:S(2)}) collective-permute-start(f32[4,4,512]{2,1,0:T(4,128)} %get-tuple-element.24), channel_id=1, source_target_pairs={{0,2},{2,0},{4,6},{6,4},{8,10},{10,8},{12,14},{14,12},{1,3},{3,1},... | collective-permute-start | bytes 98312 | tf_op jit(solution)/shard_map/ppermute | solution.py:338
  83.2 0.6 copy-start.8

commit v2 on v1

--- a/solution.py
+++ b/solution.py
@@ -10,6 +10,7 @@
 SHIFT = 16
 LANES = 128
 SUBLANES = 8
+UNROLL = 8
 
 SMEM = pl.BlockSpec(memory_space=pltpu.SMEM)
 VMEM = pl.BlockSpec(memory_space=pltpu.VMEM)
@@ -135,74 +136,87 @@
         sends[step][main + edge : main + edge + exposures] = params[...].astype(jnp.bfloat16)
 
 
-def stack_kernel(
-    groups, chunks, exposures, rows, vels, share, info, *rest
-):
+def stack_kernel(groups, chunks, exposures, rows, vels, share, info, *rest):
     blocks = rest[:groups]
     outs = rest[groups : groups + chunks]
-    main, side, windows, edge, whole_params, scalars, result, sem = rest[groups + chunks :]
+    main, side, windows, edge, whole_params, scalars, order, result, sem = rest[groups + chunks :]
     reach = rows + SHIFT
     third = reach // 2
     own = info[0]
     first_vel = info[1]
     main_rows = 2 * exposures * reach
     edge_rows = exposures * third
-    total = groups * exposures
     for g in range(groups):
         whole_params[g * exposures : (g + 1) * exposures] = (
             blocks[g][main_rows + edge_rows : main_rows + edge_rows + exposures].astype(jnp.float32).astype(jnp.int32)
         )
     fetch = pltpu.make_async_copy(whole_params, scalars, sem)
     fetch.start()
+    for g in range(groups):
+        edge[g] = blocks[g][main_rows : main_rows + edge_rows].astype(jnp.float32)
     fetch.wait()
+    filled = jnp.int32(0)
     for g in range(groups):
-        edge[...] = blocks[g][main_rows : main_rows + edge_rows].astype(jnp.float32)
-
-        def unpack(e, carry, g=g):
-            at = g * exposures + e
-            keep = scalars[at, 2 * vels].astype(jnp.float32)
+
+        def unpack(e, at, g=g):
+            order[at] = g * exposures + e
             for m in (0, 1):
                 start = pl.multiple_of(m * exposures * reach + e * reach, reach)
-                main[at, m] = blocks[g][pl.ds(start, reach)].astype(jnp.float32) * keep
-            packed = edge[pl.ds(pl.multiple_of(e * third, SUBLANES), third)] * keep
+                main[at, m] = blocks[g][pl.ds(start, reach)].astype(jnp.float32)
+            packed = edge[g, pl.ds(pl.multiple_of(e * third, SUBLANES), third)]
             for q in range(4):
                 piece = packed if q == 0 else pltpu.roll(packed, LANES - 2 * SHIFT * q, 1)
                 side[at, q // 2, (q % 2) * third : (q % 2 + 1) * third] = piece
-            return carry
-
-        lax.fori_loop(0, exposures, unpack, 0)
+            return at + scalars[g * exposures + e, 2 * vels]
+
+        filled = lax.fori_loop(0, exposures, unpack, filled, unroll=4)
+    for i in range(UNROLL):
+        order[filled + i] = 0
+        main[filled + i] = jnp.zeros(main.shape[1:], jnp.float32)
+        side[filled + i] = jnp.zeros(side.shape[1:], jnp.float32)
+    trips = (filled + UNROLL - 1) // UNROLL
 
     lane = lax.broadcasted_iota(jnp.int32, (rows, LANES), 1)
     zeros = jnp.zeros((rows, LANES), jnp.float32)
 
     def one_velocity(v, carry):
-        def gather(e, sums):
-            row_at = scalars[e, first_vel + v]
-            col_at = scalars[e, vels + first_vel + v] + SHIFT
-            turn = lax.rem(LANES - col_at, LANES)
-            from_side = lane < col_at
-            out = []
-            for m in (0, 1):
-                cells = jnp.where(
-                    from_side, side[e, m, pl.ds(row_at, rows)], main[e, m, pl.ds(row_at, rows)]
-                )
-                cells = pltpu.roll(cells, turn, 1)
-                windows[e, m] = cells
-                out.append(sums[m] + cells)
-            return tuple(out)
-
-        signal_sum, depth_sum = lax.fori_loop(0, total, gather, (zeros, zeros), unroll=2)
+        def gather(trip, sums):
+            for i in range(UNROLL):
+                e = trip * UNROLL + i
+                source = order[e]
+                row_at = scalars[source, first_vel + v]
+                col_at = scalars[source, vels + first_vel + v] + SHIFT
+                turn = lax.rem(LANES - col_at, LANES)
+                from_side = lane < col_at
+                cells = jnp.concatenate(
+                    [
+                        jnp.where(from_side, side[e, m, pl.ds(row_at, rows)], main[e, m, pl.ds(row_at, rows)])
+                        for m in (0, 1)
+                    ]
+                ).astype(jnp.bfloat16)
+                cells = pltpu.roll(cells, turn, 1).astype(jnp.float32)
+                out = []
+                for m in (0, 1):
+                    windows[e, m] = cells[m * rows : (m + 1) * rows]
+                    out.append(sums[m] + cells[m * rows : (m + 1) * rows])
+                sums = tuple(out)
+            return sums
+
+        signal_sum, depth_sum = lax.fori_loop(0, trips, gather, (zeros, zeros))
         flux = signal_sum / (depth_sum + 1.0)
 
-        def reweigh(e, sums):
-            signal = windows[e, 0]
-            depth = windows[e, 1]
-            residual = signal - flux * depth
-            base = depth + 1.0
-            weight = base / (base + residual * residual)
-            return sums[0] + weight * signal, sums[1] + weight * depth
-
-        robust = lax.fori_loop(0, total, reweigh, (zeros, zeros), unroll=2)
+        def reweigh(trip, sums):
+            for i in range(UNROLL):
+                e = trip * UNROLL + i
+                signal = windows[e, 0]
+                depth = windows[e, 1]
+                residual = signal - flux * depth
+                base = depth + 1.0
+                weight = base / (base + residual * residual)
+                sums = sums[0] + weight * signal, sums[1] + weight * depth
+            return sums
+
+        robust = lax.fori_loop(0, trips, reweigh, (zeros, zeros))
         result[v] = robust[0] / jnp.sqrt(robust[1] + 1.0)
         return carry
 
@@ -283,6 +297,7 @@
             pltpu.VMEM((chunks, edge_rows, LANES), jnp.float32),
             pltpu.VMEM((exposures, LANES), jnp.float32),
         ],
+        compiler_params=pltpu.CompilerParams(vmem_limit_bytes=16 << 20),
         name="filter_maps",
     )(info, psf_rows, psf_cols, row_shift, col_shift, exposure_ok[:, None], science, inv_var, above, below)
 
@@ -304,15 +319,17 @@
         in_specs=[SMEM] + [VMEM] * groups,
         out_specs=[VMEM] * chunks,
         scratch_shapes=[
-            pltpu.VMEM((total, 2, reach, LANES), jnp.float32),
-            pltpu.VMEM((total, 2, reach, LANES), jnp.float32),
-            pltpu.VMEM((total, 2, rows, LANES), jnp.float32),
-            pltpu.VMEM((edge_rows, LANES), jnp.float32),
+            pltpu.VMEM((total + UNROLL, 2, reach, LANES), jnp.float32),
+            pltpu.VMEM((total + UNROLL, 2, reach, LANES), jnp.float32),
+            pltpu.VMEM((total + UNROLL, 2, rows, LANES), jnp.float32),
+            pltpu.VMEM((groups, edge_rows, LANES), jnp.float32),
             pltpu.VMEM((total, LANES), jnp.int32),
             pltpu.SMEM((total, LANES), jnp.int32),
+            pltpu.SMEM((total + UNROLL,), jnp.int32),
             pltpu.VMEM((share, rows, LANES), jnp.float32),
             pltpu.SemaphoreType.DMA(()),
         ],
+        compiler_params=pltpu.CompilerParams(vmem_limit_bytes=24 << 20),
         name="stack_twice",
     )(where, *blocks)
 
@@ -331,6 +348,7 @@
             pltpu.VMEM((chunks, share, block_rows, LANES), jnp.float32),
             pltpu.VMEM((subs, share, out_rows, columns), jnp.float32),
         ],
+        compiler_params=pltpu.CompilerParams(vmem_limit_bytes=1 << 20),
         name="join_columns",
     )(place, *held)
     met = [parts[0]]
@@ -342,6 +360,7 @@
         in_specs=[SMEM] + [VMEM] * subs,
         out_specs=VMEM,
         scratch_shapes=[pltpu.VMEM((subs, share, out_rows, columns), jnp.float32)],
+        compiler_params=pltpu.CompilerParams(vmem_limit_bytes=1 << 20),
         name="join_velocities",
     )(place, *met)
     return likelihood[None]

time: 85.6 us -> 65.7 us (0.77)
  Pallas kernels: 33.1 us -> 16.5 us
  local copies, waits for them, and re-layouts: 5.66 us -> 2.06 us
  other arithmetic: 1.93 us -> 0.3 us
  waiting for transfers between devices: 31 us -> 32.6 us
    pallas_call x1, Pallas kernels: 22.4 us -> 8.54 us  [per_device(): pl.pallas_call(functools.partial(stack_kernel, groups, chunks, exposures,...]
    unnamed x26 -> x14, local copies, waits for them, and re-layouts: 3.7 us -> 0.7 us
    pallas_call x1, Pallas kernels: 7.83 us -> 6.23 us  [per_device(): pl.pallas_call(functools.partial(filter_kernel, radius, chunks), out_shap...]
    ppermute x1, waiting for transfers between devices: 7.18 us -> 8.28 us  [per_device(): lax.ppermute(jnp.where(strip == 0, tail, head), 'strip', [(0, 1), (1, 0)])]
    pallas_call x1, Pallas kernels: 1.45 us -> 0.56 us  [per_device(): pl.pallas_call(functools.partial(columns_kernel, chunks, subs), out_shape...]
  transfers between devices with their start and end apart: 12 -> 12, of which waited for: 8 -> 8; matrix products, arithmetic and copies ran while one was open for 3% -> 0% of each run, Pallas kernels for 0% -> 0%
where the time goes in v2:
time: 65.7 us; the launch traced here: 65.5 us
  waiting for transfers between devices  32.6 us (50%)
  Pallas kernels  16.5 us (25%)
  starting transfers between devices  13.9 us (21%)
  local copies, waits for them, and re-layouts  2.06 us (3%)
    ppermute x3, waiting for transfers between devices, per_device(): lax.ppermute(sends[step], 'expo', chunk_pairs(step, chunks, subs))  17.8 us
    pallas_call x1, Pallas kernels, per_device(): pl.pallas_call(functools.partial(stack_kernel, groups, chunks, exposures,...  8.54 us
    ppermute x1, waiting for transfers between devices, per_device(): lax.ppermute(jnp.where(strip == 0, tail, head), 'strip', [(0, 1), (1, 0)])  8.28 us
    pallas_call x1, Pallas kernels, per_device(): pl.pallas_call(functools.partial(filter_kernel, radius, chunks), out_shap...  6.23 us
    ppermute x3, starting transfers between devices, per_device(): lax.ppermute(pieces[step], 'expo', chunk_pairs(step, chunks, subs))  5.84 us
    ppermute x3, starting transfers between devices, per_device(): lax.ppermute(sends[step], 'expo', chunk_pairs(step, chunks, subs))  4.48 us
    ppermute x3, waiting for transfers between devices, per_device(): lax.ppermute(pieces[step], 'expo', chunk_pairs(step, chunks, subs))  4.07 us
    ppermute x1, starting transfers between devices, per_device(): lax.ppermute(jnp.where(strip == 0, tail, head), 'strip', [(0, 1), (1, 0)])  3.03 us
  transfers between devices with their start and end apart: 12, of which 8 were waited for; matrix products, arithmetic and copies ran while one was open for 0% of the time, Pallas kernels for 0%

profile of v2, /device:TPU:0, one launch (start us, length us, event | category | flops | bytes accessed | tf_op | source)
XLA Modules:
  0.0 65.5 jit_solution(15599605140581022986)
XLA Ops:
  0.0 1.3 %slice_bitcast_fusion = (bf16[1,8,24,512]{3,2,1,0:T(8,128)(2,1)S(1)}, bf16[1,8,24,512]{3,2,1,0:T(8,128)(2,1)S(1)}, bf16[1,8,24,512]{3,2,1,0:T(8,128)(2,1)S(1)}, bf16[1,8,24,512]{3,2,1,0:T(8,128)(2,1)S(1)}) fusion(bf16[8,32,512]{2,1,0:T(8,128)(2,1)} %inv_var.1, bf16[8,32,512]{2,1,0:T(8,128)(2,1)} %science.1), kind=kLoop, calls=%fused_computation.1 | loop fusion | bytes 1572864 | tf_op jit(solution)/shard_map/stack | solution.py:273
  1.3 0.0 copy-start
  1.3 0.0 copy-start.1
  1.3 0.1 maximum_select_fusion
  1.4 3.0 %collective-permute-start = (bf16[2,8,24,512]{3,2,1,0:T(8,128)(2,1)S(1)}, bf16[2,8,24,512]{3,2,1,0:T(8,128)(2,1)S(1)}, u32[]{:S(2)}, u32[]{:S(2)}) collective-permute-start(bf16[2,8,24,512]{3,2,1,0:T(8,128)(2,1)S(1)} %maximum_select_fusion), channel_id=1, source_target_pairs={{0,1},{1,0},{2,3},{3,2},{4,5},{5,4},{6,7},{7,6},{8,9},{9,8},{10,11... | collective-permute-start | bytes 1179656 | tf_op jit(solution)/shard_map/ppermute | solution.py:276
  4.4 0.0 copy-start.5
  4.4 0.0 copy-start.6
  4.4 0.7 %copy-done.6 = s32[8]{0:T(128)S(1)} copy-done((s32[8]{0:T(128)S(1)}, s32[8]{0:T(128)}, u32[]{:S(2)}) %copy-start.6) | copy-done | bytes 56
  5.1 0.1 copy.8.usable
  5.2 0.0 copy-start.4
  5.2 0.0 copy-start.3
  5.2 0.0 copy-start.2
  5.2 0.1 pad_add_fusion.2.info
  5.3 8.3 %collective-permute-done.above.below = bf16[2,8,24,512]{3,2,1,0:T(8,128)(2,1)S(1)} collective-permute-done((bf16[2,8,24,512]{3,2,1,0:T(8,128)(2,1)S(1)}, bf16[2,8,24,512]{3,2,1,0:T(8,128)(2,1)S(1)}, u32[]{:S(2)}, u32[]{:S(2)}) %collective-permute-start) | collective-permute-done | bytes 393248 | tf_op jit(solution)/shard_map/ppermute | solution.py:276
  13.5 0.0 copy-done
  13.5 0.0 copy-done.1
  13.5 0.0 copy-done.5
  13.6 0.0 copy-done.4
  13.6 0.0 copy-done.3
  13.6 0.0 copy-done.2
  13.6 6.2 %filter_maps.1 = (bf16[968,128]{1,0:T(8,128)(2,1)S(1)}, bf16[968,128]{1,0:T(8,128)(2,1)S(1)}, bf16[968,128]{1,0:T(8,128)(2,1)S(1)}, bf16[968,128]{1,0:T(8,128)(2,1)S(1)}) custom-call(s32[3]{0:T(128)S(1)} %pad_add_fusion.2.info, f32[8,9]{1,0:T(8,128)S(1)} %copy-done.2, f32[8,9]{1,0:T(8,128)S(1)} %copy-done.3, s32[8,8]{1,0:T(8,128)S(1)} %copy-done.4, ...), custom_call_target="tpu_custom_call" | custom-call | tf_op jit(solution)/shard_map/filter_maps/pallas_call | solution.py:288
  19.8 1.9 %collective-permute-start.1 = (bf16[968,128]{1,0:T(8,128)(2,1)S(1)}, bf16[968,128]{1,0:T(8,128)(2,1)S(1)}, u32[]{:S(2)}, u32[]{:S(2)}) collective-permute-start(bf16[968,128]{1,0:T(8,128)(2,1)S(1)} %get-tuple-element.16), channel_id=1, source_target_pairs={{0,4},{2,6},{4,0},{6,2},{8,12},{10,14},{12,8},{14,10},{1,5},{3,7},... | collective-permute-start | bytes 743432 | tf_op jit(solution)/shard_map/ppermute | solution.py:306
  21.7 2.6 %collective-permute-start.2 = (bf16[968,128]{1,0:T(8,128)(2,1)S(1)}, bf16[968,128]{1,0:T(8,128)(2,1)S(1)}, u32[]{:S(2)}, u32[]{:S(2)}) collective-permute-start(bf16[968,128]{1,0:T(8,128)(2,1)S(1)} %get-tuple-element.17), channel_id=1, source_target_pairs={{0,8},{2,10},{4,12},{6,14},{8,0},{10,2},{12,4},{14,6},{1,9},{3,11}... | collective-permute-start | bytes 743432 | tf_op jit(solution)/shard_map/ppermute | solution.py:306
  24.3 0.0 collective-permute-start.3
  24.3 0.0 collective-permute-start.4
  24.3 6.9 %collective-permute-done.1.rest_1_ = bf16[968,128]{1,0:T(8,128)(2,1)S(1)} collective-permute-done((bf16[968,128]{1,0:T(8,128)(2,1)S(1)}, bf16[968,128]{1,0:T(8,128)(2,1)S(1)}, u32[]{:S(2)}, u32[]{:S(2)}) %collective-permute-start.1) | collective-permute-done | bytes 247840 | tf_op jit(solution)/shard_map/ppermute | solution.py:306
  31.2 0.0 collective-permute-start.5
  31.2 10.9 %collective-permute-done.2.rest_2_ = bf16[968,128]{1,0:T(8,128)(2,1)S(1)} collective-permute-done((bf16[968,128]{1,0:T(8,128)(2,1)S(1)}, bf16[968,128]{1,0:T(8,128)(2,1)S(1)}, u32[]{:S(2)}, u32[]{:S(2)}) %collective-permute-start.2) | collective-permute-done | bytes 247840 | tf_op jit(solution)/shard_map/ppermute | solution.py:306
  42.1 0.0 collective-permute-start.6
  42.1 0.0 collective-permute-done.3.rest_3_
  42.1 0.5 collective-permute-start.7
  42.6 0.1 pad_add_fusion.1.info
  42.7 0.0 collective-permute-done.4.rest_4_
  42.7 0.0 collective-permute-done.5.rest_5_
  42.7 0.9 %collective-permute-done.6.rest_6_ = bf16[968,128]{1,0:T(8,128)(2,1)S(1)} collective-permute-done((bf16[968,128]{1,0:T(8,128)(2,1)S(1)}, bf16[968,128]{1,0:T(8,128)(2,1)S(1)}, u32[]{:S(2)}, u32[]{:S(2)}) %collective-permute-start.6) | collective-permute-done | bytes 247840 | tf_op jit(solution)/shard_map/ppermute | solution.py:309
  43.6 0.4 collective-permute-done.7.rest_7_
  44.0 8.5 %stack_twice.1 = (f32[4,8,128]{2,1,0:T(8,128)S(1)}, f32[4,8,128]{2,1,0:T(8,128)S(1)}, f32[4,8,128]{2,1,0:T(8,128)S(1)}, f32[4,8,128]{2,1,0:T(8,128)S(1)}) custom-call(s32[2]{0:T(128)S(1)} %pad_add_fusion.1.info, bf16[968,128]{1,0:T(8,128)(2,1)S(1)} %get-tuple-element.15.rest_0_, bf16[968,128]{1,0:T(8,128)(2,1)S(1)} %collective-permute-done.1.rest_1_, ...), custom_call_target="tpu_custom_call" | custom-call | tf_op jit(solution)/shard_map/stack_twice/pallas_call | solution.py:316
  52.5 3.4 %collective-permute-start.8 = (f32[4,8,128]{2,1,0:T(8,128)S(1)}, f32[4,8,128]{2,1,0:T(8,128)S(1)}, u32[]{:S(2)}, u32[]{:S(2)}) collective-permute-start(f32[4,8,128]{2,1,0:T(8,128)S(1)} %get-tuple-element.20), channel_id=1, source_target_pairs={{0,4},{2,6},{4,0},{6,2},{8,12},{10,14},{12,8},{14,10},{1,5},{3,7},... | collective-permute-start | bytes 49160 | tf_op jit(solution)/shard_map/ppermute | solution.py:338
  55.9 1.1 %collective-permute-start.9 = (f32[4,8,128]{2,1,0:T(8,128)S(1)}, f32[4,8,128]{2,1,0:T(8,128)S(1)}, u32[]{:S(2)}, u32[]{:S(2)}) collective-permute-start(f32[4,8,128]{2,1,0:T(8,128)S(1)} %get-tuple-element.21), channel_id=1, source_target_pairs={{0,8},{2,10},{4,12},{6,14},{8,0},{10,2},{12,4},{14,6},{1,9},{3,11}... | collective-permute-start | bytes 49160 | tf_op jit(solution)/shard_map/ppermute | solution.py:338
  57.0 1.4 %collective-permute-start.10 = (f32[4,8,128]{2,1,0:T(8,128)S(1)}, f32[4,8,128]{2,1,0:T(8,128)S(1)}, u32[]{:S(2)}, u32[]{:S(2)}) collective-permute-start(f32[4,8,128]{2,1,0:T(8,128)S(1)} %get-tuple-element.22), channel_id=1, source_target_pairs={{0,12},{2,14},{4,8},{6,10},{8,4},{10,6},{12,0},{14,2},{1,13},{3,15... | collective-permute-start | bytes 49160 | tf_op jit(solution)/shard_map/ppermute | solution.py:338
  58.4 0.1 pad_add_fusion.info
  58.4 0.0 collective-permute-done.8.rest_1_
  58.4 2.1 %collective-permute-done.9.rest_2_ = f32[4,8,128]{2,1,0:T(8,128)S(1)} collective-permute-done((f32[4,8,128]{2,1,0:T(8,128)S(1)}, f32[4,8,128]{2,1,0:T(8,128)S(1)}, u32[]{:S(2)}, u32[]{:S(2)}) %collective-permute-start.9) | collective-permute-done | bytes 16416 | tf_op jit(solution)/shard_map/ppermute | solution.py:338
  60.5 2.0 %collective-permute-done.10.rest_3_ = f32[4,8,128]{2,1,0:T(8,128)S(1)} collective-permute-done((f32[4,8,128]{2,1,0:T(8,128)S(1)}, f32[4,8,128]{2,1,0:T(8,128)S(1)}, u32[]{:S(2)}, u32[]{:S(2)}) %collective-permute-start.10) | collective-permute-done | bytes 16416 | tf_op jit(solution)/shard_map/ppermute | solution.py:338
  62.5 0.6 join_columns.1
  63.1 0.1 collective-permute-start.11
  63.2 1.2 %collective-permute-done.11.rest_1_ = f32[4,4,512]{2,1,0:T(4,128)S(1)} collective-permute-done((f32[4,4,512]{2,1,0:T(4,128)S(1)}, f32[4,4,512]{2,1,0:T(4,128)S(1)}, u32[]{:S(2)}, u32[]{:S(2)}) %collective-permute-start.11) | collective-permute-done | bytes 32800 | tf_op jit(solution)/shard_map/ppermute | solution.py:356
  64.4 1.2 %join_velocities.1 = f32[8,4,512]{2,1,0:T(4,128)} custom-call(s32[2]{0:T(128)S(1)} %pad_add_fusion.info, f32[4,4,512]{2,1,0:T(4,128)S(1)} %get-tuple-element.23.rest_0_, f32[4,4,512]{2,1,0:T(4,128)S(1)} %collective-permute-done.11.rest_1_), custom_call_target="tpu_custom_call" | custom-call | tf_op jit(solution)/shard_map/join_velocities/pallas_call | solution.py:357
Async XLA Ops:
  1.3 12.3 %copy-start = (bf16[8,32,512]{2,1,0:T(8,128)(2,1)S(1)}, bf16[8,32,512]{2,1,0:T(8,128)(2,1)}, u32[]{:S(2)}) copy-start(bf16[8,32,512]{2,1,0:T(8,128)(2,1)} %science.1) | copy-start | bytes 786436
  1.3 12.2 %copy-start.1 = (bf16[8,32,512]{2,1,0:T(8,128)(2,1)S(1)}, bf16[8,32,512]{2,1,0:T(8,128)(2,1)}, u32[]{:S(2)}) copy-start(bf16[8,32,512]{2,1,0:T(8,128)(2,1)} %inv_var.1) | copy-start | bytes 786436
  1.4 12.1 %collective-permute-start = (bf16[2,8,24,512]{3,2,1,0:T(8,128)(2,1)S(1)}, bf16[2,8,24,512]{3,2,1,0:T(8,128)(2,1)S(1)}, u32[]{:S(2)}, u32[]{:S(2)}) collective-permute-start(bf16[2,8,24,512]{3,2,1,0:T(8,128)(2,1)S(1)} %maximum_select_fusion), channel_id=1, source_target_pairs={{0,1},{1,0},{2,3},{3,2},{4,5},{5,4},{6,7},{7,6},{8,9},{9,8},{10,11... | collective-permute-start | bytes 1179656 | tf_op jit(solution)/shard_map/ppermute | solution.py:276
  4.4 9.1 %copy-start.5 = (s32[8,8]{1,0:T(8,128)S(1)}, s32[8,8]{1,0:T(8,128)}, u32[]{:S(2)}) copy-start(s32[8,8]{1,0:T(8,128)} %col_shift.1) | copy-start | bytes 772
  4.4 0.7 %copy-start.6 = (s32[8]{0:T(128)S(1)}, s32[8]{0:T(128)}, u32[]{:S(2)}) copy-start(s32[8]{0:T(128)} %param.13) | copy-start | bytes 100
  5.2 8.4 %copy-start.4 = (s32[8,8]{1,0:T(8,128)S(1)}, s32[8,8]{1,0:T(8,128)}, u32[]{:S(2)}) copy-start(s32[8,8]{1,0:T(8,128)} %row_shift.1) | copy-start | bytes 772
  5.2 8.4 %copy-start.3 = (f32[8,9]{1,0:T(8,128)S(1)}, f32[8,9]{1,0:T(8,128)}, u32[]{:S(2)}) copy-start(f32[8,9]{1,0:T(8,128)} %col_taps.1) | copy-start | bytes 868
  5.2 8.4 %copy-start.2 = (f32[8,9]{1,0:T(8,128)S(1)}, f32[8,9]{1,0:T(8,128)}, u32[]{:S(2)}) copy-start(f32[8,9]{1,0:T(8,128)} %row_taps.1) | copy-start | bytes 868
  19.8 11.4 %collective-permute-start.1 = (bf16[968,128]{1,0:T(8,128)(2,1)S(1)}, bf16[968,128]{1,0:T(8,128)(2,1)S(1)}, u32[]{:S(2)}, u32[]{:S(2)}) collective-permute-start(bf16[968,128]{1,0:T(8,128)(2,1)S(1)} %get-tuple-element.16), channel_id=1, source_target_pairs={{0,4},{2,6},{4,0},{6,2},{8,12},{10,14},{12,8},{14,10},{1,5},{3,7},... | collective-permute-start | bytes 743432 | tf_op jit(solution)/shard_map/ppermute | solution.py:306
  21.7 20.4 %collective-permute-start.2 = (bf16[968,128]{1,0:T(8,128)(2,1)S(1)}, bf16[968,128]{1,0:T(8,128)(2,1)S(1)}, u32[]{:S(2)}, u32[]{:S(2)}) collective-permute-start(bf16[968,128]{1,0:T(8,128)(2,1)S(1)} %get-tuple-element.17), channel_id=1, source_target_pairs={{0,8},{2,10},{4,12},{6,14},{8,0},{10,2},{12,4},{14,6},{1,9},{3,11}... | collective-permute-start | bytes 743432 | tf_op jit(solution)/shard_map/ppermute | solution.py:306
  24.3 17.8 %collective-permute-start.3 = (bf16[968,128]{1,0:T(8,128)(2,1)S(1)}, bf16[968,128]{1,0:T(8,128)(2,1)S(1)}, u32[]{:S(2)}, u32[]{:S(2)}) collective-permute-start(bf16[968,128]{1,0:T(8,128)(2,1)S(1)} %get-tuple-element.18), channel_id=1, source_target_pairs={{0,12},{2,14},{4,8},{6,10},{8,4},{10,6},{12,0},{14,2},{1,13},{3,15... | collective-permute-start | bytes 743432 | tf_op jit(solution)/shard_map/ppermute | solution.py:306
  24.3 18.4 %collective-permute-start.4 = (bf16[968,128]{1,0:T(8,128)(2,1)S(1)}, bf16[968,128]{1,0:T(8,128)(2,1)S(1)}, u32[]{:S(2)}, u32[]{:S(2)}) collective-permute-start(bf16[968,128]{1,0:T(8,128)(2,1)S(1)} %get-tuple-element.15.rest_0_), channel_id=1, source_target_pairs={{0,2},{2,0},{4,6},{6,4},{8,10},{10,8},{12,14},{14,12},{1,3},{3,1},... | collective-permute-start | bytes 743432 | tf_op jit(solution)/shard_map/ppermute | solution.py:309
  31.2 11.5 %collective-permute-start.5 = (bf16[968,128]{1,0:T(8,128)(2,1)S(1)}, bf16[968,128]{1,0:T(8,128)(2,1)S(1)}, u32[]{:S(2)}, u32[]{:S(2)}) collective-permute-start(bf16[968,128]{1,0:T(8,128)(2,1)S(1)} %collective-permute-done.1.rest_1_), channel_id=1, source_target_pairs={{0,2},{2,0},{4,6},{6,4},{8,10},{10,8},{12,14},{14,12},{1,3},{3,1},... | collective-permute-start | bytes 743432 | tf_op jit(solution)/shard_map/ppermute | solution.py:309
  42.1 1.5 %collective-permute-start.6 = (bf16[968,128]{1,0:T(8,128)(2,1)S(1)}, bf16[968,128]{1,0:T(8,128)(2,1)S(1)}, u32[]{:S(2)}, u32[]{:S(2)}) collective-permute-start(bf16[968,128]{1,0:T(8,128)(2,1)S(1)} %collective-permute-done.2.rest_2_), channel_id=1, source_target_pairs={{0,2},{2,0},{4,6},{6,4},{8,10},{10,8},{12,14},{14,12},{1,3},{3,1},... | collective-permute-start | bytes 743432 | tf_op jit(solution)/shard_map/ppermute | solution.py:309
  42.1 1.9 %collective-permute-start.7 = (bf16[968,128]{1,0:T(8,128)(2,1)S(1)}, bf16[968,128]{1,0:T(8,128)(2,1)S(1)}, u32[]{:S(2)}, u32[]{:S(2)}) collective-permute-start(bf16[968,128]{1,0:T(8,128)(2,1)S(1)} %collective-permute-done.3.rest_3_), channel_id=1, source_target_pairs={{0,2},{2,0},{4,6},{6,4},{8,10},{10,8},{12,14},{14,12},{1,3},{3,1},... | collective-permute-start | bytes 743432 | tf_op jit(solution)/shard_map/ppermute | solution.py:309
  52.5 5.9 %collective-permute-start.8 = (f32[4,8,128]{2,1,0:T(8,128)S(1)}, f32[4,8,128]{2,1,0:T(8,128)S(1)}, u32[]{:S(2)}, u32[]{:S(2)}) collective-permute-start(f32[4,8,128]{2,1,0:T(8,128)S(1)} %get-tuple-element.20), channel_id=1, source_target_pairs={{0,4},{2,6},{4,0},{6,2},{8,12},{10,14},{12,8},{14,10},{1,5},{3,7},... | collective-permute-start | bytes 49160 | tf_op jit(solution)/shard_map/ppermute | solution.py:338
  55.9 4.6 %collective-permute-start.9 = (f32[4,8,128]{2,1,0:T(8,128)S(1)}, f32[4,8,128]{2,1,0:T(8,128)S(1)}, u32[]{:S(2)}, u32[]{:S(2)}) collective-permute-start(f32[4,8,128]{2,1,0:T(8,128)S(1)} %get-tuple-element.21), channel_id=1, source_target_pairs={{0,8},{2,10},{4,12},{6,14},{8,0},{10,2},{12,4},{14,6},{1,9},{3,11}... | collective-permute-start | bytes 49160 | tf_op jit(solution)/shard_map/ppermute | solution.py:338
  57.0 5.5 %collective-permute-start.10 = (f32[4,8,128]{2,1,0:T(8,128)S(1)}, f32[4,8,128]{2,1,0:T(8,128)S(1)}, u32[]{:S(2)}, u32[]{:S(2)}) collective-permute-start(f32[4,8,128]{2,1,0:T(8,128)S(1)} %get-tuple-element.22), channel_id=1, source_target_pairs={{0,12},{2,14},{4,8},{6,10},{8,4},{10,6},{12,0},{14,2},{1,13},{3,15... | collective-permute-start | bytes 49160 | tf_op jit(solution)/shard_map/ppermute | solution.py:338
  63.1 1.3 %collective-permute-start.11 = (f32[4,4,512]{2,1,0:T(4,128)S(1)}, f32[4,4,512]{2,1,0:T(4,128)S(1)}, u32[]{:S(2)}, u32[]{:S(2)}) collective-permute-start(f32[4,4,512]{2,1,0:T(4,128)S(1)} %get-tuple-element.24), channel_id=1, source_target_pairs={{0,2},{2,0},{4,6},{6,4},{8,10},{10,8},{12,14},{14,12},{1,3},{3,1},... | collective-permute-start | bytes 98312 | tf_op jit(solution)/shard_map/ppermute | solution.py:356

commit v3 on v2

v3 whole, which is shorter than its diff:
```python
import functools

import jax
import jax.numpy as jnp
from jax import lax
from jax.experimental import pallas as pl
from jax.experimental.pallas import tpu as pltpu
from jax.sharding import PartitionSpec as P

SHIFT = 16
LANES = 128
SUBLANES = 8
UNROLL = 8

SMEM = pl.BlockSpec(memory_space=pltpu.SMEM)
VMEM = pl.BlockSpec(memory_space=pltpu.VMEM)


def partner(index, step, count):
    if count & (count - 1) == 0:
        return index ^ step
    return (index + step) % count


def chunk_pairs(step, chunks, subs):
    return [
        (j * subs + k, partner(j, step, chunks) * subs + k) for j in range(chunks) for k in range(subs)
    ]


def sub_pairs(step, chunks, subs):
    return [
        (j * subs + k, j * subs + partner(k, step, subs)) for j in range(chunks) for k in range(subs)
    ]


def column_pass(picture, col_taps, e, square):
    tiles = picture.shape[1] // LANES
    taps = col_taps.shape[1]
    lane = lax.broadcasted_iota(jnp.int32, (SUBLANES, LANES), 1)
    zero = jnp.zeros((SUBLANES, LANES), jnp.float32)
    cut = [picture[:, t * LANES : (t + 1) * LANES] for t in range(tiles)]
    totals = None
    for b in range(taps):
        step = b - taps // 2
        tap = col_taps[e, b]
        if square:
            tap = tap * tap
        moved = cut
        if step:
            turned = [pltpu.roll(c, (-step) % LANES, 1) for c in cut]
            if step > 0:
                turned = turned + [zero]
                moved = [jnp.where(lane < LANES - step, turned[t], turned[t + 1]) for t in range(tiles)]
            else:
                turned = [zero] + turned
                moved = [jnp.where(lane >= -step, turned[t + 1], turned[t]) for t in range(tiles)]
        terms = [tap * m for m in moved]
        totals = terms if totals is None else [x + y for x, y in zip(totals, terms)]
    return totals


def row_pass(colpass, row_taps, e, m, first, taps):
    tiles = colpass.shape[1]
    lane = lax.broadcasted_iota(jnp.int32, (SUBLANES, LANES), 1)
    zero = jnp.zeros((SUBLANES, LANES), jnp.float32)
    out = []
    for t in range(tiles):
        total = None
        for a in taps:
            tap = row_taps[e, a]
            if m == 1:
                tap = tap * tap
            term = tap * colpass[m, t, pl.ds(first + a, SUBLANES)]
            total = term if total is None else total + term
        out.append(pltpu.roll(total, SHIFT, 1))
    out = [zero] + out + [zero]
    return [jnp.where(lane < SHIFT, out[t], out[t + 1]) for t in range(tiles + 1)]


def pack_edges(quarters, t):
    lane = lax.broadcasted_iota(jnp.int32, (SUBLANES, LANES), 1)
    packed = jnp.zeros((SUBLANES, LANES), jnp.float32)
    for q, quarter in enumerate(quarters):
        if quarter is None:
            continue
        piece = quarter[t + 1] if q == 0 else pltpu.roll(quarter[t + 1], 2 * SHIFT * q, 1)
        inside = (lane >= 2 * SHIFT * q) & (lane < 2 * SHIFT * (q + 1))
        packed = jnp.where(inside, piece, packed)
    return packed


def inner_kernel(radius, row_taps, col_taps, science, inv_var, maps, edges, colpass):
    exposures, rows, columns = science.shape
    tiles = columns // LANES
    taps = 2 * radius + 1
    pad = SUBLANES
    colpass[:, :, 0:pad] = jnp.zeros((2, tiles, pad, LANES), jnp.float32)
    colpass[:, :, pad + rows : 2 * pad + rows] = jnp.zeros((2, tiles, pad, LANES), jnp.float32)
    parts = rows // SHIFT

    def one_exposure(e, carry):
        inverse_all = inv_var[e].astype(jnp.float32)
        product_all = science[e].astype(jnp.float32) * inverse_all
        for g in range(rows // SUBLANES):
            at = slice(g * SUBLANES, (g + 1) * SUBLANES)
            for m, picture in ((0, product_all[at]), (1, inverse_all[at])):
                for t, total in enumerate(column_pass(picture, col_taps, e, m == 1)):
                    colpass[m, t, pad + g * SUBLANES : pad + (g + 1) * SUBLANES] = total
        for p in range(parts):
            quarters = [
                row_pass(colpass, row_taps, e, m, pad + p * SHIFT + h * SUBLANES - radius, range(taps))
                for m in (0, 1)
                for h in (0, 1)
            ]
            for t in range(tiles):
                for q in range(4):
                    at = p * exposures * 2 * SHIFT + e * 2 * SHIFT + q * SUBLANES
                    maps[t, pl.ds(pl.multiple_of(at, SUBLANES), SUBLANES)] = quarters[q][t]
                at = p * exposures * SUBLANES + e * SUBLANES
                edges[t, pl.ds(pl.multiple_of(at, SUBLANES), SUBLANES)] = pack_edges(quarters, t)
        return carry

    lax.fori_loop(0, exposures, one_exposure, 0)


def outer_kernel(
    radius, chunks, info, row_taps, col_taps, usable, row_shift, col_shift, maps, edges, above, below, *rest
):
    sends, (pixels, colpass, more, more_edges, params) = rest[:chunks], rest[chunks:]
    exposures, vels = row_shift.shape
    tiles = maps.shape[0]
    parts = edges.shape[1] // (exposures * SUBLANES)
    taps = 2 * radius + 1
    pad = SUBLANES
    has_above, has_below, own = info[0] > 0, info[1] > 0, info[2]

    row = lax.broadcasted_iota(jnp.int32, (exposures, 1), 0)
    kept = jnp.zeros((exposures, 1), jnp.int32)
    for e in range(exposures):
        kept = jnp.where(row == e, usable[e], kept)
    params[...] = jnp.zeros_like(params)
    params[:, 0:vels] = row_shift[...].astype(jnp.float32)
    params[:, vels : 2 * vels] = col_shift[...].astype(jnp.float32)
    params[:, 2 * vels : 2 * vels + 1] = kept.astype(jnp.float32)
    colpass[...] = jnp.zeros_like(colpass)

    def one_exposure(e, carry):
        for kind in (0, 1):
            pixels[kind, 0:radius] = jnp.where(has_below, below[kind, e].astype(jnp.float32), 0.0)
            pixels[kind, radius : 2 * radius] = jnp.where(has_above, above[kind, e].astype(jnp.float32), 0.0)
        inverse = pixels[1]
        product = pixels[0] * inverse
        for m, picture in ((0, product), (1, inverse)):
            for t, total in enumerate(column_pass(picture, col_taps, e, m == 1)):
                colpass[m, t, pad : pad + SUBLANES] = total
        upper = [row_pass(colpass, row_taps, e, m, pad + radius, range(radius)) for m in (0, 1)]
        lower = [row_pass(colpass, row_taps, e, m, -radius, range(radius + 1, taps)) for m in (0, 1)]
        for t in range(tiles):
            for m in (0, 1):
                more[0, t, 2 * e + m] = upper[m][t]
                more[1, t, 2 * e + m] = lower[m][t]
            more_edges[0, t, e] = pack_edges([upper[0], None, upper[1], None], t)
            more_edges[1, t, e] = pack_edges([None, lower[0], None, lower[1]], t)
        return carry

    lax.fori_loop(0, exposures, one_exposure, 0)
    main = exposures * 2 * SHIFT
    size = main + exposures * SUBLANES
    for step in range(chunks):
        to = partner(own, step, chunks)
        for p in range(parts):
            for k in range(2 * exposures):
                first = maps[to, p * main + k * SHIFT : p * main + k * SHIFT + SUBLANES]
                second = maps[to, p * main + k * SHIFT + SUBLANES : p * main + (k + 1) * SHIFT]
                if p == 0:
                    first = first + more[0, to, k]
                if p == parts - 1:
                    second = second + more[1, to, k]
                at = p * size + k * SHIFT
                sends[step][at : at + SHIFT] = jnp.concatenate([first, second]).astype(jnp.bfloat16)
            packed = edges[to, p * exposures * SUBLANES : (p + 1) * exposures * SUBLANES]
            if p == 0:
                packed = packed + more_edges[0, to].reshape(packed.shape)
            if p == parts - 1:
                packed = packed + more_edges[1, to].reshape(packed.shape)
            sends[step][p * size + main : (p + 1) * size] = packed.astype(jnp.bfloat16)
        sends[step][parts * size : parts * size + exposures] = params[...].astype(jnp.bfloat16)


def stack_kernel(groups, chunks, exposures, rows, vels, info, *rest):
    bodies = rest[:groups]
    tops = rest[groups : 2 * groups]
    outs = rest[2 * groups : 2 * groups + chunks]
    main, side, windows, edge, whole_params, scalars, order, result, sem = rest[2 * groups + chunks :]
    own = info[2]
    first_vel = info[4]
    share = result.shape[0]
    parts = rows // SHIFT
    main_rows = exposures * 2 * SHIFT
    edge_rows = exposures * SUBLANES
    size = main_rows + edge_rows
    for g in range(groups):
        whole_params[g * exposures : (g + 1) * exposures] = (
            bodies[g][parts * size : parts * size + exposures].astype(jnp.float32).astype(jnp.int32)
        )
    fetch = pltpu.make_async_copy(whole_params, scalars, sem)
    fetch.start()
    for g in range(groups):
        for p in range(parts):
            edge[g, p] = bodies[g][p * size + main_rows : (p + 1) * size].astype(jnp.float32)
        edge[g, parts] = tops[g][main_rows:size].astype(jnp.float32)
    fetch.wait()
    filled = jnp.int32(0)
    for g in range(groups):

        def unpack(e, at, g=g):
            order[at] = g * exposures + e
            for p in range(parts + 1):
                source, offset = (bodies[g], p * size) if p < parts else (tops[g], 0)
                start = pl.multiple_of(offset + e * 2 * SHIFT, 2 * SUBLANES)
                both = source[pl.ds(start, 2 * SHIFT)].astype(jnp.float32)
                packed = edge[g, p, pl.ds(pl.multiple_of(e * SUBLANES, SUBLANES), SUBLANES)]
                for m in (0, 1):
                    main[at, m, p * SHIFT : (p + 1) * SHIFT] = both[m * SHIFT : (m + 1) * SHIFT]
                    for h in (0, 1):
                        q = 2 * m + h
                        piece = packed if q == 0 else pltpu.roll(packed, LANES - 2 * SHIFT * q, 1)
                        side[at, m, p * SHIFT + h * SUBLANES : p * SHIFT + (h + 1) * SUBLANES] = piece
            return at + scalars[g * exposures + e, 2 * vels]

        filled = lax.fori_loop(0, exposures, unpack, filled, unroll=4)
    for i in range(UNROLL):
        order[filled + i] = 0
        main[filled + i] = jnp.zeros(main.shape[1:], jnp.float32)
        side[filled + i] = jnp.zeros(side.shape[1:], jnp.float32)
    trips = (filled + UNROLL - 1) // UNROLL

    lane = lax.broadcasted_iota(jnp.int32, (rows, LANES), 1)
    zeros = jnp.zeros((rows, LANES), jnp.float32)

    def one_velocity(v, carry):
        def gather(trip, sums):
            for i in range(UNROLL):
                e = trip * UNROLL + i
                source = order[e]
                row_at = scalars[source, first_vel + v]
                col_at = scalars[source, vels + first_vel + v] + SHIFT
                turn = lax.rem(LANES - col_at, LANES)
                from_side = lane < col_at
                cells = jnp.concatenate(
                    [
                        jnp.where(from_side, side[e, m, pl.ds(row_at, rows)], main[e, m, pl.ds(row_at, rows)])
                        for m in (0, 1)
                    ]
                ).astype(jnp.bfloat16)
                cells = pltpu.roll(cells, turn, 1).astype(jnp.float32)
                out = []
                for m in (0, 1):
                    windows[e, m] = cells[m * rows : (m + 1) * rows]
                    out.append(sums[m] + cells[m * rows : (m + 1) * rows])
                sums = tuple(out)
            return sums

        signal_sum, depth_sum = lax.fori_loop(0, trips, gather, (zeros, zeros))
        flux = signal_sum / (depth_sum + 1.0)

        def reweigh(trip, sums):
            for i in range(UNROLL):
                e = trip * UNROLL + i
                signal = windows[e, 0]
                depth = windows[e, 1]
                residual = signal - flux * depth
                base = depth + 1.0
                weight = base / (base + residual * residual)
                sums = sums[0] + weight * signal, sums[1] + weight * depth
            return sums

        robust = lax.fori_loop(0, trips, reweigh, (zeros, zeros))
        result[v] = robust[0] / jnp.sqrt(robust[1] + 1.0)
        return carry

    lax.fori_loop(0, share, one_velocity, 0)
    block = rows // chunks
    for step in range(chunks):
        to = partner(own, step, chunks)
        outs[step][...] = result[:, pl.ds(pl.multiple_of(to * block, block), block)]


def columns_kernel(chunks, subs, info, *rest):
    pieces = rest[:chunks]
    outs = rest[chunks : chunks + subs]
    held, wide = rest[chunks + subs :]
    own_chunk, own_sub = info[2], info[3]
    for step in range(chunks):
        held[step] = pieces[step][...]
    rows = wide.shape[2]
    for c in range(chunks):
        piece = held[partner(own_chunk, c, chunks)]
        for k in range(subs):
            wide[k, :, :, c * LANES : (c + 1) * LANES] = piece[:, k * rows : (k + 1) * rows]
    for step in range(subs):
        outs[step][...] = wide[partner(own_sub, step, subs)]


def velocities_kernel(subs, info, *rest):
    pieces = rest[:subs]
    out, held = rest[subs:]
    own_sub = info[3]
    for step in range(subs):
        held[step] = pieces[step][...]
    share = held.shape[1]
    for k in range(subs):
        out[k * share : (k + 1) * share] = held[partner(own_sub, k, subs)]


def per_device(science, inv_var, psf_rows, psf_cols, row_shift, col_shift, exposure_ok):
    exposures, rows, columns = science.shape
    vels = row_shift.shape[1]
    radius = psf_rows.shape[1] // 2
    strips = lax.axis_size("strip")
    members = lax.axis_size("expo")
    chunks = columns // LANES
    subs = members // chunks
    share = vels // subs
    parts = rows // SHIFT
    strip = lax.axis_index("strip")
    me = lax.axis_index("expo")
    own_chunk = me // subs
    own_sub = me % subs
    info = jnp.stack([strip > 0, strip < strips - 1, own_chunk, own_sub, own_sub * share]).astype(jnp.int32)

    def rows_from(start):
        return jnp.stack([lax.dynamic_slice_in_dim(x, start, radius, 1) for x in (science, inv_var)])

    if strips == 2:
        met = rows_from(jnp.where(strip == 0, rows - radius, 0))
        above = below = lax.ppermute(met, "strip", [(0, 1), (1, 0)])
    else:
        above = lax.ppermute(rows_from(rows - radius), "strip", [(i, i + 1) for i in range(strips - 1)])
        below = lax.ppermute(rows_from(0), "strip", [(i + 1, i) for i in range(strips - 1)])

    map_rows = parts * exposures * 2 * SHIFT
    edge_rows = parts * exposures * SUBLANES
    maps, edges = pl.pallas_call(
        functools.partial(inner_kernel, radius),
        out_shape=[
            jax.ShapeDtypeStruct((chunks, map_rows, LANES), jnp.float32),
            jax.ShapeDtypeStruct((chunks, edge_rows, LANES), jnp.float32),
        ],
        in_specs=[SMEM] * 2 + [VMEM] * 2,
        out_specs=[VMEM] * 2,
        scratch_shapes=[pltpu.VMEM((2, chunks, rows + 2 * SUBLANES, LANES), jnp.float32)],
        compiler_params=pltpu.CompilerParams(vmem_limit_bytes=8 << 20),
        cost_estimate=pl.CostEstimate(flops=100_000_000, bytes_accessed=4_000_000, transcendentals=0),
        name="filter_inner",
    )(psf_rows, psf_cols, science, inv_var)
    sent = jax.ShapeDtypeStruct((map_rows + edge_rows + exposures, LANES), jnp.bfloat16)
    sends = pl.pallas_call(
        functools.partial(outer_kernel, radius, chunks),
        out_shape=[sent] * chunks,
        in_specs=[SMEM] * 4 + [VMEM] * 6,
        out_specs=[VMEM] * chunks,
        scratch_shapes=[
            pltpu.VMEM((2, 2 * radius, columns), jnp.float32),
            pltpu.VMEM((2, chunks, 3 * SUBLANES, LANES), jnp.float32),
            pltpu.VMEM((2, chunks, 2 * exposures, SUBLANES, LANES), jnp.float32),
            pltpu.VMEM((2, chunks, exposures, SUBLANES, LANES), jnp.float32),
            pltpu.VMEM((exposures, LANES), jnp.float32),
        ],
        compiler_params=pltpu.CompilerParams(vmem_limit_bytes=8 << 20),
        name="filter_outer",
    )(info, psf_rows, psf_cols, exposure_ok, row_shift, col_shift, maps, edges, above, below)

    top_rows = (map_rows + edge_rows) // parts
    bodies, tops = [], []
    for step in range(chunks):
        body = sends[step]
        if step:
            body = lax.ppermute(body, "expo", chunk_pairs(step, chunks, subs))
        bodies.append(body)
        tops.append(lax.ppermute(body[:top_rows], "strip", [(i + 1, i) for i in range(strips - 1)]))
    for step in range(1, subs):
        pairs = sub_pairs(step, chunks, subs)
        bodies += [lax.ppermute(block, "expo", pairs) for block in bodies[:chunks]]
        tops += [lax.ppermute(block, "expo", pairs) for block in tops[:chunks]]

    groups = len(bodies)
    block_rows = rows // chunks
    reach = rows + SHIFT
    piece = jax.ShapeDtypeStruct((share, block_rows, LANES), jnp.float32)
    total = groups * exposures
    pieces = pl.pallas_call(
        functools.partial(stack_kernel, groups, chunks, exposures, rows, vels),
        out_shape=[piece] * chunks,
        in_specs=[SMEM] + [VMEM] * (2 * groups),
        out_specs=[VMEM] * chunks,
        scratch_shapes=[
            pltpu.VMEM((total + UNROLL, 2, reach, LANES), jnp.float32),
            pltpu.VMEM((total + UNROLL, 2, reach, LANES), jnp.float32),
            pltpu.VMEM((total + UNROLL, 2, rows, LANES), jnp.float32),
            pltpu.VMEM((groups, parts + 1, exposures * SUBLANES, LANES), jnp.float32),
            pltpu.VMEM((total, LANES), jnp.int32),
            pltpu.SMEM((total, LANES), jnp.int32),
            pltpu.SMEM((total + UNROLL,), jnp.int32),
            pltpu.VMEM((share, rows, LANES), jnp.float32),
            pltpu.SemaphoreType.DMA(()),
        ],
        compiler_params=pltpu.CompilerParams(vmem_limit_bytes=24 << 20),
        name="stack_twice",
    )(info, *bodies, *tops)

    held = [pieces[0]]
    for step in range(1, chunks):
        held.append(lax.ppermute(pieces[step], "expo", chunk_pairs(step, chunks, subs)))
    out_rows = block_rows // subs
    wide = jax.ShapeDtypeStruct((share, out_rows, columns), jnp.float32)
    parts = pl.pallas_call(
        functools.partial(columns_kernel, chunks, subs),
        out_shape=[wide] * subs,
        in_specs=[SMEM] + [VMEM] * chunks,
        out_specs=[VMEM] * subs,
        scratch_shapes=[
            pltpu.VMEM((chunks, share, block_rows, LANES), jnp.float32),
            pltpu.VMEM((subs, share, out_rows, columns), jnp.float32),
        ],
        compiler_params=pltpu.CompilerParams(vmem_limit_bytes=1 << 20),
        name="join_columns",
    )(info, *held)
    met = [parts[0]]
    for step in range(1, subs):
        met.append(lax.ppermute(parts[step], "expo", sub_pairs(step, chunks, subs)))
    likelihood = pl.pallas_call(
        functools.partial(velocities_kernel, subs),
        out_shape=jax.ShapeDtypeStruct((vels, out_rows, columns), jnp.float32),
        in_specs=[SMEM] + [VMEM] * subs,
        out_specs=VMEM,
        scratch_shapes=[pltpu.VMEM((subs, share, out_rows, columns), jnp.float32)],
        compiler_params=pltpu.CompilerParams(vmem_limit_bytes=1 << 20),
        name="join_velocities",
    )(info, *met)
    return likelihood[None]


def solution(mesh):
    in_specs = (
        P(("field", "expo"), "strip", None),
        P(("field", "expo"), "strip", None),
        P(("field", "expo"), None),
        P(("field", "expo"), None),
        P(("field", "expo"), None),
        P(("field", "expo"), None),
        P(("field", "expo")),
    )
    out_specs = P("strip", "field", "expo", None)
    return jax.shard_map(
        per_device, mesh=mesh, in_specs=in_specs, out_specs=out_specs, check_vma=False
    )
```

time: 65.7 us -> 61.1 us (0.930)
  waiting for transfers between devices: 32.6 us -> 21.8 us
  starting transfers between devices: 13.9 us -> 18.3 us
  local copies, waits for them, and re-layouts: 2.06 us -> 3.27 us
  Pallas kernels: 16.5 us -> 17.2 us
    ppermute x8 -> x16, waiting for transfers between devices: 27.4 us -> 16.3 us  [the longest x4 11.1 us: per_device(): lax.ppermute(body[:top_rows], 'strip', [(i + 1, i) for i in range(strips...]
    ppermute x8 -> x16, starting transfers between devices: 8.03 us -> 13.8 us  [the longest x4 5.16 us: per_device(): lax.ppermute(body[:top_rows], 'strip', [(i + 1, i) for i in range(strips...]
    unnamed x14, local copies, waits for them, and re-layouts: 0.7 us -> 2.21 us
    ppermute x3, starting transfers between devices: 5.84 us -> 4.45 us  [per_device(): lax.ppermute(pieces[step], 'expo', chunk_pairs(step, chunks, subs))]
    pallas_call x1 -> x2, Pallas kernels: 6.23 us -> 7.57 us  [the longest x1 4.29 us: per_device(): pl.pallas_call(functools.partial(inner_kernel, radius), out_shape=[jax.Sh...]
  transfers between devices with their start and end apart: 12 -> 20, of which waited for: 8 -> 9; matrix products, arithmetic and copies ran while one was open for 0% -> 0% of each run, Pallas kernels for 0% -> 7%
where the time goes in v3:
time: 61.1 us; the launch traced here: 60.8 us
  waiting for transfers between devices  21.8 us (36%)
  starting transfers between devices  18.3 us (30%)
  Pallas kernels  17.2 us (28%)
  local copies, waits for them, and re-layouts  3.27 us (5%)
    ppermute x4, waiting for transfers between devices, per_device(): lax.ppermute(body[:top_rows], 'strip', [(i + 1, i) for i in range(strips...  11.1 us
    pallas_call x1, Pallas kernels, per_device(): pl.pallas_call(functools.partial(stack_kernel, groups, chunks, exposures,...  7.91 us
    ppermute x4, starting transfers between devices, per_device(): lax.ppermute(body[:top_rows], 'strip', [(i + 1, i) for i in range(strips...  5.16 us
    ppermute x3, starting transfers between devices, per_device(): body = lax.ppermute(body, 'expo', chunk_pairs(step, chunks, subs))  4.45 us
    ppermute x3, starting transfers between devices, per_device(): lax.ppermute(pieces[step], 'expo', chunk_pairs(step, chunks, subs))  4.45 us
    ppermute x3, waiting for transfers between devices, per_device(): lax.ppermute(pieces[step], 'expo', chunk_pairs(step, chunks, subs))  4.33 us
    pallas_call x1, Pallas kernels, per_device(): pl.pallas_call(functools.partial(inner_kernel, radius), out_shape=[jax.Sh...  4.29 us
    ppermute x3, waiting for transfers between devices, per_device(): body = lax.ppermute(body, 'expo', chunk_pairs(step, chunks, subs))  4.25 us
  transfers between devices with their start and end apart: 20, of which 9 were waited for; matrix products, arithmetic and copies ran while one was open for 0% of the time, Pallas kernels for 7%

profile of v3, /device:TPU:0, one launch (start us, length us, event | category | flops | bytes accessed | tf_op | source)
XLA Modules:
  0.0 60.8 jit_solution(7182962295308229062)
XLA Ops:
  0.0 1.0 %dynamic-slice_bitcast_fusion = (bf16[1,8,4,512]{3,2,1,0:T(4,128)(2,1)S(1)}, bf16[1,8,4,512]{3,2,1,0:T(4,128)(2,1)S(1)}) fusion(bf16[8,32,512]{2,1,0:T(8,128)(2,1)} %inv_var.1, s32[]{:T(128)S(6)} %select_n.19, bf16[8,32,512]{2,1,0:T(8,128)(2,1)} %science.1), kind=kLoop, calls=%fused_computation.1 | loop fusion | bytes 131076 | tf_op jit(solution)/shard_map/stack | solution.py:334
  1.0 3.0 %collective-permute-start = (bf16[2,8,4,512]{3,2,1,0:T(4,128)(2,1)S(1)}, bf16[2,8,4,512]{3,2,1,0:T(4,128)(2,1)S(1)}, u32[]{:S(2)}, u32[]{:S(2)}) collective-permute-start(bf16[2,8,4,512]{3,2,1,0:T(4,128)(2,1)S(1)} %pad_maximum_fusion), channel_id=1, source_target_pairs={{0,1},{1,0},{2,3},{3,2},{4,5},{5,4},{6,7},{7,6},{8,9},{9,8},{10,11... | collective-permute-start | bytes 196616 | tf_op jit(solution)/shard_map/ppermute | solution.py:338
  4.0 0.1 stack.40.info
  4.1 0.6 copy-done.2
  4.7 0.0 copy-done.3
  4.8 0.9 %copy-done.1 = bf16[8,32,512]{2,1,0:T(8,128)(2,1)S(1)} copy-done((bf16[8,32,512]{2,1,0:T(8,128)(2,1)S(1)}, bf16[8,32,512]{2,1,0:T(8,128)(2,1)}, u32[]{:S(2)}) %copy-start.1) | copy-done | bytes 262168
  5.7 4.3 %filter_inner.1 = (f32[4,512,128]{2,1,0:T(8,128)S(1)}, f32[4,128,128]{2,1,0:T(8,128)S(1)}) custom-call(f32[8,9]{1,0:T(8,128)S(1)} %copy-done.2, f32[8,9]{1,0:T(8,128)S(1)} %copy-done.3, bf16[8,32,512]{2,1,0:T(8,128)(2,1)S(1)} %copy-done, bf16[8,32,512]{2,1,0:T(8,128)(2,1)S(1)} %copy-done.1), custom_call_target="tpu_custom_call" | custom-call | flops 100000000 | bytes 4000000 | tf_op jit(solution)/shard_map/filter_inner/pallas_call | solution.py:345
  10.0 0.0 collective-permute-done.above.below
  10.0 0.0 copy-start.6
  10.0 0.6 %copy-done.6 = s32[8]{0:T(128)S(1)} copy-done((s32[8]{0:T(128)S(1)}, s32[8]{0:T(128)}, u32[]{:S(2)}) %copy-start.6) | copy-done | bytes 56
  10.7 3.3 %filter_outer.1 = (bf16[648,128]{1,0:T(8,128)(2,1)S(1)}, bf16[648,128]{1,0:T(8,128)(2,1)S(1)}, bf16[648,128]{1,0:T(8,128)(2,1)S(1)}, bf16[648,128]{1,0:T(8,128)(2,1)S(1)}) custom-call(s32[5]{0:T(128)S(1)} %stack.40.info, f32[8,9]{1,0:T(8,128)S(1)} %copy-done.2, f32[8,9]{1,0:T(8,128)S(1)} %copy-done.3, s32[8]{0:T(128)S(1)} %copy-done.6, ...), custom_call_target="tpu_custom_call" | custom-call | tf_op jit(solution)/shard_map/filter_outer/pallas_call | solution.py:359
  14.0 1.6 %collective-permute-start.1 = (bf16[648,128]{1,0:T(8,128)(2,1)S(1)}, bf16[648,128]{1,0:T(8,128)(2,1)S(1)}, u32[]{:S(2)}, u32[]{:S(2)}) collective-permute-start(bf16[648,128]{1,0:T(8,128)(2,1)S(1)} %get-tuple-element.20), channel_id=1, source_target_pairs={{0,4},{2,6},{4,0},{6,2},{8,12},{10,14},{12,8},{14,10},{1,5},{3,7},... | collective-permute-start | bytes 497672 | tf_op jit(solution)/shard_map/ppermute | solution.py:380
  15.6 2.6 %collective-permute-start.2 = (bf16[648,128]{1,0:T(8,128)(2,1)S(1)}, bf16[648,128]{1,0:T(8,128)(2,1)S(1)}, u32[]{:S(2)}, u32[]{:S(2)}) collective-permute-start(bf16[648,128]{1,0:T(8,128)(2,1)S(1)} %get-tuple-element.21), channel_id=1, source_target_pairs={{0,8},{2,10},{4,12},{6,14},{8,0},{10,2},{12,4},{14,6},{1,9},{3,11}... | collective-permute-start | bytes 497672 | tf_op jit(solution)/shard_map/ppermute | solution.py:380
  18.2 0.2 collective-permute-start.3
  18.4 0.0 collective-permute-start.4
  18.4 1.3 %collective-permute-start.8 = (bf16[320,128]{1,0:T(8,128)(2,1)S(1)}, bf16[320,128]{1,0:T(8,128)(2,1)S(1)}, u32[]{:S(2)}, u32[]{:S(2)}) collective-permute-start(bf16[320,128]{1,0:T(8,128)(2,1)S(1)} %slice.12), channel_id=1, source_target_pairs={{1,0},{3,2},{5,4},{7,6},{9,8},{11,10},{13,12},{15,14},{17,16},{19,... | collective-permute-start | bytes 245768 | tf_op jit(solution)/shard_map/ppermute | solution.py:382
  19.7 5.4 %collective-permute-done.8.rest_8_ = bf16[320,128]{1,0:T(8,128)(2,1)S(1)} collective-permute-done((bf16[320,128]{1,0:T(8,128)(2,1)S(1)}, bf16[320,128]{1,0:T(8,128)(2,1)S(1)}, u32[]{:S(2)}, u32[]{:S(2)}) %collective-permute-start.8) | collective-permute-done | bytes 81952 | tf_op jit(solution)/shard_map/ppermute | solution.py:382
  25.2 0.0 collective-permute-done.1.rest_1_
  25.2 1.3 %collective-permute-start.9 = (bf16[320,128]{1,0:T(8,128)(2,1)S(1)}, bf16[320,128]{1,0:T(8,128)(2,1)S(1)}, u32[]{:S(2)}, u32[]{:S(2)}) collective-permute-start(bf16[320,128]{1,0:T(8,128)(2,1)S(1)} %slice.16), channel_id=1, source_target_pairs={{1,0},{3,2},{5,4},{7,6},{9,8},{11,10},{13,12},{15,14},{17,16},{19,... | collective-permute-start | bytes 245768 | tf_op jit(solution)/shard_map/ppermute | solution.py:382
  26.5 4.2 %collective-permute-done.2.rest_2_ = bf16[648,128]{1,0:T(8,128)(2,1)S(1)} collective-permute-done((bf16[648,128]{1,0:T(8,128)(2,1)S(1)}, bf16[648,128]{1,0:T(8,128)(2,1)S(1)}, u32[]{:S(2)}, u32[]{:S(2)}) %collective-permute-start.2) | collective-permute-done | bytes 165920 | tf_op jit(solution)/shard_map/ppermute | solution.py:380
  30.7 1.3 %collective-permute-start.10 = (bf16[320,128]{1,0:T(8,128)(2,1)S(1)}, bf16[320,128]{1,0:T(8,128)(2,1)S(1)}, u32[]{:S(2)}, u32[]{:S(2)}) collective-permute-start(bf16[320,128]{1,0:T(8,128)(2,1)S(1)} %slice.17), channel_id=1, source_target_pairs={{1,0},{3,2},{5,4},{7,6},{9,8},{11,10},{13,12},{15,14},{17,16},{19,... | collective-permute-start | bytes 245768 | tf_op jit(solution)/shard_map/ppermute | solution.py:382
  32.0 0.1 collective-permute-start.5
  32.1 0.5 collective-permute-start.6
  32.6 0.0 collective-permute-done.4.rest_4_
  32.6 0.1 collective-permute-start.7
  32.7 0.0 collective-permute-done.9.rest_9_
  32.7 1.3 %collective-permute-start.11 = (bf16[320,128]{1,0:T(8,128)(2,1)S(1)}, bf16[320,128]{1,0:T(8,128)(2,1)S(1)}, u32[]{:S(2)}, u32[]{:S(2)}) collective-permute-start(bf16[320,128]{1,0:T(8,128)(2,1)S(1)} %slice.18), channel_id=1, source_target_pairs={{1,0},{3,2},{5,4},{7,6},{9,8},{11,10},{13,12},{15,14},{17,16},{19,... | collective-permute-start | bytes 245768 | tf_op jit(solution)/shard_map/ppermute | solution.py:382
  34.0 3.0 %collective-permute-done.10.rest_10_ = bf16[320,128]{1,0:T(8,128)(2,1)S(1)} collective-permute-done((bf16[320,128]{1,0:T(8,128)(2,1)S(1)}, bf16[320,128]{1,0:T(8,128)(2,1)S(1)}, u32[]{:S(2)}, u32[]{:S(2)}) %collective-permute-start.10) | collective-permute-done | bytes 81952 | tf_op jit(solution)/shard_map/ppermute | solution.py:382
  37.1 0.0 collective-permute-start.13
  37.1 2.6 %collective-permute-done.11.rest_11_ = bf16[320,128]{1,0:T(8,128)(2,1)S(1)} collective-permute-done((bf16[320,128]{1,0:T(8,128)(2,1)S(1)}, bf16[320,128]{1,0:T(8,128)(2,1)S(1)}, u32[]{:S(2)}, u32[]{:S(2)}) %collective-permute-start.11) | collective-permute-done | bytes 81952 | tf_op jit(solution)/shard_map/ppermute | solution.py:382
  39.7 0.0 collective-permute-start.14
  39.7 0.0 collective-permute-done.13.rest_13_
  39.7 0.5 collective-permute-start.15
  40.2 0.8 %collective-permute-done.14.rest_14_ = bf16[320,128]{1,0:T(8,128)(2,1)S(1)} collective-permute-done((bf16[320,128]{1,0:T(8,128)(2,1)S(1)}, bf16[320,128]{1,0:T(8,128)(2,1)S(1)}, u32[]{:S(2)}, u32[]{:S(2)}) %collective-permute-start.14) | collective-permute-done | bytes 81952 | tf_op jit(solution)/shard_map/ppermute | solution.py:386
  40.9 0.2 collective-permute-done.15.rest_15_
  41.1 0.0 collective-permute-done.5.rest_5_
  41.1 0.0 collective-permute-done.6.rest_6_
  41.1 0.0 collective-permute-done.7.rest_7_
  41.1 7.9 %stack_twice.1 = (f32[4,8,128]{2,1,0:T(8,128)S(1)}, f32[4,8,128]{2,1,0:T(8,128)S(1)}, f32[4,8,128]{2,1,0:T(8,128)S(1)}, f32[4,8,128]{2,1,0:T(8,128)S(1)}) custom-call(s32[5]{0:T(128)S(1)} %stack.40.info, bf16[648,128]{1,0:T(8,128)(2,1)S(1)} %get-tuple-element.19.rest_0_, bf16[648,128]{1,0:T(8,128)(2,1)S(1)} %collective-permute-done.1.rest_1_, ...), custom_call_target="tpu_custom_call" | custom-call | tf_op jit(solution)/shard_map/stack_twice/pallas_call | solution.py:393
  49.0 0.5 collective-permute-start.16
  49.5 2.8 %collective-permute-start.17 = (f32[4,8,128]{2,1,0:T(8,128)S(1)}, f32[4,8,128]{2,1,0:T(8,128)S(1)}, u32[]{:S(2)}, u32[]{:S(2)}) collective-permute-start(f32[4,8,128]{2,1,0:T(8,128)S(1)} %get-tuple-element.25), channel_id=1, source_target_pairs={{0,8},{2,10},{4,12},{6,14},{8,0},{10,2},{12,4},{14,6},{1,9},{3,11}... | collective-permute-start | bytes 49160 | tf_op jit(solution)/shard_map/ppermute | solution.py:415
  52.3 1.2 %collective-permute-start.18 = (f32[4,8,128]{2,1,0:T(8,128)S(1)}, f32[4,8,128]{2,1,0:T(8,128)S(1)}, u32[]{:S(2)}, u32[]{:S(2)}) collective-permute-start(f32[4,8,128]{2,1,0:T(8,128)S(1)} %get-tuple-element.26), channel_id=1, source_target_pairs={{0,12},{2,14},{4,8},{6,10},{8,4},{10,6},{12,0},{14,2},{1,13},{3,15... | collective-permute-start | bytes 49160 | tf_op jit(solution)/shard_map/ppermute | solution.py:415
  53.5 0.7 %collective-permute-done.17.rest_2_ = f32[4,8,128]{2,1,0:T(8,128)S(1)} collective-permute-done((f32[4,8,128]{2,1,0:T(8,128)S(1)}, f32[4,8,128]{2,1,0:T(8,128)S(1)}, u32[]{:S(2)}, u32[]{:S(2)}) %collective-permute-start.17) | collective-permute-done | bytes 16416 | tf_op jit(solution)/shard_map/ppermute | solution.py:415
  54.2 3.7 %collective-permute-done.18.rest_3_ = f32[4,8,128]{2,1,0:T(8,128)S(1)} collective-permute-done((f32[4,8,128]{2,1,0:T(8,128)S(1)}, f32[4,8,128]{2,1,0:T(8,128)S(1)}, u32[]{:S(2)}, u32[]{:S(2)}) %collective-permute-start.18) | collective-permute-done | bytes 16416 | tf_op jit(solution)/shard_map/ppermute | solution.py:415
  57.8 0.6 join_columns.1
  58.4 0.1 collective-permute-start.19
  58.5 1.2 %collective-permute-done.19.rest_1_ = f32[4,4,512]{2,1,0:T(4,128)S(1)} collective-permute-done((f32[4,4,512]{2,1,0:T(4,128)S(1)}, f32[4,4,512]{2,1,0:T(4,128)S(1)}, u32[]{:S(2)}, u32[]{:S(2)}) %collective-permute-start.19) | collective-permute-done | bytes 32800 | tf_op jit(solution)/shard_map/ppermute | solution.py:432
  59.7 1.2 %join_velocities.1 = f32[8,4,512]{2,1,0:T(4,128)} custom-call(s32[5]{0:T(128)S(1)} %stack.40.info, f32[4,4,512]{2,1,0:T(4,128)S(1)} %get-tuple-element.27.rest_0_, f32[4,4,512]{2,1,0:T(4,128)S(1)} %collective-permute-done.19.rest_1_), custom_call_target="tpu_custom_call" | custom-call | tf_op jit(solution)/shard_map/join_velocities/pallas_call | solution.py:433
  (18 shorter events, 0.1 us)
Async XLA Ops:
  0.0 4.1 %copy-start = (bf16[8,32,512]{2,1,0:T(8,128)(2,1)S(1)}, bf16[8,32,512]{2,1,0:T(8,128)(2,1)}, u32[]{:S(2)}) copy-start(bf16[8,32,512]{2,1,0:T(8,128)(2,1)} %science.1) | copy-start | bytes 786436
  1.0 9.0 %collective-permute-start = (bf16[2,8,4,512]{3,2,1,0:T(4,128)(2,1)S(1)}, bf16[2,8,4,512]{3,2,1,0:T(4,128)(2,1)S(1)}, u32[]{:S(2)}, u32[]{:S(2)}) collective-permute-start(bf16[2,8,4,512]{3,2,1,0:T(4,128)(2,1)S(1)} %pad_maximum_fusion), channel_id=1, source_target_pairs={{0,1},{1,0},{2,3},{3,2},{4,5},{5,4},{6,7},{7,6},{8,9},{9,8},{10,11... | collective-permute-start | bytes 196616 | tf_op jit(solution)/shard_map/ppermute | solution.py:338
  4.0 0.7 %copy-start.2 = (f32[8,9]{1,0:T(8,128)S(1)}, f32[8,9]{1,0:T(8,128)}, u32[]{:S(2)}) copy-start(f32[8,9]{1,0:T(8,128)} %row_taps.3) | copy-start | bytes 868
  4.0 0.7 %copy-start.3 = (f32[8,9]{1,0:T(8,128)S(1)}, f32[8,9]{1,0:T(8,128)}, u32[]{:S(2)}) copy-start(f32[8,9]{1,0:T(8,128)} %col_taps.3) | copy-start | bytes 868
  4.7 0.9 %copy-start.1 = (bf16[8,32,512]{2,1,0:T(8,128)(2,1)S(1)}, bf16[8,32,512]{2,1,0:T(8,128)(2,1)}, u32[]{:S(2)}) copy-start(bf16[8,32,512]{2,1,0:T(8,128)(2,1)} %inv_var.1) | copy-start | bytes 786436
  5.7 4.3 %copy-start.4 = (s32[8,8]{1,0:T(8,128)S(1)}, s32[8,8]{1,0:T(8,128)}, u32[]{:S(2)}) copy-start(s32[8,8]{1,0:T(8,128)} %row_shift.1) | copy-start | bytes 772
  5.7 4.3 %copy-start.5 = (s32[8,8]{1,0:T(8,128)S(1)}, s32[8,8]{1,0:T(8,128)}, u32[]{:S(2)}) copy-start(s32[8,8]{1,0:T(8,128)} %col_shift.1) | copy-start | bytes 772
  10.0 0.7 %copy-start.6 = (s32[8]{0:T(128)S(1)}, s32[8]{0:T(128)}, u32[]{:S(2)}) copy-start(s32[8]{0:T(128)} %usable.1) | copy-start | bytes 100
  14.0 11.2 %collective-permute-start.1 = (bf16[648,128]{1,0:T(8,128)(2,1)S(1)}, bf16[648,128]{1,0:T(8,128)(2,1)S(1)}, u32[]{:S(2)}, u32[]{:S(2)}) collective-permute-start(bf16[648,128]{1,0:T(8,128)(2,1)S(1)} %get-tuple-element.20), channel_id=1, source_target_pairs={{0,4},{2,6},{4,0},{6,2},{8,12},{10,14},{12,8},{14,10},{1,5},{3,7},... | collective-permute-start | bytes 497672 | tf_op jit(solution)/shard_map/ppermute | solution.py:380
  15.6 15.1 %collective-permute-start.2 = (bf16[648,128]{1,0:T(8,128)(2,1)S(1)}, bf16[648,128]{1,0:T(8,128)(2,1)S(1)}, u32[]{:S(2)}, u32[]{:S(2)}) collective-permute-start(bf16[648,128]{1,0:T(8,128)(2,1)S(1)} %get-tuple-element.21), channel_id=1, source_target_pairs={{0,8},{2,10},{4,12},{6,14},{8,0},{10,2},{12,4},{14,6},{1,9},{3,11}... | collective-permute-start | bytes 497672 | tf_op jit(solution)/shard_map/ppermute | solution.py:380
  18.2 13.9 %collective-permute-start.3 = (bf16[648,128]{1,0:T(8,128)(2,1)S(1)}, bf16[648,128]{1,0:T(8,128)(2,1)S(1)}, u32[]{:S(2)}, u32[]{:S(2)}) collective-permute-start(bf16[648,128]{1,0:T(8,128)(2,1)S(1)} %get-tuple-element.22), channel_id=1, source_target_pairs={{0,12},{2,14},{4,8},{6,10},{8,4},{10,6},{12,0},{14,2},{1,13},{3,15... | collective-permute-start | bytes 497672 | tf_op jit(solution)/shard_map/ppermute | solution.py:380
  18.4 14.2 %collective-permute-start.4 = (bf16[648,128]{1,0:T(8,128)(2,1)S(1)}, bf16[648,128]{1,0:T(8,128)(2,1)S(1)}, u32[]{:S(2)}, u32[]{:S(2)}) collective-permute-start(bf16[648,128]{1,0:T(8,128)(2,1)S(1)} %get-tuple-element.19.rest_0_), channel_id=1, source_target_pairs={{0,2},{2,0},{4,6},{6,4},{8,10},{10,8},{12,14},{14,12},{1,3},{3,1},... | collective-permute-start | bytes 497672 | tf_op jit(solution)/shard_map/ppermute | solution.py:385
  18.4 6.7 %collective-permute-start.8 = (bf16[320,128]{1,0:T(8,128)(2,1)S(1)}, bf16[320,128]{1,0:T(8,128)(2,1)S(1)}, u32[]{:S(2)}, u32[]{:S(2)}) collective-permute-start(bf16[320,128]{1,0:T(8,128)(2,1)S(1)} %slice.12), channel_id=1, source_target_pairs={{1,0},{3,2},{5,4},{7,6},{9,8},{11,10},{13,12},{15,14},{17,16},{19,... | collective-permute-start | bytes 245768 | tf_op jit(solution)/shard_map/ppermute | solution.py:382
  25.2 6.9 %collective-permute-start.12 = (bf16[320,128]{1,0:T(8,128)(2,1)S(1)}, bf16[320,128]{1,0:T(8,128)(2,1)S(1)}, u32[]{:S(2)}, u32[]{:S(2)}) collective-permute-start(bf16[320,128]{1,0:T(8,128)(2,1)S(1)} %collective-permute-done.8.rest_8_), channel_id=1, source_target_pairs={{0,2},{2,0},{4,6},{6,4},{8,10},{10,8},{12,14},{14,12},{1,3},{3,1},... | collective-permute-start | bytes 245768 | tf_op jit(solution)/shard_map/ppermute | solution.py:386
  25.2 7.5 %collective-permute-start.9 = (bf16[320,128]{1,0:T(8,128)(2,1)S(1)}, bf16[320,128]{1,0:T(8,128)(2,1)S(1)}, u32[]{:S(2)}, u32[]{:S(2)}) collective-permute-start(bf16[320,128]{1,0:T(8,128)(2,1)S(1)} %slice.16), channel_id=1, source_target_pairs={{1,0},{3,2},{5,4},{7,6},{9,8},{11,10},{13,12},{15,14},{17,16},{19,... | collective-permute-start | bytes 245768 | tf_op jit(solution)/shard_map/ppermute | solution.py:382
  30.7 6.3 %collective-permute-start.10 = (bf16[320,128]{1,0:T(8,128)(2,1)S(1)}, bf16[320,128]{1,0:T(8,128)(2,1)S(1)}, u32[]{:S(2)}, u32[]{:S(2)}) collective-permute-start(bf16[320,128]{1,0:T(8,128)(2,1)S(1)} %slice.17), channel_id=1, source_target_pairs={{1,0},{3,2},{5,4},{7,6},{9,8},{11,10},{13,12},{15,14},{17,16},{19,... | collective-permute-start | bytes 245768 | tf_op jit(solution)/shard_map/ppermute | solution.py:382
  32.0 9.1 %collective-permute-start.5 = (bf16[648,128]{1,0:T(8,128)(2,1)S(1)}, bf16[648,128]{1,0:T(8,128)(2,1)S(1)}, u32[]{:S(2)}, u32[]{:S(2)}) collective-permute-start(bf16[648,128]{1,0:T(8,128)(2,1)S(1)} %collective-permute-done.1.rest_1_), channel_id=1, source_target_pairs={{0,2},{2,0},{4,6},{6,4},{8,10},{10,8},{12,14},{14,12},{1,3},{3,1},... | collective-permute-start | bytes 497672 | tf_op jit(solution)/shard_map/ppermute | solution.py:385
  32.1 9.0 %collective-permute-start.6 = (bf16[648,128]{1,0:T(8,128)(2,1)S(1)}, bf16[648,128]{1,0:T(8,128)(2,1)S(1)}, u32[]{:S(2)}, u32[]{:S(2)}) collective-permute-start(bf16[648,128]{1,0:T(8,128)(2,1)S(1)} %collective-permute-done.2.rest_2_), channel_id=1, source_target_pairs={{0,2},{2,0},{4,6},{6,4},{8,10},{10,8},{12,14},{14,12},{1,3},{3,1},... | collective-permute-start | bytes 497672 | tf_op jit(solution)/shard_map/ppermute | solution.py:385
  32.6 8.5 %collective-permute-start.7 = (bf16[648,128]{1,0:T(8,128)(2,1)S(1)}, bf16[648,128]{1,0:T(8,128)(2,1)S(1)}, u32[]{:S(2)}, u32[]{:S(2)}) collective-permute-start(bf16[648,128]{1,0:T(8,128)(2,1)S(1)} %collective-permute-done.3.rest_3_), channel_id=1, source_target_pairs={{0,2},{2,0},{4,6},{6,4},{8,10},{10,8},{12,14},{14,12},{1,3},{3,1},... | collective-permute-start | bytes 497672 | tf_op jit(solution)/shard_map/ppermute | solution.py:385
  32.7 6.9 %collective-permute-start.11 = (bf16[320,128]{1,0:T(8,128)(2,1)S(1)}, bf16[320,128]{1,0:T(8,128)(2,1)S(1)}, u32[]{:S(2)}, u32[]{:S(2)}) collective-permute-start(bf16[320,128]{1,0:T(8,128)(2,1)S(1)} %slice.18), channel_id=1, source_target_pairs={{1,0},{3,2},{5,4},{7,6},{9,8},{11,10},{13,12},{15,14},{17,16},{19,... | collective-permute-start | bytes 245768 | tf_op jit(solution)/shard_map/ppermute | solution.py:382
  37.1 2.6 %collective-permute-start.13 = (bf16[320,128]{1,0:T(8,128)(2,1)S(1)}, bf16[320,128]{1,0:T(8,128)(2,1)S(1)}, u32[]{:S(2)}, u32[]{:S(2)}) collective-permute-start(bf16[320,128]{1,0:T(8,128)(2,1)S(1)} %collective-permute-done.9.rest_9_), channel_id=1, source_target_pairs={{0,2},{2,0},{4,6},{6,4},{8,10},{10,8},{12,14},{14,12},{1,3},{3,1},... | collective-permute-start | bytes 245768 | tf_op jit(solution)/shard_map/ppermute | solution.py:386
  39.7 1.3 %collective-permute-start.14 = (bf16[320,128]{1,0:T(8,128)(2,1)S(1)}, bf16[320,128]{1,0:T(8,128)(2,1)S(1)}, u32[]{:S(2)}, u32[]{:S(2)}) collective-permute-start(bf16[320,128]{1,0:T(8,128)(2,1)S(1)} %collective-permute-done.10.rest_10_), channel_id=1, source_target_pairs={{0,2},{2,0},{4,6},{6,4},{8,10},{10,8},{12,14},{14,12},{1,3},{3,1},... | collective-permute-start | bytes 245768 | tf_op jit(solution)/shard_map/ppermute | solution.py:386
  39.7 1.4 %collective-permute-start.15 = (bf16[320,128]{1,0:T(8,128)(2,1)S(1)}, bf16[320,128]{1,0:T(8,128)(2,1)S(1)}, u32[]{:S(2)}, u32[]{:S(2)}) collective-permute-start(bf16[320,128]{1,0:T(8,128)(2,1)S(1)} %collective-permute-done.11.rest_11_), channel_id=1, source_target_pairs={{0,2},{2,0},{4,6},{6,4},{8,10},{10,8},{12,14},{14,12},{1,3},{3,1},... | collective-permute-start | bytes 245768 | tf_op jit(solution)/shard_map/ppermute | solution.py:386
  49.0 4.5 %collective-permute-start.16 = (f32[4,8,128]{2,1,0:T(8,128)S(1)}, f32[4,8,128]{2,1,0:T(8,128)S(1)}, u32[]{:S(2)}, u32[]{:S(2)}) collective-permute-start(f32[4,8,128]{2,1,0:T(8,128)S(1)} %get-tuple-element.24), channel_id=1, source_target_pairs={{0,4},{2,6},{4,0},{6,2},{8,12},{10,14},{12,8},{14,10},{1,5},{3,7},... | collective-permute-start | bytes 49160 | tf_op jit(solution)/shard_map/ppermute | solution.py:415
  49.5 4.6 %collective-permute-start.17 = (f32[4,8,128]{2,1,0:T(8,128)S(1)}, f32[4,8,128]{2,1,0:T(8,128)S(1)}, u32[]{:S(2)}, u32[]{:S(2)}) collective-permute-start(f32[4,8,128]{2,1,0:T(8,128)S(1)} %get-tuple-element.25), channel_id=1, source_target_pairs={{0,8},{2,10},{4,12},{6,14},{8,0},{10,2},{12,4},{14,6},{1,9},{3,11}... | collective-permute-start | bytes 49160 | tf_op jit(solution)/shard_map/ppermute | solution.py:415
  52.3 5.5 %collective-permute-start.18 = (f32[4,8,128]{2,1,0:T(8,128)S(1)}, f32[4,8,128]{2,1,0:T(8,128)S(1)}, u32[]{:S(2)}, u32[]{:S(2)}) collective-permute-start(f32[4,8,128]{2,1,0:T(8,128)S(1)} %get-tuple-element.26), channel_id=1, source_target_pairs={{0,12},{2,14},{4,8},{6,10},{8,4},{10,6},{12,0},{14,2},{1,13},{3,15... | collective-permute-start | bytes 49160 | tf_op jit(solution)/shard_map/ppermute | solution.py:415
  58.4 1.3 %collective-permute-start.19 = (f32[4,4,512]{2,1,0:T(4,128)S(1)}, f32[4,4,512]{2,1,0:T(4,128)S(1)}, u32[]{:S(2)}, u32[]{:S(2)}) collective-permute-start(f32[4,4,512]{2,1,0:T(4,128)S(1)} %get-tuple-element.28), channel_id=1, source_target_pairs={{0,2},{2,0},{4,6},{6,4},{8,10},{10,8},{12,14},{14,12},{1,3},{3,1},... | collective-permute-start | bytes 98312 | tf_op jit(solution)/shard_map/ppermute | solution.py:432

commit v4 on v3

--- a/solution.py
+++ b/solution.py
@@ -121,16 +121,16 @@
                 edges[t, pl.ds(pl.multiple_of(at, SUBLANES), SUBLANES)] = pack_edges(quarters, t)
         return carry
 
-    lax.fori_loop(0, exposures, one_exposure, 0)
+    lax.fori_loop(0, exposures, one_exposure, 0, unroll=2)
 
 
 def outer_kernel(
     radius, chunks, info, row_taps, col_taps, usable, row_shift, col_shift, maps, edges, above, below, *rest
 ):
-    sends, (pixels, colpass, more, more_edges, params) = rest[:chunks], rest[chunks:]
     exposures, vels = row_shift.shape
     tiles = maps.shape[0]
     parts = edges.shape[1] // (exposures * SUBLANES)
+    sends, (pixels, colpass, more, more_edges, params) = rest[: chunks * parts], rest[chunks * parts :]
     taps = 2 * radius + 1
     pad = SUBLANES
     has_above, has_below, own = info[0] > 0, info[1] > 0, info[2]
@@ -164,12 +164,12 @@
             more_edges[1, t, e] = pack_edges([None, lower[0], None, lower[1]], t)
         return carry
 
-    lax.fori_loop(0, exposures, one_exposure, 0)
+    lax.fori_loop(0, exposures, one_exposure, 0, unroll=4)
     main = exposures * 2 * SHIFT
-    size = main + exposures * SUBLANES
     for step in range(chunks):
         to = partner(own, step, chunks)
         for p in range(parts):
+            out = sends[step * parts + p]
             for k in range(2 * exposures):
                 first = maps[to, p * main + k * SHIFT : p * main + k * SHIFT + SUBLANES]
                 second = maps[to, p * main + k * SHIFT + SUBLANES : p * main + (k + 1) * SHIFT]
@@ -177,39 +177,38 @@
                     first = first + more[0, to, k]
                 if p == parts - 1:
                     second = second + more[1, to, k]
-                at = p * size + k * SHIFT
-                sends[step][at : at + SHIFT] = jnp.concatenate([first, second]).astype(jnp.bfloat16)
+                out[k * SHIFT : (k + 1) * SHIFT] = jnp.concatenate([first, second]).astype(jnp.bfloat16)
             packed = edges[to, p * exposures * SUBLANES : (p + 1) * exposures * SUBLANES]
             if p == 0:
                 packed = packed + more_edges[0, to].reshape(packed.shape)
             if p == parts - 1:
                 packed = packed + more_edges[1, to].reshape(packed.shape)
-            sends[step][p * size + main : (p + 1) * size] = packed.astype(jnp.bfloat16)
-        sends[step][parts * size : parts * size + exposures] = params[...].astype(jnp.bfloat16)
+            out[main : main + exposures * SUBLANES] = packed.astype(jnp.bfloat16)
+            if p == parts - 1:
+                tail = main + exposures * SUBLANES
+                out[tail : tail + exposures] = params[...].astype(jnp.bfloat16)
 
 
 def stack_kernel(groups, chunks, exposures, rows, vels, info, *rest):
-    bodies = rest[:groups]
-    tops = rest[groups : 2 * groups]
-    outs = rest[2 * groups : 2 * groups + chunks]
-    main, side, windows, edge, whole_params, scalars, order, result, sem = rest[2 * groups + chunks :]
+    parts = rows // SHIFT
+    blocks = [rest[p * groups : (p + 1) * groups] for p in range(parts + 1)]
+    rest = rest[(parts + 1) * groups :]
+    outs = rest[:chunks]
+    main, side, windows, edge, whole_params, scalars, order, result, sem = rest[chunks:]
     own = info[2]
     first_vel = info[4]
     share = result.shape[0]
-    parts = rows // SHIFT
     main_rows = exposures * 2 * SHIFT
-    edge_rows = exposures * SUBLANES
-    size = main_rows + edge_rows
+    size = main_rows + exposures * SUBLANES
     for g in range(groups):
         whole_params[g * exposures : (g + 1) * exposures] = (
-            bodies[g][parts * size : parts * size + exposures].astype(jnp.float32).astype(jnp.int32)
+            blocks[parts - 1][g][size : size + exposures].astype(jnp.float32).astype(jnp.int32)
         )
     fetch = pltpu.make_async_copy(whole_params, scalars, sem)
     fetch.start()
     for g in range(groups):
-        for p in range(parts):
-            edge[g, p] = bodies[g][p * size + main_rows : (p + 1) * size].astype(jnp.float32)
-        edge[g, parts] = tops[g][main_rows:size].astype(jnp.float32)
+        for p in range(parts + 1):
+            edge[g, p] = blocks[p][g][main_rows:size].astype(jnp.float32)
     fetch.wait()
     filled = jnp.int32(0)
     for g in range(groups):
@@ -217,9 +216,8 @@
         def unpack(e, at, g=g):
             order[at] = g * exposures + e
             for p in range(parts + 1):
-                source, offset = (bodies[g], p * size) if p < parts else (tops[g], 0)
-                start = pl.multiple_of(offset + e * 2 * SHIFT, 2 * SUBLANES)
-                both = source[pl.ds(start, 2 * SHIFT)].astype(jnp.float32)
+                start = pl.multiple_of(e * 2 * SHIFT, 2 * SHIFT)
+                both = blocks[p][g][pl.ds(start, 2 * SHIFT)].astype(jnp.float32)
                 packed = edge[g, p, pl.ds(pl.multiple_of(e * SUBLANES, SUBLANES), SUBLANES)]
                 for m in (0, 1):
                     main[at, m, p * SHIFT : (p + 1) * SHIFT] = both[m * SHIFT : (m + 1) * SHIFT]
@@ -355,12 +353,16 @@
         cost_estimate=pl.CostEstimate(flops=100_000_000, bytes_accessed=4_000_000, transcendentals=0),
         name="filter_inner",
     )(psf_rows, psf_cols, science, inv_var)
-    sent = jax.ShapeDtypeStruct((map_rows + edge_rows + exposures, LANES), jnp.bfloat16)
+    block = exposures * (2 * SHIFT + SUBLANES)
+    sent = [
+        jax.ShapeDtypeStruct((block + (exposures if p == parts - 1 else 0), LANES), jnp.bfloat16)
+        for p in range(parts)
+    ]
     sends = pl.pallas_call(
         functools.partial(outer_kernel, radius, chunks),
-        out_shape=[sent] * chunks,
+        out_shape=sent * chunks,
         in_specs=[SMEM] * 4 + [VMEM] * 6,
-        out_specs=[VMEM] * chunks,
+        out_specs=[VMEM] * (chunks * parts),
         scratch_shapes=[
             pltpu.VMEM((2, 2 * radius, columns), jnp.float32),
             pltpu.VMEM((2, chunks, 3 * SUBLANES, LANES), jnp.float32),
@@ -372,20 +374,21 @@
         name="filter_outer",
     )(info, psf_rows, psf_cols, exposure_ok, row_shift, col_shift, maps, edges, above, below)
 
-    top_rows = (map_rows + edge_rows) // parts
-    bodies, tops = [], []
+    blocks = [[[None] * chunks for _ in range(subs)] for _ in range(parts + 1)]
+    up = [(i + 1, i) for i in range(strips - 1)]
     for step in range(chunks):
-        body = sends[step]
-        if step:
-            body = lax.ppermute(body, "expo", chunk_pairs(step, chunks, subs))
-        bodies.append(body)
-        tops.append(lax.ppermute(body[:top_rows], "strip", [(i + 1, i) for i in range(strips - 1)]))
-    for step in range(1, subs):
-        pairs = sub_pairs(step, chunks, subs)
-        bodies += [lax.ppermute(block, "expo", pairs) for block in bodies[:chunks]]
-        tops += [lax.ppermute(block, "expo", pairs) for block in tops[:chunks]]
-
-    groups = len(bodies)
+        for p in range(parts):
+            blocks[p][0][step] = sends[step * parts + p]
+            if step:
+                blocks[p][0][step] = lax.ppermute(sends[step * parts + p], "expo", chunk_pairs(step, chunks, subs))
+        blocks[parts][0][step] = lax.ppermute(blocks[0][0][step], "strip", up)
+    for p in range(parts + 1):
+        for u in range(1, subs):
+            for step in range(chunks):
+                blocks[p][u][step] = lax.ppermute(blocks[p][0][step], "expo", sub_pairs(u, chunks, subs))
+    blocks = [[block for sub in part for block in sub] for part in blocks]
+
+    groups = len(blocks[0])
     block_rows = rows // chunks
     reach = rows + SHIFT
     piece = jax.ShapeDtypeStruct((share, block_rows, LANES), jnp.float32)
@@ -393,7 +396,7 @@
     pieces = pl.pallas_call(
         functools.partial(stack_kernel, groups, chunks, exposures, rows, vels),
         out_shape=[piece] * chunks,
-        in_specs=[SMEM] + [VMEM] * (2 * groups),
+        in_specs=[SMEM] + [VMEM] * ((parts + 1) * groups),
         out_specs=[VMEM] * chunks,
         scratch_shapes=[
             pltpu.VMEM((total + UNROLL, 2, reach, LANES), jnp.float32),
@@ -408,7 +411,7 @@
         ],
         compiler_params=pltpu.CompilerParams(vmem_limit_bytes=24 << 20),
         name="stack_twice",
-    )(info, *bodies, *tops)
+    )(info, *[block for part in blocks for block in part])
 
     held = [pieces[0]]
     for step in range(1, chunks):
@@ -453,6 +456,5 @@
         P(("field", "expo")),
     )
     out_specs = P("strip", "field", "expo", None)
-    return jax.shard_map(
-        per_device, mesh=mesh, in_specs=in_specs, out_specs=out_specs, check_vma=False
-    )
+
+    return jax.shard_map(per_device, mesh=mesh, in_specs=in_specs, out_specs=out_specs, check_vma=False)

time: 61.1 us -> 59.4 us (0.972)
  waiting for transfers between devices: 21.8 us -> 13.2 us
  starting transfers between devices: 18.3 us -> 26.3 us
  Pallas kernels: 17.2 us -> 16.1 us
    ppermute x15 -> x22, starting transfers between devices: 10.8 us -> 18.8 us  [the longest x6 11 us: per_device(): lax.ppermute(sends[step * parts + p], 'expo', chunk_pairs(step, chunks, s...]
    ppermute x15 -> x22, waiting for transfers between devices: 16.3 us -> 8.32 us  [the longest x4 4.68 us: per_device(): blocks[parts][0][step] = lax.ppermute(blocks[0][0][step], 'strip', up)]
    pallas_call x1, Pallas kernels: 3.29 us -> 2.39 us  [per_device(): pl.pallas_call(functools.partial(outer_kernel, radius, chunks), out_shape...]
    ppermute x3, waiting for transfers between devices: 4.33 us -> 3.65 us  [per_device(): lax.ppermute(pieces[step], 'expo', chunk_pairs(step, chunks, subs))]
  transfers between devices with their start and end apart: 20 -> 27, of which waited for: 9 -> 12; matrix products, arithmetic and copies ran while one was open for 0% -> 0% of each run, Pallas kernels for 7% -> 7%
where the time goes in v4:
time: 59.4 us; the launch traced here: 59.1 us
  starting transfers between devices  26.3 us (44%)
  Pallas kernels  16.1 us (27%)
  waiting for transfers between devices  13.2 us (22%)
  local copies, waits for them, and re-layouts  3.24 us (5%)
    ppermute x6, starting transfers between devices, per_device(): lax.ppermute(sends[step * parts + p], 'expo', chunk_pairs(step, chunks, s...  11 us
    pallas_call x1, Pallas kernels, per_device(): pl.pallas_call(functools.partial(stack_kernel, groups, chunks, exposures,...  7.87 us
    ppermute x4, starting transfers between devices, per_device(): blocks[parts][0][step] = lax.ppermute(blocks[0][0][step], 'strip', up)  5.13 us
    ppermute x4, waiting for transfers between devices, per_device(): blocks[parts][0][step] = lax.ppermute(blocks[0][0][step], 'strip', up)  4.68 us
    ppermute x3, starting transfers between devices, per_device(): lax.ppermute(pieces[step], 'expo', chunk_pairs(step, chunks, subs))  4.45 us
    pallas_call x1, Pallas kernels, per_device(): pl.pallas_call(functools.partial(inner_kernel, radius), out_shape=[jax.Sh...  4.13 us
    ppermute x3, waiting for transfers between devices, per_device(): lax.ppermute(pieces[step], 'expo', chunk_pairs(step, chunks, subs))  3.65 us
    ppermute x1, starting transfers between devices, per_device(): above = below = lax.ppermute(met, 'strip', [(0, 1), (1, 0)])  3.03 us
  transfers between devices with their start and end apart: 27, of which 12 were waited for; matrix products, arithmetic and copies ran while one was open for 0% of the time, Pallas kernels for 7%

profile of v4, /device:TPU:0, one launch (start us, length us, event | category | flops | bytes accessed | tf_op | source)
XLA Modules:
  0.0 59.1 jit_solution(11187628840443402112)
XLA Ops:
  0.0 1.0 %dynamic-slice_bitcast_fusion = (bf16[1,8,4,512]{3,2,1,0:T(4,128)(2,1)S(1)}, bf16[1,8,4,512]{3,2,1,0:T(4,128)(2,1)S(1)}) fusion(bf16[8,32,512]{2,1,0:T(8,128)(2,1)} %inv_var.1, s32[]{:T(128)S(6)} %select_n.19, bf16[8,32,512]{2,1,0:T(8,128)(2,1)} %science.1), kind=kLoop, calls=%fused_computation.1 | loop fusion | bytes 131076 | tf_op jit(solution)/shard_map/stack | solution.py:332
  1.0 3.0 %collective-permute-start = (bf16[2,8,4,512]{3,2,1,0:T(4,128)(2,1)S(1)}, bf16[2,8,4,512]{3,2,1,0:T(4,128)(2,1)S(1)}, u32[]{:S(2)}, u32[]{:S(2)}) collective-permute-start(bf16[2,8,4,512]{3,2,1,0:T(4,128)(2,1)S(1)} %pad_maximum_fusion), channel_id=1, source_target_pairs={{0,1},{1,0},{2,3},{3,2},{4,5},{5,4},{6,7},{7,6},{8,9},{9,8},{10,11... | collective-permute-start | bytes 196616 | tf_op jit(solution)/shard_map/ppermute | solution.py:336
  4.0 0.1 stack.40.info
  4.1 0.6 %copy-done.2 = f32[8,9]{1,0:T(8,128)S(1)} copy-done((f32[8,9]{1,0:T(8,128)S(1)}, f32[8,9]{1,0:T(8,128)}, u32[]{:S(2)}) %copy-start.2) | copy-done | bytes 312
  4.7 0.0 copy-done.3
  4.8 0.9 %copy-done.1 = bf16[8,32,512]{2,1,0:T(8,128)(2,1)S(1)} copy-done((bf16[8,32,512]{2,1,0:T(8,128)(2,1)S(1)}, bf16[8,32,512]{2,1,0:T(8,128)(2,1)}, u32[]{:S(2)}) %copy-start.1) | copy-done | bytes 262168
  5.7 4.1 %filter_inner.1 = (f32[4,512,128]{2,1,0:T(8,128)S(1)}, f32[4,128,128]{2,1,0:T(8,128)S(1)}) custom-call(f32[8,9]{1,0:T(8,128)S(1)} %copy-done.2, f32[8,9]{1,0:T(8,128)S(1)} %copy-done.3, bf16[8,32,512]{2,1,0:T(8,128)(2,1)S(1)} %copy-done, bf16[8,32,512]{2,1,0:T(8,128)(2,1)S(1)} %copy-done.1), custom_call_target="tpu_custom_call" | custom-call | flops 100000000 | bytes 4000000 | tf_op jit(solution)/shard_map/filter_inner/pallas_call | solution.py:343
  9.8 0.0 collective-permute-done.above.below
  9.9 0.0 copy-start.6
  9.9 0.6 %copy-done.6 = s32[8]{0:T(128)S(1)} copy-done((s32[8]{0:T(128)S(1)}, s32[8]{0:T(128)}, u32[]{:S(2)}) %copy-start.6) | copy-done | bytes 56
  10.5 2.4 %filter_outer.1 = (bf16[320,128]{1,0:T(8,128)(2,1)S(1)}, bf16[328,128]{1,0:T(8,128)(2,1)S(1)}, bf16[320,128]{1,0:T(8,128)(2,1)S(1)}, bf16[328,128]{1,0:T(8,128)(...) custom-call(s32[5]{0:T(128)S(1)} %stack.40.info, ...), custom_call_target="tpu_custom_call" | custom-call | tf_op jit(solution)/shard_map/filter_outer/pallas_call | solution.py:361
  12.9 1.6 %collective-permute-start.1 = (bf16[320,128]{1,0:T(8,128)(2,1)S(1)}, bf16[320,128]{1,0:T(8,128)(2,1)S(1)}, u32[]{:S(2)}, u32[]{:S(2)}) collective-permute-start(bf16[320,128]{1,0:T(8,128)(2,1)S(1)} %get-tuple-element.24), channel_id=1, source_target_pairs={{0,4},{2,6},{4,0},{6,2},{8,12},{10,14},{12,8},{14,10},{1,5},{3,7},... | collective-permute-start | bytes 245768 | tf_op jit(solution)/shard_map/ppermute | solution.py:383
  14.5 2.6 %collective-permute-start.2 = (bf16[320,128]{1,0:T(8,128)(2,1)S(1)}, bf16[320,128]{1,0:T(8,128)(2,1)S(1)}, u32[]{:S(2)}, u32[]{:S(2)}) collective-permute-start(bf16[320,128]{1,0:T(8,128)(2,1)S(1)} %get-tuple-element.25), channel_id=1, source_target_pairs={{0,8},{2,10},{4,12},{6,14},{8,0},{10,2},{12,4},{14,6},{1,9},{3,11}... | collective-permute-start | bytes 245768 | tf_op jit(solution)/shard_map/ppermute | solution.py:383
  17.1 0.2 collective-permute-start.3
  17.4 1.3 %collective-permute-start.15 = (bf16[320,128]{1,0:T(8,128)(2,1)S(1)}, bf16[320,128]{1,0:T(8,128)(2,1)S(1)}, u32[]{:S(2)}, u32[]{:S(2)}) collective-permute-start(bf16[320,128]{1,0:T(8,128)(2,1)S(1)} %get-tuple-element.23.rest_0_), channel_id=1, source_target_pairs={{1,0},{3,2},{5,4},{7,6},{9,8},{11,10},{13,12},{15,14},{17,16},{19,... | collective-permute-start | bytes 245768 | tf_op jit(solution)/shard_map/ppermute | solution.py:384
  18.6 0.7 %collective-permute-start.8 = (bf16[328,128]{1,0:T(8,128)(2,1)S(1)}, bf16[328,128]{1,0:T(8,128)(2,1)S(1)}, u32[]{:S(2)}, u32[]{:S(2)}) collective-permute-start(bf16[328,128]{1,0:T(8,128)(2,1)S(1)} %get-tuple-element.28), channel_id=1, source_target_pairs={{0,4},{2,6},{4,0},{6,2},{8,12},{10,14},{12,8},{14,10},{1,5},{3,7},... | collective-permute-start | bytes 251912 | tf_op jit(solution)/shard_map/ppermute | solution.py:383
  19.4 3.5 %collective-permute-start.9 = (bf16[328,128]{1,0:T(8,128)(2,1)S(1)}, bf16[328,128]{1,0:T(8,128)(2,1)S(1)}, u32[]{:S(2)}, u32[]{:S(2)}) collective-permute-start(bf16[328,128]{1,0:T(8,128)(2,1)S(1)} %get-tuple-element.29), channel_id=1, source_target_pairs={{0,8},{2,10},{4,12},{6,14},{8,0},{10,2},{12,4},{14,6},{1,9},{3,11}... | collective-permute-start | bytes 251912 | tf_op jit(solution)/shard_map/ppermute | solution.py:383
  22.9 1.5 %collective-permute-done.3.rest_3_ = bf16[320,128]{1,0:T(8,128)(2,1)S(1)} collective-permute-done((bf16[320,128]{1,0:T(8,128)(2,1)S(1)}, bf16[320,128]{1,0:T(8,128)(2,1)S(1)}, u32[]{:S(2)}, u32[]{:S(2)}) %collective-permute-start.3) | collective-permute-done | bytes 81952 | tf_op jit(solution)/shard_map/ppermute | solution.py:383
  24.3 2.3 %collective-permute-start.10 = (bf16[328,128]{1,0:T(8,128)(2,1)S(1)}, bf16[328,128]{1,0:T(8,128)(2,1)S(1)}, u32[]{:S(2)}, u32[]{:S(2)}) collective-permute-start(bf16[328,128]{1,0:T(8,128)(2,1)S(1)} %get-tuple-element.30), channel_id=1, source_target_pairs={{0,12},{2,14},{4,8},{6,10},{8,4},{10,6},{12,0},{14,2},{1,13},{3,15... | collective-permute-start | bytes 251912 | tf_op jit(solution)/shard_map/ppermute | solution.py:383
  26.6 0.2 collective-permute-start.11
  26.9 1.3 %collective-permute-start.16 = (bf16[320,128]{1,0:T(8,128)(2,1)S(1)}, bf16[320,128]{1,0:T(8,128)(2,1)S(1)}, u32[]{:S(2)}, u32[]{:S(2)}) collective-permute-start(bf16[320,128]{1,0:T(8,128)(2,1)S(1)} %collective-permute-done.1.rest_1_), channel_id=1, source_target_pairs={{1,0},{3,2},{5,4},{7,6},{9,8},{11,10},{13,12},{15,14},{17,16},{19,... | collective-permute-start | bytes 245768 | tf_op jit(solution)/shard_map/ppermute | solution.py:384
  28.2 0.3 collective-permute-start.5
  28.5 1.2 %collective-permute-done.9.rest_10_ = bf16[328,128]{1,0:T(8,128)(2,1)S(1)} collective-permute-done((bf16[328,128]{1,0:T(8,128)(2,1)S(1)}, bf16[328,128]{1,0:T(8,128)(2,1)S(1)}, u32[]{:S(2)}, u32[]{:S(2)}) %collective-permute-start.9) | collective-permute-done | bytes 84000 | tf_op jit(solution)/shard_map/ppermute | solution.py:383
  29.7 1.3 %collective-permute-start.17 = (bf16[320,128]{1,0:T(8,128)(2,1)S(1)}, bf16[320,128]{1,0:T(8,128)(2,1)S(1)}, u32[]{:S(2)}, u32[]{:S(2)}) collective-permute-start(bf16[320,128]{1,0:T(8,128)(2,1)S(1)} %collective-permute-done.2.rest_2_), channel_id=1, source_target_pairs={{1,0},{3,2},{5,4},{7,6},{9,8},{11,10},{13,12},{15,14},{17,16},{19,... | collective-permute-start | bytes 245768 | tf_op jit(solution)/shard_map/ppermute | solution.py:384
  31.0 0.1 collective-permute-start.6
  31.1 1.3 %collective-permute-start.18 = (bf16[320,128]{1,0:T(8,128)(2,1)S(1)}, bf16[320,128]{1,0:T(8,128)(2,1)S(1)}, u32[]{:S(2)}, u32[]{:S(2)}) collective-permute-start(bf16[320,128]{1,0:T(8,128)(2,1)S(1)} %collective-permute-done.3.rest_3_), channel_id=1, source_target_pairs={{1,0},{3,2},{5,4},{7,6},{9,8},{11,10},{13,12},{15,14},{17,16},{19,... | collective-permute-start | bytes 245768 | tf_op jit(solution)/shard_map/ppermute | solution.py:384
  32.4 0.9 %collective-permute-done.16.rest_17_ = bf16[320,128]{1,0:T(8,128)(2,1)S(1)} collective-permute-done((bf16[320,128]{1,0:T(8,128)(2,1)S(1)}, bf16[320,128]{1,0:T(8,128)(2,1)S(1)}, u32[]{:S(2)}, u32[]{:S(2)}) %collective-permute-start.16) | collective-permute-done | bytes 81952 | tf_op jit(solution)/shard_map/ppermute | solution.py:384
  33.4 0.5 collective-permute-start.7
  33.9 2.2 %collective-permute-done.17.rest_18_ = bf16[320,128]{1,0:T(8,128)(2,1)S(1)} collective-permute-done((bf16[320,128]{1,0:T(8,128)(2,1)S(1)}, bf16[320,128]{1,0:T(8,128)(2,1)S(1)}, u32[]{:S(2)}, u32[]{:S(2)}) %collective-permute-start.17) | collective-permute-done | bytes 81952 | tf_op jit(solution)/shard_map/ppermute | solution.py:384
  36.1 0.5 collective-permute-start.13
  36.6 1.6 %collective-permute-done.18.rest_19_ = bf16[320,128]{1,0:T(8,128)(2,1)S(1)} collective-permute-done((bf16[320,128]{1,0:T(8,128)(2,1)S(1)}, bf16[320,128]{1,0:T(8,128)(2,1)S(1)}, u32[]{:S(2)}, u32[]{:S(2)}) %collective-permute-start.18) | collective-permute-done | bytes 81952 | tf_op jit(solution)/shard_map/ppermute | solution.py:384
  38.1 0.5 collective-permute-start.20
  38.7 0.1 collective-permute-start.21
  38.7 0.4 collective-permute-start.22
  39.2 0.2 collective-permute-done.14.rest_15_
  39.4 0.2 collective-permute-done.20.rest_21_
  39.6 0.4 collective-permute-done.21.rest_22_
  39.9 0.2 collective-permute-done.22.rest_23_
  40.1 7.9 %stack_twice.1 = (f32[4,8,128]{2,1,0:T(8,128)S(1)}, f32[4,8,128]{2,1,0:T(8,128)S(1)}, f32[4,8,128]{2,1,0:T(8,128)S(1)}, f32[4,8,128]{2,1,0:T(8,128)S(1)}) custom-call(s32[5]{0:T(128)S(1)} %stack.40.info, bf16[320,128]{1,0:T(8,128)(2,1)S(1)} %get-tuple-element.23.rest_0_, bf16[320,128]{1,0:T(8,128)(2,1)S(1)} %collective-permute-done.1.rest_1_, ...), custom_call_target="tpu_custom_call" | custom-call | tf_op jit(solution)/shard_map/stack_twice/pallas_call | solution.py:396
  48.0 1.6 %collective-permute-start.23 = (f32[4,8,128]{2,1,0:T(8,128)S(1)}, f32[4,8,128]{2,1,0:T(8,128)S(1)}, u32[]{:S(2)}, u32[]{:S(2)}) collective-permute-start(f32[4,8,128]{2,1,0:T(8,128)S(1)} %get-tuple-element.32), channel_id=1, source_target_pairs={{0,4},{2,6},{4,0},{6,2},{8,12},{10,14},{12,8},{14,10},{1,5},{3,7},... | collective-permute-start | bytes 49160 | tf_op jit(solution)/shard_map/ppermute | solution.py:418
  49.6 1.0 %collective-permute-start.24 = (f32[4,8,128]{2,1,0:T(8,128)S(1)}, f32[4,8,128]{2,1,0:T(8,128)S(1)}, u32[]{:S(2)}, u32[]{:S(2)}) collective-permute-start(f32[4,8,128]{2,1,0:T(8,128)S(1)} %get-tuple-element.33), channel_id=1, source_target_pairs={{0,8},{2,10},{4,12},{6,14},{8,0},{10,2},{12,4},{14,6},{1,9},{3,11}... | collective-permute-start | bytes 49160 | tf_op jit(solution)/shard_map/ppermute | solution.py:418
  50.5 1.9 %collective-permute-start.25 = (f32[4,8,128]{2,1,0:T(8,128)S(1)}, f32[4,8,128]{2,1,0:T(8,128)S(1)}, u32[]{:S(2)}, u32[]{:S(2)}) collective-permute-start(f32[4,8,128]{2,1,0:T(8,128)S(1)} %get-tuple-element.34), channel_id=1, source_target_pairs={{0,12},{2,14},{4,8},{6,10},{8,4},{10,6},{12,0},{14,2},{1,13},{3,15... | collective-permute-start | bytes 49160 | tf_op jit(solution)/shard_map/ppermute | solution.py:418
  52.4 1.9 %collective-permute-done.24.rest_2_ = f32[4,8,128]{2,1,0:T(8,128)S(1)} collective-permute-done((f32[4,8,128]{2,1,0:T(8,128)S(1)}, f32[4,8,128]{2,1,0:T(8,128)S(1)}, u32[]{:S(2)}, u32[]{:S(2)}) %collective-permute-start.24) | collective-permute-done | bytes 16416 | tf_op jit(solution)/shard_map/ppermute | solution.py:418
  54.3 1.7 %collective-permute-done.25.rest_3_ = f32[4,8,128]{2,1,0:T(8,128)S(1)} collective-permute-done((f32[4,8,128]{2,1,0:T(8,128)S(1)}, f32[4,8,128]{2,1,0:T(8,128)S(1)}, u32[]{:S(2)}, u32[]{:S(2)}) %collective-permute-start.25) | collective-permute-done | bytes 16416 | tf_op jit(solution)/shard_map/ppermute | solution.py:418
  56.1 0.6 join_columns.1
  56.6 0.1 collective-permute-start.26
  56.7 1.2 %collective-permute-done.26.rest_1_ = f32[4,4,512]{2,1,0:T(4,128)S(1)} collective-permute-done((f32[4,4,512]{2,1,0:T(4,128)S(1)}, f32[4,4,512]{2,1,0:T(4,128)S(1)}, u32[]{:S(2)}, u32[]{:S(2)}) %collective-permute-start.26) | collective-permute-done | bytes 32800 | tf_op jit(solution)/shard_map/ppermute | solution.py:435
  57.9 1.2 %join_velocities.1 = f32[8,4,512]{2,1,0:T(4,128)} custom-call(s32[5]{0:T(128)S(1)} %stack.40.info, f32[4,4,512]{2,1,0:T(4,128)S(1)} %get-tuple-element.35.rest_0_, f32[4,4,512]{2,1,0:T(4,128)S(1)} %collective-permute-done.26.rest_1_), custom_call_target="tpu_custom_call" | custom-call | tf_op jit(solution)/shard_map/join_velocities/pallas_call | solution.py:436
  (28 shorter events, 0.1 us)
Async XLA Ops:
  0.0 4.1 %copy-start = (bf16[8,32,512]{2,1,0:T(8,128)(2,1)S(1)}, bf16[8,32,512]{2,1,0:T(8,128)(2,1)}, u32[]{:S(2)}) copy-start(bf16[8,32,512]{2,1,0:T(8,128)(2,1)} %science.1) | copy-start | bytes 786436
  1.0 8.8 %collective-permute-start = (bf16[2,8,4,512]{3,2,1,0:T(4,128)(2,1)S(1)}, bf16[2,8,4,512]{3,2,1,0:T(4,128)(2,1)S(1)}, u32[]{:S(2)}, u32[]{:S(2)}) collective-permute-start(bf16[2,8,4,512]{3,2,1,0:T(4,128)(2,1)S(1)} %pad_maximum_fusion), channel_id=1, source_target_pairs={{0,1},{1,0},{2,3},{3,2},{4,5},{5,4},{6,7},{7,6},{8,9},{9,8},{10,11... | collective-permute-start | bytes 196616 | tf_op jit(solution)/shard_map/ppermute | solution.py:336
  4.0 0.7 %copy-start.2 = (f32[8,9]{1,0:T(8,128)S(1)}, f32[8,9]{1,0:T(8,128)}, u32[]{:S(2)}) copy-start(f32[8,9]{1,0:T(8,128)} %row_taps.3) | copy-start | bytes 868
  4.0 0.7 %copy-start.3 = (f32[8,9]{1,0:T(8,128)S(1)}, f32[8,9]{1,0:T(8,128)}, u32[]{:S(2)}) copy-start(f32[8,9]{1,0:T(8,128)} %col_taps.3) | copy-start | bytes 868
  4.7 0.9 %copy-start.1 = (bf16[8,32,512]{2,1,0:T(8,128)(2,1)S(1)}, bf16[8,32,512]{2,1,0:T(8,128)(2,1)}, u32[]{:S(2)}) copy-start(bf16[8,32,512]{2,1,0:T(8,128)(2,1)} %inv_var.1) | copy-start | bytes 786436
  5.7 4.2 %copy-start.4 = (s32[8,8]{1,0:T(8,128)S(1)}, s32[8,8]{1,0:T(8,128)}, u32[]{:S(2)}) copy-start(s32[8,8]{1,0:T(8,128)} %row_shift.1) | copy-start | bytes 772
  5.7 4.2 %copy-start.5 = (s32[8,8]{1,0:T(8,128)S(1)}, s32[8,8]{1,0:T(8,128)}, u32[]{:S(2)}) copy-start(s32[8,8]{1,0:T(8,128)} %col_shift.1) | copy-start | bytes 772
  9.9 0.7 %copy-start.6 = (s32[8]{0:T(128)S(1)}, s32[8]{0:T(128)}, u32[]{:S(2)}) copy-start(s32[8]{0:T(128)} %usable.1) | copy-start | bytes 100
  12.9 6.5 %collective-permute-start.1 = (bf16[320,128]{1,0:T(8,128)(2,1)S(1)}, bf16[320,128]{1,0:T(8,128)(2,1)S(1)}, u32[]{:S(2)}, u32[]{:S(2)}) collective-permute-start(bf16[320,128]{1,0:T(8,128)(2,1)S(1)} %get-tuple-element.24), channel_id=1, source_target_pairs={{0,4},{2,6},{4,0},{6,2},{8,12},{10,14},{12,8},{14,10},{1,5},{3,7},... | collective-permute-start | bytes 245768 | tf_op jit(solution)/shard_map/ppermute | solution.py:383
  14.5 8.3 %collective-permute-start.2 = (bf16[320,128]{1,0:T(8,128)(2,1)S(1)}, bf16[320,128]{1,0:T(8,128)(2,1)S(1)}, u32[]{:S(2)}, u32[]{:S(2)}) collective-permute-start(bf16[320,128]{1,0:T(8,128)(2,1)S(1)} %get-tuple-element.25), channel_id=1, source_target_pairs={{0,8},{2,10},{4,12},{6,14},{8,0},{10,2},{12,4},{14,6},{1,9},{3,11}... | collective-permute-start | bytes 245768 | tf_op jit(solution)/shard_map/ppermute | solution.py:383
  17.1 7.2 %collective-permute-start.3 = (bf16[320,128]{1,0:T(8,128)(2,1)S(1)}, bf16[320,128]{1,0:T(8,128)(2,1)S(1)}, u32[]{:S(2)}, u32[]{:S(2)}) collective-permute-start(bf16[320,128]{1,0:T(8,128)(2,1)S(1)} %get-tuple-element.26), channel_id=1, source_target_pairs={{0,12},{2,14},{4,8},{6,10},{8,4},{10,6},{12,0},{14,2},{1,13},{3,15... | collective-permute-start | bytes 245768 | tf_op jit(solution)/shard_map/ppermute | solution.py:383
  17.4 9.3 %collective-permute-start.15 = (bf16[320,128]{1,0:T(8,128)(2,1)S(1)}, bf16[320,128]{1,0:T(8,128)(2,1)S(1)}, u32[]{:S(2)}, u32[]{:S(2)}) collective-permute-start(bf16[320,128]{1,0:T(8,128)(2,1)S(1)} %get-tuple-element.23.rest_0_), channel_id=1, source_target_pairs={{1,0},{3,2},{5,4},{7,6},{9,8},{11,10},{13,12},{15,14},{17,16},{19,... | collective-permute-start | bytes 245768 | tf_op jit(solution)/shard_map/ppermute | solution.py:384
  18.6 9.5 %collective-permute-start.8 = (bf16[328,128]{1,0:T(8,128)(2,1)S(1)}, bf16[328,128]{1,0:T(8,128)(2,1)S(1)}, u32[]{:S(2)}, u32[]{:S(2)}) collective-permute-start(bf16[328,128]{1,0:T(8,128)(2,1)S(1)} %get-tuple-element.28), channel_id=1, source_target_pairs={{0,4},{2,6},{4,0},{6,2},{8,12},{10,14},{12,8},{14,10},{1,5},{3,7},... | collective-permute-start | bytes 251912 | tf_op jit(solution)/shard_map/ppermute | solution.py:383
  19.4 10.4 %collective-permute-start.9 = (bf16[328,128]{1,0:T(8,128)(2,1)S(1)}, bf16[328,128]{1,0:T(8,128)(2,1)S(1)}, u32[]{:S(2)}, u32[]{:S(2)}) collective-permute-start(bf16[328,128]{1,0:T(8,128)(2,1)S(1)} %get-tuple-element.29), channel_id=1, source_target_pairs={{0,8},{2,10},{4,12},{6,14},{8,0},{10,2},{12,4},{14,6},{1,9},{3,11}... | collective-permute-start | bytes 251912 | tf_op jit(solution)/shard_map/ppermute | solution.py:383
  22.9 4.0 %collective-permute-start.4 = (bf16[320,128]{1,0:T(8,128)(2,1)S(1)}, bf16[320,128]{1,0:T(8,128)(2,1)S(1)}, u32[]{:S(2)}, u32[]{:S(2)}) collective-permute-start(bf16[320,128]{1,0:T(8,128)(2,1)S(1)} %get-tuple-element.23.rest_0_), channel_id=1, source_target_pairs={{0,2},{2,0},{4,6},{6,4},{8,10},{10,8},{12,14},{14,12},{1,3},{3,1},... | collective-permute-start | bytes 245768 | tf_op jit(solution)/shard_map/ppermute | solution.py:388
  24.3 6.7 %collective-permute-start.10 = (bf16[328,128]{1,0:T(8,128)(2,1)S(1)}, bf16[328,128]{1,0:T(8,128)(2,1)S(1)}, u32[]{:S(2)}, u32[]{:S(2)}) collective-permute-start(bf16[328,128]{1,0:T(8,128)(2,1)S(1)} %get-tuple-element.30), channel_id=1, source_target_pairs={{0,12},{2,14},{4,8},{6,10},{8,4},{10,6},{12,0},{14,2},{1,13},{3,15... | collective-permute-start | bytes 251912 | tf_op jit(solution)/shard_map/ppermute | solution.py:383
  26.6 4.5 %collective-permute-start.11 = (bf16[328,128]{1,0:T(8,128)(2,1)S(1)}, bf16[328,128]{1,0:T(8,128)(2,1)S(1)}, u32[]{:S(2)}, u32[]{:S(2)}) collective-permute-start(bf16[328,128]{1,0:T(8,128)(2,1)S(1)} %get-tuple-element.27.rest_8_), channel_id=1, source_target_pairs={{0,2},{2,0},{4,6},{6,4},{8,10},{10,8},{12,14},{14,12},{1,3},{3,1},... | collective-permute-start | bytes 251912 | tf_op jit(solution)/shard_map/ppermute | solution.py:388
  26.9 6.5 %collective-permute-start.16 = (bf16[320,128]{1,0:T(8,128)(2,1)S(1)}, bf16[320,128]{1,0:T(8,128)(2,1)S(1)}, u32[]{:S(2)}, u32[]{:S(2)}) collective-permute-start(bf16[320,128]{1,0:T(8,128)(2,1)S(1)} %collective-permute-done.1.rest_1_), channel_id=1, source_target_pairs={{1,0},{3,2},{5,4},{7,6},{9,8},{11,10},{13,12},{15,14},{17,16},{19,... | collective-permute-start | bytes 245768 | tf_op jit(solution)/shard_map/ppermute | solution.py:384
  28.2 5.2 %collective-permute-start.5 = (bf16[320,128]{1,0:T(8,128)(2,1)S(1)}, bf16[320,128]{1,0:T(8,128)(2,1)S(1)}, u32[]{:S(2)}, u32[]{:S(2)}) collective-permute-start(bf16[320,128]{1,0:T(8,128)(2,1)S(1)} %collective-permute-done.1.rest_1_), channel_id=1, source_target_pairs={{0,2},{2,0},{4,6},{6,4},{8,10},{10,8},{12,14},{14,12},{1,3},{3,1},... | collective-permute-start | bytes 245768 | tf_op jit(solution)/shard_map/ppermute | solution.py:388
  29.7 6.3 %collective-permute-start.17 = (bf16[320,128]{1,0:T(8,128)(2,1)S(1)}, bf16[320,128]{1,0:T(8,128)(2,1)S(1)}, u32[]{:S(2)}, u32[]{:S(2)}) collective-permute-start(bf16[320,128]{1,0:T(8,128)(2,1)S(1)} %collective-permute-done.2.rest_2_), channel_id=1, source_target_pairs={{1,0},{3,2},{5,4},{7,6},{9,8},{11,10},{13,12},{15,14},{17,16},{19,... | collective-permute-start | bytes 245768 | tf_op jit(solution)/shard_map/ppermute | solution.py:384
  31.0 5.0 %collective-permute-start.6 = (bf16[320,128]{1,0:T(8,128)(2,1)S(1)}, bf16[320,128]{1,0:T(8,128)(2,1)S(1)}, u32[]{:S(2)}, u32[]{:S(2)}) collective-permute-start(bf16[320,128]{1,0:T(8,128)(2,1)S(1)} %collective-permute-done.2.rest_2_), channel_id=1, source_target_pairs={{0,2},{2,0},{4,6},{6,4},{8,10},{10,8},{12,14},{14,12},{1,3},{3,1},... | collective-permute-start | bytes 245768 | tf_op jit(solution)/shard_map/ppermute | solution.py:388
  31.1 7.0 %collective-permute-start.18 = (bf16[320,128]{1,0:T(8,128)(2,1)S(1)}, bf16[320,128]{1,0:T(8,128)(2,1)S(1)}, u32[]{:S(2)}, u32[]{:S(2)}) collective-permute-start(bf16[320,128]{1,0:T(8,128)(2,1)S(1)} %collective-permute-done.3.rest_3_), channel_id=1, source_target_pairs={{1,0},{3,2},{5,4},{7,6},{9,8},{11,10},{13,12},{15,14},{17,16},{19,... | collective-permute-start | bytes 245768 | tf_op jit(solution)/shard_map/ppermute | solution.py:384
  33.4 5.3 %collective-permute-start.12 = (bf16[328,128]{1,0:T(8,128)(2,1)S(1)}, bf16[328,128]{1,0:T(8,128)(2,1)S(1)}, u32[]{:S(2)}, u32[]{:S(2)}) collective-permute-start(bf16[328,128]{1,0:T(8,128)(2,1)S(1)} %collective-permute-done.8.rest_9_), channel_id=1, source_target_pairs={{0,2},{2,0},{4,6},{6,4},{8,10},{10,8},{12,14},{14,12},{1,3},{3,1},... | collective-permute-start | bytes 251912 | tf_op jit(solution)/shard_map/ppermute | solution.py:388
  33.4 4.8 %collective-permute-start.7 = (bf16[320,128]{1,0:T(8,128)(2,1)S(1)}, bf16[320,128]{1,0:T(8,128)(2,1)S(1)}, u32[]{:S(2)}, u32[]{:S(2)}) collective-permute-start(bf16[320,128]{1,0:T(8,128)(2,1)S(1)} %collective-permute-done.3.rest_3_), channel_id=1, source_target_pairs={{0,2},{2,0},{4,6},{6,4},{8,10},{10,8},{12,14},{14,12},{1,3},{3,1},... | collective-permute-start | bytes 245768 | tf_op jit(solution)/shard_map/ppermute | solution.py:388
  36.1 2.6 %collective-permute-start.19 = (bf16[320,128]{1,0:T(8,128)(2,1)S(1)}, bf16[320,128]{1,0:T(8,128)(2,1)S(1)}, u32[]{:S(2)}, u32[]{:S(2)}) collective-permute-start(bf16[320,128]{1,0:T(8,128)(2,1)S(1)} %collective-permute-done.15.rest_16_), channel_id=1, source_target_pairs={{0,2},{2,0},{4,6},{6,4},{8,10},{10,8},{12,14},{14,12},{1,3},{3,1},... | collective-permute-start | bytes 245768 | tf_op jit(solution)/shard_map/ppermute | solution.py:388
  36.1 3.1 %collective-permute-start.13 = (bf16[328,128]{1,0:T(8,128)(2,1)S(1)}, bf16[328,128]{1,0:T(8,128)(2,1)S(1)}, u32[]{:S(2)}, u32[]{:S(2)}) collective-permute-start(bf16[328,128]{1,0:T(8,128)(2,1)S(1)} %collective-permute-done.9.rest_10_), channel_id=1, source_target_pairs={{0,2},{2,0},{4,6},{6,4},{8,10},{10,8},{12,14},{14,12},{1,3},{3,1},... | collective-permute-start | bytes 251912 | tf_op jit(solution)/shard_map/ppermute | solution.py:388
  38.1 1.3 %collective-permute-start.14 = (bf16[328,128]{1,0:T(8,128)(2,1)S(1)}, bf16[328,128]{1,0:T(8,128)(2,1)S(1)}, u32[]{:S(2)}, u32[]{:S(2)}) collective-permute-start(bf16[328,128]{1,0:T(8,128)(2,1)S(1)} %collective-permute-done.10.rest_11_), channel_id=1, source_target_pairs={{0,2},{2,0},{4,6},{6,4},{8,10},{10,8},{12,14},{14,12},{1,3},{3,1},... | collective-permute-start | bytes 251912 | tf_op jit(solution)/shard_map/ppermute | solution.py:388
  38.1 1.4 %collective-permute-start.20 = (bf16[320,128]{1,0:T(8,128)(2,1)S(1)}, bf16[320,128]{1,0:T(8,128)(2,1)S(1)}, u32[]{:S(2)}, u32[]{:S(2)}) collective-permute-start(bf16[320,128]{1,0:T(8,128)(2,1)S(1)} %collective-permute-done.16.rest_17_), channel_id=1, source_target_pairs={{0,2},{2,0},{4,6},{6,4},{8,10},{10,8},{12,14},{14,12},{1,3},{3,1},... | collective-permute-start | bytes 245768 | tf_op jit(solution)/shard_map/ppermute | solution.py:388
  38.7 1.3 %collective-permute-start.21 = (bf16[320,128]{1,0:T(8,128)(2,1)S(1)}, bf16[320,128]{1,0:T(8,128)(2,1)S(1)}, u32[]{:S(2)}, u32[]{:S(2)}) collective-permute-start(bf16[320,128]{1,0:T(8,128)(2,1)S(1)} %collective-permute-done.17.rest_18_), channel_id=1, source_target_pairs={{0,2},{2,0},{4,6},{6,4},{8,10},{10,8},{12,14},{14,12},{1,3},{3,1},... | collective-permute-start | bytes 245768 | tf_op jit(solution)/shard_map/ppermute | solution.py:388
  38.7 1.4 %collective-permute-start.22 = (bf16[320,128]{1,0:T(8,128)(2,1)S(1)}, bf16[320,128]{1,0:T(8,128)(2,1)S(1)}, u32[]{:S(2)}, u32[]{:S(2)}) collective-permute-start(bf16[320,128]{1,0:T(8,128)(2,1)S(1)} %collective-permute-done.18.rest_19_), channel_id=1, source_target_pairs={{0,2},{2,0},{4,6},{6,4},{8,10},{10,8},{12,14},{14,12},{1,3},{3,1},... | collective-permute-start | bytes 245768 | tf_op jit(solution)/shard_map/ppermute | solution.py:388
  48.0 4.5 %collective-permute-start.23 = (f32[4,8,128]{2,1,0:T(8,128)S(1)}, f32[4,8,128]{2,1,0:T(8,128)S(1)}, u32[]{:S(2)}, u32[]{:S(2)}) collective-permute-start(f32[4,8,128]{2,1,0:T(8,128)S(1)} %get-tuple-element.32), channel_id=1, source_target_pairs={{0,4},{2,6},{4,0},{6,2},{8,12},{10,14},{12,8},{14,10},{1,5},{3,7},... | collective-permute-start | bytes 49160 | tf_op jit(solution)/shard_map/ppermute | solution.py:418
  49.6 4.8 %collective-permute-start.24 = (f32[4,8,128]{2,1,0:T(8,128)S(1)}, f32[4,8,128]{2,1,0:T(8,128)S(1)}, u32[]{:S(2)}, u32[]{:S(2)}) collective-permute-start(f32[4,8,128]{2,1,0:T(8,128)S(1)} %get-tuple-element.33), channel_id=1, source_target_pairs={{0,8},{2,10},{4,12},{6,14},{8,0},{10,2},{12,4},{14,6},{1,9},{3,11}... | collective-permute-start | bytes 49160 | tf_op jit(solution)/shard_map/ppermute | solution.py:418
  50.5 5.5 %collective-permute-start.25 = (f32[4,8,128]{2,1,0:T(8,128)S(1)}, f32[4,8,128]{2,1,0:T(8,128)S(1)}, u32[]{:S(2)}, u32[]{:S(2)}) collective-permute-start(f32[4,8,128]{2,1,0:T(8,128)S(1)} %get-tuple-element.34), channel_id=1, source_target_pairs={{0,12},{2,14},{4,8},{6,10},{8,4},{10,6},{12,0},{14,2},{1,13},{3,15... | collective-permute-start | bytes 49160 | tf_op jit(solution)/shard_map/ppermute | solution.py:418
  56.6 1.3 %collective-permute-start.26 = (f32[4,4,512]{2,1,0:T(4,128)S(1)}, f32[4,4,512]{2,1,0:T(4,128)S(1)}, u32[]{:S(2)}, u32[]{:S(2)}) collective-permute-start(f32[4,4,512]{2,1,0:T(4,128)S(1)} %get-tuple-element.36), channel_id=1, source_target_pairs={{0,2},{2,0},{4,6},{6,4},{8,10},{10,8},{12,14},{14,12},{1,3},{3,1},... | collective-permute-start | bytes 98312 | tf_op jit(solution)/shard_map/ppermute | solution.py:435

commit v5 on v4

--- a/solution.py
+++ b/solution.py
@@ -10,7 +10,7 @@
 SHIFT = 16
 LANES = 128
 SUBLANES = 8
-UNROLL = 8
+UNROLL = 4
 
 SMEM = pl.BlockSpec(memory_space=pltpu.SMEM)
 VMEM = pl.BlockSpec(memory_space=pltpu.VMEM)
@@ -194,7 +194,8 @@
     blocks = [rest[p * groups : (p + 1) * groups] for p in range(parts + 1)]
     rest = rest[(parts + 1) * groups :]
     outs = rest[:chunks]
-    main, side, windows, edge, whole_params, scalars, order, result, sem = rest[chunks:]
+    main, side, even, odd, edge, whole_params, scalars, order, result, sem = rest[chunks:]
+    windows = (even, odd)
     own = info[2]
     first_vel = info[4]
     share = result.shape[0]
@@ -210,22 +211,27 @@
         for p in range(parts + 1):
             edge[g, p] = blocks[p][g][main_rows:size].astype(jnp.float32)
     fetch.wait()
+    has_below = info[1].astype(jnp.float32)
     filled = jnp.int32(0)
     for g in range(groups):
 
         def unpack(e, at, g=g):
-            order[at] = g * exposures + e
+            source = g * exposures + e
+            order[at] = source
             for p in range(parts + 1):
                 start = pl.multiple_of(e * 2 * SHIFT, 2 * SHIFT)
                 both = blocks[p][g][pl.ds(start, 2 * SHIFT)].astype(jnp.float32)
                 packed = edge[g, p, pl.ds(pl.multiple_of(e * SUBLANES, SUBLANES), SUBLANES)]
+                if p == parts:
+                    both = both * has_below
+                    packed = packed * has_below
                 for m in (0, 1):
                     main[at, m, p * SHIFT : (p + 1) * SHIFT] = both[m * SHIFT : (m + 1) * SHIFT]
                     for h in (0, 1):
                         q = 2 * m + h
                         piece = packed if q == 0 else pltpu.roll(packed, LANES - 2 * SHIFT * q, 1)
                         side[at, m, p * SHIFT + h * SUBLANES : p * SHIFT + (h + 1) * SUBLANES] = piece
-            return at + scalars[g * exposures + e, 2 * vels]
+            return at + scalars[source, 2 * vels]
 
         filled = lax.fori_loop(0, exposures, unpack, filled, unroll=4)
     for i in range(UNROLL):
@@ -235,50 +241,57 @@
     trips = (filled + UNROLL - 1) // UNROLL
 
     lane = lax.broadcasted_iota(jnp.int32, (rows, LANES), 1)
-    zeros = jnp.zeros((rows, LANES), jnp.float32)
-
-    def one_velocity(v, carry):
-        def gather(trip, sums):
+
+    def gather(v, e, sums):
+        source = order[e]
+        row_at = scalars[source, first_vel + v]
+        col_at = scalars[source, vels + first_vel + v] + SHIFT
+        from_side = lane < col_at
+        cells = jnp.concatenate(
+            [
+                jnp.where(from_side, side[e, m, pl.ds(row_at, rows)], main[e, m, pl.ds(row_at, rows)])
+                for m in (0, 1)
+            ]
+        ).astype(jnp.bfloat16)
+        cells = pltpu.roll(cells, (LANES - col_at) & (LANES - 1), 1).astype(jnp.float32)
+        windows[v % 2][e, 0] = cells[:rows]
+        windows[v % 2][e, 1] = cells[rows:]
+        return sums[0] + cells[:rows], sums[1] + cells[rows:]
+
+    def reweigh(v, e, flux, sums):
+        signal = windows[v % 2][e, 0]
+        depth = windows[v % 2][e, 1]
+        residual = signal - flux * depth
+        base = depth + 1.0
+        weight = base / (base + residual * residual)
+        return sums[0] + weight * signal, sums[1] + weight * depth
+
+    def over_exposures(step, start):
+        def trip(t, sums):
             for i in range(UNROLL):
-                e = trip * UNROLL + i
-                source = order[e]
-                row_at = scalars[source, first_vel + v]
-                col_at = scalars[source, vels + first_vel + v] + SHIFT
-                turn = lax.rem(LANES - col_at, LANES)
-                from_side = lane < col_at
-                cells = jnp.concatenate(
-                    [
-                        jnp.where(from_side, side[e, m, pl.ds(row_at, rows)], main[e, m, pl.ds(row_at, rows)])
-                        for m in (0, 1)
-                    ]
-                ).astype(jnp.bfloat16)
-                cells = pltpu.roll(cells, turn, 1).astype(jnp.float32)
-                out = []
-                for m in (0, 1):
-                    windows[e, m] = cells[m * rows : (m + 1) * rows]
-                    out.append(sums[m] + cells[m * rows : (m + 1) * rows])
-                sums = tuple(out)
+                sums = step(t * UNROLL + i, sums)
             return sums
 
-        signal_sum, depth_sum = lax.fori_loop(0, trips, gather, (zeros, zeros))
-        flux = signal_sum / (depth_sum + 1.0)
-
-        def reweigh(trip, sums):
-            for i in range(UNROLL):
-                e = trip * UNROLL + i
-                signal = windows[e, 0]
-                depth = windows[e, 1]
-                residual = signal - flux * depth
-                base = depth + 1.0
-                weight = base / (base + residual * residual)
-                sums = sums[0] + weight * signal, sums[1] + weight * depth
-            return sums
-
-        robust = lax.fori_loop(0, trips, reweigh, (zeros, zeros))
-        result[v] = robust[0] / jnp.sqrt(robust[1] + 1.0)
-        return carry
-
-    lax.fori_loop(0, share, one_velocity, 0)
+        return lax.fori_loop(0, trips, trip, start)
+
+    zeros = main[filled, 0, 0:rows]
+    none = (zeros, zeros)
+
+    sums = over_exposures(functools.partial(gather, 0), none)
+    for v in range(share):
+        flux = sums[0] / (sums[1] + 1.0)
+
+        def weigh(e, sums, v=v, flux=flux):
+            return reweigh(v, e, flux, sums)
+
+        def both(e, sums, v=v, weigh=weigh):
+            return gather(v + 1, e, sums[:2]) + weigh(e, sums[2:])
+
+        if v + 1 < share:
+            sums = over_exposures(both, none + none)
+        else:
+            sums = none + over_exposures(weigh, none)
+        result[v] = sums[2] / jnp.sqrt(sums[3] + 1.0)
     block = rows // chunks
     for step in range(chunks):
         to = partner(own, step, chunks)
@@ -375,7 +388,7 @@
     )(info, psf_rows, psf_cols, exposure_ok, row_shift, col_shift, maps, edges, above, below)
 
     blocks = [[[None] * chunks for _ in range(subs)] for _ in range(parts + 1)]
-    up = [(i + 1, i) for i in range(strips - 1)]
+    up = [((i + 1) % strips, i) for i in range(strips)]
     for step in range(chunks):
         for p in range(parts):
             blocks[p][0][step] = sends[step * parts + p]
@@ -401,6 +414,7 @@
         scratch_shapes=[
             pltpu.VMEM((total + UNROLL, 2, reach, LANES), jnp.float32),
             pltpu.VMEM((total + UNROLL, 2, reach, LANES), jnp.float32),
+            pltpu.VMEM((total + UNROLL, 2, rows, LANES), jnp.float32),
             pltpu.VMEM((total + UNROLL, 2, rows, LANES), jnp.float32),
             pltpu.VMEM((groups, parts + 1, exposures * SUBLANES, LANES), jnp.float32),
             pltpu.VMEM((total, LANES), jnp.int32),

time: 59.4 us -> 59.3 us (level)
  starting transfers between devices: 26.3 us -> 24.6 us
  Pallas kernels: 16.1 us -> 17.5 us
    ppermute x4, starting transfers between devices: 5.13 us -> 3.26 us  [per_device(): blocks[parts][0][step] = lax.ppermute(blocks[0][0][step], 'strip', up)]
    pallas_call x1, Pallas kernels: 7.87 us -> 9.21 us  [per_device(): pl.pallas_call(functools.partial(stack_kernel, groups, chunks, exposures,...]
    ppermute x4, waiting for transfers between devices: 4.68 us -> 3.75 us  [per_device(): blocks[parts][0][step] = lax.ppermute(blocks[0][0][step], 'strip', up)]
    ppermute x3, waiting for transfers between devices: 3.65 us -> 4.35 us  [per_device(): lax.ppermute(pieces[step], 'expo', chunk_pairs(step, chunks, subs))]
    ppermute x6, waiting for transfers between devices: 2.71 us -> 3.34 us  [per_device(): lax.ppermute(sends[step * parts + p], 'expo', chunk_pairs(step, chunks, s...]
where the time goes in v5:
time: 59.3 us; the launch traced here: 59 us
  starting transfers between devices  24.6 us (41%)
  Pallas kernels  17.5 us (30%)
  waiting for transfers between devices  13.6 us (23%)
  local copies, waits for them, and re-layouts  3.24 us (5%)
    ppermute x6, starting transfers between devices, per_device(): lax.ppermute(sends[step * parts + p], 'expo', chunk_pairs(step, chunks, s...  11.5 us
    pallas_call x1, Pallas kernels, per_device(): pl.pallas_call(functools.partial(stack_kernel, groups, chunks, exposures,...  9.21 us
    ppermute x3, starting transfers between devices, per_device(): lax.ppermute(pieces[step], 'expo', chunk_pairs(step, chunks, subs))  4.45 us
    ppermute x3, waiting for transfers between devices, per_device(): lax.ppermute(pieces[step], 'expo', chunk_pairs(step, chunks, subs))  4.35 us
    pallas_call x1, Pallas kernels, per_device(): pl.pallas_call(functools.partial(inner_kernel, radius), out_shape=[jax.Sh...  4.13 us
    ppermute x4, waiting for transfers between devices, per_device(): blocks[parts][0][step] = lax.ppermute(blocks[0][0][step], 'strip', up)  3.75 us
    ppermute x6, waiting for transfers between devices, per_device(): lax.ppermute(sends[step * parts + p], 'expo', chunk_pairs(step, chunks, s...  3.34 us
    ppermute x4, starting transfers between devices, per_device(): blocks[parts][0][step] = lax.ppermute(blocks[0][0][step], 'strip', up)  3.26 us
  transfers between devices with their start and end apart: 27, of which 12 were waited for; matrix products, arithmetic and copies ran while one was open for 0% of the time, Pallas kernels for 7%

profile of v5, /device:TPU:0, one launch (start us, length us, event | category | flops | bytes accessed | tf_op | source)
XLA Modules:
  0.0 59.0 jit_solution(5936529123889419661)
XLA Ops:
  0.0 1.0 %dynamic-slice_bitcast_fusion = (bf16[1,8,4,512]{3,2,1,0:T(4,128)(2,1)S(1)}, bf16[1,8,4,512]{3,2,1,0:T(4,128)(2,1)S(1)}) fusion(bf16[8,32,512]{2,1,0:T(8,128)(2,1)} %inv_var.1, s32[]{:T(128)S(6)} %select_n.19, bf16[8,32,512]{2,1,0:T(8,128)(2,1)} %science.1), kind=kLoop, calls=%fused_computation.1 | loop fusion | bytes 131076 | tf_op jit(solution)/shard_map/stack | solution.py:345
  1.0 3.0 %collective-permute-start = (bf16[2,8,4,512]{3,2,1,0:T(4,128)(2,1)S(1)}, bf16[2,8,4,512]{3,2,1,0:T(4,128)(2,1)S(1)}, u32[]{:S(2)}, u32[]{:S(2)}) collective-permute-start(bf16[2,8,4,512]{3,2,1,0:T(4,128)(2,1)S(1)} %pad_maximum_fusion), channel_id=1, source_target_pairs={{0,1},{1,0},{2,3},{3,2},{4,5},{5,4},{6,7},{7,6},{8,9},{9,8},{10,11... | collective-permute-start | bytes 196616 | tf_op jit(solution)/shard_map/ppermute | solution.py:349
  4.0 0.1 stack.40.info
  4.1 0.6 %copy-done.2 = f32[8,9]{1,0:T(8,128)S(1)} copy-done((f32[8,9]{1,0:T(8,128)S(1)}, f32[8,9]{1,0:T(8,128)}, u32[]{:S(2)}) %copy-start.2) | copy-done | bytes 312
  4.7 0.0 copy-done.3
  4.8 0.9 %copy-done.1 = bf16[8,32,512]{2,1,0:T(8,128)(2,1)S(1)} copy-done((bf16[8,32,512]{2,1,0:T(8,128)(2,1)S(1)}, bf16[8,32,512]{2,1,0:T(8,128)(2,1)}, u32[]{:S(2)}) %copy-start.1) | copy-done | bytes 262168
  5.7 4.1 %filter_inner.1 = (f32[4,512,128]{2,1,0:T(8,128)S(1)}, f32[4,128,128]{2,1,0:T(8,128)S(1)}) custom-call(f32[8,9]{1,0:T(8,128)S(1)} %copy-done.2, f32[8,9]{1,0:T(8,128)S(1)} %copy-done.3, bf16[8,32,512]{2,1,0:T(8,128)(2,1)S(1)} %copy-done, bf16[8,32,512]{2,1,0:T(8,128)(2,1)S(1)} %copy-done.1), custom_call_target="tpu_custom_call" | custom-call | flops 100000000 | bytes 4000000 | tf_op jit(solution)/shard_map/filter_inner/pallas_call | solution.py:356
  9.8 0.0 collective-permute-done.above.below
  9.9 0.0 copy-start.6
  9.9 0.6 %copy-done.6 = s32[8]{0:T(128)S(1)} copy-done((s32[8]{0:T(128)S(1)}, s32[8]{0:T(128)}, u32[]{:S(2)}) %copy-start.6) | copy-done | bytes 56
  10.5 2.4 %filter_outer.1 = (bf16[320,128]{1,0:T(8,128)(2,1)S(1)}, bf16[328,128]{1,0:T(8,128)(2,1)S(1)}, bf16[320,128]{1,0:T(8,128)(2,1)S(1)}, bf16[328,128]{1,0:T(8,128)(...) custom-call(s32[5]{0:T(128)S(1)} %stack.40.info, ...), custom_call_target="tpu_custom_call" | custom-call | tf_op jit(solution)/shard_map/filter_outer/pallas_call | solution.py:374
  12.9 1.6 %collective-permute-start.1 = (bf16[320,128]{1,0:T(8,128)(2,1)S(1)}, bf16[320,128]{1,0:T(8,128)(2,1)S(1)}, u32[]{:S(2)}, u32[]{:S(2)}) collective-permute-start(bf16[320,128]{1,0:T(8,128)(2,1)S(1)} %get-tuple-element.24), channel_id=1, source_target_pairs={{0,4},{2,6},{4,0},{6,2},{8,12},{10,14},{12,8},{14,10},{1,5},{3,7},... | collective-permute-start | bytes 245768 | tf_op jit(solution)/shard_map/ppermute | solution.py:396
  14.5 2.6 %collective-permute-start.2 = (bf16[320,128]{1,0:T(8,128)(2,1)S(1)}, bf16[320,128]{1,0:T(8,128)(2,1)S(1)}, u32[]{:S(2)}, u32[]{:S(2)}) collective-permute-start(bf16[320,128]{1,0:T(8,128)(2,1)S(1)} %get-tuple-element.25), channel_id=1, source_target_pairs={{0,8},{2,10},{4,12},{6,14},{8,0},{10,2},{12,4},{14,6},{1,9},{3,11}... | collective-permute-start | bytes 245768 | tf_op jit(solution)/shard_map/ppermute | solution.py:396
  17.1 0.2 collective-permute-start.3
  17.4 0.3 collective-permute-start.15
  17.7 0.9 %collective-permute-start.8 = (bf16[328,128]{1,0:T(8,128)(2,1)S(1)}, bf16[328,128]{1,0:T(8,128)(2,1)S(1)}, u32[]{:S(2)}, u32[]{:S(2)}) collective-permute-start(bf16[328,128]{1,0:T(8,128)(2,1)S(1)} %get-tuple-element.28), channel_id=1, source_target_pairs={{0,4},{2,6},{4,0},{6,2},{8,12},{10,14},{12,8},{14,10},{1,5},{3,7},... | collective-permute-start | bytes 251912 | tf_op jit(solution)/shard_map/ppermute | solution.py:396
  18.6 0.0 collective-permute-done.1.rest_1_
  18.6 3.5 %collective-permute-start.9 = (bf16[328,128]{1,0:T(8,128)(2,1)S(1)}, bf16[328,128]{1,0:T(8,128)(2,1)S(1)}, u32[]{:S(2)}, u32[]{:S(2)}) collective-permute-start(bf16[328,128]{1,0:T(8,128)(2,1)S(1)} %get-tuple-element.29), channel_id=1, source_target_pairs={{0,8},{2,10},{4,12},{6,14},{8,0},{10,2},{12,4},{14,6},{1,9},{3,11}... | collective-permute-start | bytes 251912 | tf_op jit(solution)/shard_map/ppermute | solution.py:396
  22.1 2.3 %collective-permute-done.2.rest_2_ = bf16[320,128]{1,0:T(8,128)(2,1)S(1)} collective-permute-done((bf16[320,128]{1,0:T(8,128)(2,1)S(1)}, bf16[320,128]{1,0:T(8,128)(2,1)S(1)}, u32[]{:S(2)}, u32[]{:S(2)}) %collective-permute-start.2) | collective-permute-done | bytes 81952 | tf_op jit(solution)/shard_map/ppermute | solution.py:396
  24.4 2.7 %collective-permute-start.10 = (bf16[328,128]{1,0:T(8,128)(2,1)S(1)}, bf16[328,128]{1,0:T(8,128)(2,1)S(1)}, u32[]{:S(2)}, u32[]{:S(2)}) collective-permute-start(bf16[328,128]{1,0:T(8,128)(2,1)S(1)} %get-tuple-element.30), channel_id=1, source_target_pairs={{0,12},{2,14},{4,8},{6,10},{8,4},{10,6},{12,0},{14,2},{1,13},{3,15... | collective-permute-start | bytes 251912 | tf_op jit(solution)/shard_map/ppermute | solution.py:396
  27.1 0.2 collective-permute-start.11
  27.3 0.5 collective-permute-start.16
  27.8 0.0 collective-permute-start.5
  27.8 1.0 %collective-permute-done.9.rest_10_ = bf16[328,128]{1,0:T(8,128)(2,1)S(1)} collective-permute-done((bf16[328,128]{1,0:T(8,128)(2,1)S(1)}, bf16[328,128]{1,0:T(8,128)(2,1)S(1)}, u32[]{:S(2)}, u32[]{:S(2)}) %collective-permute-start.9) | collective-permute-done | bytes 84000 | tf_op jit(solution)/shard_map/ppermute | solution.py:396
  28.8 2.3 %collective-permute-start.17 = (bf16[320,128]{1,0:T(8,128)(2,1)S(1)}, bf16[320,128]{1,0:T(8,128)(2,1)S(1)}, u32[]{:S(2)}, u32[]{:S(2)}) collective-permute-start(bf16[320,128]{1,0:T(8,128)(2,1)S(1)} %collective-permute-done.2.rest_2_), channel_id=1, source_target_pairs={{1,0},{0,1},{3,2},{2,3},{5,4},{4,5},{7,6},{6,7},{9,8},{8,9},{11,10... | collective-permute-start | bytes 245768 | tf_op jit(solution)/shard_map/ppermute | solution.py:397
  31.2 0.1 collective-permute-start.18
  31.3 1.4 %collective-permute-done.16.rest_17_ = bf16[320,128]{1,0:T(8,128)(2,1)S(1)} collective-permute-done((bf16[320,128]{1,0:T(8,128)(2,1)S(1)}, bf16[320,128]{1,0:T(8,128)(2,1)S(1)}, u32[]{:S(2)}, u32[]{:S(2)}) %collective-permute-start.16) | collective-permute-done | bytes 81952 | tf_op jit(solution)/shard_map/ppermute | solution.py:397
  32.6 0.5 collective-permute-start.7
  33.1 0.7 %collective-permute-done.17.rest_18_ = bf16[320,128]{1,0:T(8,128)(2,1)S(1)} collective-permute-done((bf16[320,128]{1,0:T(8,128)(2,1)S(1)}, bf16[320,128]{1,0:T(8,128)(2,1)S(1)}, u32[]{:S(2)}, u32[]{:S(2)}) %collective-permute-start.17) | collective-permute-done | bytes 81952 | tf_op jit(solution)/shard_map/ppermute | solution.py:397
  33.8 0.5 collective-permute-start.13
  34.3 1.7 %collective-permute-done.18.rest_19_ = bf16[320,128]{1,0:T(8,128)(2,1)S(1)} collective-permute-done((bf16[320,128]{1,0:T(8,128)(2,1)S(1)}, bf16[320,128]{1,0:T(8,128)(2,1)S(1)}, u32[]{:S(2)}, u32[]{:S(2)}) %collective-permute-start.18) | collective-permute-done | bytes 81952 | tf_op jit(solution)/shard_map/ppermute | solution.py:397
  36.0 0.5 collective-permute-start.20
  36.5 0.1 collective-permute-start.21
  36.6 0.4 collective-permute-start.22
  37.1 0.2 collective-permute-done.14.rest_15_
  37.3 0.2 collective-permute-done.20.rest_21_
  37.5 0.4 collective-permute-done.21.rest_22_
  37.8 0.2 collective-permute-done.22.rest_23_
  38.0 9.2 %stack_twice.1 = (f32[4,8,128]{2,1,0:T(8,128)S(1)}, f32[4,8,128]{2,1,0:T(8,128)S(1)}, f32[4,8,128]{2,1,0:T(8,128)S(1)}, f32[4,8,128]{2,1,0:T(8,128)S(1)}) custom-call(s32[5]{0:T(128)S(1)} %stack.40.info, bf16[320,128]{1,0:T(8,128)(2,1)S(1)} %get-tuple-element.23.rest_0_, bf16[320,128]{1,0:T(8,128)(2,1)S(1)} %collective-permute-done.1.rest_1_, ...), custom_call_target="tpu_custom_call" | custom-call | tf_op jit(solution)/shard_map/stack_twice/pallas_call | solution.py:409
  47.2 1.8 %collective-permute-start.23 = (f32[4,8,128]{2,1,0:T(8,128)S(1)}, f32[4,8,128]{2,1,0:T(8,128)S(1)}, u32[]{:S(2)}, u32[]{:S(2)}) collective-permute-start(f32[4,8,128]{2,1,0:T(8,128)S(1)} %get-tuple-element.32), channel_id=1, source_target_pairs={{0,4},{2,6},{4,0},{6,2},{8,12},{10,14},{12,8},{14,10},{1,5},{3,7},... | collective-permute-start | bytes 49160 | tf_op jit(solution)/shard_map/ppermute | solution.py:432
  49.0 1.5 %collective-permute-start.24 = (f32[4,8,128]{2,1,0:T(8,128)S(1)}, f32[4,8,128]{2,1,0:T(8,128)S(1)}, u32[]{:S(2)}, u32[]{:S(2)}) collective-permute-start(f32[4,8,128]{2,1,0:T(8,128)S(1)} %get-tuple-element.33), channel_id=1, source_target_pairs={{0,8},{2,10},{4,12},{6,14},{8,0},{10,2},{12,4},{14,6},{1,9},{3,11}... | collective-permute-start | bytes 49160 | tf_op jit(solution)/shard_map/ppermute | solution.py:432
  50.5 1.2 %collective-permute-start.25 = (f32[4,8,128]{2,1,0:T(8,128)S(1)}, f32[4,8,128]{2,1,0:T(8,128)S(1)}, u32[]{:S(2)}, u32[]{:S(2)}) collective-permute-start(f32[4,8,128]{2,1,0:T(8,128)S(1)} %get-tuple-element.34), channel_id=1, source_target_pairs={{0,12},{2,14},{4,8},{6,10},{8,4},{10,6},{12,0},{14,2},{1,13},{3,15... | collective-permute-start | bytes 49160 | tf_op jit(solution)/shard_map/ppermute | solution.py:432
  51.7 2.0 %collective-permute-done.24.rest_2_ = f32[4,8,128]{2,1,0:T(8,128)S(1)} collective-permute-done((f32[4,8,128]{2,1,0:T(8,128)S(1)}, f32[4,8,128]{2,1,0:T(8,128)S(1)}, u32[]{:S(2)}, u32[]{:S(2)}) %collective-permute-start.24) | collective-permute-done | bytes 16416 | tf_op jit(solution)/shard_map/ppermute | solution.py:432
  53.6 2.4 %collective-permute-done.25.rest_3_ = f32[4,8,128]{2,1,0:T(8,128)S(1)} collective-permute-done((f32[4,8,128]{2,1,0:T(8,128)S(1)}, f32[4,8,128]{2,1,0:T(8,128)S(1)}, u32[]{:S(2)}, u32[]{:S(2)}) %collective-permute-start.25) | collective-permute-done | bytes 16416 | tf_op jit(solution)/shard_map/ppermute | solution.py:432
  56.0 0.6 join_columns.1
  56.6 0.1 collective-permute-start.26
  56.7 1.2 %collective-permute-done.26.rest_1_ = f32[4,4,512]{2,1,0:T(4,128)S(1)} collective-permute-done((f32[4,4,512]{2,1,0:T(4,128)S(1)}, f32[4,4,512]{2,1,0:T(4,128)S(1)}, u32[]{:S(2)}, u32[]{:S(2)}) %collective-permute-start.26) | collective-permute-done | bytes 32800 | tf_op jit(solution)/shard_map/ppermute | solution.py:449
  57.9 1.2 %join_velocities.1 = f32[8,4,512]{2,1,0:T(4,128)} custom-call(s32[5]{0:T(128)S(1)} %stack.40.info, f32[4,4,512]{2,1,0:T(4,128)S(1)} %get-tuple-element.35.rest_0_, f32[4,4,512]{2,1,0:T(4,128)S(1)} %collective-permute-done.26.rest_1_), custom_call_target="tpu_custom_call" | custom-call | tf_op jit(solution)/shard_map/join_velocities/pallas_call | solution.py:450
  (28 shorter events, 0.1 us)
Async XLA Ops:
  0.0 4.1 %copy-start = (bf16[8,32,512]{2,1,0:T(8,128)(2,1)S(1)}, bf16[8,32,512]{2,1,0:T(8,128)(2,1)}, u32[]{:S(2)}) copy-start(bf16[8,32,512]{2,1,0:T(8,128)(2,1)} %science.1) | copy-start | bytes 786436
  1.0 8.8 %collective-permute-start = (bf16[2,8,4,512]{3,2,1,0:T(4,128)(2,1)S(1)}, bf16[2,8,4,512]{3,2,1,0:T(4,128)(2,1)S(1)}, u32[]{:S(2)}, u32[]{:S(2)}) collective-permute-start(bf16[2,8,4,512]{3,2,1,0:T(4,128)(2,1)S(1)} %pad_maximum_fusion), channel_id=1, source_target_pairs={{0,1},{1,0},{2,3},{3,2},{4,5},{5,4},{6,7},{7,6},{8,9},{9,8},{10,11... | collective-permute-start | bytes 196616 | tf_op jit(solution)/shard_map/ppermute | solution.py:349
  4.0 0.7 %copy-start.2 = (f32[8,9]{1,0:T(8,128)S(1)}, f32[8,9]{1,0:T(8,128)}, u32[]{:S(2)}) copy-start(f32[8,9]{1,0:T(8,128)} %row_taps.3) | copy-start | bytes 868
  4.0 0.7 %copy-start.3 = (f32[8,9]{1,0:T(8,128)S(1)}, f32[8,9]{1,0:T(8,128)}, u32[]{:S(2)}) copy-start(f32[8,9]{1,0:T(8,128)} %col_taps.3) | copy-start | bytes 868
  4.7 0.9 %copy-start.1 = (bf16[8,32,512]{2,1,0:T(8,128)(2,1)S(1)}, bf16[8,32,512]{2,1,0:T(8,128)(2,1)}, u32[]{:S(2)}) copy-start(bf16[8,32,512]{2,1,0:T(8,128)(2,1)} %inv_var.1) | copy-start | bytes 786436
  5.7 4.2 %copy-start.4 = (s32[8,8]{1,0:T(8,128)S(1)}, s32[8,8]{1,0:T(8,128)}, u32[]{:S(2)}) copy-start(s32[8,8]{1,0:T(8,128)} %row_shift.1) | copy-start | bytes 772
  5.7 4.2 %copy-start.5 = (s32[8,8]{1,0:T(8,128)S(1)}, s32[8,8]{1,0:T(8,128)}, u32[]{:S(2)}) copy-start(s32[8,8]{1,0:T(8,128)} %col_shift.1) | copy-start | bytes 772
  9.9 0.7 %copy-start.6 = (s32[8]{0:T(128)S(1)}, s32[8]{0:T(128)}, u32[]{:S(2)}) copy-start(s32[8]{0:T(128)} %usable.1) | copy-start | bytes 100
  12.9 5.7 %collective-permute-start.1 = (bf16[320,128]{1,0:T(8,128)(2,1)S(1)}, bf16[320,128]{1,0:T(8,128)(2,1)S(1)}, u32[]{:S(2)}, u32[]{:S(2)}) collective-permute-start(bf16[320,128]{1,0:T(8,128)(2,1)S(1)} %get-tuple-element.24), channel_id=1, source_target_pairs={{0,4},{2,6},{4,0},{6,2},{8,12},{10,14},{12,8},{14,10},{1,5},{3,7},... | collective-permute-start | bytes 245768 | tf_op jit(solution)/shard_map/ppermute | solution.py:396
  14.5 9.9 %collective-permute-start.2 = (bf16[320,128]{1,0:T(8,128)(2,1)S(1)}, bf16[320,128]{1,0:T(8,128)(2,1)S(1)}, u32[]{:S(2)}, u32[]{:S(2)}) collective-permute-start(bf16[320,128]{1,0:T(8,128)(2,1)S(1)} %get-tuple-element.25), channel_id=1, source_target_pairs={{0,8},{2,10},{4,12},{6,14},{8,0},{10,2},{12,4},{14,6},{1,9},{3,11}... | collective-permute-start | bytes 245768 | tf_op jit(solution)/shard_map/ppermute | solution.py:396
  17.1 7.3 %collective-permute-start.3 = (bf16[320,128]{1,0:T(8,128)(2,1)S(1)}, bf16[320,128]{1,0:T(8,128)(2,1)S(1)}, u32[]{:S(2)}, u32[]{:S(2)}) collective-permute-start(bf16[320,128]{1,0:T(8,128)(2,1)S(1)} %get-tuple-element.26), channel_id=1, source_target_pairs={{0,12},{2,14},{4,8},{6,10},{8,4},{10,6},{12,0},{14,2},{1,13},{3,15... | collective-permute-start | bytes 245768 | tf_op jit(solution)/shard_map/ppermute | solution.py:396
  17.4 9.7 %collective-permute-start.15 = (bf16[320,128]{1,0:T(8,128)(2,1)S(1)}, bf16[320,128]{1,0:T(8,128)(2,1)S(1)}, u32[]{:S(2)}, u32[]{:S(2)}) collective-permute-start(bf16[320,128]{1,0:T(8,128)(2,1)S(1)} %get-tuple-element.23.rest_0_), channel_id=1, source_target_pairs={{1,0},{0,1},{3,2},{2,3},{5,4},{4,5},{7,6},{6,7},{9,8},{8,9},{11,10... | collective-permute-start | bytes 245768 | tf_op jit(solution)/shard_map/ppermute | solution.py:397
  17.7 10.2 %collective-permute-start.8 = (bf16[328,128]{1,0:T(8,128)(2,1)S(1)}, bf16[328,128]{1,0:T(8,128)(2,1)S(1)}, u32[]{:S(2)}, u32[]{:S(2)}) collective-permute-start(bf16[328,128]{1,0:T(8,128)(2,1)S(1)} %get-tuple-element.28), channel_id=1, source_target_pairs={{0,4},{2,6},{4,0},{6,2},{8,12},{10,14},{12,8},{14,10},{1,5},{3,7},... | collective-permute-start | bytes 251912 | tf_op jit(solution)/shard_map/ppermute | solution.py:396
  18.6 10.3 %collective-permute-start.9 = (bf16[328,128]{1,0:T(8,128)(2,1)S(1)}, bf16[328,128]{1,0:T(8,128)(2,1)S(1)}, u32[]{:S(2)}, u32[]{:S(2)}) collective-permute-start(bf16[328,128]{1,0:T(8,128)(2,1)S(1)} %get-tuple-element.29), channel_id=1, source_target_pairs={{0,8},{2,10},{4,12},{6,14},{8,0},{10,2},{12,4},{14,6},{1,9},{3,11}... | collective-permute-start | bytes 251912 | tf_op jit(solution)/shard_map/ppermute | solution.py:396
  24.4 2.9 %collective-permute-start.4 = (bf16[320,128]{1,0:T(8,128)(2,1)S(1)}, bf16[320,128]{1,0:T(8,128)(2,1)S(1)}, u32[]{:S(2)}, u32[]{:S(2)}) collective-permute-start(bf16[320,128]{1,0:T(8,128)(2,1)S(1)} %get-tuple-element.23.rest_0_), channel_id=1, source_target_pairs={{0,2},{2,0},{4,6},{6,4},{8,10},{10,8},{12,14},{14,12},{1,3},{3,1},... | collective-permute-start | bytes 245768 | tf_op jit(solution)/shard_map/ppermute | solution.py:401
  24.4 6.8 %collective-permute-start.10 = (bf16[328,128]{1,0:T(8,128)(2,1)S(1)}, bf16[328,128]{1,0:T(8,128)(2,1)S(1)}, u32[]{:S(2)}, u32[]{:S(2)}) collective-permute-start(bf16[328,128]{1,0:T(8,128)(2,1)S(1)} %get-tuple-element.30), channel_id=1, source_target_pairs={{0,12},{2,14},{4,8},{6,10},{8,4},{10,6},{12,0},{14,2},{1,13},{3,15... | collective-permute-start | bytes 251912 | tf_op jit(solution)/shard_map/ppermute | solution.py:396
  27.1 4.1 %collective-permute-start.11 = (bf16[328,128]{1,0:T(8,128)(2,1)S(1)}, bf16[328,128]{1,0:T(8,128)(2,1)S(1)}, u32[]{:S(2)}, u32[]{:S(2)}) collective-permute-start(bf16[328,128]{1,0:T(8,128)(2,1)S(1)} %get-tuple-element.27.rest_8_), channel_id=1, source_target_pairs={{0,2},{2,0},{4,6},{6,4},{8,10},{10,8},{12,14},{14,12},{1,3},{3,1},... | collective-permute-start | bytes 251912 | tf_op jit(solution)/shard_map/ppermute | solution.py:401
  27.3 5.3 %collective-permute-start.16 = (bf16[320,128]{1,0:T(8,128)(2,1)S(1)}, bf16[320,128]{1,0:T(8,128)(2,1)S(1)}, u32[]{:S(2)}, u32[]{:S(2)}) collective-permute-start(bf16[320,128]{1,0:T(8,128)(2,1)S(1)} %collective-permute-done.1.rest_1_), channel_id=1, source_target_pairs={{1,0},{0,1},{3,2},{2,3},{5,4},{4,5},{7,6},{6,7},{9,8},{8,9},{11,10... | collective-permute-start | bytes 245768 | tf_op jit(solution)/shard_map/ppermute | solution.py:397
  27.8 4.8 %collective-permute-start.5 = (bf16[320,128]{1,0:T(8,128)(2,1)S(1)}, bf16[320,128]{1,0:T(8,128)(2,1)S(1)}, u32[]{:S(2)}, u32[]{:S(2)}) collective-permute-start(bf16[320,128]{1,0:T(8,128)(2,1)S(1)} %collective-permute-done.1.rest_1_), channel_id=1, source_target_pairs={{0,2},{2,0},{4,6},{6,4},{8,10},{10,8},{12,14},{14,12},{1,3},{3,1},... | collective-permute-start | bytes 245768 | tf_op jit(solution)/shard_map/ppermute | solution.py:401
  28.8 5.0 %collective-permute-start.17 = (bf16[320,128]{1,0:T(8,128)(2,1)S(1)}, bf16[320,128]{1,0:T(8,128)(2,1)S(1)}, u32[]{:S(2)}, u32[]{:S(2)}) collective-permute-start(bf16[320,128]{1,0:T(8,128)(2,1)S(1)} %collective-permute-done.2.rest_2_), channel_id=1, source_target_pairs={{1,0},{0,1},{3,2},{2,3},{5,4},{4,5},{7,6},{6,7},{9,8},{8,9},{11,10... | collective-permute-start | bytes 245768 | tf_op jit(solution)/shard_map/ppermute | solution.py:397
  31.2 2.7 %collective-permute-start.6 = (bf16[320,128]{1,0:T(8,128)(2,1)S(1)}, bf16[320,128]{1,0:T(8,128)(2,1)S(1)}, u32[]{:S(2)}, u32[]{:S(2)}) collective-permute-start(bf16[320,128]{1,0:T(8,128)(2,1)S(1)} %collective-permute-done.2.rest_2_), channel_id=1, source_target_pairs={{0,2},{2,0},{4,6},{6,4},{8,10},{10,8},{12,14},{14,12},{1,3},{3,1},... | collective-permute-start | bytes 245768 | tf_op jit(solution)/shard_map/ppermute | solution.py:401
  31.2 4.9 %collective-permute-start.18 = (bf16[320,128]{1,0:T(8,128)(2,1)S(1)}, bf16[320,128]{1,0:T(8,128)(2,1)S(1)}, u32[]{:S(2)}, u32[]{:S(2)}) collective-permute-start(bf16[320,128]{1,0:T(8,128)(2,1)S(1)} %collective-permute-done.3.rest_3_), channel_id=1, source_target_pairs={{1,0},{0,1},{3,2},{2,3},{5,4},{4,5},{7,6},{6,7},{9,8},{8,9},{11,10... | collective-permute-start | bytes 245768 | tf_op jit(solution)/shard_map/ppermute | solution.py:397
  32.6 4.0 %collective-permute-start.12 = (bf16[328,128]{1,0:T(8,128)(2,1)S(1)}, bf16[328,128]{1,0:T(8,128)(2,1)S(1)}, u32[]{:S(2)}, u32[]{:S(2)}) collective-permute-start(bf16[328,128]{1,0:T(8,128)(2,1)S(1)} %collective-permute-done.8.rest_9_), channel_id=1, source_target_pairs={{0,2},{2,0},{4,6},{6,4},{8,10},{10,8},{12,14},{14,12},{1,3},{3,1},... | collective-permute-start | bytes 251912 | tf_op jit(solution)/shard_map/ppermute | solution.py:401
  32.6 3.4 %collective-permute-start.7 = (bf16[320,128]{1,0:T(8,128)(2,1)S(1)}, bf16[320,128]{1,0:T(8,128)(2,1)S(1)}, u32[]{:S(2)}, u32[]{:S(2)}) collective-permute-start(bf16[320,128]{1,0:T(8,128)(2,1)S(1)} %collective-permute-done.3.rest_3_), channel_id=1, source_target_pairs={{0,2},{2,0},{4,6},{6,4},{8,10},{10,8},{12,14},{14,12},{1,3},{3,1},... | collective-permute-start | bytes 245768 | tf_op jit(solution)/shard_map/ppermute | solution.py:401
  33.8 2.7 %collective-permute-start.19 = (bf16[320,128]{1,0:T(8,128)(2,1)S(1)}, bf16[320,128]{1,0:T(8,128)(2,1)S(1)}, u32[]{:S(2)}, u32[]{:S(2)}) collective-permute-start(bf16[320,128]{1,0:T(8,128)(2,1)S(1)} %collective-permute-done.15.rest_16_), channel_id=1, source_target_pairs={{0,2},{2,0},{4,6},{6,4},{8,10},{10,8},{12,14},{14,12},{1,3},{3,1},... | collective-permute-start | bytes 245768 | tf_op jit(solution)/shard_map/ppermute | solution.py:401
  33.8 3.2 %collective-permute-start.13 = (bf16[328,128]{1,0:T(8,128)(2,1)S(1)}, bf16[328,128]{1,0:T(8,128)(2,1)S(1)}, u32[]{:S(2)}, u32[]{:S(2)}) collective-permute-start(bf16[328,128]{1,0:T(8,128)(2,1)S(1)} %collective-permute-done.9.rest_10_), channel_id=1, source_target_pairs={{0,2},{2,0},{4,6},{6,4},{8,10},{10,8},{12,14},{14,12},{1,3},{3,1},... | collective-permute-start | bytes 251912 | tf_op jit(solution)/shard_map/ppermute | solution.py:401
  36.0 1.3 %collective-permute-start.14 = (bf16[328,128]{1,0:T(8,128)(2,1)S(1)}, bf16[328,128]{1,0:T(8,128)(2,1)S(1)}, u32[]{:S(2)}, u32[]{:S(2)}) collective-permute-start(bf16[328,128]{1,0:T(8,128)(2,1)S(1)} %collective-permute-done.10.rest_11_), channel_id=1, source_target_pairs={{0,2},{2,0},{4,6},{6,4},{8,10},{10,8},{12,14},{14,12},{1,3},{3,1},... | collective-permute-start | bytes 251912 | tf_op jit(solution)/shard_map/ppermute | solution.py:401
  36.0 1.4 %collective-permute-start.20 = (bf16[320,128]{1,0:T(8,128)(2,1)S(1)}, bf16[320,128]{1,0:T(8,128)(2,1)S(1)}, u32[]{:S(2)}, u32[]{:S(2)}) collective-permute-start(bf16[320,128]{1,0:T(8,128)(2,1)S(1)} %collective-permute-done.16.rest_17_), channel_id=1, source_target_pairs={{0,2},{2,0},{4,6},{6,4},{8,10},{10,8},{12,14},{14,12},{1,3},{3,1},... | collective-permute-start | bytes 245768 | tf_op jit(solution)/shard_map/ppermute | solution.py:401
  36.5 1.3 %collective-permute-start.21 = (bf16[320,128]{1,0:T(8,128)(2,1)S(1)}, bf16[320,128]{1,0:T(8,128)(2,1)S(1)}, u32[]{:S(2)}, u32[]{:S(2)}) collective-permute-start(bf16[320,128]{1,0:T(8,128)(2,1)S(1)} %collective-permute-done.17.rest_18_), channel_id=1, source_target_pairs={{0,2},{2,0},{4,6},{6,4},{8,10},{10,8},{12,14},{14,12},{1,3},{3,1},... | collective-permute-start | bytes 245768 | tf_op jit(solution)/shard_map/ppermute | solution.py:401
  36.6 1.4 %collective-permute-start.22 = (bf16[320,128]{1,0:T(8,128)(2,1)S(1)}, bf16[320,128]{1,0:T(8,128)(2,1)S(1)}, u32[]{:S(2)}, u32[]{:S(2)}) collective-permute-start(bf16[320,128]{1,0:T(8,128)(2,1)S(1)} %collective-permute-done.18.rest_19_), channel_id=1, source_target_pairs={{0,2},{2,0},{4,6},{6,4},{8,10},{10,8},{12,14},{14,12},{1,3},{3,1},... | collective-permute-start | bytes 245768 | tf_op jit(solution)/shard_map/ppermute | solution.py:401
  47.2 4.5 %collective-permute-start.23 = (f32[4,8,128]{2,1,0:T(8,128)S(1)}, f32[4,8,128]{2,1,0:T(8,128)S(1)}, u32[]{:S(2)}, u32[]{:S(2)}) collective-permute-start(f32[4,8,128]{2,1,0:T(8,128)S(1)} %get-tuple-element.32), channel_id=1, source_target_pairs={{0,4},{2,6},{4,0},{6,2},{8,12},{10,14},{12,8},{14,10},{1,5},{3,7},... | collective-permute-start | bytes 49160 | tf_op jit(solution)/shard_map/ppermute | solution.py:432
  49.0 4.6 %collective-permute-start.24 = (f32[4,8,128]{2,1,0:T(8,128)S(1)}, f32[4,8,128]{2,1,0:T(8,128)S(1)}, u32[]{:S(2)}, u32[]{:S(2)}) collective-permute-start(f32[4,8,128]{2,1,0:T(8,128)S(1)} %get-tuple-element.33), channel_id=1, source_target_pairs={{0,8},{2,10},{4,12},{6,14},{8,0},{10,2},{12,4},{14,6},{1,9},{3,11}... | collective-permute-start | bytes 49160 | tf_op jit(solution)/shard_map/ppermute | solution.py:432
  50.5 5.5 %collective-permute-start.25 = (f32[4,8,128]{2,1,0:T(8,128)S(1)}, f32[4,8,128]{2,1,0:T(8,128)S(1)}, u32[]{:S(2)}, u32[]{:S(2)}) collective-permute-start(f32[4,8,128]{2,1,0:T(8,128)S(1)} %get-tuple-element.34), channel_id=1, source_target_pairs={{0,12},{2,14},{4,8},{6,10},{8,4},{10,6},{12,0},{14,2},{1,13},{3,15... | collective-permute-start | bytes 49160 | tf_op jit(solution)/shard_map/ppermute | solution.py:432
  56.6 1.3 %collective-permute-start.26 = (f32[4,4,512]{2,1,0:T(4,128)S(1)}, f32[4,4,512]{2,1,0:T(4,128)S(1)}, u32[]{:S(2)}, u32[]{:S(2)}) collective-permute-start(f32[4,4,512]{2,1,0:T(4,128)S(1)} %get-tuple-element.36), channel_id=1, source_target_pairs={{0,2},{2,0},{4,6},{6,4},{8,10},{10,8},{12,14},{14,12},{1,3},{3,1},... | collective-permute-start | bytes 98312 | tf_op jit(solution)/shard_map/ppermute | solution.py:449

commit v6 on v5

--- a/solution.py
+++ b/solution.py
@@ -10,7 +10,7 @@
 SHIFT = 16
 LANES = 128
 SUBLANES = 8
-UNROLL = 4
+UNROLL = 16
 
 SMEM = pl.BlockSpec(memory_space=pltpu.SMEM)
 VMEM = pl.BlockSpec(memory_space=pltpu.VMEM)
@@ -194,50 +194,47 @@
     blocks = [rest[p * groups : (p + 1) * groups] for p in range(parts + 1)]
     rest = rest[(parts + 1) * groups :]
     outs = rest[:chunks]
-    main, side, even, odd, edge, whole_params, scalars, order, result, sem = rest[chunks:]
+    main, side, even, odd, whole_params, scalars, order, result, sem = rest[chunks:]
     windows = (even, odd)
     own = info[2]
     first_vel = info[4]
     share = result.shape[0]
     main_rows = exposures * 2 * SHIFT
     size = main_rows + exposures * SUBLANES
+    total = groups * exposures
+    whole_params[total:] = jnp.zeros((exposures, LANES), jnp.int32)
     for g in range(groups):
         whole_params[g * exposures : (g + 1) * exposures] = (
             blocks[parts - 1][g][size : size + exposures].astype(jnp.float32).astype(jnp.int32)
         )
     fetch = pltpu.make_async_copy(whole_params, scalars, sem)
     fetch.start()
+    has_below = info[1].astype(jnp.float32)
     for g in range(groups):
         for p in range(parts + 1):
-            edge[g, p] = blocks[p][g][main_rows:size].astype(jnp.float32)
+            packed = blocks[p][g][main_rows:size]
+            for q in range(4):
+                piece = packed if q == 0 else pltpu.roll(packed, LANES - 2 * SHIFT * q, 1)
+                piece = piece.astype(jnp.float32)
+                if p == parts:
+                    piece = piece * has_below
+                at = p * SHIFT + (q % 2) * SUBLANES
+                for e in range(exposures):
+                    side[g * exposures + e, q // 2, at : at + SUBLANES] = piece[e * SUBLANES : (e + 1) * SUBLANES]
+            for k in range(2 * exposures):
+                cells = blocks[p][g][k * SHIFT : (k + 1) * SHIFT].astype(jnp.float32)
+                if p == parts:
+                    cells = cells * has_below
+                main[g * exposures + k // 2, k % 2, p * SHIFT : (p + 1) * SHIFT] = cells
+    main[total] = jnp.zeros(main.shape[1:], jnp.float32)
+    side[total] = jnp.zeros(side.shape[1:], jnp.float32)
     fetch.wait()
-    has_below = info[1].astype(jnp.float32)
     filled = jnp.int32(0)
-    for g in range(groups):
-
-        def unpack(e, at, g=g):
-            source = g * exposures + e
-            order[at] = source
-            for p in range(parts + 1):
-                start = pl.multiple_of(e * 2 * SHIFT, 2 * SHIFT)
-                both = blocks[p][g][pl.ds(start, 2 * SHIFT)].astype(jnp.float32)
-                packed = edge[g, p, pl.ds(pl.multiple_of(e * SUBLANES, SUBLANES), SUBLANES)]
-                if p == parts:
-                    both = both * has_below
-                    packed = packed * has_below
-                for m in (0, 1):
-                    main[at, m, p * SHIFT : (p + 1) * SHIFT] = both[m * SHIFT : (m + 1) * SHIFT]
-                    for h in (0, 1):
-                        q = 2 * m + h
-                        piece = packed if q == 0 else pltpu.roll(packed, LANES - 2 * SHIFT * q, 1)
-                        side[at, m, p * SHIFT + h * SUBLANES : p * SHIFT + (h + 1) * SUBLANES] = piece
-            return at + scalars[source, 2 * vels]
-
-        filled = lax.fori_loop(0, exposures, unpack, filled, unroll=4)
+    for source in range(total):
+        order[filled] = source
+        filled = filled + scalars[source, 2 * vels]
     for i in range(UNROLL):
-        order[filled + i] = 0
-        main[filled + i] = jnp.zeros(main.shape[1:], jnp.float32)
-        side[filled + i] = jnp.zeros(side.shape[1:], jnp.float32)
+        order[filled + i] = total
     trips = (filled + UNROLL - 1) // UNROLL
 
     lane = lax.broadcasted_iota(jnp.int32, (rows, LANES), 1)
@@ -249,7 +246,7 @@
         from_side = lane < col_at
         cells = jnp.concatenate(
             [
-                jnp.where(from_side, side[e, m, pl.ds(row_at, rows)], main[e, m, pl.ds(row_at, rows)])
+                jnp.where(from_side, side[source, m, pl.ds(row_at, rows)], main[source, m, pl.ds(row_at, rows)])
                 for m in (0, 1)
             ]
         ).astype(jnp.bfloat16)
@@ -274,7 +271,7 @@
 
         return lax.fori_loop(0, trips, trip, start)
 
-    zeros = main[filled, 0, 0:rows]
+    zeros = main[total, 0, 0:rows]
     none = (zeros, zeros)
 
     sums = over_exposures(functools.partial(gather, 0), none)
@@ -412,13 +409,12 @@
         in_specs=[SMEM] + [VMEM] * ((parts + 1) * groups),
         out_specs=[VMEM] * chunks,
         scratch_shapes=[
-            pltpu.VMEM((total + UNROLL, 2, reach, LANES), jnp.float32),
-            pltpu.VMEM((total + UNROLL, 2, reach, LANES), jnp.float32),
+            pltpu.VMEM((total + 1, 2, reach, LANES), jnp.float32),
+            pltpu.VMEM((total + 1, 2, reach, LANES), jnp.float32),
             pltpu.VMEM((total + UNROLL, 2, rows, LANES), jnp.float32),
             pltpu.VMEM((total + UNROLL, 2, rows, LANES), jnp.float32),
-            pltpu.VMEM((groups, parts + 1, exposures * SUBLANES, LANES), jnp.float32),
-            pltpu.VMEM((total, LANES), jnp.int32),
-            pltpu.SMEM((total, LANES), jnp.int32),
+            pltpu.VMEM((total + exposures, LANES), jnp.int32),
+            pltpu.SMEM((total + exposures, LANES), jnp.int32),
             pltpu.SMEM((total + UNROLL,), jnp.int32),
             pltpu.VMEM((share, rows, LANES), jnp.float32),
             pltpu.SemaphoreType.DMA(()),

time: 59.3 us -> 55.3 us (0.933)
  Pallas kernels: 17.5 us -> 13.5 us
    pallas_call x1, Pallas kernels: 9.21 us -> 5.27 us  [per_device(): pl.pallas_call(functools.partial(stack_kernel, groups, chunks, exposures,...]
  transfers between devices with their start and end apart: 27 -> 27, of which waited for: 12 -> 12; matrix products, arithmetic and copies ran while one was open for 0% -> 0% of each run, Pallas kernels for 7% -> 8%
where the time goes in v6:
time: 55.3 us; the launch traced here: 55.1 us
  starting transfers between devices  24.6 us (44%)
  waiting for transfers between devices  13.6 us (25%)
  Pallas kernels  13.5 us (24%)
  local copies, waits for them, and re-layouts  3.24 us (6%)
    ppermute x6, starting transfers between devices, per_device(): lax.ppermute(sends[step * parts + p], 'expo', chunk_pairs(step, chunks, s...  11.5 us
    pallas_call x1, Pallas kernels, per_device(): pl.pallas_call(functools.partial(stack_kernel, groups, chunks, exposures,...  5.27 us
    ppermute x3, starting transfers between devices, per_device(): lax.ppermute(pieces[step], 'expo', chunk_pairs(step, chunks, subs))  4.45 us
    ppermute x3, waiting for transfers between devices, per_device(): lax.ppermute(pieces[step], 'expo', chunk_pairs(step, chunks, subs))  4.36 us
    pallas_call x1, Pallas kernels, per_device(): pl.pallas_call(functools.partial(inner_kernel, radius), out_shape=[jax.Sh...  4.13 us
    ppermute x4, waiting for transfers between devices, per_device(): blocks[parts][0][step] = lax.ppermute(blocks[0][0][step], 'strip', up)  3.75 us
    ppermute x6, waiting for transfers between devices, per_device(): lax.ppermute(sends[step * parts + p], 'expo', chunk_pairs(step, chunks, s...  3.34 us
    ppermute x4, starting transfers between devices, per_device(): blocks[parts][0][step] = lax.ppermute(blocks[0][0][step], 'strip', up)  3.26 us
  transfers between devices with their start and end apart: 27, of which 12 were waited for; matrix products, arithmetic and copies ran while one was open for 0% of the time, Pallas kernels for 8%

profile of v6, /device:TPU:0, one launch (start us, length us, event | category | flops | bytes accessed | tf_op | source)
XLA Modules:
  0.0 55.1 jit_solution(11384541500946273851)
XLA Ops:
  0.0 1.0 %dynamic-slice_bitcast_fusion = (bf16[1,8,4,512]{3,2,1,0:T(4,128)(2,1)S(1)}, bf16[1,8,4,512]{3,2,1,0:T(4,128)(2,1)S(1)}) fusion(bf16[8,32,512]{2,1,0:T(8,128)(2,1)} %inv_var.1, s32[]{:T(128)S(6)} %select_n.19, bf16[8,32,512]{2,1,0:T(8,128)(2,1)} %science.1), kind=kLoop, calls=%fused_computation.1 | loop fusion | bytes 131076 | tf_op jit(solution)/shard_map/stack | solution.py:342
  1.0 3.0 %collective-permute-start = (bf16[2,8,4,512]{3,2,1,0:T(4,128)(2,1)S(1)}, bf16[2,8,4,512]{3,2,1,0:T(4,128)(2,1)S(1)}, u32[]{:S(2)}, u32[]{:S(2)}) collective-permute-start(bf16[2,8,4,512]{3,2,1,0:T(4,128)(2,1)S(1)} %pad_maximum_fusion), channel_id=1, source_target_pairs={{0,1},{1,0},{2,3},{3,2},{4,5},{5,4},{6,7},{7,6},{8,9},{9,8},{10,11... | collective-permute-start | bytes 196616 | tf_op jit(solution)/shard_map/ppermute | solution.py:346
  4.0 0.1 stack.40.info
  4.1 0.6 %copy-done.2 = f32[8,9]{1,0:T(8,128)S(1)} copy-done((f32[8,9]{1,0:T(8,128)S(1)}, f32[8,9]{1,0:T(8,128)}, u32[]{:S(2)}) %copy-start.2) | copy-done | bytes 312
  4.7 0.0 copy-done.3
  4.8 0.9 %copy-done.1 = bf16[8,32,512]{2,1,0:T(8,128)(2,1)S(1)} copy-done((bf16[8,32,512]{2,1,0:T(8,128)(2,1)S(1)}, bf16[8,32,512]{2,1,0:T(8,128)(2,1)}, u32[]{:S(2)}) %copy-start.1) | copy-done | bytes 262168
  5.7 4.1 %filter_inner.1 = (f32[4,512,128]{2,1,0:T(8,128)S(1)}, f32[4,128,128]{2,1,0:T(8,128)S(1)}) custom-call(f32[8,9]{1,0:T(8,128)S(1)} %copy-done.2, f32[8,9]{1,0:T(8,128)S(1)} %copy-done.3, bf16[8,32,512]{2,1,0:T(8,128)(2,1)S(1)} %copy-done, bf16[8,32,512]{2,1,0:T(8,128)(2,1)S(1)} %copy-done.1), custom_call_target="tpu_custom_call" | custom-call | flops 100000000 | bytes 4000000 | tf_op jit(solution)/shard_map/filter_inner/pallas_call | solution.py:353
  9.8 0.0 collective-permute-done.above.below
  9.9 0.0 copy-start.6
  9.9 0.6 %copy-done.6 = s32[8]{0:T(128)S(1)} copy-done((s32[8]{0:T(128)S(1)}, s32[8]{0:T(128)}, u32[]{:S(2)}) %copy-start.6) | copy-done | bytes 56
  10.5 2.4 %filter_outer.1 = (bf16[320,128]{1,0:T(8,128)(2,1)S(1)}, bf16[328,128]{1,0:T(8,128)(2,1)S(1)}, bf16[320,128]{1,0:T(8,128)(2,1)S(1)}, bf16[328,128]{1,0:T(8,128)(...) custom-call(s32[5]{0:T(128)S(1)} %stack.40.info, ...), custom_call_target="tpu_custom_call" | custom-call | tf_op jit(solution)/shard_map/filter_outer/pallas_call | solution.py:371
  12.9 1.6 %collective-permute-start.1 = (bf16[320,128]{1,0:T(8,128)(2,1)S(1)}, bf16[320,128]{1,0:T(8,128)(2,1)S(1)}, u32[]{:S(2)}, u32[]{:S(2)}) collective-permute-start(bf16[320,128]{1,0:T(8,128)(2,1)S(1)} %get-tuple-element.24), channel_id=1, source_target_pairs={{0,4},{2,6},{4,0},{6,2},{8,12},{10,14},{12,8},{14,10},{1,5},{3,7},... | collective-permute-start | bytes 245768 | tf_op jit(solution)/shard_map/ppermute | solution.py:393
  14.5 2.6 %collective-permute-start.2 = (bf16[320,128]{1,0:T(8,128)(2,1)S(1)}, bf16[320,128]{1,0:T(8,128)(2,1)S(1)}, u32[]{:S(2)}, u32[]{:S(2)}) collective-permute-start(bf16[320,128]{1,0:T(8,128)(2,1)S(1)} %get-tuple-element.25), channel_id=1, source_target_pairs={{0,8},{2,10},{4,12},{6,14},{8,0},{10,2},{12,4},{14,6},{1,9},{3,11}... | collective-permute-start | bytes 245768 | tf_op jit(solution)/shard_map/ppermute | solution.py:393
  17.1 0.2 collective-permute-start.3
  17.4 0.3 collective-permute-start.15
  17.7 0.9 %collective-permute-start.8 = (bf16[328,128]{1,0:T(8,128)(2,1)S(1)}, bf16[328,128]{1,0:T(8,128)(2,1)S(1)}, u32[]{:S(2)}, u32[]{:S(2)}) collective-permute-start(bf16[328,128]{1,0:T(8,128)(2,1)S(1)} %get-tuple-element.28), channel_id=1, source_target_pairs={{0,4},{2,6},{4,0},{6,2},{8,12},{10,14},{12,8},{14,10},{1,5},{3,7},... | collective-permute-start | bytes 251912 | tf_op jit(solution)/shard_map/ppermute | solution.py:393
  18.6 0.0 collective-permute-done.1.rest_1_
  18.6 3.5 %collective-permute-start.9 = (bf16[328,128]{1,0:T(8,128)(2,1)S(1)}, bf16[328,128]{1,0:T(8,128)(2,1)S(1)}, u32[]{:S(2)}, u32[]{:S(2)}) collective-permute-start(bf16[328,128]{1,0:T(8,128)(2,1)S(1)} %get-tuple-element.29), channel_id=1, source_target_pairs={{0,8},{2,10},{4,12},{6,14},{8,0},{10,2},{12,4},{14,6},{1,9},{3,11}... | collective-permute-start | bytes 251912 | tf_op jit(solution)/shard_map/ppermute | solution.py:393
  22.1 2.3 %collective-permute-done.2.rest_2_ = bf16[320,128]{1,0:T(8,128)(2,1)S(1)} collective-permute-done((bf16[320,128]{1,0:T(8,128)(2,1)S(1)}, bf16[320,128]{1,0:T(8,128)(2,1)S(1)}, u32[]{:S(2)}, u32[]{:S(2)}) %collective-permute-start.2) | collective-permute-done | bytes 81952 | tf_op jit(solution)/shard_map/ppermute | solution.py:393
  24.4 2.7 %collective-permute-start.10 = (bf16[328,128]{1,0:T(8,128)(2,1)S(1)}, bf16[328,128]{1,0:T(8,128)(2,1)S(1)}, u32[]{:S(2)}, u32[]{:S(2)}) collective-permute-start(bf16[328,128]{1,0:T(8,128)(2,1)S(1)} %get-tuple-element.30), channel_id=1, source_target_pairs={{0,12},{2,14},{4,8},{6,10},{8,4},{10,6},{12,0},{14,2},{1,13},{3,15... | collective-permute-start | bytes 251912 | tf_op jit(solution)/shard_map/ppermute | solution.py:393
  27.1 0.2 collective-permute-start.11
  27.3 0.5 collective-permute-start.16
  27.8 0.0 collective-permute-start.5
  27.8 1.0 %collective-permute-done.9.rest_10_ = bf16[328,128]{1,0:T(8,128)(2,1)S(1)} collective-permute-done((bf16[328,128]{1,0:T(8,128)(2,1)S(1)}, bf16[328,128]{1,0:T(8,128)(2,1)S(1)}, u32[]{:S(2)}, u32[]{:S(2)}) %collective-permute-start.9) | collective-permute-done | bytes 84000 | tf_op jit(solution)/shard_map/ppermute | solution.py:393
  28.8 2.3 %collective-permute-start.17 = (bf16[320,128]{1,0:T(8,128)(2,1)S(1)}, bf16[320,128]{1,0:T(8,128)(2,1)S(1)}, u32[]{:S(2)}, u32[]{:S(2)}) collective-permute-start(bf16[320,128]{1,0:T(8,128)(2,1)S(1)} %collective-permute-done.2.rest_2_), channel_id=1, source_target_pairs={{1,0},{0,1},{3,2},{2,3},{5,4},{4,5},{7,6},{6,7},{9,8},{8,9},{11,10... | collective-permute-start | bytes 245768 | tf_op jit(solution)/shard_map/ppermute | solution.py:394
  31.2 0.1 collective-permute-start.18
  31.3 1.4 %collective-permute-done.16.rest_17_ = bf16[320,128]{1,0:T(8,128)(2,1)S(1)} collective-permute-done((bf16[320,128]{1,0:T(8,128)(2,1)S(1)}, bf16[320,128]{1,0:T(8,128)(2,1)S(1)}, u32[]{:S(2)}, u32[]{:S(2)}) %collective-permute-start.16) | collective-permute-done | bytes 81952 | tf_op jit(solution)/shard_map/ppermute | solution.py:394
  32.6 0.5 collective-permute-start.7
  33.1 0.7 %collective-permute-done.17.rest_18_ = bf16[320,128]{1,0:T(8,128)(2,1)S(1)} collective-permute-done((bf16[320,128]{1,0:T(8,128)(2,1)S(1)}, bf16[320,128]{1,0:T(8,128)(2,1)S(1)}, u32[]{:S(2)}, u32[]{:S(2)}) %collective-permute-start.17) | collective-permute-done | bytes 81952 | tf_op jit(solution)/shard_map/ppermute | solution.py:394
  33.8 0.5 collective-permute-start.13
  34.3 1.7 %collective-permute-done.18.rest_19_ = bf16[320,128]{1,0:T(8,128)(2,1)S(1)} collective-permute-done((bf16[320,128]{1,0:T(8,128)(2,1)S(1)}, bf16[320,128]{1,0:T(8,128)(2,1)S(1)}, u32[]{:S(2)}, u32[]{:S(2)}) %collective-permute-start.18) | collective-permute-done | bytes 81952 | tf_op jit(solution)/shard_map/ppermute | solution.py:394
  36.0 0.5 collective-permute-start.20
  36.5 0.1 collective-permute-start.21
  36.6 0.4 collective-permute-start.22
  37.1 0.2 collective-permute-done.14.rest_15_
  37.3 0.2 collective-permute-done.20.rest_21_
  37.5 0.4 collective-permute-done.21.rest_22_
  37.8 0.2 collective-permute-done.22.rest_23_
  38.0 5.3 %stack_twice.1 = (f32[4,8,128]{2,1,0:T(8,128)S(1)}, f32[4,8,128]{2,1,0:T(8,128)S(1)}, f32[4,8,128]{2,1,0:T(8,128)S(1)}, f32[4,8,128]{2,1,0:T(8,128)S(1)}) custom-call(s32[5]{0:T(128)S(1)} %stack.40.info, bf16[320,128]{1,0:T(8,128)(2,1)S(1)} %get-tuple-element.23.rest_0_, bf16[320,128]{1,0:T(8,128)(2,1)S(1)} %collective-permute-done.1.rest_1_, ...), custom_call_target="tpu_custom_call" | custom-call | tf_op jit(solution)/shard_map/stack_twice/pallas_call | solution.py:406
  43.3 1.8 %collective-permute-start.23 = (f32[4,8,128]{2,1,0:T(8,128)S(1)}, f32[4,8,128]{2,1,0:T(8,128)S(1)}, u32[]{:S(2)}, u32[]{:S(2)}) collective-permute-start(f32[4,8,128]{2,1,0:T(8,128)S(1)} %get-tuple-element.32), channel_id=1, source_target_pairs={{0,4},{2,6},{4,0},{6,2},{8,12},{10,14},{12,8},{14,10},{1,5},{3,7},... | collective-permute-start | bytes 49160 | tf_op jit(solution)/shard_map/ppermute | solution.py:428
  45.1 1.5 %collective-permute-start.24 = (f32[4,8,128]{2,1,0:T(8,128)S(1)}, f32[4,8,128]{2,1,0:T(8,128)S(1)}, u32[]{:S(2)}, u32[]{:S(2)}) collective-permute-start(f32[4,8,128]{2,1,0:T(8,128)S(1)} %get-tuple-element.33), channel_id=1, source_target_pairs={{0,8},{2,10},{4,12},{6,14},{8,0},{10,2},{12,4},{14,6},{1,9},{3,11}... | collective-permute-start | bytes 49160 | tf_op jit(solution)/shard_map/ppermute | solution.py:428
  46.6 1.2 %collective-permute-start.25 = (f32[4,8,128]{2,1,0:T(8,128)S(1)}, f32[4,8,128]{2,1,0:T(8,128)S(1)}, u32[]{:S(2)}, u32[]{:S(2)}) collective-permute-start(f32[4,8,128]{2,1,0:T(8,128)S(1)} %get-tuple-element.34), channel_id=1, source_target_pairs={{0,12},{2,14},{4,8},{6,10},{8,4},{10,6},{12,0},{14,2},{1,13},{3,15... | collective-permute-start | bytes 49160 | tf_op jit(solution)/shard_map/ppermute | solution.py:428
  47.7 2.0 %collective-permute-done.24.rest_2_ = f32[4,8,128]{2,1,0:T(8,128)S(1)} collective-permute-done((f32[4,8,128]{2,1,0:T(8,128)S(1)}, f32[4,8,128]{2,1,0:T(8,128)S(1)}, u32[]{:S(2)}, u32[]{:S(2)}) %collective-permute-start.24) | collective-permute-done | bytes 16416 | tf_op jit(solution)/shard_map/ppermute | solution.py:428
  49.7 2.4 %collective-permute-done.25.rest_3_ = f32[4,8,128]{2,1,0:T(8,128)S(1)} collective-permute-done((f32[4,8,128]{2,1,0:T(8,128)S(1)}, f32[4,8,128]{2,1,0:T(8,128)S(1)}, u32[]{:S(2)}, u32[]{:S(2)}) %collective-permute-start.25) | collective-permute-done | bytes 16416 | tf_op jit(solution)/shard_map/ppermute | solution.py:428
  52.1 0.6 %join_columns.1 = (f32[4,4,512]{2,1,0:T(4,128)S(1)}, f32[4,4,512]{2,1,0:T(4,128)S(1)}) custom-call(s32[5]{0:T(128)S(1)} %stack.40.info, f32[4,8,128]{2,1,0:T(8,128)S(1)} %get-tuple-element.31.rest_0_, f32[4,8,128]{2,1,0:T(8,128)S(1)} %collective-permute-done.23.rest_1_, f32[4,8,128]{2,1,0:T(8,128)S(1)} %collective-permute-done.24.rest_2_, ...), custom_call_target="tpu_custom_call" | custom-call | tf_op jit(solution)/shard_map/join_columns/pallas_call | solution.py:431
  52.7 0.1 collective-permute-start.26
  52.7 1.2 %collective-permute-done.26.rest_1_ = f32[4,4,512]{2,1,0:T(4,128)S(1)} collective-permute-done((f32[4,4,512]{2,1,0:T(4,128)S(1)}, f32[4,4,512]{2,1,0:T(4,128)S(1)}, u32[]{:S(2)}, u32[]{:S(2)}) %collective-permute-start.26) | collective-permute-done | bytes 32800 | tf_op jit(solution)/shard_map/ppermute | solution.py:445
  53.9 1.2 %join_velocities.1 = f32[8,4,512]{2,1,0:T(4,128)} custom-call(s32[5]{0:T(128)S(1)} %stack.40.info, f32[4,4,512]{2,1,0:T(4,128)S(1)} %get-tuple-element.35.rest_0_, f32[4,4,512]{2,1,0:T(4,128)S(1)} %collective-permute-done.26.rest_1_), custom_call_target="tpu_custom_call" | custom-call | tf_op jit(solution)/shard_map/join_velocities/pallas_call | solution.py:446
  (28 shorter events, 0.1 us)
Async XLA Ops:
  0.0 4.1 %copy-start = (bf16[8,32,512]{2,1,0:T(8,128)(2,1)S(1)}, bf16[8,32,512]{2,1,0:T(8,128)(2,1)}, u32[]{:S(2)}) copy-start(bf16[8,32,512]{2,1,0:T(8,128)(2,1)} %science.1) | copy-start | bytes 786436
  1.0 8.8 %collective-permute-start = (bf16[2,8,4,512]{3,2,1,0:T(4,128)(2,1)S(1)}, bf16[2,8,4,512]{3,2,1,0:T(4,128)(2,1)S(1)}, u32[]{:S(2)}, u32[]{:S(2)}) collective-permute-start(bf16[2,8,4,512]{3,2,1,0:T(4,128)(2,1)S(1)} %pad_maximum_fusion), channel_id=1, source_target_pairs={{0,1},{1,0},{2,3},{3,2},{4,5},{5,4},{6,7},{7,6},{8,9},{9,8},{10,11... | collective-permute-start | bytes 196616 | tf_op jit(solution)/shard_map/ppermute | solution.py:346
  4.0 0.7 %copy-start.2 = (f32[8,9]{1,0:T(8,128)S(1)}, f32[8,9]{1,0:T(8,128)}, u32[]{:S(2)}) copy-start(f32[8,9]{1,0:T(8,128)} %row_taps.3) | copy-start | bytes 868
  4.0 0.7 %copy-start.3 = (f32[8,9]{1,0:T(8,128)S(1)}, f32[8,9]{1,0:T(8,128)}, u32[]{:S(2)}) copy-start(f32[8,9]{1,0:T(8,128)} %col_taps.3) | copy-start | bytes 868
  4.7 0.9 %copy-start.1 = (bf16[8,32,512]{2,1,0:T(8,128)(2,1)S(1)}, bf16[8,32,512]{2,1,0:T(8,128)(2,1)}, u32[]{:S(2)}) copy-start(bf16[8,32,512]{2,1,0:T(8,128)(2,1)} %inv_var.1) | copy-start | bytes 786436
  5.7 4.2 %copy-start.4 = (s32[8,8]{1,0:T(8,128)S(1)}, s32[8,8]{1,0:T(8,128)}, u32[]{:S(2)}) copy-start(s32[8,8]{1,0:T(8,128)} %row_shift.1) | copy-start | bytes 772
  5.7 4.2 %copy-start.5 = (s32[8,8]{1,0:T(8,128)S(1)}, s32[8,8]{1,0:T(8,128)}, u32[]{:S(2)}) copy-start(s32[8,8]{1,0:T(8,128)} %col_shift.1) | copy-start | bytes 772
  9.9 0.7 %copy-start.6 = (s32[8]{0:T(128)S(1)}, s32[8]{0:T(128)}, u32[]{:S(2)}) copy-start(s32[8]{0:T(128)} %usable.1) | copy-start | bytes 100
  12.9 5.7 %collective-permute-start.1 = (bf16[320,128]{1,0:T(8,128)(2,1)S(1)}, bf16[320,128]{1,0:T(8,128)(2,1)S(1)}, u32[]{:S(2)}, u32[]{:S(2)}) collective-permute-start(bf16[320,128]{1,0:T(8,128)(2,1)S(1)} %get-tuple-element.24), channel_id=1, source_target_pairs={{0,4},{2,6},{4,0},{6,2},{8,12},{10,14},{12,8},{14,10},{1,5},{3,7},... | collective-permute-start | bytes 245768 | tf_op jit(solution)/shard_map/ppermute | solution.py:393
  14.5 9.9 %collective-permute-start.2 = (bf16[320,128]{1,0:T(8,128)(2,1)S(1)}, bf16[320,128]{1,0:T(8,128)(2,1)S(1)}, u32[]{:S(2)}, u32[]{:S(2)}) collective-permute-start(bf16[320,128]{1,0:T(8,128)(2,1)S(1)} %get-tuple-element.25), channel_id=1, source_target_pairs={{0,8},{2,10},{4,12},{6,14},{8,0},{10,2},{12,4},{14,6},{1,9},{3,11}... | collective-permute-start | bytes 245768 | tf_op jit(solution)/shard_map/ppermute | solution.py:393
  17.1 7.3 %collective-permute-start.3 = (bf16[320,128]{1,0:T(8,128)(2,1)S(1)}, bf16[320,128]{1,0:T(8,128)(2,1)S(1)}, u32[]{:S(2)}, u32[]{:S(2)}) collective-permute-start(bf16[320,128]{1,0:T(8,128)(2,1)S(1)} %get-tuple-element.26), channel_id=1, source_target_pairs={{0,12},{2,14},{4,8},{6,10},{8,4},{10,6},{12,0},{14,2},{1,13},{3,15... | collective-permute-start | bytes 245768 | tf_op jit(solution)/shard_map/ppermute | solution.py:393
  17.4 9.7 %collective-permute-start.15 = (bf16[320,128]{1,0:T(8,128)(2,1)S(1)}, bf16[320,128]{1,0:T(8,128)(2,1)S(1)}, u32[]{:S(2)}, u32[]{:S(2)}) collective-permute-start(bf16[320,128]{1,0:T(8,128)(2,1)S(1)} %get-tuple-element.23.rest_0_), channel_id=1, source_target_pairs={{1,0},{0,1},{3,2},{2,3},{5,4},{4,5},{7,6},{6,7},{9,8},{8,9},{11,10... | collective-permute-start | bytes 245768 | tf_op jit(solution)/shard_map/ppermute | solution.py:394
  17.7 10.2 %collective-permute-start.8 = (bf16[328,128]{1,0:T(8,128)(2,1)S(1)}, bf16[328,128]{1,0:T(8,128)(2,1)S(1)}, u32[]{:S(2)}, u32[]{:S(2)}) collective-permute-start(bf16[328,128]{1,0:T(8,128)(2,1)S(1)} %get-tuple-element.28), channel_id=1, source_target_pairs={{0,4},{2,6},{4,0},{6,2},{8,12},{10,14},{12,8},{14,10},{1,5},{3,7},... | collective-permute-start | bytes 251912 | tf_op jit(solution)/shard_map/ppermute | solution.py:393
  18.6 10.3 %collective-permute-start.9 = (bf16[328,128]{1,0:T(8,128)(2,1)S(1)}, bf16[328,128]{1,0:T(8,128)(2,1)S(1)}, u32[]{:S(2)}, u32[]{:S(2)}) collective-permute-start(bf16[328,128]{1,0:T(8,128)(2,1)S(1)} %get-tuple-element.29), channel_id=1, source_target_pairs={{0,8},{2,10},{4,12},{6,14},{8,0},{10,2},{12,4},{14,6},{1,9},{3,11}... | collective-permute-start | bytes 251912 | tf_op jit(solution)/shard_map/ppermute | solution.py:393
  24.4 2.9 %collective-permute-start.4 = (bf16[320,128]{1,0:T(8,128)(2,1)S(1)}, bf16[320,128]{1,0:T(8,128)(2,1)S(1)}, u32[]{:S(2)}, u32[]{:S(2)}) collective-permute-start(bf16[320,128]{1,0:T(8,128)(2,1)S(1)} %get-tuple-element.23.rest_0_), channel_id=1, source_target_pairs={{0,2},{2,0},{4,6},{6,4},{8,10},{10,8},{12,14},{14,12},{1,3},{3,1},... | collective-permute-start | bytes 245768 | tf_op jit(solution)/shard_map/ppermute | solution.py:398
  24.4 6.8 %collective-permute-start.10 = (bf16[328,128]{1,0:T(8,128)(2,1)S(1)}, bf16[328,128]{1,0:T(8,128)(2,1)S(1)}, u32[]{:S(2)}, u32[]{:S(2)}) collective-permute-start(bf16[328,128]{1,0:T(8,128)(2,1)S(1)} %get-tuple-element.30), channel_id=1, source_target_pairs={{0,12},{2,14},{4,8},{6,10},{8,4},{10,6},{12,0},{14,2},{1,13},{3,15... | collective-permute-start | bytes 251912 | tf_op jit(solution)/shard_map/ppermute | solution.py:393
  27.1 4.1 %collective-permute-start.11 = (bf16[328,128]{1,0:T(8,128)(2,1)S(1)}, bf16[328,128]{1,0:T(8,128)(2,1)S(1)}, u32[]{:S(2)}, u32[]{:S(2)}) collective-permute-start(bf16[328,128]{1,0:T(8,128)(2,1)S(1)} %get-tuple-element.27.rest_8_), channel_id=1, source_target_pairs={{0,2},{2,0},{4,6},{6,4},{8,10},{10,8},{12,14},{14,12},{1,3},{3,1},... | collective-permute-start | bytes 251912 | tf_op jit(solution)/shard_map/ppermute | solution.py:398
  27.3 5.3 %collective-permute-start.16 = (bf16[320,128]{1,0:T(8,128)(2,1)S(1)}, bf16[320,128]{1,0:T(8,128)(2,1)S(1)}, u32[]{:S(2)}, u32[]{:S(2)}) collective-permute-start(bf16[320,128]{1,0:T(8,128)(2,1)S(1)} %collective-permute-done.1.rest_1_), channel_id=1, source_target_pairs={{1,0},{0,1},{3,2},{2,3},{5,4},{4,5},{7,6},{6,7},{9,8},{8,9},{11,10... | collective-permute-start | bytes 245768 | tf_op jit(solution)/shard_map/ppermute | solution.py:394
  27.8 4.8 %collective-permute-start.5 = (bf16[320,128]{1,0:T(8,128)(2,1)S(1)}, bf16[320,128]{1,0:T(8,128)(2,1)S(1)}, u32[]{:S(2)}, u32[]{:S(2)}) collective-permute-start(bf16[320,128]{1,0:T(8,128)(2,1)S(1)} %collective-permute-done.1.rest_1_), channel_id=1, source_target_pairs={{0,2},{2,0},{4,6},{6,4},{8,10},{10,8},{12,14},{14,12},{1,3},{3,1},... | collective-permute-start | bytes 245768 | tf_op jit(solution)/shard_map/ppermute | solution.py:398
  28.8 5.0 %collective-permute-start.17 = (bf16[320,128]{1,0:T(8,128)(2,1)S(1)}, bf16[320,128]{1,0:T(8,128)(2,1)S(1)}, u32[]{:S(2)}, u32[]{:S(2)}) collective-permute-start(bf16[320,128]{1,0:T(8,128)(2,1)S(1)} %collective-permute-done.2.rest_2_), channel_id=1, source_target_pairs={{1,0},{0,1},{3,2},{2,3},{5,4},{4,5},{7,6},{6,7},{9,8},{8,9},{11,10... | collective-permute-start | bytes 245768 | tf_op jit(solution)/shard_map/ppermute | solution.py:394
  31.2 2.7 %collective-permute-start.6 = (bf16[320,128]{1,0:T(8,128)(2,1)S(1)}, bf16[320,128]{1,0:T(8,128)(2,1)S(1)}, u32[]{:S(2)}, u32[]{:S(2)}) collective-permute-start(bf16[320,128]{1,0:T(8,128)(2,1)S(1)} %collective-permute-done.2.rest_2_), channel_id=1, source_target_pairs={{0,2},{2,0},{4,6},{6,4},{8,10},{10,8},{12,14},{14,12},{1,3},{3,1},... | collective-permute-start | bytes 245768 | tf_op jit(solution)/shard_map/ppermute | solution.py:398
  31.2 4.9 %collective-permute-start.18 = (bf16[320,128]{1,0:T(8,128)(2,1)S(1)}, bf16[320,128]{1,0:T(8,128)(2,1)S(1)}, u32[]{:S(2)}, u32[]{:S(2)}) collective-permute-start(bf16[320,128]{1,0:T(8,128)(2,1)S(1)} %collective-permute-done.3.rest_3_), channel_id=1, source_target_pairs={{1,0},{0,1},{3,2},{2,3},{5,4},{4,5},{7,6},{6,7},{9,8},{8,9},{11,10... | collective-permute-start | bytes 245768 | tf_op jit(solution)/shard_map/ppermute | solution.py:394
  32.6 4.0 %collective-permute-start.12 = (bf16[328,128]{1,0:T(8,128)(2,1)S(1)}, bf16[328,128]{1,0:T(8,128)(2,1)S(1)}, u32[]{:S(2)}, u32[]{:S(2)}) collective-permute-start(bf16[328,128]{1,0:T(8,128)(2,1)S(1)} %collective-permute-done.8.rest_9_), channel_id=1, source_target_pairs={{0,2},{2,0},{4,6},{6,4},{8,10},{10,8},{12,14},{14,12},{1,3},{3,1},... | collective-permute-start | bytes 251912 | tf_op jit(solution)/shard_map/ppermute | solution.py:398
  32.6 3.4 %collective-permute-start.7 = (bf16[320,128]{1,0:T(8,128)(2,1)S(1)}, bf16[320,128]{1,0:T(8,128)(2,1)S(1)}, u32[]{:S(2)}, u32[]{:S(2)}) collective-permute-start(bf16[320,128]{1,0:T(8,128)(2,1)S(1)} %collective-permute-done.3.rest_3_), channel_id=1, source_target_pairs={{0,2},{2,0},{4,6},{6,4},{8,10},{10,8},{12,14},{14,12},{1,3},{3,1},... | collective-permute-start | bytes 245768 | tf_op jit(solution)/shard_map/ppermute | solution.py:398
  33.8 2.7 %collective-permute-start.19 = (bf16[320,128]{1,0:T(8,128)(2,1)S(1)}, bf16[320,128]{1,0:T(8,128)(2,1)S(1)}, u32[]{:S(2)}, u32[]{:S(2)}) collective-permute-start(bf16[320,128]{1,0:T(8,128)(2,1)S(1)} %collective-permute-done.15.rest_16_), channel_id=1, source_target_pairs={{0,2},{2,0},{4,6},{6,4},{8,10},{10,8},{12,14},{14,12},{1,3},{3,1},... | collective-permute-start | bytes 245768 | tf_op jit(solution)/shard_map/ppermute | solution.py:398
  33.8 3.2 %collective-permute-start.13 = (bf16[328,128]{1,0:T(8,128)(2,1)S(1)}, bf16[328,128]{1,0:T(8,128)(2,1)S(1)}, u32[]{:S(2)}, u32[]{:S(2)}) collective-permute-start(bf16[328,128]{1,0:T(8,128)(2,1)S(1)} %collective-permute-done.9.rest_10_), channel_id=1, source_target_pairs={{0,2},{2,0},{4,6},{6,4},{8,10},{10,8},{12,14},{14,12},{1,3},{3,1},... | collective-permute-start | bytes 251912 | tf_op jit(solution)/shard_map/ppermute | solution.py:398
  36.0 1.3 %collective-permute-start.14 = (bf16[328,128]{1,0:T(8,128)(2,1)S(1)}, bf16[328,128]{1,0:T(8,128)(2,1)S(1)}, u32[]{:S(2)}, u32[]{:S(2)}) collective-permute-start(bf16[328,128]{1,0:T(8,128)(2,1)S(1)} %collective-permute-done.10.rest_11_), channel_id=1, source_target_pairs={{0,2},{2,0},{4,6},{6,4},{8,10},{10,8},{12,14},{14,12},{1,3},{3,1},... | collective-permute-start | bytes 251912 | tf_op jit(solution)/shard_map/ppermute | solution.py:398
  36.0 1.4 %collective-permute-start.20 = (bf16[320,128]{1,0:T(8,128)(2,1)S(1)}, bf16[320,128]{1,0:T(8,128)(2,1)S(1)}, u32[]{:S(2)}, u32[]{:S(2)}) collective-permute-start(bf16[320,128]{1,0:T(8,128)(2,1)S(1)} %collective-permute-done.16.rest_17_), channel_id=1, source_target_pairs={{0,2},{2,0},{4,6},{6,4},{8,10},{10,8},{12,14},{14,12},{1,3},{3,1},... | collective-permute-start | bytes 245768 | tf_op jit(solution)/shard_map/ppermute | solution.py:398
  36.5 1.3 %collective-permute-start.21 = (bf16[320,128]{1,0:T(8,128)(2,1)S(1)}, bf16[320,128]{1,0:T(8,128)(2,1)S(1)}, u32[]{:S(2)}, u32[]{:S(2)}) collective-permute-start(bf16[320,128]{1,0:T(8,128)(2,1)S(1)} %collective-permute-done.17.rest_18_), channel_id=1, source_target_pairs={{0,2},{2,0},{4,6},{6,4},{8,10},{10,8},{12,14},{14,12},{1,3},{3,1},... | collective-permute-start | bytes 245768 | tf_op jit(solution)/shard_map/ppermute | solution.py:398
  36.6 1.4 %collective-permute-start.22 = (bf16[320,128]{1,0:T(8,128)(2,1)S(1)}, bf16[320,128]{1,0:T(8,128)(2,1)S(1)}, u32[]{:S(2)}, u32[]{:S(2)}) collective-permute-start(bf16[320,128]{1,0:T(8,128)(2,1)S(1)} %collective-permute-done.18.rest_19_), channel_id=1, source_target_pairs={{0,2},{2,0},{4,6},{6,4},{8,10},{10,8},{12,14},{14,12},{1,3},{3,1},... | collective-permute-start | bytes 245768 | tf_op jit(solution)/shard_map/ppermute | solution.py:398
  43.3 4.5 %collective-permute-start.23 = (f32[4,8,128]{2,1,0:T(8,128)S(1)}, f32[4,8,128]{2,1,0:T(8,128)S(1)}, u32[]{:S(2)}, u32[]{:S(2)}) collective-permute-start(f32[4,8,128]{2,1,0:T(8,128)S(1)} %get-tuple-element.32), channel_id=1, source_target_pairs={{0,4},{2,6},{4,0},{6,2},{8,12},{10,14},{12,8},{14,10},{1,5},{3,7},... | collective-permute-start | bytes 49160 | tf_op jit(solution)/shard_map/ppermute | solution.py:428
  45.1 4.6 %collective-permute-start.24 = (f32[4,8,128]{2,1,0:T(8,128)S(1)}, f32[4,8,128]{2,1,0:T(8,128)S(1)}, u32[]{:S(2)}, u32[]{:S(2)}) collective-permute-start(f32[4,8,128]{2,1,0:T(8,128)S(1)} %get-tuple-element.33), channel_id=1, source_target_pairs={{0,8},{2,10},{4,12},{6,14},{8,0},{10,2},{12,4},{14,6},{1,9},{3,11}... | collective-permute-start | bytes 49160 | tf_op jit(solution)/shard_map/ppermute | solution.py:428
  46.6 5.5 %collective-permute-start.25 = (f32[4,8,128]{2,1,0:T(8,128)S(1)}, f32[4,8,128]{2,1,0:T(8,128)S(1)}, u32[]{:S(2)}, u32[]{:S(2)}) collective-permute-start(f32[4,8,128]{2,1,0:T(8,128)S(1)} %get-tuple-element.34), channel_id=1, source_target_pairs={{0,12},{2,14},{4,8},{6,10},{8,4},{10,6},{12,0},{14,2},{1,13},{3,15... | collective-permute-start | bytes 49160 | tf_op jit(solution)/shard_map/ppermute | solution.py:428
  52.7 1.3 %collective-permute-start.26 = (f32[4,4,512]{2,1,0:T(4,128)S(1)}, f32[4,4,512]{2,1,0:T(4,128)S(1)}, u32[]{:S(2)}, u32[]{:S(2)}) collective-permute-start(f32[4,4,512]{2,1,0:T(4,128)S(1)} %get-tuple-element.36), channel_id=1, source_target_pairs={{0,2},{2,0},{4,6},{6,4},{8,10},{10,8},{12,14},{14,12},{1,3},{3,1},... | collective-permute-start | bytes 98312 | tf_op jit(solution)/shard_map/ppermute | solution.py:445

commit v7 on v6

--- a/solution.py
+++ b/solution.py
@@ -14,6 +14,7 @@
 
 SMEM = pl.BlockSpec(memory_space=pltpu.SMEM)
 VMEM = pl.BlockSpec(memory_space=pltpu.VMEM)
+HBM = pl.BlockSpec(memory_space=pltpu.HBM)
 
 
 def partner(index, step, count):
@@ -90,13 +91,57 @@
     return packed
 
 
-def inner_kernel(radius, row_taps, col_taps, science, inv_var, maps, edges, colpass):
+def inner_kernel(
+    radius,
+    science_hbm,
+    inv_var_hbm,
+    row_taps_hbm,
+    col_taps_hbm,
+    row_shift_hbm,
+    col_shift_hbm,
+    usable_hbm,
+    maps,
+    edges,
+    params,
+    science,
+    inv_var,
+    row_taps,
+    col_taps,
+    row_shift,
+    col_shift,
+    usable,
+    colpass,
+    sems,
+):
     exposures, rows, columns = science.shape
     tiles = columns // LANES
     taps = 2 * radius + 1
+    vels = row_shift.shape[1]
     pad = SUBLANES
+    pairs = (
+        (row_taps_hbm, row_taps),
+        (col_taps_hbm, col_taps),
+        (science_hbm, science),
+        (inv_var_hbm, inv_var),
+        (row_shift_hbm, row_shift),
+        (col_shift_hbm, col_shift),
+        (usable_hbm, usable),
+    )
+    copies = [pltpu.make_async_copy(source, target, sems.at[i]) for i, (source, target) in enumerate(pairs)]
+    for copy in copies:
+        copy.start()
     colpass[:, :, 0:pad] = jnp.zeros((2, tiles, pad, LANES), jnp.float32)
     colpass[:, :, pad + rows : 2 * pad + rows] = jnp.zeros((2, tiles, pad, LANES), jnp.float32)
+    params[...] = jnp.zeros_like(params)
+    for copy in copies:
+        copy.wait()
+    row = lax.broadcasted_iota(jnp.int32, (exposures, 1), 0)
+    kept = jnp.zeros((exposures, 1), jnp.int32)
+    for e in range(exposures):
+        kept = jnp.where(row == e, usable[e], kept)
+    params[:, 0:vels] = row_shift[...].astype(jnp.float32)
+    params[:, vels : 2 * vels] = col_shift[...].astype(jnp.float32)
+    params[:, 2 * vels : 2 * vels + 1] = kept.astype(jnp.float32)
     parts = rows // SHIFT
 
     def one_exposure(e, carry):
@@ -125,24 +170,16 @@
 
 
 def outer_kernel(
-    radius, chunks, info, row_taps, col_taps, usable, row_shift, col_shift, maps, edges, above, below, *rest
+    radius, chunks, info, row_taps, col_taps, maps, edges, params, above, below, *rest
 ):
-    exposures, vels = row_shift.shape
+    exposures = params.shape[0]
     tiles = maps.shape[0]
     parts = edges.shape[1] // (exposures * SUBLANES)
-    sends, (pixels, colpass, more, more_edges, params) = rest[: chunks * parts], rest[chunks * parts :]
+    sends, (pixels, colpass, more, more_edges) = rest[: chunks * parts], rest[chunks * parts :]
     taps = 2 * radius + 1
     pad = SUBLANES
     has_above, has_below, own = info[0] > 0, info[1] > 0, info[2]
 
-    row = lax.broadcasted_iota(jnp.int32, (exposures, 1), 0)
-    kept = jnp.zeros((exposures, 1), jnp.int32)
-    for e in range(exposures):
-        kept = jnp.where(row == e, usable[e], kept)
-    params[...] = jnp.zeros_like(params)
-    params[:, 0:vels] = row_shift[...].astype(jnp.float32)
-    params[:, vels : 2 * vels] = col_shift[...].astype(jnp.float32)
-    params[:, 2 * vels : 2 * vels + 1] = kept.astype(jnp.float32)
     colpass[...] = jnp.zeros_like(colpass)
 
     def one_exposure(e, carry):
@@ -350,19 +387,30 @@
 
     map_rows = parts * exposures * 2 * SHIFT
     edge_rows = parts * exposures * SUBLANES
-    maps, edges = pl.pallas_call(
+    maps, edges, params = pl.pallas_call(
         functools.partial(inner_kernel, radius),
         out_shape=[
             jax.ShapeDtypeStruct((chunks, map_rows, LANES), jnp.float32),
             jax.ShapeDtypeStruct((chunks, edge_rows, LANES), jnp.float32),
+            jax.ShapeDtypeStruct((exposures, LANES), jnp.float32),
         ],
-        in_specs=[SMEM] * 2 + [VMEM] * 2,
-        out_specs=[VMEM] * 2,
-        scratch_shapes=[pltpu.VMEM((2, chunks, rows + 2 * SUBLANES, LANES), jnp.float32)],
+        in_specs=[HBM] * 7,
+        out_specs=[VMEM] * 3,
+        scratch_shapes=[
+            pltpu.VMEM(science.shape, science.dtype),
+            pltpu.VMEM(inv_var.shape, inv_var.dtype),
+            pltpu.SMEM(psf_rows.shape, jnp.float32),
+            pltpu.SMEM(psf_cols.shape, jnp.float32),
+            pltpu.VMEM(row_shift.shape, jnp.int32),
+            pltpu.VMEM(col_shift.shape, jnp.int32),
+            pltpu.SMEM(exposure_ok.shape, jnp.int32),
+            pltpu.VMEM((2, chunks, rows + 2 * SUBLANES, LANES), jnp.float32),
+            pltpu.SemaphoreType.DMA((7,)),
+        ],
         compiler_params=pltpu.CompilerParams(vmem_limit_bytes=8 << 20),
         cost_estimate=pl.CostEstimate(flops=100_000_000, bytes_accessed=4_000_000, transcendentals=0),
         name="filter_inner",
-    )(psf_rows, psf_cols, science, inv_var)
+    )(*[pltpu.with_memory_space_constraint(x, pltpu.HBM) for x in (science, inv_var, psf_rows, psf_cols, row_shift, col_shift, exposure_ok)])
     block = exposures * (2 * SHIFT + SUBLANES)
     sent = [
         jax.ShapeDtypeStruct((block + (exposures if p == parts - 1 else 0), LANES), jnp.bfloat16)
@@ -371,18 +419,17 @@
     sends = pl.pallas_call(
         functools.partial(outer_kernel, radius, chunks),
         out_shape=sent * chunks,
-        in_specs=[SMEM] * 4 + [VMEM] * 6,
+        in_specs=[SMEM] * 3 + [VMEM] * 5,
         out_specs=[VMEM] * (chunks * parts),
         scratch_shapes=[
             pltpu.VMEM((2, 2 * radius, columns), jnp.float32),
             pltpu.VMEM((2, chunks, 3 * SUBLANES, LANES), jnp.float32),
             pltpu.VMEM((2, chunks, 2 * exposures, SUBLANES, LANES), jnp.float32),
             pltpu.VMEM((2, chunks, exposures, SUBLANES, LANES), jnp.float32),
-            pltpu.VMEM((exposures, LANES), jnp.float32),
         ],
         compiler_params=pltpu.CompilerParams(vmem_limit_bytes=8 << 20),
         name="filter_outer",
-    )(info, psf_rows, psf_cols, exposure_ok, row_shift, col_shift, maps, edges, above, below)
+    )(info, psf_rows, psf_cols, maps, edges, params, above, below)
 
     blocks = [[[None] * chunks for _ in range(subs)] for _ in range(parts + 1)]
     up = [((i + 1) % strips, i) for i in range(strips)]

time: 55.3 us -> 54.1 us (0.978)
  local copies, waits for them, and re-layouts: 3.24 us -> 1.66 us
    unnamed x14 -> x4, local copies, waits for them, and re-layouts: 2.21 us -> 0.67 us
  transfers between devices with their start and end apart: 27 -> 27, of which waited for: 12 -> 12; matrix products, arithmetic and copies ran while one was open for 0% -> 0% of each run, Pallas kernels for 8% -> 9%
where the time goes in v7:
time: 54.1 us; the launch traced here: 53.9 us
  starting transfers between devices  24.6 us (45%)
  Pallas kernels  14 us (26%)
  waiting for transfers between devices  13.6 us (25%)
  local copies, waits for them, and re-layouts  1.66 us (3%)
    ppermute x6, starting transfers between devices, per_device(): lax.ppermute(sends[step * parts + p], 'expo', chunk_pairs(step, chunks, s...  11.5 us
    pallas_call x1, Pallas kernels, per_device(): pl.pallas_call(functools.partial(stack_kernel, groups, chunks, exposures,...  5.27 us
    pallas_call x1, Pallas kernels, per_device(): pl.pallas_call(functools.partial(inner_kernel, radius), out_shape=[jax.Sh...  4.65 us
    ppermute x3, starting transfers between devices, per_device(): lax.ppermute(pieces[step], 'expo', chunk_pairs(step, chunks, subs))  4.45 us
    ppermute x3, waiting for transfers between devices, per_device(): lax.ppermute(pieces[step], 'expo', chunk_pairs(step, chunks, subs))  4.36 us
    ppermute x4, waiting for transfers between devices, per_device(): blocks[parts][0][step] = lax.ppermute(blocks[0][0][step], 'strip', up)  3.75 us
    ppermute x6, waiting for transfers between devices, per_device(): lax.ppermute(sends[step * parts + p], 'expo', chunk_pairs(step, chunks, s...  3.34 us
    ppermute x4, starting transfers between devices, per_device(): blocks[parts][0][step] = lax.ppermute(blocks[0][0][step], 'strip', up)  3.26 us
  transfers between devices with their start and end apart: 27, of which 12 were waited for; matrix products, arithmetic and copies ran while one was open for 0% of the time, Pallas kernels for 9%

profile of v7, /device:TPU:0, one launch (start us, length us, event | category | flops | bytes accessed | tf_op | source)
XLA Modules:
  0.0 53.9 jit_solution(3317818864998004509)
XLA Ops:
  0.0 0.9 %dynamic-slice_bitcast_fusion = (bf16[1,8,4,512]{3,2,1,0:T(4,128)(2,1)S(1)}, bf16[1,8,4,512]{3,2,1,0:T(4,128)(2,1)S(1)}) fusion(bf16[8,32,512]{2,1,0:T(8,128)(2,1)} %inv_var_hbm.1, s32[]{:T(128)S(6)} %select_n.19, bf16[8,32,512]{2,1,0:T(8,128)(2,1)} %science_hbm.1), kind=kLoop, calls=%fused_computation.1 | loop fusion | bytes 131076 | tf_op jit(solution)/shard_map/stack | solution.py:379
  1.0 3.0 %collective-permute-start = (bf16[2,8,4,512]{3,2,1,0:T(4,128)(2,1)S(1)}, bf16[2,8,4,512]{3,2,1,0:T(4,128)(2,1)S(1)}, u32[]{:S(2)}, u32[]{:S(2)}) collective-permute-start(bf16[2,8,4,512]{3,2,1,0:T(4,128)(2,1)S(1)} %pad_maximum_fusion), channel_id=1, source_target_pairs={{0,1},{1,0},{2,3},{3,2},{4,5},{5,4},{6,7},{7,6},{8,9},{9,8},{10,11... | collective-permute-start | bytes 196616 | tf_op jit(solution)/shard_map/ppermute | solution.py:383
  4.0 0.1 stack.40.info
  4.1 4.7 %filter_inner.1 = (f32[4,512,128]{2,1,0:T(8,128)S(1)}, f32[4,128,128]{2,1,0:T(8,128)S(1)}, f32[8,128]{1,0:T(8,128)S(1)}) custom-call(bf16[8,32,512]{2,1,0:T(8,128)(2,1)} %science_hbm.1, bf16[8,32,512]{2,1,0:T(8,128)(2,1)} %inv_var_hbm.1, f32[8,9]{1,0:T(8,128)} %row_taps.1, f32[8,9]{1,0:T(8,128)} %col_taps.1, s32[8,8]{1,0:T(8,128)} %row_shift_hbm.1, ...), custom_call_target="tpu_custom_call" | custom-call | flops 100000000 | bytes 4000000 | tf_op jit(solution)/shard_map/filter_inner/pallas_call | solution.py:390
  8.7 0.0 copy-start
  8.8 0.7 %copy-done = f32[8,9]{1,0:T(8,128)S(1)} copy-done((f32[8,9]{1,0:T(8,128)S(1)}, f32[8,9]{1,0:T(8,128)}, u32[]{:S(2)}) %copy-start) | copy-done | bytes 312
  9.4 2.3 %filter_outer.1 = (bf16[320,128]{1,0:T(8,128)(2,1)S(1)}, bf16[328,128]{1,0:T(8,128)(2,1)S(1)}, bf16[320,128]{1,0:T(8,128)(2,1)S(1)}, bf16[328,128]{1,0:T(8,128)(...) custom-call(s32[5]{0:T(128)S(1)} %stack.40.info, ...), custom_call_target="tpu_custom_call" | custom-call | tf_op jit(solution)/shard_map/filter_outer/pallas_call | solution.py:419
  11.7 1.6 %collective-permute-start.1 = (bf16[320,128]{1,0:T(8,128)(2,1)S(1)}, bf16[320,128]{1,0:T(8,128)(2,1)S(1)}, u32[]{:S(2)}, u32[]{:S(2)}) collective-permute-start(bf16[320,128]{1,0:T(8,128)(2,1)S(1)} %get-tuple-element.26), channel_id=1, source_target_pairs={{0,4},{2,6},{4,0},{6,2},{8,12},{10,14},{12,8},{14,10},{1,5},{3,7},... | collective-permute-start | bytes 245768 | tf_op jit(solution)/shard_map/ppermute | solution.py:440
  13.4 2.6 %collective-permute-start.2 = (bf16[320,128]{1,0:T(8,128)(2,1)S(1)}, bf16[320,128]{1,0:T(8,128)(2,1)S(1)}, u32[]{:S(2)}, u32[]{:S(2)}) collective-permute-start(bf16[320,128]{1,0:T(8,128)(2,1)S(1)} %get-tuple-element.27), channel_id=1, source_target_pairs={{0,8},{2,10},{4,12},{6,14},{8,0},{10,2},{12,4},{14,6},{1,9},{3,11}... | collective-permute-start | bytes 245768 | tf_op jit(solution)/shard_map/ppermute | solution.py:440
  16.0 0.2 collective-permute-start.3
  16.2 0.3 collective-permute-start.15
  16.5 0.9 %collective-permute-start.8 = (bf16[328,128]{1,0:T(8,128)(2,1)S(1)}, bf16[328,128]{1,0:T(8,128)(2,1)S(1)}, u32[]{:S(2)}, u32[]{:S(2)}) collective-permute-start(bf16[328,128]{1,0:T(8,128)(2,1)S(1)} %get-tuple-element.30), channel_id=1, source_target_pairs={{0,4},{2,6},{4,0},{6,2},{8,12},{10,14},{12,8},{14,10},{1,5},{3,7},... | collective-permute-start | bytes 251912 | tf_op jit(solution)/shard_map/ppermute | solution.py:440
  17.4 3.5 %collective-permute-start.9 = (bf16[328,128]{1,0:T(8,128)(2,1)S(1)}, bf16[328,128]{1,0:T(8,128)(2,1)S(1)}, u32[]{:S(2)}, u32[]{:S(2)}) collective-permute-start(bf16[328,128]{1,0:T(8,128)(2,1)S(1)} %get-tuple-element.31), channel_id=1, source_target_pairs={{0,8},{2,10},{4,12},{6,14},{8,0},{10,2},{12,4},{14,6},{1,9},{3,11}... | collective-permute-start | bytes 251912 | tf_op jit(solution)/shard_map/ppermute | solution.py:440
  20.9 2.3 %collective-permute-done.2.rest_2_ = bf16[320,128]{1,0:T(8,128)(2,1)S(1)} collective-permute-done((bf16[320,128]{1,0:T(8,128)(2,1)S(1)}, bf16[320,128]{1,0:T(8,128)(2,1)S(1)}, u32[]{:S(2)}, u32[]{:S(2)}) %collective-permute-start.2) | collective-permute-done | bytes 81952 | tf_op jit(solution)/shard_map/ppermute | solution.py:440
  23.2 0.0 collective-permute-start.4
  23.2 0.0 collective-permute-done.3.rest_3_
  23.2 2.7 %collective-permute-start.10 = (bf16[328,128]{1,0:T(8,128)(2,1)S(1)}, bf16[328,128]{1,0:T(8,128)(2,1)S(1)}, u32[]{:S(2)}, u32[]{:S(2)}) collective-permute-start(bf16[328,128]{1,0:T(8,128)(2,1)S(1)} %get-tuple-element.32), channel_id=1, source_target_pairs={{0,12},{2,14},{4,8},{6,10},{8,4},{10,6},{12,0},{14,2},{1,13},{3,15... | collective-permute-start | bytes 251912 | tf_op jit(solution)/shard_map/ppermute | solution.py:440
  25.9 0.2 collective-permute-start.11
  26.1 0.5 collective-permute-start.16
  26.7 0.0 collective-permute-done.8.rest_9_
  26.7 0.0 collective-permute-start.5
  26.7 1.0 %collective-permute-done.9.rest_10_ = bf16[328,128]{1,0:T(8,128)(2,1)S(1)} collective-permute-done((bf16[328,128]{1,0:T(8,128)(2,1)S(1)}, bf16[328,128]{1,0:T(8,128)(2,1)S(1)}, u32[]{:S(2)}, u32[]{:S(2)}) %collective-permute-start.9) | collective-permute-done | bytes 84000 | tf_op jit(solution)/shard_map/ppermute | solution.py:440
  27.7 2.3 %collective-permute-start.17 = (bf16[320,128]{1,0:T(8,128)(2,1)S(1)}, bf16[320,128]{1,0:T(8,128)(2,1)S(1)}, u32[]{:S(2)}, u32[]{:S(2)}) collective-permute-start(bf16[320,128]{1,0:T(8,128)(2,1)S(1)} %collective-permute-done.2.rest_2_), channel_id=1, source_target_pairs={{1,0},{0,1},{3,2},{2,3},{5,4},{4,5},{7,6},{6,7},{9,8},{8,9},{11,10... | collective-permute-start | bytes 245768 | tf_op jit(solution)/shard_map/ppermute | solution.py:441
  30.0 0.0 collective-permute-done.10.rest_11_
  30.0 0.0 collective-permute-start.6
  30.0 0.1 collective-permute-start.18
  30.1 1.4 %collective-permute-done.16.rest_17_ = bf16[320,128]{1,0:T(8,128)(2,1)S(1)} collective-permute-done((bf16[320,128]{1,0:T(8,128)(2,1)S(1)}, bf16[320,128]{1,0:T(8,128)(2,1)S(1)}, u32[]{:S(2)}, u32[]{:S(2)}) %collective-permute-start.16) | collective-permute-done | bytes 81952 | tf_op jit(solution)/shard_map/ppermute | solution.py:441
  31.4 0.5 collective-permute-start.7
  32.0 0.7 %collective-permute-done.17.rest_18_ = bf16[320,128]{1,0:T(8,128)(2,1)S(1)} collective-permute-done((bf16[320,128]{1,0:T(8,128)(2,1)S(1)}, bf16[320,128]{1,0:T(8,128)(2,1)S(1)}, u32[]{:S(2)}, u32[]{:S(2)}) %collective-permute-start.17) | collective-permute-done | bytes 81952 | tf_op jit(solution)/shard_map/ppermute | solution.py:441
  32.7 0.5 collective-permute-start.13
  33.2 1.7 %collective-permute-done.18.rest_19_ = bf16[320,128]{1,0:T(8,128)(2,1)S(1)} collective-permute-done((bf16[320,128]{1,0:T(8,128)(2,1)S(1)}, bf16[320,128]{1,0:T(8,128)(2,1)S(1)}, u32[]{:S(2)}, u32[]{:S(2)}) %collective-permute-start.18) | collective-permute-done | bytes 81952 | tf_op jit(solution)/shard_map/ppermute | solution.py:441
  34.9 0.5 collective-permute-start.20
  35.4 0.1 collective-permute-start.21
  35.4 0.4 collective-permute-start.22
  35.9 0.2 collective-permute-done.14.rest_15_
  36.1 0.2 collective-permute-done.20.rest_21_
  36.3 0.4 collective-permute-done.21.rest_22_
  36.7 0.2 collective-permute-done.22.rest_23_
  36.8 5.3 %stack_twice.1 = (f32[4,8,128]{2,1,0:T(8,128)S(1)}, f32[4,8,128]{2,1,0:T(8,128)S(1)}, f32[4,8,128]{2,1,0:T(8,128)S(1)}, f32[4,8,128]{2,1,0:T(8,128)S(1)}) custom-call(s32[5]{0:T(128)S(1)} %stack.40.info, bf16[320,128]{1,0:T(8,128)(2,1)S(1)} %get-tuple-element.25.rest_0_, bf16[320,128]{1,0:T(8,128)(2,1)S(1)} %collective-permute-done.1.rest_1_, ...), custom_call_target="tpu_custom_call" | custom-call | tf_op jit(solution)/shard_map/stack_twice/pallas_call | solution.py:453
  42.1 1.8 %collective-permute-start.23 = (f32[4,8,128]{2,1,0:T(8,128)S(1)}, f32[4,8,128]{2,1,0:T(8,128)S(1)}, u32[]{:S(2)}, u32[]{:S(2)}) collective-permute-start(f32[4,8,128]{2,1,0:T(8,128)S(1)} %get-tuple-element.34), channel_id=1, source_target_pairs={{0,4},{2,6},{4,0},{6,2},{8,12},{10,14},{12,8},{14,10},{1,5},{3,7},... | collective-permute-start | bytes 49160 | tf_op jit(solution)/shard_map/ppermute | solution.py:475
  43.9 1.5 %collective-permute-start.24 = (f32[4,8,128]{2,1,0:T(8,128)S(1)}, f32[4,8,128]{2,1,0:T(8,128)S(1)}, u32[]{:S(2)}, u32[]{:S(2)}) collective-permute-start(f32[4,8,128]{2,1,0:T(8,128)S(1)} %get-tuple-element.35), channel_id=1, source_target_pairs={{0,8},{2,10},{4,12},{6,14},{8,0},{10,2},{12,4},{14,6},{1,9},{3,11}... | collective-permute-start | bytes 49160 | tf_op jit(solution)/shard_map/ppermute | solution.py:475
  45.4 1.2 %collective-permute-start.25 = (f32[4,8,128]{2,1,0:T(8,128)S(1)}, f32[4,8,128]{2,1,0:T(8,128)S(1)}, u32[]{:S(2)}, u32[]{:S(2)}) collective-permute-start(f32[4,8,128]{2,1,0:T(8,128)S(1)} %get-tuple-element.36), channel_id=1, source_target_pairs={{0,12},{2,14},{4,8},{6,10},{8,4},{10,6},{12,0},{14,2},{1,13},{3,15... | collective-permute-start | bytes 49160 | tf_op jit(solution)/shard_map/ppermute | solution.py:475
  46.5 2.0 %collective-permute-done.24.rest_2_ = f32[4,8,128]{2,1,0:T(8,128)S(1)} collective-permute-done((f32[4,8,128]{2,1,0:T(8,128)S(1)}, f32[4,8,128]{2,1,0:T(8,128)S(1)}, u32[]{:S(2)}, u32[]{:S(2)}) %collective-permute-start.24) | collective-permute-done | bytes 16416 | tf_op jit(solution)/shard_map/ppermute | solution.py:475
  48.5 2.4 %collective-permute-done.25.rest_3_ = f32[4,8,128]{2,1,0:T(8,128)S(1)} collective-permute-done((f32[4,8,128]{2,1,0:T(8,128)S(1)}, f32[4,8,128]{2,1,0:T(8,128)S(1)}, u32[]{:S(2)}, u32[]{:S(2)}) %collective-permute-start.25) | collective-permute-done | bytes 16416 | tf_op jit(solution)/shard_map/ppermute | solution.py:475
  50.9 0.6 %join_columns.1 = (f32[4,4,512]{2,1,0:T(4,128)S(1)}, f32[4,4,512]{2,1,0:T(4,128)S(1)}) custom-call(s32[5]{0:T(128)S(1)} %stack.40.info, f32[4,8,128]{2,1,0:T(8,128)S(1)} %get-tuple-element.33.rest_0_, f32[4,8,128]{2,1,0:T(8,128)S(1)} %collective-permute-done.23.rest_1_, f32[4,8,128]{2,1,0:T(8,128)S(1)} %collective-permute-done.24.rest_2_, ...), custom_call_target="tpu_custom_call" | custom-call | tf_op jit(solution)/shard_map/join_columns/pallas_call | solution.py:478
  51.5 0.1 collective-permute-start.26
  51.6 1.2 %collective-permute-done.26.rest_1_ = f32[4,4,512]{2,1,0:T(4,128)S(1)} collective-permute-done((f32[4,4,512]{2,1,0:T(4,128)S(1)}, f32[4,4,512]{2,1,0:T(4,128)S(1)}, u32[]{:S(2)}, u32[]{:S(2)}) %collective-permute-start.26) | collective-permute-done | bytes 32800 | tf_op jit(solution)/shard_map/ppermute | solution.py:492
  52.8 1.2 %join_velocities.1 = f32[8,4,512]{2,1,0:T(4,128)} custom-call(s32[5]{0:T(128)S(1)} %stack.40.info, f32[4,4,512]{2,1,0:T(4,128)S(1)} %get-tuple-element.37.rest_0_, f32[4,4,512]{2,1,0:T(4,128)S(1)} %collective-permute-done.26.rest_1_), custom_call_target="tpu_custom_call" | custom-call | tf_op jit(solution)/shard_map/join_velocities/pallas_call | solution.py:493
  (18 shorter events, 0.1 us)
Async XLA Ops:
  1.0 7.8 %collective-permute-start = (bf16[2,8,4,512]{3,2,1,0:T(4,128)(2,1)S(1)}, bf16[2,8,4,512]{3,2,1,0:T(4,128)(2,1)S(1)}, u32[]{:S(2)}, u32[]{:S(2)}) collective-permute-start(bf16[2,8,4,512]{3,2,1,0:T(4,128)(2,1)S(1)} %pad_maximum_fusion), channel_id=1, source_target_pairs={{0,1},{1,0},{2,3},{3,2},{4,5},{5,4},{6,7},{7,6},{8,9},{9,8},{10,11... | collective-permute-start | bytes 196616 | tf_op jit(solution)/shard_map/ppermute | solution.py:383
  4.1 4.7 %copy-start.1 = (f32[8,9]{1,0:T(8,128)S(1)}, f32[8,9]{1,0:T(8,128)}, u32[]{:S(2)}) copy-start(f32[8,9]{1,0:T(8,128)} %col_taps.1) | copy-start | bytes 868
  8.7 0.7 %copy-start = (f32[8,9]{1,0:T(8,128)S(1)}, f32[8,9]{1,0:T(8,128)}, u32[]{:S(2)}) copy-start(f32[8,9]{1,0:T(8,128)} %row_taps.1) | copy-start | bytes 868
  11.7 5.7 %collective-permute-start.1 = (bf16[320,128]{1,0:T(8,128)(2,1)S(1)}, bf16[320,128]{1,0:T(8,128)(2,1)S(1)}, u32[]{:S(2)}, u32[]{:S(2)}) collective-permute-start(bf16[320,128]{1,0:T(8,128)(2,1)S(1)} %get-tuple-element.26), channel_id=1, source_target_pairs={{0,4},{2,6},{4,0},{6,2},{8,12},{10,14},{12,8},{14,10},{1,5},{3,7},... | collective-permute-start | bytes 245768 | tf_op jit(solution)/shard_map/ppermute | solution.py:440
  13.4 9.9 %collective-permute-start.2 = (bf16[320,128]{1,0:T(8,128)(2,1)S(1)}, bf16[320,128]{1,0:T(8,128)(2,1)S(1)}, u32[]{:S(2)}, u32[]{:S(2)}) collective-permute-start(bf16[320,128]{1,0:T(8,128)(2,1)S(1)} %get-tuple-element.27), channel_id=1, source_target_pairs={{0,8},{2,10},{4,12},{6,14},{8,0},{10,2},{12,4},{14,6},{1,9},{3,11}... | collective-permute-start | bytes 245768 | tf_op jit(solution)/shard_map/ppermute | solution.py:440
  16.0 7.3 %collective-permute-start.3 = (bf16[320,128]{1,0:T(8,128)(2,1)S(1)}, bf16[320,128]{1,0:T(8,128)(2,1)S(1)}, u32[]{:S(2)}, u32[]{:S(2)}) collective-permute-start(bf16[320,128]{1,0:T(8,128)(2,1)S(1)} %get-tuple-element.28), channel_id=1, source_target_pairs={{0,12},{2,14},{4,8},{6,10},{8,4},{10,6},{12,0},{14,2},{1,13},{3,15... | collective-permute-start | bytes 245768 | tf_op jit(solution)/shard_map/ppermute | solution.py:440
  16.2 9.7 %collective-permute-start.15 = (bf16[320,128]{1,0:T(8,128)(2,1)S(1)}, bf16[320,128]{1,0:T(8,128)(2,1)S(1)}, u32[]{:S(2)}, u32[]{:S(2)}) collective-permute-start(bf16[320,128]{1,0:T(8,128)(2,1)S(1)} %get-tuple-element.25.rest_0_), channel_id=1, source_target_pairs={{1,0},{0,1},{3,2},{2,3},{5,4},{4,5},{7,6},{6,7},{9,8},{8,9},{11,10... | collective-permute-start | bytes 245768 | tf_op jit(solution)/shard_map/ppermute | solution.py:441
  16.5 10.2 %collective-permute-start.8 = (bf16[328,128]{1,0:T(8,128)(2,1)S(1)}, bf16[328,128]{1,0:T(8,128)(2,1)S(1)}, u32[]{:S(2)}, u32[]{:S(2)}) collective-permute-start(bf16[328,128]{1,0:T(8,128)(2,1)S(1)} %get-tuple-element.30), channel_id=1, source_target_pairs={{0,4},{2,6},{4,0},{6,2},{8,12},{10,14},{12,8},{14,10},{1,5},{3,7},... | collective-permute-start | bytes 251912 | tf_op jit(solution)/shard_map/ppermute | solution.py:440
  17.4 10.3 %collective-permute-start.9 = (bf16[328,128]{1,0:T(8,128)(2,1)S(1)}, bf16[328,128]{1,0:T(8,128)(2,1)S(1)}, u32[]{:S(2)}, u32[]{:S(2)}) collective-permute-start(bf16[328,128]{1,0:T(8,128)(2,1)S(1)} %get-tuple-element.31), channel_id=1, source_target_pairs={{0,8},{2,10},{4,12},{6,14},{8,0},{10,2},{12,4},{14,6},{1,9},{3,11}... | collective-permute-start | bytes 251912 | tf_op jit(solution)/shard_map/ppermute | solution.py:440
  23.2 2.9 %collective-permute-start.4 = (bf16[320,128]{1,0:T(8,128)(2,1)S(1)}, bf16[320,128]{1,0:T(8,128)(2,1)S(1)}, u32[]{:S(2)}, u32[]{:S(2)}) collective-permute-start(bf16[320,128]{1,0:T(8,128)(2,1)S(1)} %get-tuple-element.25.rest_0_), channel_id=1, source_target_pairs={{0,2},{2,0},{4,6},{6,4},{8,10},{10,8},{12,14},{14,12},{1,3},{3,1},... | collective-permute-start | bytes 245768 | tf_op jit(solution)/shard_map/ppermute | solution.py:445
  23.2 6.8 %collective-permute-start.10 = (bf16[328,128]{1,0:T(8,128)(2,1)S(1)}, bf16[328,128]{1,0:T(8,128)(2,1)S(1)}, u32[]{:S(2)}, u32[]{:S(2)}) collective-permute-start(bf16[328,128]{1,0:T(8,128)(2,1)S(1)} %get-tuple-element.32), channel_id=1, source_target_pairs={{0,12},{2,14},{4,8},{6,10},{8,4},{10,6},{12,0},{14,2},{1,13},{3,15... | collective-permute-start | bytes 251912 | tf_op jit(solution)/shard_map/ppermute | solution.py:440
  25.9 4.1 %collective-permute-start.11 = (bf16[328,128]{1,0:T(8,128)(2,1)S(1)}, bf16[328,128]{1,0:T(8,128)(2,1)S(1)}, u32[]{:S(2)}, u32[]{:S(2)}) collective-permute-start(bf16[328,128]{1,0:T(8,128)(2,1)S(1)} %get-tuple-element.29.rest_8_), channel_id=1, source_target_pairs={{0,2},{2,0},{4,6},{6,4},{8,10},{10,8},{12,14},{14,12},{1,3},{3,1},... | collective-permute-start | bytes 251912 | tf_op jit(solution)/shard_map/ppermute | solution.py:445
  26.1 5.3 %collective-permute-start.16 = (bf16[320,128]{1,0:T(8,128)(2,1)S(1)}, bf16[320,128]{1,0:T(8,128)(2,1)S(1)}, u32[]{:S(2)}, u32[]{:S(2)}) collective-permute-start(bf16[320,128]{1,0:T(8,128)(2,1)S(1)} %collective-permute-done.1.rest_1_), channel_id=1, source_target_pairs={{1,0},{0,1},{3,2},{2,3},{5,4},{4,5},{7,6},{6,7},{9,8},{8,9},{11,10... | collective-permute-start | bytes 245768 | tf_op jit(solution)/shard_map/ppermute | solution.py:441
  26.7 4.8 %collective-permute-start.5 = (bf16[320,128]{1,0:T(8,128)(2,1)S(1)}, bf16[320,128]{1,0:T(8,128)(2,1)S(1)}, u32[]{:S(2)}, u32[]{:S(2)}) collective-permute-start(bf16[320,128]{1,0:T(8,128)(2,1)S(1)} %collective-permute-done.1.rest_1_), channel_id=1, source_target_pairs={{0,2},{2,0},{4,6},{6,4},{8,10},{10,8},{12,14},{14,12},{1,3},{3,1},... | collective-permute-start | bytes 245768 | tf_op jit(solution)/shard_map/ppermute | solution.py:445
  27.7 5.0 %collective-permute-start.17 = (bf16[320,128]{1,0:T(8,128)(2,1)S(1)}, bf16[320,128]{1,0:T(8,128)(2,1)S(1)}, u32[]{:S(2)}, u32[]{:S(2)}) collective-permute-start(bf16[320,128]{1,0:T(8,128)(2,1)S(1)} %collective-permute-done.2.rest_2_), channel_id=1, source_target_pairs={{1,0},{0,1},{3,2},{2,3},{5,4},{4,5},{7,6},{6,7},{9,8},{8,9},{11,10... | collective-permute-start | bytes 245768 | tf_op jit(solution)/shard_map/ppermute | solution.py:441
  30.0 2.7 %collective-permute-start.6 = (bf16[320,128]{1,0:T(8,128)(2,1)S(1)}, bf16[320,128]{1,0:T(8,128)(2,1)S(1)}, u32[]{:S(2)}, u32[]{:S(2)}) collective-permute-start(bf16[320,128]{1,0:T(8,128)(2,1)S(1)} %collective-permute-done.2.rest_2_), channel_id=1, source_target_pairs={{0,2},{2,0},{4,6},{6,4},{8,10},{10,8},{12,14},{14,12},{1,3},{3,1},... | collective-permute-start | bytes 245768 | tf_op jit(solution)/shard_map/ppermute | solution.py:445
  30.0 4.9 %collective-permute-start.18 = (bf16[320,128]{1,0:T(8,128)(2,1)S(1)}, bf16[320,128]{1,0:T(8,128)(2,1)S(1)}, u32[]{:S(2)}, u32[]{:S(2)}) collective-permute-start(bf16[320,128]{1,0:T(8,128)(2,1)S(1)} %collective-permute-done.3.rest_3_), channel_id=1, source_target_pairs={{1,0},{0,1},{3,2},{2,3},{5,4},{4,5},{7,6},{6,7},{9,8},{8,9},{11,10... | collective-permute-start | bytes 245768 | tf_op jit(solution)/shard_map/ppermute | solution.py:441
  31.4 4.0 %collective-permute-start.12 = (bf16[328,128]{1,0:T(8,128)(2,1)S(1)}, bf16[328,128]{1,0:T(8,128)(2,1)S(1)}, u32[]{:S(2)}, u32[]{:S(2)}) collective-permute-start(bf16[328,128]{1,0:T(8,128)(2,1)S(1)} %collective-permute-done.8.rest_9_), channel_id=1, source_target_pairs={{0,2},{2,0},{4,6},{6,4},{8,10},{10,8},{12,14},{14,12},{1,3},{3,1},... | collective-permute-start | bytes 251912 | tf_op jit(solution)/shard_map/ppermute | solution.py:445
  31.4 3.4 %collective-permute-start.7 = (bf16[320,128]{1,0:T(8,128)(2,1)S(1)}, bf16[320,128]{1,0:T(8,128)(2,1)S(1)}, u32[]{:S(2)}, u32[]{:S(2)}) collective-permute-start(bf16[320,128]{1,0:T(8,128)(2,1)S(1)} %collective-permute-done.3.rest_3_), channel_id=1, source_target_pairs={{0,2},{2,0},{4,6},{6,4},{8,10},{10,8},{12,14},{14,12},{1,3},{3,1},... | collective-permute-start | bytes 245768 | tf_op jit(solution)/shard_map/ppermute | solution.py:445
  32.7 2.7 %collective-permute-start.19 = (bf16[320,128]{1,0:T(8,128)(2,1)S(1)}, bf16[320,128]{1,0:T(8,128)(2,1)S(1)}, u32[]{:S(2)}, u32[]{:S(2)}) collective-permute-start(bf16[320,128]{1,0:T(8,128)(2,1)S(1)} %collective-permute-done.15.rest_16_), channel_id=1, source_target_pairs={{0,2},{2,0},{4,6},{6,4},{8,10},{10,8},{12,14},{14,12},{1,3},{3,1},... | collective-permute-start | bytes 245768 | tf_op jit(solution)/shard_map/ppermute | solution.py:445
  32.7 3.2 %collective-permute-start.13 = (bf16[328,128]{1,0:T(8,128)(2,1)S(1)}, bf16[328,128]{1,0:T(8,128)(2,1)S(1)}, u32[]{:S(2)}, u32[]{:S(2)}) collective-permute-start(bf16[328,128]{1,0:T(8,128)(2,1)S(1)} %collective-permute-done.9.rest_10_), channel_id=1, source_target_pairs={{0,2},{2,0},{4,6},{6,4},{8,10},{10,8},{12,14},{14,12},{1,3},{3,1},... | collective-permute-start | bytes 251912 | tf_op jit(solution)/shard_map/ppermute | solution.py:445
  34.9 1.3 %collective-permute-start.14 = (bf16[328,128]{1,0:T(8,128)(2,1)S(1)}, bf16[328,128]{1,0:T(8,128)(2,1)S(1)}, u32[]{:S(2)}, u32[]{:S(2)}) collective-permute-start(bf16[328,128]{1,0:T(8,128)(2,1)S(1)} %collective-permute-done.10.rest_11_), channel_id=1, source_target_pairs={{0,2},{2,0},{4,6},{6,4},{8,10},{10,8},{12,14},{14,12},{1,3},{3,1},... | collective-permute-start | bytes 251912 | tf_op jit(solution)/shard_map/ppermute | solution.py:445
  34.9 1.4 %collective-permute-start.20 = (bf16[320,128]{1,0:T(8,128)(2,1)S(1)}, bf16[320,128]{1,0:T(8,128)(2,1)S(1)}, u32[]{:S(2)}, u32[]{:S(2)}) collective-permute-start(bf16[320,128]{1,0:T(8,128)(2,1)S(1)} %collective-permute-done.16.rest_17_), channel_id=1, source_target_pairs={{0,2},{2,0},{4,6},{6,4},{8,10},{10,8},{12,14},{14,12},{1,3},{3,1},... | collective-permute-start | bytes 245768 | tf_op jit(solution)/shard_map/ppermute | solution.py:445
  35.4 1.3 %collective-permute-start.21 = (bf16[320,128]{1,0:T(8,128)(2,1)S(1)}, bf16[320,128]{1,0:T(8,128)(2,1)S(1)}, u32[]{:S(2)}, u32[]{:S(2)}) collective-permute-start(bf16[320,128]{1,0:T(8,128)(2,1)S(1)} %collective-permute-done.17.rest_18_), channel_id=1, source_target_pairs={{0,2},{2,0},{4,6},{6,4},{8,10},{10,8},{12,14},{14,12},{1,3},{3,1},... | collective-permute-start | bytes 245768 | tf_op jit(solution)/shard_map/ppermute | solution.py:445
  35.4 1.4 %collective-permute-start.22 = (bf16[320,128]{1,0:T(8,128)(2,1)S(1)}, bf16[320,128]{1,0:T(8,128)(2,1)S(1)}, u32[]{:S(2)}, u32[]{:S(2)}) collective-permute-start(bf16[320,128]{1,0:T(8,128)(2,1)S(1)} %collective-permute-done.18.rest_19_), channel_id=1, source_target_pairs={{0,2},{2,0},{4,6},{6,4},{8,10},{10,8},{12,14},{14,12},{1,3},{3,1},... | collective-permute-start | bytes 245768 | tf_op jit(solution)/shard_map/ppermute | solution.py:445
  42.1 4.5 %collective-permute-start.23 = (f32[4,8,128]{2,1,0:T(8,128)S(1)}, f32[4,8,128]{2,1,0:T(8,128)S(1)}, u32[]{:S(2)}, u32[]{:S(2)}) collective-permute-start(f32[4,8,128]{2,1,0:T(8,128)S(1)} %get-tuple-element.34), channel_id=1, source_target_pairs={{0,4},{2,6},{4,0},{6,2},{8,12},{10,14},{12,8},{14,10},{1,5},{3,7},... | collective-permute-start | bytes 49160 | tf_op jit(solution)/shard_map/ppermute | solution.py:475
  43.9 4.6 %collective-permute-start.24 = (f32[4,8,128]{2,1,0:T(8,128)S(1)}, f32[4,8,128]{2,1,0:T(8,128)S(1)}, u32[]{:S(2)}, u32[]{:S(2)}) collective-permute-start(f32[4,8,128]{2,1,0:T(8,128)S(1)} %get-tuple-element.35), channel_id=1, source_target_pairs={{0,8},{2,10},{4,12},{6,14},{8,0},{10,2},{12,4},{14,6},{1,9},{3,11}... | collective-permute-start | bytes 49160 | tf_op jit(solution)/shard_map/ppermute | solution.py:475
  45.4 5.5 %collective-permute-start.25 = (f32[4,8,128]{2,1,0:T(8,128)S(1)}, f32[4,8,128]{2,1,0:T(8,128)S(1)}, u32[]{:S(2)}, u32[]{:S(2)}) collective-permute-start(f32[4,8,128]{2,1,0:T(8,128)S(1)} %get-tuple-element.36), channel_id=1, source_target_pairs={{0,12},{2,14},{4,8},{6,10},{8,4},{10,6},{12,0},{14,2},{1,13},{3,15... | collective-permute-start | bytes 49160 | tf_op jit(solution)/shard_map/ppermute | solution.py:475
  51.5 1.3 %collective-permute-start.26 = (f32[4,4,512]{2,1,0:T(4,128)S(1)}, f32[4,4,512]{2,1,0:T(4,128)S(1)}, u32[]{:S(2)}, u32[]{:S(2)}) collective-permute-start(f32[4,4,512]{2,1,0:T(4,128)S(1)} %get-tuple-element.38), channel_id=1, source_target_pairs={{0,2},{2,0},{4,6},{6,4},{8,10},{10,8},{12,14},{14,12},{1,3},{3,1},... | collective-permute-start | bytes 98312 | tf_op jit(solution)/shard_map/ppermute | solution.py:492

commit v8 on v7

--- a/solution.py
+++ b/solution.py
@@ -35,16 +35,34 @@
     ]
 
 
-def column_pass(picture, col_taps, e, square):
+def split_rows(subs, parts):
+    return subs == 2 and parts == 2
+
+
+def strip_pairs(strips, chunks):
+    same, cross = [], []
+    for x in range(strips):
+        after = (x + 1) % strips
+        for j in range(chunks):
+            first, second = 2 * j * strips, (2 * j + 1) * strips
+            same += [(first + x, first + x), (second + after, second + x)]
+            cross += [(second + x, first + x), (first + after, second + x)]
+    return same, cross
+
+
+def row_pairs(step, chunks):
+    return [(2 * j + h, chunks * h + partner(j, step, chunks)) for j in range(chunks) for h in (0, 1)]
+
+
+def column_pass(picture, col_tap, taps, e, square):
     tiles = picture.shape[1] // LANES
-    taps = col_taps.shape[1]
     lane = lax.broadcasted_iota(jnp.int32, (SUBLANES, LANES), 1)
     zero = jnp.zeros((SUBLANES, LANES), jnp.float32)
     cut = [picture[:, t * LANES : (t + 1) * LANES] for t in range(tiles)]
     totals = None
     for b in range(taps):
         step = b - taps // 2
-        tap = col_taps[e, b]
+        tap = col_tap(e, b)
         if square:
             tap = tap * tap
         moved = cut
@@ -61,7 +79,7 @@
     return totals
 
 
-def row_pass(colpass, row_taps, e, m, first, taps):
+def row_pass(colpass, row_tap, e, m, first, taps):
     tiles = colpass.shape[1]
     lane = lax.broadcasted_iota(jnp.int32, (SUBLANES, LANES), 1)
     zero = jnp.zeros((SUBLANES, LANES), jnp.float32)
@@ -69,7 +87,7 @@
     for t in range(tiles):
         total = None
         for a in taps:
-            tap = row_taps[e, a]
+            tap = row_tap(e, a)
             if m == 1:
                 tap = tap * tap
             term = tap * colpass[m, t, pl.ds(first + a, SUBLANES)]
@@ -103,6 +121,7 @@
     maps,
     edges,
     params,
+    tap_rows,
     science,
     inv_var,
     row_taps,
@@ -144,17 +163,26 @@
     params[:, 2 * vels : 2 * vels + 1] = kept.astype(jnp.float32)
     parts = rows // SHIFT
 
+    def row_tap(e, a):
+        return row_taps[e, a]
+
+    def col_tap(e, b):
+        return col_taps[e, b]
+
     def one_exposure(e, carry):
+        for a in range(taps):
+            tap_rows[e, a : a + 1] = jnp.full((1, LANES), row_taps[e, a])
+            tap_rows[e, taps + a : taps + a + 1] = jnp.full((1, LANES), col_taps[e, a])
         inverse_all = inv_var[e].astype(jnp.float32)
         product_all = science[e].astype(jnp.float32) * inverse_all
         for g in range(rows // SUBLANES):
             at = slice(g * SUBLANES, (g + 1) * SUBLANES)
             for m, picture in ((0, product_all[at]), (1, inverse_all[at])):
-                for t, total in enumerate(column_pass(picture, col_taps, e, m == 1)):
+                for t, total in enumerate(column_pass(picture, col_tap, taps, e, m == 1)):
                     colpass[m, t, pad + g * SUBLANES : pad + (g + 1) * SUBLANES] = total
         for p in range(parts):
             quarters = [
-                row_pass(colpass, row_taps, e, m, pad + p * SHIFT + h * SUBLANES - radius, range(taps))
+                row_pass(colpass, row_tap, e, m, pad + p * SHIFT + h * SUBLANES - radius, range(taps))
                 for m in (0, 1)
                 for h in (0, 1)
             ]
@@ -170,7 +198,7 @@
 
 
 def outer_kernel(
-    radius, chunks, info, row_taps, col_taps, maps, edges, params, above, below, *rest
+    radius, chunks, info, maps, edges, params, tap_rows, above, below, *rest
 ):
     exposures = params.shape[0]
     tiles = maps.shape[0]
@@ -182,6 +210,12 @@
 
     colpass[...] = jnp.zeros_like(colpass)
 
+    def row_tap(e, a):
+        return tap_rows[e, a : a + 1]
+
+    def col_tap(e, b):
+        return tap_rows[e, taps + b : taps + b + 1]
+
     def one_exposure(e, carry):
         for kind in (0, 1):
             pixels[kind, 0:radius] = jnp.where(has_below, below[kind, e].astype(jnp.float32), 0.0)
@@ -189,10 +223,10 @@
         inverse = pixels[1]
         product = pixels[0] * inverse
         for m, picture in ((0, product), (1, inverse)):
-            for t, total in enumerate(column_pass(picture, col_taps, e, m == 1)):
+            for t, total in enumerate(column_pass(picture, col_tap, taps, e, m == 1)):
                 colpass[m, t, pad : pad + SUBLANES] = total
-        upper = [row_pass(colpass, row_taps, e, m, pad + radius, range(radius)) for m in (0, 1)]
-        lower = [row_pass(colpass, row_taps, e, m, -radius, range(radius + 1, taps)) for m in (0, 1)]
+        upper = [row_pass(colpass, row_tap, e, m, pad + radius, range(radius)) for m in (0, 1)]
+        lower = [row_pass(colpass, row_tap, e, m, -radius, range(radius + 1, taps)) for m in (0, 1)]
         for t in range(tiles):
             for m in (0, 1):
                 more[0, t, 2 * e + m] = upper[m][t]
@@ -226,43 +260,58 @@
                 out[tail : tail + exposures] = params[...].astype(jnp.bfloat16)
 
 
-def stack_kernel(groups, chunks, exposures, rows, vels, info, *rest):
-    parts = rows // SHIFT
-    blocks = [rest[p * groups : (p + 1) * groups] for p in range(parts + 1)]
-    rest = rest[(parts + 1) * groups :]
-    outs = rest[:chunks]
-    main, side, even, odd, whole_params, scalars, order, result, sem = rest[chunks:]
-    windows = (even, odd)
-    own = info[2]
-    first_vel = info[4]
-    share = result.shape[0]
+def unpack_all(blocks, kept_as, main, side, exposures):
     main_rows = exposures * 2 * SHIFT
     size = main_rows + exposures * SUBLANES
+    for g, group in enumerate(blocks):
+        for q in range(4):
+            turned = []
+            for block in group:
+                packed = block[main_rows:size]
+                piece = packed if q == 0 else pltpu.roll(packed, LANES - 2 * SHIFT * q, 1)
+                turned.append(piece.astype(jnp.float32))
+            for p, piece in enumerate(kept_as(turned)):
+                at = p * SHIFT + (q % 2) * SUBLANES
+                for e in range(exposures):
+                    side[g * exposures + e, q // 2, at : at + SUBLANES] = piece[e * SUBLANES : (e + 1) * SUBLANES]
+        for k in range(2 * exposures):
+            cells = [block[k * SHIFT : (k + 1) * SHIFT].astype(jnp.float32) for block in group]
+            for p, piece in enumerate(kept_as(cells)):
+                main[g * exposures + k // 2, k % 2, p * SHIFT : (p + 1) * SHIFT] = piece
+
+
+def stack_kernel(groups, per_group, exposures, vels, halves, info, *rest):
+    blocks = [[rest[p * groups + g] for p in range(per_group)] for g in range(groups)]
+    rest = rest[per_group * groups :]
+    main, side, even, odd, whole_params, scalars, order, result, sem = rest[-9:]
+    outs = rest[:-9]
+    windows = (even, odd)
+    own_sub, first_vel = info[3], info[4]
+    share, rows = result.shape[0], result.shape[1]
+    size = exposures * (2 * SHIFT + SUBLANES)
     total = groups * exposures
     whole_params[total:] = jnp.zeros((exposures, LANES), jnp.int32)
     for g in range(groups):
         whole_params[g * exposures : (g + 1) * exposures] = (
-            blocks[parts - 1][g][size : size + exposures].astype(jnp.float32).astype(jnp.int32)
+            blocks[g][1][size : size + exposures].astype(jnp.float32).astype(jnp.int32)
         )
     fetch = pltpu.make_async_copy(whole_params, scalars, sem)
     fetch.start()
-    has_below = info[1].astype(jnp.float32)
-    for g in range(groups):
-        for p in range(parts + 1):
-            packed = blocks[p][g][main_rows:size]
-            for q in range(4):
-                piece = packed if q == 0 else pltpu.roll(packed, LANES - 2 * SHIFT * q, 1)
-                piece = piece.astype(jnp.float32)
-                if p == parts:
-                    piece = piece * has_below
-                at = p * SHIFT + (q % 2) * SUBLANES
-                for e in range(exposures):
-                    side[g * exposures + e, q // 2, at : at + SUBLANES] = piece[e * SUBLANES : (e + 1) * SUBLANES]
-            for k in range(2 * exposures):
-                cells = blocks[p][g][k * SHIFT : (k + 1) * SHIFT].astype(jnp.float32)
-                if p == parts:
-                    cells = cells * has_below
-                main[g * exposures + k // 2, k % 2, p * SHIFT : (p + 1) * SHIFT] = cells
+    has_below = info[1] > 0
+    if halves:
+        second = own_sub > 0
+        valid = has_below | (own_sub == 0)
+
+        def kept_as(cells):
+            outer, inner = jnp.where(valid, cells[0], 0.0), cells[1]
+            return jnp.where(second, inner, outer), jnp.where(second, outer, inner)
+
+    else:
+
+        def kept_as(cells):
+            return *cells[:-1], jnp.where(has_below, cells[-1], 0.0)
+
+    unpack_all(blocks, kept_as, main, side, exposures)
     main[total] = jnp.zeros(main.shape[1:], jnp.float32)
     side[total] = jnp.zeros(side.shape[1:], jnp.float32)
     fetch.wait()
@@ -326,10 +375,20 @@
         else:
             sums = none + over_exposures(weigh, none)
         result[v] = sums[2] / jnp.sqrt(sums[3] + 1.0)
-    block = rows // chunks
+    block = rows // len(outs)
+    for step, out in enumerate(outs):
+        to = partner(info[2], step, len(outs))
+        out[...] = result[:, pl.ds(pl.multiple_of(to * block, block), block)]
+
+
+def rows_kernel(chunks, info, *rest):
+    pieces = rest[:chunks]
+    out, held = rest[chunks:]
     for step in range(chunks):
-        to = partner(own, step, chunks)
-        outs[step][...] = result[:, pl.ds(pl.multiple_of(to * block, block), block)]
+        held[step] = pieces[step][...]
+    own = (info[2] * 2 + info[3]) % chunks
+    for c in range(chunks):
+        out[:, :, c * LANES : (c + 1) * LANES] = held[partner(own, c, chunks)]
 
 
 def columns_kernel(chunks, subs, info, *rest):
@@ -359,7 +418,8 @@
         out[k * share : (k + 1) * share] = held[partner(own_sub, k, subs)]
 
 
-def per_device(science, inv_var, psf_rows, psf_cols, row_shift, col_shift, exposure_ok):
+def per_device(*arguments):
+    science, inv_var, psf_rows, psf_cols, row_shift, col_shift, exposure_ok = arguments
     exposures, rows, columns = science.shape
     vels = row_shift.shape[1]
     radius = psf_rows.shape[1] // 2
@@ -373,7 +433,8 @@
     me = lax.axis_index("expo")
     own_chunk = me // subs
     own_sub = me % subs
-    info = jnp.stack([strip > 0, strip < strips - 1, own_chunk, own_sub, own_sub * share]).astype(jnp.int32)
+    first_vel = 0 if split_rows(subs, parts) else own_sub * share
+    info = jnp.stack([strip > 0, strip < strips - 1, own_chunk, own_sub, first_vel]).astype(jnp.int32)
 
     def rows_from(start):
         return jnp.stack([lax.dynamic_slice_in_dim(x, start, radius, 1) for x in (science, inv_var)])
@@ -386,16 +447,18 @@
         below = lax.ppermute(rows_from(0), "strip", [(i + 1, i) for i in range(strips - 1)])
 
     map_rows = parts * exposures * 2 * SHIFT
+    tap_room = -(-2 * psf_rows.shape[1] // SUBLANES) * SUBLANES
     edge_rows = parts * exposures * SUBLANES
-    maps, edges, params = pl.pallas_call(
+    maps, edges, params, tap_rows = pl.pallas_call(
         functools.partial(inner_kernel, radius),
         out_shape=[
             jax.ShapeDtypeStruct((chunks, map_rows, LANES), jnp.float32),
             jax.ShapeDtypeStruct((chunks, edge_rows, LANES), jnp.float32),
             jax.ShapeDtypeStruct((exposures, LANES), jnp.float32),
+            jax.ShapeDtypeStruct((exposures, tap_room, LANES), jnp.float32),
         ],
         in_specs=[HBM] * 7,
-        out_specs=[VMEM] * 3,
+        out_specs=[VMEM] * 4,
         scratch_shapes=[
             pltpu.VMEM(science.shape, science.dtype),
             pltpu.VMEM(inv_var.shape, inv_var.dtype),
@@ -410,7 +473,7 @@
         compiler_params=pltpu.CompilerParams(vmem_limit_bytes=8 << 20),
         cost_estimate=pl.CostEstimate(flops=100_000_000, bytes_accessed=4_000_000, transcendentals=0),
         name="filter_inner",
-    )(*[pltpu.with_memory_space_constraint(x, pltpu.HBM) for x in (science, inv_var, psf_rows, psf_cols, row_shift, col_shift, exposure_ok)])
+    )(*[pltpu.with_memory_space_constraint(x, pltpu.HBM) for x in arguments])
     block = exposures * (2 * SHIFT + SUBLANES)
     sent = [
         jax.ShapeDtypeStruct((block + (exposures if p == parts - 1 else 0), LANES), jnp.bfloat16)
@@ -419,7 +482,7 @@
     sends = pl.pallas_call(
         functools.partial(outer_kernel, radius, chunks),
         out_shape=sent * chunks,
-        in_specs=[SMEM] * 3 + [VMEM] * 5,
+        in_specs=[SMEM] + [VMEM] * 6,
         out_specs=[VMEM] * (chunks * parts),
         scratch_shapes=[
             pltpu.VMEM((2, 2 * radius, columns), jnp.float32),
@@ -429,46 +492,76 @@
         ],
         compiler_params=pltpu.CompilerParams(vmem_limit_bytes=8 << 20),
         name="filter_outer",
-    )(info, psf_rows, psf_cols, maps, edges, params, above, below)
-
-    blocks = [[[None] * chunks for _ in range(subs)] for _ in range(parts + 1)]
-    up = [((i + 1) % strips, i) for i in range(strips)]
+    )(info, maps, edges, params, tap_rows, above, below)
+
+    halves = split_rows(subs, parts)
+    arrived = []
     for step in range(chunks):
-        for p in range(parts):
-            blocks[p][0][step] = sends[step * parts + p]
-            if step:
-                blocks[p][0][step] = lax.ppermute(sends[step * parts + p], "expo", chunk_pairs(step, chunks, subs))
-        blocks[parts][0][step] = lax.ppermute(blocks[0][0][step], "strip", up)
-    for p in range(parts + 1):
-        for u in range(1, subs):
-            for step in range(chunks):
-                blocks[p][u][step] = lax.ppermute(blocks[p][0][step], "expo", sub_pairs(u, chunks, subs))
-    blocks = [[block for sub in part for block in sub] for part in blocks]
+        arrived.append(
+            [
+                lax.ppermute(sends[step * parts + p], "expo", chunk_pairs(step, chunks, subs))
+                if step
+                else sends[p]
+                for p in range(parts)
+            ]
+        )
+    if halves:
+        both = ("expo", "strip")
+        same, cross = strip_pairs(strips, chunks)
+        swap = sub_pairs(1, chunks, subs)
+        outer = [lax.ppermute(arrived[s][0], both, same) for s in range(chunks)]
+        outer += [lax.ppermute(arrived[s][0], both, cross) for s in range(chunks)]
+        inner = [arrived[s][1] for s in range(chunks)]
+        inner += [lax.ppermute(arrived[s][1], "expo", swap) for s in range(chunks)]
+        blocks = [outer, inner]
+        stacked_rows, share = rows // subs, vels
+    else:
+        up = [((i + 1) % strips, i) for i in range(strips)]
+        blocks = [[block[p] for block in arrived] for p in range(parts)]
+        blocks.append([lax.ppermute(arrived[step][0], "strip", up) for step in range(chunks)])
+        for part in blocks:
+            for u in range(1, subs):
+                pairs = sub_pairs(u, chunks, subs)
+                part += [lax.ppermute(part[step], "expo", pairs) for step in range(chunks)]
+        stacked_rows = rows
 
     groups = len(blocks[0])
-    block_rows = rows // chunks
-    reach = rows + SHIFT
+    block_rows = stacked_rows // chunks
+    reach = stacked_rows + SHIFT
     piece = jax.ShapeDtypeStruct((share, block_rows, LANES), jnp.float32)
     total = groups * exposures
     pieces = pl.pallas_call(
-        functools.partial(stack_kernel, groups, chunks, exposures, rows, vels),
+        functools.partial(stack_kernel, groups, len(blocks), exposures, vels, halves),
         out_shape=[piece] * chunks,
-        in_specs=[SMEM] + [VMEM] * ((parts + 1) * groups),
+        in_specs=[SMEM] + [VMEM] * (len(blocks) * groups),
         out_specs=[VMEM] * chunks,
         scratch_shapes=[
             pltpu.VMEM((total + 1, 2, reach, LANES), jnp.float32),
             pltpu.VMEM((total + 1, 2, reach, LANES), jnp.float32),
-            pltpu.VMEM((total + UNROLL, 2, rows, LANES), jnp.float32),
-            pltpu.VMEM((total + UNROLL, 2, rows, LANES), jnp.float32),
+            pltpu.VMEM((total + UNROLL, 2, stacked_rows, LANES), jnp.float32),
+            pltpu.VMEM((total + UNROLL, 2, stacked_rows, LANES), jnp.float32),
             pltpu.VMEM((total + exposures, LANES), jnp.int32),
             pltpu.SMEM((total + exposures, LANES), jnp.int32),
             pltpu.SMEM((total + UNROLL,), jnp.int32),
-            pltpu.VMEM((share, rows, LANES), jnp.float32),
+            pltpu.VMEM((share, stacked_rows, LANES), jnp.float32),
             pltpu.SemaphoreType.DMA(()),
         ],
         compiler_params=pltpu.CompilerParams(vmem_limit_bytes=24 << 20),
         name="stack_twice",
     )(info, *[block for part in blocks for block in part])
+
+    if halves:
+        held = [lax.ppermute(pieces[t], "expo", row_pairs(t, chunks)) for t in range(chunks)]
+        likelihood = pl.pallas_call(
+            functools.partial(rows_kernel, chunks),
+            out_shape=jax.ShapeDtypeStruct((vels, block_rows, columns), jnp.float32),
+            in_specs=[SMEM] + [VMEM] * chunks,
+            out_specs=VMEM,
+            scratch_shapes=[pltpu.VMEM((chunks, vels, block_rows, LANES), jnp.float32)],
+            compiler_params=pltpu.CompilerParams(vmem_limit_bytes=1 << 20),
+            name="join_rows",
+        )(info, *held)
+        return likelihood[None]
 
     held = [pieces[0]]
     for step in range(1, chunks):

time: 54.1 us -> 58.7 us (1.085); the launches traced: 53.9 us -> 57.9 us
  starting transfers between devices: 24.6 us -> 33.7 us
  waiting for transfers between devices: 13.6 us -> 8.91 us
  local copies, waits for them, and re-layouts: 1.66 us -> 0.99 us
    ppermute x20 -> x16, starting transfers between devices: 10.1 us -> 18.6 us  [the longest x4 11.5 us: per_device(): lax.ppermute(pieces[t], 'expo', row_pairs(t, chunks))]
    ppermute x20 -> x16, waiting for transfers between devices: 10.2 us -> 5.33 us  [the longest x4 3.91 us: per_device(): lax.ppermute(pieces[t], 'expo', row_pairs(t, chunks))]
    unnamed x4 -> x0, local copies, waits for them, and re-layouts: 0.67 us -> none
    ppermute x6, starting transfers between devices: 11.5 us -> 12.1 us  [per_device(): lax.ppermute(sends[step * parts + p], 'expo', chunk_pairs(step, chunks, s...]
    pallas_call x3 -> x2, Pallas kernels: 7.02 us -> 7.32 us  [the longest x1 6.13 us: per_device(): pl.pallas_call(functools.partial(stack_kernel, groups, len(blocks), expos...]
  transfers between devices with their start and end apart: 27 -> 23, of which waited for: 12 -> 5; matrix products, arithmetic and copies ran while one was open for 0% -> 0% of each run, Pallas kernels for 9% -> 8%
where the time goes in v8:
time: 58.7 us; the launch traced here: 57.9 us
  starting transfers between devices  33.7 us (57%)
  Pallas kernels  14.1 us (24%)
  waiting for transfers between devices  8.91 us (15%)
  local copies, waits for them, and re-layouts  0.99 us (2%)
    ppermute x6, starting transfers between devices, per_device(): lax.ppermute(sends[step * parts + p], 'expo', chunk_pairs(step, chunks, s...  12.1 us
    ppermute x4, starting transfers between devices, per_device(): lax.ppermute(pieces[t], 'expo', row_pairs(t, chunks))  11.5 us
    pallas_call x1, Pallas kernels, per_device(): pl.pallas_call(functools.partial(stack_kernel, groups, len(blocks), expos...  6.13 us
    pallas_call x1, Pallas kernels, per_device(): pl.pallas_call(functools.partial(inner_kernel, radius), out_shape=[jax.Sh...  4.65 us
    ppermute x4, waiting for transfers between devices, per_device(): lax.ppermute(pieces[t], 'expo', row_pairs(t, chunks))  3.91 us
    ppermute x6, waiting for transfers between devices, per_device(): lax.ppermute(sends[step * parts + p], 'expo', chunk_pairs(step, chunks, s...  3.58 us
    ppermute x1, starting transfers between devices, per_device(): above = below = lax.ppermute(met, 'strip', [(0, 1), (1, 0)])  3.03 us
    ppermute x4, starting transfers between devices, per_device(): outer = [lax.ppermute(arrived[s][0], both, same) for s in range(chunks)]  2.62 us
  transfers between devices with their start and end apart: 23, of which 5 were waited for; matrix products, arithmetic and copies ran while one was open for 0% of the time, Pallas kernels for 8%

profile of v8, /device:TPU:0, one launch (start us, length us, event | category | flops | bytes accessed | tf_op | source)
XLA Modules:
  0.0 57.9 jit_solution(11427269812607005370)
XLA Ops:
  0.0 0.9 %dynamic-slice_bitcast_fusion = (bf16[1,8,4,512]{3,2,1,0:T(4,128)(2,1)S(1)}, bf16[1,8,4,512]{3,2,1,0:T(4,128)(2,1)S(1)}) fusion(bf16[8,32,512]{2,1,0:T(8,128)(2,1)} %inv_var_hbm.1, s32[]{:T(128)S(6)} %select_n.19, bf16[8,32,512]{2,1,0:T(8,128)(2,1)} %science_hbm.1), kind=kLoop, calls=%fused_computation.1 | loop fusion | bytes 131076 | tf_op jit(solution)/shard_map/stack | solution.py:440
  1.0 3.0 %collective-permute-start = (bf16[2,8,4,512]{3,2,1,0:T(4,128)(2,1)S(1)}, bf16[2,8,4,512]{3,2,1,0:T(4,128)(2,1)S(1)}, u32[]{:S(2)}, u32[]{:S(2)}) collective-permute-start(bf16[2,8,4,512]{3,2,1,0:T(4,128)(2,1)S(1)} %pad_maximum_fusion), channel_id=1, source_target_pairs={{0,1},{1,0},{2,3},{3,2},{4,5},{5,4},{6,7},{7,6},{8,9},{9,8},{10,11... | collective-permute-start | bytes 196616 | tf_op jit(solution)/shard_map/ppermute | solution.py:444
  4.0 0.1 stack.36.info
  4.1 4.6 %filter_inner.1 = (f32[4,512,128]{2,1,0:T(8,128)S(1)}, f32[4,128,128]{2,1,0:T(8,128)S(1)}, f32[8,128]{1,0:T(8,128)S(1)}, f32[8,24,128]{2,1,0:T(8,128)S(1)}) custom-call(bf16[8,32,512]{2,1,0:T(8,128)(2,1)} %science_hbm.1, bf16[8,32,512]{2,1,0:T(8,128)(2,1)} %inv_var_hbm.1, f32[8,9]{1,0:T(8,128)} %row_taps_hbm.1, f32[8,9]{1,0:T(8,128)} %col_taps_hbm.1, ...), custom_call_target="tpu_custom_call" | custom-call | flops 100000000 | bytes 4000000 | tf_op jit(solution)/shard_map/filter_inner/pallas_call | solution.py:452
  8.7 0.0 collective-permute-done.above.below
  8.7 2.1 %filter_outer.1 = (bf16[320,128]{1,0:T(8,128)(2,1)S(1)}, bf16[328,128]{1,0:T(8,128)(2,1)S(1)}, bf16[320,128]{1,0:T(8,128)(2,1)S(1)}, bf16[328,128]{1,0:T(8,128)(...) custom-call(s32[5]{0:T(128)S(1)} %stack.36.info, ...), custom_call_target="tpu_custom_call" | custom-call | tf_op jit(solution)/shard_map/filter_outer/pallas_call | solution.py:482
  10.9 1.6 %collective-permute-start.2 = (bf16[320,128]{1,0:T(8,128)(2,1)S(1)}, bf16[320,128]{1,0:T(8,128)(2,1)S(1)}, u32[]{:S(2)}, u32[]{:S(2)}) collective-permute-start(bf16[320,128]{1,0:T(8,128)(2,1)S(1)} %get-tuple-element.26), channel_id=1, source_target_pairs={{0,4},{2,6},{4,0},{6,2},{8,12},{10,14},{12,8},{14,10},{1,5},{3,7},... | collective-permute-start | bytes 245768 | tf_op jit(solution)/shard_map/ppermute | solution.py:502
  12.5 2.6 %collective-permute-start.4 = (bf16[320,128]{1,0:T(8,128)(2,1)S(1)}, bf16[320,128]{1,0:T(8,128)(2,1)S(1)}, u32[]{:S(2)}, u32[]{:S(2)}) collective-permute-start(bf16[320,128]{1,0:T(8,128)(2,1)S(1)} %get-tuple-element.27), channel_id=1, source_target_pairs={{0,8},{2,10},{4,12},{6,14},{8,0},{10,2},{12,4},{14,6},{1,9},{3,11}... | collective-permute-start | bytes 245768 | tf_op jit(solution)/shard_map/ppermute | solution.py:502
  15.1 0.2 collective-permute-start.6
  15.4 0.0 collective-permute-start.8
  15.4 0.7 %collective-permute-start.12 = (bf16[328,128]{1,0:T(8,128)(2,1)S(1)}, bf16[328,128]{1,0:T(8,128)(2,1)S(1)}, u32[]{:S(2)}, u32[]{:S(2)}) collective-permute-start(bf16[328,128]{1,0:T(8,128)(2,1)S(1)} %get-tuple-element.30), channel_id=1, source_target_pairs={{0,4},{2,6},{4,0},{6,2},{8,12},{10,14},{12,8},{14,10},{1,5},{3,7},... | collective-permute-start | bytes 251912 | tf_op jit(solution)/shard_map/ppermute | solution.py:502
  16.0 0.0 collective-permute-done.2
  16.0 3.5 %collective-permute-start.13 = (bf16[328,128]{1,0:T(8,128)(2,1)S(1)}, bf16[328,128]{1,0:T(8,128)(2,1)S(1)}, u32[]{:S(2)}, u32[]{:S(2)}) collective-permute-start(bf16[328,128]{1,0:T(8,128)(2,1)S(1)} %get-tuple-element.31), channel_id=1, source_target_pairs={{0,8},{2,10},{4,12},{6,14},{8,0},{10,2},{12,4},{14,6},{1,9},{3,11}... | collective-permute-start | bytes 251912 | tf_op jit(solution)/shard_map/ppermute | solution.py:502
  19.5 1.2 %collective-permute-done.4 = bf16[320,128]{1,0:T(8,128)(2,1)S(1)} collective-permute-done((bf16[320,128]{1,0:T(8,128)(2,1)S(1)}, bf16[320,128]{1,0:T(8,128)(2,1)S(1)}, u32[]{:S(2)}, u32[]{:S(2)}) %collective-permute-start.4) | collective-permute-done | bytes 81952 | tf_op jit(solution)/shard_map/ppermute | solution.py:502
  20.7 3.5 %collective-permute-start.14 = (bf16[328,128]{1,0:T(8,128)(2,1)S(1)}, bf16[328,128]{1,0:T(8,128)(2,1)S(1)}, u32[]{:S(2)}, u32[]{:S(2)}) collective-permute-start(bf16[328,128]{1,0:T(8,128)(2,1)S(1)} %get-tuple-element.32), channel_id=1, source_target_pairs={{0,12},{2,14},{4,8},{6,10},{8,4},{10,6},{12,0},{14,2},{1,13},{3,15... | collective-permute-start | bytes 251912 | tf_op jit(solution)/shard_map/ppermute | solution.py:502
  24.2 0.0 collective-permute-done.6
  24.2 0.7 %collective-permute-start.1 = (bf16[320,128]{1,0:T(8,128)(2,1)S(1)}, bf16[320,128]{1,0:T(8,128)(2,1)S(1)}, u32[]{:S(2)}, u32[]{:S(2)}) collective-permute-start(bf16[320,128]{1,0:T(8,128)(2,1)S(1)} %get-tuple-element.25), channel_id=1, source_target_pairs={{0,0},{3,2},{4,4},{7,6},{8,8},{11,10},{12,12},{15,14},{1,1},{2,3},... | collective-permute-start | bytes 245768 | tf_op jit(solution)/shard_map/ppermute | solution.py:512
  24.8 0.0 collective-permute-done.8.rest_4_
  24.9 0.1 collective-permute-start.15
  24.9 0.0 collective-permute-done.1.rest_0_
  24.9 0.6 %collective-permute-start.9 = (bf16[320,128]{1,0:T(8,128)(2,1)S(1)}, bf16[320,128]{1,0:T(8,128)(2,1)S(1)}, u32[]{:S(2)}, u32[]{:S(2)}) collective-permute-start(bf16[320,128]{1,0:T(8,128)(2,1)S(1)} %collective-permute-done.2), channel_id=1, source_target_pairs={{2,0},{1,2},{6,4},{5,6},{10,8},{9,10},{14,12},{13,14},{3,1},{0,3},... | collective-permute-start | bytes 245768 | tf_op jit(solution)/shard_map/ppermute | solution.py:513
  25.6 0.7 %collective-permute-start.3 = (bf16[320,128]{1,0:T(8,128)(2,1)S(1)}, bf16[320,128]{1,0:T(8,128)(2,1)S(1)}, u32[]{:S(2)}, u32[]{:S(2)}) collective-permute-start(bf16[320,128]{1,0:T(8,128)(2,1)S(1)} %collective-permute-done.2), channel_id=1, source_target_pairs={{0,0},{3,2},{4,4},{7,6},{8,8},{11,10},{12,12},{15,14},{1,1},{2,3},... | collective-permute-start | bytes 245768 | tf_op jit(solution)/shard_map/ppermute | solution.py:512
  26.2 2.4 %collective-permute-done.13.rest_10_ = bf16[328,128]{1,0:T(8,128)(2,1)S(1)} collective-permute-done((bf16[328,128]{1,0:T(8,128)(2,1)S(1)}, bf16[328,128]{1,0:T(8,128)(2,1)S(1)}, u32[]{:S(2)}, u32[]{:S(2)}) %collective-permute-start.13) | collective-permute-done | bytes 84000 | tf_op jit(solution)/shard_map/ppermute | solution.py:502
  28.6 0.2 collective-permute-start.10
  28.8 0.0 collective-permute-done.14.rest_11_
  28.8 0.7 %collective-permute-start.5 = (bf16[320,128]{1,0:T(8,128)(2,1)S(1)}, bf16[320,128]{1,0:T(8,128)(2,1)S(1)}, u32[]{:S(2)}, u32[]{:S(2)}) collective-permute-start(bf16[320,128]{1,0:T(8,128)(2,1)S(1)} %collective-permute-done.4), channel_id=1, source_target_pairs={{0,0},{3,2},{4,4},{7,6},{8,8},{11,10},{12,12},{15,14},{1,1},{2,3},... | collective-permute-start | bytes 245768 | tf_op jit(solution)/shard_map/ppermute | solution.py:512
  29.5 1.9 %collective-permute-start.16 = (bf16[328,128]{1,0:T(8,128)(2,1)S(1)}, bf16[328,128]{1,0:T(8,128)(2,1)S(1)}, u32[]{:S(2)}, u32[]{:S(2)}) collective-permute-start(bf16[328,128]{1,0:T(8,128)(2,1)S(1)} %collective-permute-done.12.rest_9_), channel_id=1, source_target_pairs={{0,2},{2,0},{4,6},{6,4},{8,10},{10,8},{12,14},{14,12},{1,3},{3,1},... | collective-permute-start | bytes 251912 | tf_op jit(solution)/shard_map/ppermute | solution.py:515
  31.4 0.0 collective-permute-done.9.rest_5_
  31.4 0.1 collective-permute-start.17
  31.5 0.0 collective-permute-done.3.rest_1_
  31.5 0.4 collective-permute-start.18
  31.9 0.0 collective-permute-done.10.rest_6_
  31.9 1.2 %collective-permute-start.11 = (bf16[320,128]{1,0:T(8,128)(2,1)S(1)}, bf16[320,128]{1,0:T(8,128)(2,1)S(1)}, u32[]{:S(2)}, u32[]{:S(2)}) collective-permute-start(bf16[320,128]{1,0:T(8,128)(2,1)S(1)} %collective-permute-done.6), channel_id=1, source_target_pairs={{2,0},{1,2},{6,4},{5,6},{10,8},{9,10},{14,12},{13,14},{3,1},{0,3},... | collective-permute-start | bytes 245768 | tf_op jit(solution)/shard_map/ppermute | solution.py:513
  33.1 0.0 collective-permute-done.5.rest_2_
  33.1 0.7 %collective-permute-start.7 = (bf16[320,128]{1,0:T(8,128)(2,1)S(1)}, bf16[320,128]{1,0:T(8,128)(2,1)S(1)}, u32[]{:S(2)}, u32[]{:S(2)}) collective-permute-start(bf16[320,128]{1,0:T(8,128)(2,1)S(1)} %collective-permute-done.6), channel_id=1, source_target_pairs={{0,0},{3,2},{4,4},{7,6},{8,8},{11,10},{12,12},{15,14},{1,1},{2,3},... | collective-permute-start | bytes 245768 | tf_op jit(solution)/shard_map/ppermute | solution.py:512
  33.8 1.4 %collective-permute-done.11.rest_7_ = bf16[320,128]{1,0:T(8,128)(2,1)S(1)} collective-permute-done((bf16[320,128]{1,0:T(8,128)(2,1)S(1)}, bf16[320,128]{1,0:T(8,128)(2,1)S(1)}, u32[]{:S(2)}, u32[]{:S(2)}) %collective-permute-start.11) | collective-permute-done | bytes 81952 | tf_op jit(solution)/shard_map/ppermute | solution.py:513
  35.2 0.0 collective-permute-done.7.rest_3_
  35.2 0.0 collective-permute-done.16.rest_13_
  35.2 0.0 collective-permute-done.17.rest_14_
  35.2 6.1 %stack_twice.1 = (f32[8,4,128]{2,1,0:T(4,128)S(1)}, f32[8,4,128]{2,1,0:T(4,128)S(1)}, f32[8,4,128]{2,1,0:T(4,128)S(1)}, f32[8,4,128]{2,1,0:T(4,128)S(1)}) custom-call(s32[5]{0:T(128)S(1)} %stack.36.info, bf16[320,128]{1,0:T(8,128)(2,1)S(1)} %collective-permute-done.1.rest_0_, bf16[320,128]{1,0:T(8,128)(2,1)S(1)} %collective-permute-done.3.rest_1_, ...), custom_call_target="tpu_custom_call" | custom-call | tf_op jit(solution)/shard_map/stack_twice/pallas_call | solution.py:533
  41.3 0.7 %collective-permute-start.19 = (f32[8,4,128]{2,1,0:T(4,128)S(1)}, f32[8,4,128]{2,1,0:T(4,128)S(1)}, u32[]{:S(2)}, u32[]{:S(2)}) collective-permute-start(f32[8,4,128]{2,1,0:T(4,128)S(1)} %get-tuple-element.33), channel_id=1, source_target_pairs={{0,0},{2,8},{4,2},{6,10},{8,4},{10,12},{12,6},{14,14},{1,1},{3,9},... | collective-permute-start | bytes 49160 | tf_op jit(solution)/shard_map/ppermute | solution.py:554
  42.0 5.7 %collective-permute-start.20 = (f32[8,4,128]{2,1,0:T(4,128)S(1)}, f32[8,4,128]{2,1,0:T(4,128)S(1)}, u32[]{:S(2)}, u32[]{:S(2)}) collective-permute-start(f32[8,4,128]{2,1,0:T(4,128)S(1)} %get-tuple-element.34), channel_id=1, source_target_pairs={{0,2},{2,10},{4,0},{6,8},{8,6},{10,14},{12,4},{14,12},{1,3},{3,11}... | collective-permute-start | bytes 49160 | tf_op jit(solution)/shard_map/ppermute | solution.py:554
  47.6 1.7 %collective-permute-start.21 = (f32[8,4,128]{2,1,0:T(4,128)S(1)}, f32[8,4,128]{2,1,0:T(4,128)S(1)}, u32[]{:S(2)}, u32[]{:S(2)}) collective-permute-start(f32[8,4,128]{2,1,0:T(4,128)S(1)} %get-tuple-element.35), channel_id=1, source_target_pairs={{0,4},{2,12},{4,6},{6,14},{8,0},{10,8},{12,2},{14,10},{1,5},{3,13}... | collective-permute-start | bytes 49160 | tf_op jit(solution)/shard_map/ppermute | solution.py:554
  49.3 3.5 %collective-permute-start.22 = (f32[8,4,128]{2,1,0:T(4,128)S(1)}, f32[8,4,128]{2,1,0:T(4,128)S(1)}, u32[]{:S(2)}, u32[]{:S(2)}) collective-permute-start(f32[8,4,128]{2,1,0:T(4,128)S(1)} %get-tuple-element.36), channel_id=1, source_target_pairs={{0,6},{2,14},{4,4},{6,12},{8,2},{10,10},{12,0},{14,8},{1,7},{3,15}... | collective-permute-start | bytes 49160 | tf_op jit(solution)/shard_map/ppermute | solution.py:554
  52.8 0.0 collective-permute-done.19.rest_0_
  52.8 0.2 collective-permute-done.21.rest_2_
  53.0 3.7 %collective-permute-done.22.rest_3_ = f32[8,4,128]{2,1,0:T(4,128)S(1)} collective-permute-done((f32[8,4,128]{2,1,0:T(4,128)S(1)}, f32[8,4,128]{2,1,0:T(4,128)S(1)}, u32[]{:S(2)}, u32[]{:S(2)}) %collective-permute-start.22) | collective-permute-done | bytes 16416 | tf_op jit(solution)/shard_map/ppermute | solution.py:554
  56.7 1.2 %join_rows.1 = f32[8,4,512]{2,1,0:T(4,128)} custom-call(s32[5]{0:T(128)S(1)} %stack.36.info, f32[8,4,128]{2,1,0:T(4,128)S(1)} %collective-permute-done.19.rest_0_, f32[8,4,128]{2,1,0:T(4,128)S(1)} %collective-permute-done.20.rest_1_, f32[8,4,128]{2,1,0:T(4,128)S(1)} %collective-permute-done.21.rest_2_, f32[8,4,128]{2,1,0:T(4,128)S(1)} %collective-permute-done.22.rest_3_), custom_call_target="tpu_custom_call" | custom-call | tf_op jit(solution)/shard_map/join_rows/pallas_call | solution.py:555
  (5 shorter events, 0.1 us)
Async XLA Ops:
  1.0 7.8 %collective-permute-start = (bf16[2,8,4,512]{3,2,1,0:T(4,128)(2,1)S(1)}, bf16[2,8,4,512]{3,2,1,0:T(4,128)(2,1)S(1)}, u32[]{:S(2)}, u32[]{:S(2)}) collective-permute-start(bf16[2,8,4,512]{3,2,1,0:T(4,128)(2,1)S(1)} %pad_maximum_fusion), channel_id=1, source_target_pairs={{0,1},{1,0},{2,3},{3,2},{4,5},{5,4},{6,7},{7,6},{8,9},{9,8},{10,11... | collective-permute-start | bytes 196616 | tf_op jit(solution)/shard_map/ppermute | solution.py:444
  10.9 5.1 %collective-permute-start.2 = (bf16[320,128]{1,0:T(8,128)(2,1)S(1)}, bf16[320,128]{1,0:T(8,128)(2,1)S(1)}, u32[]{:S(2)}, u32[]{:S(2)}) collective-permute-start(bf16[320,128]{1,0:T(8,128)(2,1)S(1)} %get-tuple-element.26), channel_id=1, source_target_pairs={{0,4},{2,6},{4,0},{6,2},{8,12},{10,14},{12,8},{14,10},{1,5},{3,7},... | collective-permute-start | bytes 245768 | tf_op jit(solution)/shard_map/ppermute | solution.py:502
  12.5 8.2 %collective-permute-start.4 = (bf16[320,128]{1,0:T(8,128)(2,1)S(1)}, bf16[320,128]{1,0:T(8,128)(2,1)S(1)}, u32[]{:S(2)}, u32[]{:S(2)}) collective-permute-start(bf16[320,128]{1,0:T(8,128)(2,1)S(1)} %get-tuple-element.27), channel_id=1, source_target_pairs={{0,8},{2,10},{4,12},{6,14},{8,0},{10,2},{12,4},{14,6},{1,9},{3,11}... | collective-permute-start | bytes 245768 | tf_op jit(solution)/shard_map/ppermute | solution.py:502
  15.1 9.0 %collective-permute-start.6 = (bf16[320,128]{1,0:T(8,128)(2,1)S(1)}, bf16[320,128]{1,0:T(8,128)(2,1)S(1)}, u32[]{:S(2)}, u32[]{:S(2)}) collective-permute-start(bf16[320,128]{1,0:T(8,128)(2,1)S(1)} %get-tuple-element.28), channel_id=1, source_target_pairs={{0,12},{2,14},{4,8},{6,10},{8,4},{10,6},{12,0},{14,2},{1,13},{3,15... | collective-permute-start | bytes 245768 | tf_op jit(solution)/shard_map/ppermute | solution.py:502
  15.4 9.5 %collective-permute-start.8 = (bf16[320,128]{1,0:T(8,128)(2,1)S(1)}, bf16[320,128]{1,0:T(8,128)(2,1)S(1)}, u32[]{:S(2)}, u32[]{:S(2)}) collective-permute-start(bf16[320,128]{1,0:T(8,128)(2,1)S(1)} %get-tuple-element.25), channel_id=1, source_target_pairs={{2,0},{1,2},{6,4},{5,6},{10,8},{9,10},{14,12},{13,14},{3,1},{0,3},... | collective-permute-start | bytes 245768 | tf_op jit(solution)/shard_map/ppermute | solution.py:513
  15.4 10.2 %collective-permute-start.12 = (bf16[328,128]{1,0:T(8,128)(2,1)S(1)}, bf16[328,128]{1,0:T(8,128)(2,1)S(1)}, u32[]{:S(2)}, u32[]{:S(2)}) collective-permute-start(bf16[328,128]{1,0:T(8,128)(2,1)S(1)} %get-tuple-element.30), channel_id=1, source_target_pairs={{0,4},{2,6},{4,0},{6,2},{8,12},{10,14},{12,8},{14,10},{1,5},{3,7},... | collective-permute-start | bytes 251912 | tf_op jit(solution)/shard_map/ppermute | solution.py:502
  16.0 12.6 %collective-permute-start.13 = (bf16[328,128]{1,0:T(8,128)(2,1)S(1)}, bf16[328,128]{1,0:T(8,128)(2,1)S(1)}, u32[]{:S(2)}, u32[]{:S(2)}) collective-permute-start(bf16[328,128]{1,0:T(8,128)(2,1)S(1)} %get-tuple-element.31), channel_id=1, source_target_pairs={{0,8},{2,10},{4,12},{6,14},{8,0},{10,2},{12,4},{14,6},{1,9},{3,11}... | collective-permute-start | bytes 251912 | tf_op jit(solution)/shard_map/ppermute | solution.py:502
  20.7 8.1 %collective-permute-start.14 = (bf16[328,128]{1,0:T(8,128)(2,1)S(1)}, bf16[328,128]{1,0:T(8,128)(2,1)S(1)}, u32[]{:S(2)}, u32[]{:S(2)}) collective-permute-start(bf16[328,128]{1,0:T(8,128)(2,1)S(1)} %get-tuple-element.32), channel_id=1, source_target_pairs={{0,12},{2,14},{4,8},{6,10},{8,4},{10,6},{12,0},{14,2},{1,13},{3,15... | collective-permute-start | bytes 251912 | tf_op jit(solution)/shard_map/ppermute | solution.py:502
  24.2 0.8 %collective-permute-start.1 = (bf16[320,128]{1,0:T(8,128)(2,1)S(1)}, bf16[320,128]{1,0:T(8,128)(2,1)S(1)}, u32[]{:S(2)}, u32[]{:S(2)}) collective-permute-start(bf16[320,128]{1,0:T(8,128)(2,1)S(1)} %get-tuple-element.25), channel_id=1, source_target_pairs={{0,0},{3,2},{4,4},{7,6},{8,8},{11,10},{12,12},{15,14},{1,1},{2,3},... | collective-permute-start | bytes 245768 | tf_op jit(solution)/shard_map/ppermute | solution.py:512
  24.9 4.6 %collective-permute-start.15 = (bf16[328,128]{1,0:T(8,128)(2,1)S(1)}, bf16[328,128]{1,0:T(8,128)(2,1)S(1)}, u32[]{:S(2)}, u32[]{:S(2)}) collective-permute-start(bf16[328,128]{1,0:T(8,128)(2,1)S(1)} %get-tuple-element.29.rest_8_), channel_id=1, source_target_pairs={{0,2},{2,0},{4,6},{6,4},{8,10},{10,8},{12,14},{14,12},{1,3},{3,1},... | collective-permute-start | bytes 251912 | tf_op jit(solution)/shard_map/ppermute | solution.py:515
  24.9 6.4 %collective-permute-start.9 = (bf16[320,128]{1,0:T(8,128)(2,1)S(1)}, bf16[320,128]{1,0:T(8,128)(2,1)S(1)}, u32[]{:S(2)}, u32[]{:S(2)}) collective-permute-start(bf16[320,128]{1,0:T(8,128)(2,1)S(1)} %collective-permute-done.2), channel_id=1, source_target_pairs={{2,0},{1,2},{6,4},{5,6},{10,8},{9,10},{14,12},{13,14},{3,1},{0,3},... | collective-permute-start | bytes 245768 | tf_op jit(solution)/shard_map/ppermute | solution.py:513
  25.6 5.9 %collective-permute-start.3 = (bf16[320,128]{1,0:T(8,128)(2,1)S(1)}, bf16[320,128]{1,0:T(8,128)(2,1)S(1)}, u32[]{:S(2)}, u32[]{:S(2)}) collective-permute-start(bf16[320,128]{1,0:T(8,128)(2,1)S(1)} %collective-permute-done.2), channel_id=1, source_target_pairs={{0,0},{3,2},{4,4},{7,6},{8,8},{11,10},{12,12},{15,14},{1,1},{2,3},... | collective-permute-start | bytes 245768 | tf_op jit(solution)/shard_map/ppermute | solution.py:512
  28.6 3.3 %collective-permute-start.10 = (bf16[320,128]{1,0:T(8,128)(2,1)S(1)}, bf16[320,128]{1,0:T(8,128)(2,1)S(1)}, u32[]{:S(2)}, u32[]{:S(2)}) collective-permute-start(bf16[320,128]{1,0:T(8,128)(2,1)S(1)} %collective-permute-done.4), channel_id=1, source_target_pairs={{2,0},{1,2},{6,4},{5,6},{10,8},{9,10},{14,12},{13,14},{3,1},{0,3},... | collective-permute-start | bytes 245768 | tf_op jit(solution)/shard_map/ppermute | solution.py:513
  28.8 4.3 %collective-permute-start.5 = (bf16[320,128]{1,0:T(8,128)(2,1)S(1)}, bf16[320,128]{1,0:T(8,128)(2,1)S(1)}, u32[]{:S(2)}, u32[]{:S(2)}) collective-permute-start(bf16[320,128]{1,0:T(8,128)(2,1)S(1)} %collective-permute-done.4), channel_id=1, source_target_pairs={{0,0},{3,2},{4,4},{7,6},{8,8},{11,10},{12,12},{15,14},{1,1},{2,3},... | collective-permute-start | bytes 245768 | tf_op jit(solution)/shard_map/ppermute | solution.py:512
  29.5 5.6 %collective-permute-start.16 = (bf16[328,128]{1,0:T(8,128)(2,1)S(1)}, bf16[328,128]{1,0:T(8,128)(2,1)S(1)}, u32[]{:S(2)}, u32[]{:S(2)}) collective-permute-start(bf16[328,128]{1,0:T(8,128)(2,1)S(1)} %collective-permute-done.12.rest_9_), channel_id=1, source_target_pairs={{0,2},{2,0},{4,6},{6,4},{8,10},{10,8},{12,14},{14,12},{1,3},{3,1},... | collective-permute-start | bytes 251912 | tf_op jit(solution)/shard_map/ppermute | solution.py:515
  31.4 3.8 %collective-permute-start.17 = (bf16[328,128]{1,0:T(8,128)(2,1)S(1)}, bf16[328,128]{1,0:T(8,128)(2,1)S(1)}, u32[]{:S(2)}, u32[]{:S(2)}) collective-permute-start(bf16[328,128]{1,0:T(8,128)(2,1)S(1)} %collective-permute-done.13.rest_10_), channel_id=1, source_target_pairs={{0,2},{2,0},{4,6},{6,4},{8,10},{10,8},{12,14},{14,12},{1,3},{3,1},... | collective-permute-start | bytes 251912 | tf_op jit(solution)/shard_map/ppermute | solution.py:515
  31.5 3.7 %collective-permute-start.18 = (bf16[328,128]{1,0:T(8,128)(2,1)S(1)}, bf16[328,128]{1,0:T(8,128)(2,1)S(1)}, u32[]{:S(2)}, u32[]{:S(2)}) collective-permute-start(bf16[328,128]{1,0:T(8,128)(2,1)S(1)} %collective-permute-done.14.rest_11_), channel_id=1, source_target_pairs={{0,2},{2,0},{4,6},{6,4},{8,10},{10,8},{12,14},{14,12},{1,3},{3,1},... | collective-permute-start | bytes 251912 | tf_op jit(solution)/shard_map/ppermute | solution.py:515
  31.9 3.2 %collective-permute-start.11 = (bf16[320,128]{1,0:T(8,128)(2,1)S(1)}, bf16[320,128]{1,0:T(8,128)(2,1)S(1)}, u32[]{:S(2)}, u32[]{:S(2)}) collective-permute-start(bf16[320,128]{1,0:T(8,128)(2,1)S(1)} %collective-permute-done.6), channel_id=1, source_target_pairs={{2,0},{1,2},{6,4},{5,6},{10,8},{9,10},{14,12},{13,14},{3,1},{0,3},... | collective-permute-start | bytes 245768 | tf_op jit(solution)/shard_map/ppermute | solution.py:513
  33.1 2.1 %collective-permute-start.7 = (bf16[320,128]{1,0:T(8,128)(2,1)S(1)}, bf16[320,128]{1,0:T(8,128)(2,1)S(1)}, u32[]{:S(2)}, u32[]{:S(2)}) collective-permute-start(bf16[320,128]{1,0:T(8,128)(2,1)S(1)} %collective-permute-done.6), channel_id=1, source_target_pairs={{0,0},{3,2},{4,4},{7,6},{8,8},{11,10},{12,12},{15,14},{1,1},{2,3},... | collective-permute-start | bytes 245768 | tf_op jit(solution)/shard_map/ppermute | solution.py:512
  41.3 11.5 %collective-permute-start.19 = (f32[8,4,128]{2,1,0:T(4,128)S(1)}, f32[8,4,128]{2,1,0:T(4,128)S(1)}, u32[]{:S(2)}, u32[]{:S(2)}) collective-permute-start(f32[8,4,128]{2,1,0:T(4,128)S(1)} %get-tuple-element.33), channel_id=1, source_target_pairs={{0,0},{2,8},{4,2},{6,10},{8,4},{10,12},{12,6},{14,14},{1,1},{3,9},... | collective-permute-start | bytes 49160 | tf_op jit(solution)/shard_map/ppermute | solution.py:554
  42.0 10.9 %collective-permute-start.20 = (f32[8,4,128]{2,1,0:T(4,128)S(1)}, f32[8,4,128]{2,1,0:T(4,128)S(1)}, u32[]{:S(2)}, u32[]{:S(2)}) collective-permute-start(f32[8,4,128]{2,1,0:T(4,128)S(1)} %get-tuple-element.34), channel_id=1, source_target_pairs={{0,2},{2,10},{4,0},{6,8},{8,6},{10,14},{12,4},{14,12},{1,3},{3,11}... | collective-permute-start | bytes 49160 | tf_op jit(solution)/shard_map/ppermute | solution.py:554
  47.6 5.4 %collective-permute-start.21 = (f32[8,4,128]{2,1,0:T(4,128)S(1)}, f32[8,4,128]{2,1,0:T(4,128)S(1)}, u32[]{:S(2)}, u32[]{:S(2)}) collective-permute-start(f32[8,4,128]{2,1,0:T(4,128)S(1)} %get-tuple-element.35), channel_id=1, source_target_pairs={{0,4},{2,12},{4,6},{6,14},{8,0},{10,8},{12,2},{14,10},{1,5},{3,13}... | collective-permute-start | bytes 49160 | tf_op jit(solution)/shard_map/ppermute | solution.py:554
  49.3 7.4 %collective-permute-start.22 = (f32[8,4,128]{2,1,0:T(4,128)S(1)}, f32[8,4,128]{2,1,0:T(4,128)S(1)}, u32[]{:S(2)}, u32[]{:S(2)}) collective-permute-start(f32[8,4,128]{2,1,0:T(4,128)S(1)} %get-tuple-element.36), channel_id=1, source_target_pairs={{0,6},{2,14},{4,4},{6,12},{8,2},{10,10},{12,0},{14,8},{1,7},{3,15}... | collective-permute-start | bytes 49160 | tf_op jit(solution)/shard_map/ppermute | solution.py:554

commit v9 on v7

--- a/solution.py
+++ b/solution.py
@@ -11,6 +11,7 @@
 LANES = 128
 SUBLANES = 8
 UNROLL = 16
+TAIL = 4
 
 SMEM = pl.BlockSpec(memory_space=pltpu.SMEM)
 VMEM = pl.BlockSpec(memory_space=pltpu.VMEM)
@@ -35,16 +36,15 @@
     ]
 
 
-def column_pass(picture, col_taps, e, square):
+def column_pass(picture, col_tap, taps, e, square):
     tiles = picture.shape[1] // LANES
-    taps = col_taps.shape[1]
     lane = lax.broadcasted_iota(jnp.int32, (SUBLANES, LANES), 1)
     zero = jnp.zeros((SUBLANES, LANES), jnp.float32)
     cut = [picture[:, t * LANES : (t + 1) * LANES] for t in range(tiles)]
     totals = None
     for b in range(taps):
         step = b - taps // 2
-        tap = col_taps[e, b]
+        tap = col_tap(e, b)
         if square:
             tap = tap * tap
         moved = cut
@@ -61,7 +61,7 @@
     return totals
 
 
-def row_pass(colpass, row_taps, e, m, first, taps):
+def row_pass(colpass, row_tap, e, m, first, taps):
     tiles = colpass.shape[1]
     lane = lax.broadcasted_iota(jnp.int32, (SUBLANES, LANES), 1)
     zero = jnp.zeros((SUBLANES, LANES), jnp.float32)
@@ -69,7 +69,7 @@
     for t in range(tiles):
         total = None
         for a in taps:
-            tap = row_taps[e, a]
+            tap = row_tap(e, a)
             if m == 1:
                 tap = tap * tap
             term = tap * colpass[m, t, pl.ds(first + a, SUBLANES)]
@@ -103,6 +103,7 @@
     maps,
     edges,
     params,
+    tap_rows,
     science,
     inv_var,
     row_taps,
@@ -144,17 +145,26 @@
     params[:, 2 * vels : 2 * vels + 1] = kept.astype(jnp.float32)
     parts = rows // SHIFT
 
+    def row_tap(e, a):
+        return row_taps[e, a]
+
+    def col_tap(e, b):
+        return col_taps[e, b]
+
     def one_exposure(e, carry):
+        for a in range(taps):
+            tap_rows[e, a : a + 1] = jnp.full((1, LANES), row_taps[e, a])
+            tap_rows[e, taps + a : taps + a + 1] = jnp.full((1, LANES), col_taps[e, a])
         inverse_all = inv_var[e].astype(jnp.float32)
         product_all = science[e].astype(jnp.float32) * inverse_all
         for g in range(rows // SUBLANES):
             at = slice(g * SUBLANES, (g + 1) * SUBLANES)
             for m, picture in ((0, product_all[at]), (1, inverse_all[at])):
-                for t, total in enumerate(column_pass(picture, col_taps, e, m == 1)):
+                for t, total in enumerate(column_pass(picture, col_tap, taps, e, m == 1)):
                     colpass[m, t, pad + g * SUBLANES : pad + (g + 1) * SUBLANES] = total
         for p in range(parts):
             quarters = [
-                row_pass(colpass, row_taps, e, m, pad + p * SHIFT + h * SUBLANES - radius, range(taps))
+                row_pass(colpass, row_tap, e, m, pad + p * SHIFT + h * SUBLANES - radius, range(taps))
                 for m in (0, 1)
                 for h in (0, 1)
             ]
@@ -170,7 +180,7 @@
 
 
 def outer_kernel(
-    radius, chunks, info, row_taps, col_taps, maps, edges, params, above, below, *rest
+    radius, chunks, info, maps, edges, params, tap_rows, above, below, *rest
 ):
     exposures = params.shape[0]
     tiles = maps.shape[0]
@@ -182,6 +192,12 @@
 
     colpass[...] = jnp.zeros_like(colpass)
 
+    def row_tap(e, a):
+        return tap_rows[e, a : a + 1]
+
+    def col_tap(e, b):
+        return tap_rows[e, taps + b : taps + b + 1]
+
     def one_exposure(e, carry):
         for kind in (0, 1):
             pixels[kind, 0:radius] = jnp.where(has_below, below[kind, e].astype(jnp.float32), 0.0)
@@ -189,10 +205,10 @@
         inverse = pixels[1]
         product = pixels[0] * inverse
         for m, picture in ((0, product), (1, inverse)):
-            for t, total in enumerate(column_pass(picture, col_taps, e, m == 1)):
+            for t, total in enumerate(column_pass(picture, col_tap, taps, e, m == 1)):
                 colpass[m, t, pad : pad + SUBLANES] = total
-        upper = [row_pass(colpass, row_taps, e, m, pad + radius, range(radius)) for m in (0, 1)]
-        lower = [row_pass(colpass, row_taps, e, m, -radius, range(radius + 1, taps)) for m in (0, 1)]
+        upper = [row_pass(colpass, row_tap, e, m, pad + radius, range(radius)) for m in (0, 1)]
+        lower = [row_pass(colpass, row_tap, e, m, -radius, range(radius + 1, taps)) for m in (0, 1)]
         for t in range(tiles):
             for m in (0, 1):
                 more[0, t, 2 * e + m] = upper[m][t]
@@ -270,9 +286,10 @@
     for source in range(total):
         order[filled] = source
         filled = filled + scalars[source, 2 * vels]
-    for i in range(UNROLL):
+    for i in range(TAIL):
         order[filled + i] = total
-    trips = (filled + UNROLL - 1) // UNROLL
+    trips = filled // UNROLL
+    tail_trips = (filled - trips * UNROLL + TAIL - 1) // TAIL
 
     lane = lax.broadcasted_iota(jnp.int32, (rows, LANES), 1)
 
@@ -306,7 +323,12 @@
                 sums = step(t * UNROLL + i, sums)
             return sums
 
-        return lax.fori_loop(0, trips, trip, start)
+        def tail_trip(t, sums):
+            for i in range(TAIL):
+                sums = step(trips * UNROLL + t * TAIL + i, sums)
+            return sums
+
+        return lax.fori_loop(0, tail_trips, tail_trip, lax.fori_loop(0, trips, trip, start))
 
     zeros = main[total, 0, 0:rows]
     none = (zeros, zeros)
@@ -332,34 +354,23 @@
         outs[step][...] = result[:, pl.ds(pl.multiple_of(to * block, block), block)]
 
 
-def columns_kernel(chunks, subs, info, *rest):
-    pieces = rest[:chunks]
-    outs = rest[chunks : chunks + subs]
-    held, wide = rest[chunks + subs :]
+def join_kernel(chunks, subs, info, *rest):
+    pieces = rest[: chunks * subs]
+    out, held = rest[chunks * subs :]
     own_chunk, own_sub = info[2], info[3]
-    for step in range(chunks):
-        held[step] = pieces[step][...]
-    rows = wide.shape[2]
-    for c in range(chunks):
-        piece = held[partner(own_chunk, c, chunks)]
-        for k in range(subs):
-            wide[k, :, :, c * LANES : (c + 1) * LANES] = piece[:, k * rows : (k + 1) * rows]
-    for step in range(subs):
-        outs[step][...] = wide[partner(own_sub, step, subs)]
-
-
-def velocities_kernel(subs, info, *rest):
-    pieces = rest[:subs]
-    out, held = rest[subs:]
-    own_sub = info[3]
-    for step in range(subs):
-        held[step] = pieces[step][...]
-    share = held.shape[1]
+    share, rows = held.shape[2], out.shape[1]
+    for u in range(subs):
+        for step in range(chunks):
+            held[u, step] = pieces[u * chunks + step][...]
     for k in range(subs):
-        out[k * share : (k + 1) * share] = held[partner(own_sub, k, subs)]
-
-
-def per_device(science, inv_var, psf_rows, psf_cols, row_shift, col_shift, exposure_ok):
+        for c in range(chunks):
+            block = held.at[partner(own_sub, k, subs), partner(own_chunk, c, chunks)]
+            for v in range(share):
+                out[k * share + v, :, c * LANES : (c + 1) * LANES] = block[v, pl.ds(own_sub * rows, rows)]
+
+
+def per_device(*arguments):
+    science, inv_var, psf_rows, psf_cols, row_shift, col_shift, exposure_ok = arguments
     exposures, rows, columns = science.shape
     vels = row_shift.shape[1]
     radius = psf_rows.shape[1] // 2
@@ -386,16 +397,18 @@
         below = lax.ppermute(rows_from(0), "strip", [(i + 1, i) for i in range(strips - 1)])
 
     map_rows = parts * exposures * 2 * SHIFT
+    tap_room = -(-2 * psf_rows.shape[1] // SUBLANES) * SUBLANES
     edge_rows = parts * exposures * SUBLANES
-    maps, edges, params = pl.pallas_call(
+    maps, edges, params, tap_rows = pl.pallas_call(
         functools.partial(inner_kernel, radius),
         out_shape=[
             jax.ShapeDtypeStruct((chunks, map_rows, LANES), jnp.float32),
             jax.ShapeDtypeStruct((chunks, edge_rows, LANES), jnp.float32),
             jax.ShapeDtypeStruct((exposures, LANES), jnp.float32),
+            jax.ShapeDtypeStruct((exposures, tap_room, LANES), jnp.float32),
         ],
         in_specs=[HBM] * 7,
-        out_specs=[VMEM] * 3,
+        out_specs=[VMEM] * 4,
         scratch_shapes=[
             pltpu.VMEM(science.shape, science.dtype),
             pltpu.VMEM(inv_var.shape, inv_var.dtype),
@@ -410,7 +423,7 @@
         compiler_params=pltpu.CompilerParams(vmem_limit_bytes=8 << 20),
         cost_estimate=pl.CostEstimate(flops=100_000_000, bytes_accessed=4_000_000, transcendentals=0),
         name="filter_inner",
-    )(*[pltpu.with_memory_space_constraint(x, pltpu.HBM) for x in (science, inv_var, psf_rows, psf_cols, row_shift, col_shift, exposure_ok)])
+    )(*[pltpu.with_memory_space_constraint(x, pltpu.HBM) for x in arguments])
     block = exposures * (2 * SHIFT + SUBLANES)
     sent = [
         jax.ShapeDtypeStruct((block + (exposures if p == parts - 1 else 0), LANES), jnp.bfloat16)
@@ -419,7 +432,7 @@
     sends = pl.pallas_call(
         functools.partial(outer_kernel, radius, chunks),
         out_shape=sent * chunks,
-        in_specs=[SMEM] * 3 + [VMEM] * 5,
+        in_specs=[SMEM] + [VMEM] * 6,
         out_specs=[VMEM] * (chunks * parts),
         scratch_shapes=[
             pltpu.VMEM((2, 2 * radius, columns), jnp.float32),
@@ -429,7 +442,7 @@
         ],
         compiler_params=pltpu.CompilerParams(vmem_limit_bytes=8 << 20),
         name="filter_outer",
-    )(info, psf_rows, psf_cols, maps, edges, params, above, below)
+    )(info, maps, edges, params, tap_rows, above, below)
 
     blocks = [[[None] * chunks for _ in range(subs)] for _ in range(parts + 1)]
     up = [((i + 1) % strips, i) for i in range(strips)]
@@ -473,32 +486,20 @@
     held = [pieces[0]]
     for step in range(1, chunks):
         held.append(lax.ppermute(pieces[step], "expo", chunk_pairs(step, chunks, subs)))
+    groups = [held]
+    for u in range(1, subs):
+        pairs = sub_pairs(u, chunks, subs)
+        groups.append([lax.ppermute(held[step], "expo", pairs) for step in range(chunks)])
     out_rows = block_rows // subs
-    wide = jax.ShapeDtypeStruct((share, out_rows, columns), jnp.float32)
-    parts = pl.pallas_call(
-        functools.partial(columns_kernel, chunks, subs),
-        out_shape=[wide] * subs,
-        in_specs=[SMEM] + [VMEM] * chunks,
-        out_specs=[VMEM] * subs,
-        scratch_shapes=[
-            pltpu.VMEM((chunks, share, block_rows, LANES), jnp.float32),
-            pltpu.VMEM((subs, share, out_rows, columns), jnp.float32),
-        ],
-        compiler_params=pltpu.CompilerParams(vmem_limit_bytes=1 << 20),
-        name="join_columns",
-    )(info, *held)
-    met = [parts[0]]
-    for step in range(1, subs):
-        met.append(lax.ppermute(parts[step], "expo", sub_pairs(step, chunks, subs)))
     likelihood = pl.pallas_call(
-        functools.partial(velocities_kernel, subs),
+        functools.partial(join_kernel, chunks, subs),
         out_shape=jax.ShapeDtypeStruct((vels, out_rows, columns), jnp.float32),
-        in_specs=[SMEM] + [VMEM] * subs,
+        in_specs=[SMEM] + [VMEM] * (chunks * subs),
         out_specs=VMEM,
-        scratch_shapes=[pltpu.VMEM((subs, share, out_rows, columns), jnp.float32)],
-        compiler_params=pltpu.CompilerParams(vmem_limit_bytes=1 << 20),
-        name="join_velocities",
-    )(info, *met)
+        scratch_shapes=[pltpu.VMEM((subs, chunks, share, block_rows, LANES), jnp.float32)],
+        compiler_params=pltpu.CompilerParams(vmem_limit_bytes=2 << 20),
+        name="join_all",
+    )(info, *[block for group in groups for block in group])
     return likelihood[None]
 
 

time: 54.1 us -> 52.7 us (0.974)
  Pallas kernels: 14 us -> 13.3 us
  local copies, waits for them, and re-layouts: 1.66 us -> 0.99 us
  waiting for transfers between devices: 13.6 us -> 13 us
    unnamed x4 -> x0, local copies, waits for them, and re-layouts: 0.67 us -> none
    pallas_call x2 -> x1, Pallas kernels: 1.75 us -> 1.19 us  [per_device(): pl.pallas_call(functools.partial(join_kernel, chunks, subs), out_shape=ja...]
    ppermute x1 -> x4, waiting for transfers between devices: 1.19 us -> 1.17 us  [per_device(): lax.ppermute(held[step], 'expo', pairs)]
  transfers between devices with their start and end apart: 27 -> 30, of which waited for: 12 -> 12; matrix products, arithmetic and copies ran while one was open for 0% -> 0% of each run, Pallas kernels for 9% -> 9%
where the time goes in v9:
time: 52.7 us; the launch traced here: 52.5 us
  starting transfers between devices  25 us (47%)
  Pallas kernels  13.3 us (25%)
  waiting for transfers between devices  13 us (25%)
  local copies, waits for them, and re-layouts  0.99 us (2%)
    ppermute x6, starting transfers between devices, per_device(): lax.ppermute(sends[step * parts + p], 'expo', chunk_pairs(step, chunks, s...  11.5 us
    pallas_call x1, Pallas kernels, per_device(): pl.pallas_call(functools.partial(stack_kernel, groups, chunks, exposures,...  5.28 us
    pallas_call x1, Pallas kernels, per_device(): pl.pallas_call(functools.partial(inner_kernel, radius), out_shape=[jax.Sh...  4.65 us
    ppermute x3, starting transfers between devices, per_device(): lax.ppermute(pieces[step], 'expo', chunk_pairs(step, chunks, subs))  4.45 us
    ppermute x3, waiting for transfers between devices, per_device(): lax.ppermute(pieces[step], 'expo', chunk_pairs(step, chunks, subs))  3.85 us
    ppermute x4, waiting for transfers between devices, per_device(): blocks[parts][0][step] = lax.ppermute(blocks[0][0][step], 'strip', up)  3.75 us
    ppermute x6, waiting for transfers between devices, per_device(): lax.ppermute(sends[step * parts + p], 'expo', chunk_pairs(step, chunks, s...  3.34 us
    ppermute x4, starting transfers between devices, per_device(): blocks[parts][0][step] = lax.ppermute(blocks[0][0][step], 'strip', up)  3.26 us
  transfers between devices with their start and end apart: 30, of which 12 were waited for; matrix products, arithmetic and copies ran while one was open for 0% of the time, Pallas kernels for 9%

profile of v9, /device:TPU:0, one launch (start us, length us, event | category | flops | bytes accessed | tf_op | source)
XLA Modules:
  0.0 52.5 jit_solution(6924876190982096588)
XLA Ops:
  0.0 0.9 %dynamic-slice_bitcast_fusion = (bf16[1,8,4,512]{3,2,1,0:T(4,128)(2,1)S(1)}, bf16[1,8,4,512]{3,2,1,0:T(4,128)(2,1)S(1)}) fusion(bf16[8,32,512]{2,1,0:T(8,128)(2,1)} %inv_var_hbm.1, s32[]{:T(128)S(6)} %select_n.19, bf16[8,32,512]{2,1,0:T(8,128)(2,1)} %science_hbm.1), kind=kLoop, calls=%fused_computation.1 | loop fusion | bytes 131076 | tf_op jit(solution)/shard_map/stack | solution.py:390
  1.0 3.0 %collective-permute-start = (bf16[2,8,4,512]{3,2,1,0:T(4,128)(2,1)S(1)}, bf16[2,8,4,512]{3,2,1,0:T(4,128)(2,1)S(1)}, u32[]{:S(2)}, u32[]{:S(2)}) collective-permute-start(bf16[2,8,4,512]{3,2,1,0:T(4,128)(2,1)S(1)} %pad_maximum_fusion), channel_id=1, source_target_pairs={{0,1},{1,0},{2,3},{3,2},{4,5},{5,4},{6,7},{7,6},{8,9},{9,8},{10,11... | collective-permute-start | bytes 196616 | tf_op jit(solution)/shard_map/ppermute | solution.py:394
  4.0 0.1 stack.40.info
  4.1 4.6 %filter_inner.1 = (f32[4,512,128]{2,1,0:T(8,128)S(1)}, f32[4,128,128]{2,1,0:T(8,128)S(1)}, f32[8,128]{1,0:T(8,128)S(1)}, f32[8,24,128]{2,1,0:T(8,128)S(1)}) custom-call(bf16[8,32,512]{2,1,0:T(8,128)(2,1)} %science_hbm.1, bf16[8,32,512]{2,1,0:T(8,128)(2,1)} %inv_var_hbm.1, f32[8,9]{1,0:T(8,128)} %row_taps_hbm.1, f32[8,9]{1,0:T(8,128)} %col_taps_hbm.1, ...), custom_call_target="tpu_custom_call" | custom-call | flops 100000000 | bytes 4000000 | tf_op jit(solution)/shard_map/filter_inner/pallas_call | solution.py:402
  8.7 2.1 %filter_outer.1 = (bf16[320,128]{1,0:T(8,128)(2,1)S(1)}, bf16[328,128]{1,0:T(8,128)(2,1)S(1)}, bf16[320,128]{1,0:T(8,128)(2,1)S(1)}, bf16[328,128]{1,0:T(8,128)(...) custom-call(s32[5]{0:T(128)S(1)} %stack.40.info, ...), custom_call_target="tpu_custom_call" | custom-call | tf_op jit(solution)/shard_map/filter_outer/pallas_call | solution.py:432
  10.9 1.6 %collective-permute-start.1 = (bf16[320,128]{1,0:T(8,128)(2,1)S(1)}, bf16[320,128]{1,0:T(8,128)(2,1)S(1)}, u32[]{:S(2)}, u32[]{:S(2)}) collective-permute-start(bf16[320,128]{1,0:T(8,128)(2,1)S(1)} %get-tuple-element.26), channel_id=1, source_target_pairs={{0,4},{2,6},{4,0},{6,2},{8,12},{10,14},{12,8},{14,10},{1,5},{3,7},... | collective-permute-start | bytes 245768 | tf_op jit(solution)/shard_map/ppermute | solution.py:453
  12.5 2.6 %collective-permute-start.2 = (bf16[320,128]{1,0:T(8,128)(2,1)S(1)}, bf16[320,128]{1,0:T(8,128)(2,1)S(1)}, u32[]{:S(2)}, u32[]{:S(2)}) collective-permute-start(bf16[320,128]{1,0:T(8,128)(2,1)S(1)} %get-tuple-element.27), channel_id=1, source_target_pairs={{0,8},{2,10},{4,12},{6,14},{8,0},{10,2},{12,4},{14,6},{1,9},{3,11}... | collective-permute-start | bytes 245768 | tf_op jit(solution)/shard_map/ppermute | solution.py:453
  15.1 0.2 collective-permute-start.3
  15.4 0.3 collective-permute-start.15
  15.7 0.9 %collective-permute-start.8 = (bf16[328,128]{1,0:T(8,128)(2,1)S(1)}, bf16[328,128]{1,0:T(8,128)(2,1)S(1)}, u32[]{:S(2)}, u32[]{:S(2)}) collective-permute-start(bf16[328,128]{1,0:T(8,128)(2,1)S(1)} %get-tuple-element.30), channel_id=1, source_target_pairs={{0,4},{2,6},{4,0},{6,2},{8,12},{10,14},{12,8},{14,10},{1,5},{3,7},... | collective-permute-start | bytes 251912 | tf_op jit(solution)/shard_map/ppermute | solution.py:453
  16.6 3.5 %collective-permute-start.9 = (bf16[328,128]{1,0:T(8,128)(2,1)S(1)}, bf16[328,128]{1,0:T(8,128)(2,1)S(1)}, u32[]{:S(2)}, u32[]{:S(2)}) collective-permute-start(bf16[328,128]{1,0:T(8,128)(2,1)S(1)} %get-tuple-element.31), channel_id=1, source_target_pairs={{0,8},{2,10},{4,12},{6,14},{8,0},{10,2},{12,4},{14,6},{1,9},{3,11}... | collective-permute-start | bytes 251912 | tf_op jit(solution)/shard_map/ppermute | solution.py:453
  20.1 2.3 %collective-permute-done.2.rest_2_ = bf16[320,128]{1,0:T(8,128)(2,1)S(1)} collective-permute-done((bf16[320,128]{1,0:T(8,128)(2,1)S(1)}, bf16[320,128]{1,0:T(8,128)(2,1)S(1)}, u32[]{:S(2)}, u32[]{:S(2)}) %collective-permute-start.2) | collective-permute-done | bytes 81952 | tf_op jit(solution)/shard_map/ppermute | solution.py:453
  22.4 0.0 collective-permute-start.4
  22.4 0.0 collective-permute-done.3.rest_3_
  22.4 2.7 %collective-permute-start.10 = (bf16[328,128]{1,0:T(8,128)(2,1)S(1)}, bf16[328,128]{1,0:T(8,128)(2,1)S(1)}, u32[]{:S(2)}, u32[]{:S(2)}) collective-permute-start(bf16[328,128]{1,0:T(8,128)(2,1)S(1)} %get-tuple-element.32), channel_id=1, source_target_pairs={{0,12},{2,14},{4,8},{6,10},{8,4},{10,6},{12,0},{14,2},{1,13},{3,15... | collective-permute-start | bytes 251912 | tf_op jit(solution)/shard_map/ppermute | solution.py:453
  25.1 0.2 collective-permute-start.11
  25.3 0.0 collective-permute-done.4.rest_4_
  25.3 0.5 %collective-permute-start.16 = (bf16[320,128]{1,0:T(8,128)(2,1)S(1)}, bf16[320,128]{1,0:T(8,128)(2,1)S(1)}, u32[]{:S(2)}, u32[]{:S(2)}) collective-permute-start(bf16[320,128]{1,0:T(8,128)(2,1)S(1)} %collective-permute-done.1.rest_1_), channel_id=1, source_target_pairs={{1,0},{0,1},{3,2},{2,3},{5,4},{4,5},{7,6},{6,7},{9,8},{8,9},{11,10... | collective-permute-start | bytes 245768 | tf_op jit(solution)/shard_map/ppermute | solution.py:454
  25.8 0.0 collective-permute-done.8.rest_9_
  25.8 0.0 collective-permute-start.5
  25.9 1.0 %collective-permute-done.9.rest_10_ = bf16[328,128]{1,0:T(8,128)(2,1)S(1)} collective-permute-done((bf16[328,128]{1,0:T(8,128)(2,1)S(1)}, bf16[328,128]{1,0:T(8,128)(2,1)S(1)}, u32[]{:S(2)}, u32[]{:S(2)}) %collective-permute-start.9) | collective-permute-done | bytes 84000 | tf_op jit(solution)/shard_map/ppermute | solution.py:453
  26.8 2.3 %collective-permute-start.17 = (bf16[320,128]{1,0:T(8,128)(2,1)S(1)}, bf16[320,128]{1,0:T(8,128)(2,1)S(1)}, u32[]{:S(2)}, u32[]{:S(2)}) collective-permute-start(bf16[320,128]{1,0:T(8,128)(2,1)S(1)} %collective-permute-done.2.rest_2_), channel_id=1, source_target_pairs={{1,0},{0,1},{3,2},{2,3},{5,4},{4,5},{7,6},{6,7},{9,8},{8,9},{11,10... | collective-permute-start | bytes 245768 | tf_op jit(solution)/shard_map/ppermute | solution.py:454
  29.2 0.0 collective-permute-done.10.rest_11_
  29.2 0.0 collective-permute-start.6
  29.2 0.0 collective-permute-done.11.rest_12_
  29.2 0.1 collective-permute-start.18
  29.3 1.4 %collective-permute-done.16.rest_17_ = bf16[320,128]{1,0:T(8,128)(2,1)S(1)} collective-permute-done((bf16[320,128]{1,0:T(8,128)(2,1)S(1)}, bf16[320,128]{1,0:T(8,128)(2,1)S(1)}, u32[]{:S(2)}, u32[]{:S(2)}) %collective-permute-start.16) | collective-permute-done | bytes 81952 | tf_op jit(solution)/shard_map/ppermute | solution.py:454
  30.6 0.0 collective-permute-done.5.rest_5_
  30.6 0.5 collective-permute-start.7
  31.1 0.7 %collective-permute-done.17.rest_18_ = bf16[320,128]{1,0:T(8,128)(2,1)S(1)} collective-permute-done((bf16[320,128]{1,0:T(8,128)(2,1)S(1)}, bf16[320,128]{1,0:T(8,128)(2,1)S(1)}, u32[]{:S(2)}, u32[]{:S(2)}) %collective-permute-start.17) | collective-permute-done | bytes 81952 | tf_op jit(solution)/shard_map/ppermute | solution.py:454
  31.8 0.5 collective-permute-start.13
  32.4 1.7 %collective-permute-done.18.rest_19_ = bf16[320,128]{1,0:T(8,128)(2,1)S(1)} collective-permute-done((bf16[320,128]{1,0:T(8,128)(2,1)S(1)}, bf16[320,128]{1,0:T(8,128)(2,1)S(1)}, u32[]{:S(2)}, u32[]{:S(2)}) %collective-permute-start.18) | collective-permute-done | bytes 81952 | tf_op jit(solution)/shard_map/ppermute | solution.py:454
  34.0 0.5 collective-permute-start.20
  34.6 0.1 collective-permute-start.21
  34.6 0.4 collective-permute-start.22
  35.1 0.2 collective-permute-done.14.rest_15_
  35.3 0.2 collective-permute-done.20.rest_21_
  35.5 0.4 collective-permute-done.21.rest_22_
  35.8 0.2 collective-permute-done.22.rest_23_
  36.0 5.3 %stack_twice.1 = (f32[4,8,128]{2,1,0:T(8,128)S(1)}, f32[4,8,128]{2,1,0:T(8,128)S(1)}, f32[4,8,128]{2,1,0:T(8,128)S(1)}, f32[4,8,128]{2,1,0:T(8,128)S(1)}) custom-call(s32[5]{0:T(128)S(1)} %stack.40.info, bf16[320,128]{1,0:T(8,128)(2,1)S(1)} %get-tuple-element.25.rest_0_, bf16[320,128]{1,0:T(8,128)(2,1)S(1)} %collective-permute-done.1.rest_1_, ...), custom_call_target="tpu_custom_call" | custom-call | tf_op jit(solution)/shard_map/stack_twice/pallas_call | solution.py:466
  41.3 1.8 %collective-permute-start.23 = (f32[4,8,128]{2,1,0:T(8,128)S(1)}, f32[4,8,128]{2,1,0:T(8,128)S(1)}, u32[]{:S(2)}, u32[]{:S(2)}) collective-permute-start(f32[4,8,128]{2,1,0:T(8,128)S(1)} %get-tuple-element.34), channel_id=1, source_target_pairs={{0,4},{2,6},{4,0},{6,2},{8,12},{10,14},{12,8},{14,10},{1,5},{3,7},... | collective-permute-start | bytes 49160 | tf_op jit(solution)/shard_map/ppermute | solution.py:488
  43.1 1.5 %collective-permute-start.24 = (f32[4,8,128]{2,1,0:T(8,128)S(1)}, f32[4,8,128]{2,1,0:T(8,128)S(1)}, u32[]{:S(2)}, u32[]{:S(2)}) collective-permute-start(f32[4,8,128]{2,1,0:T(8,128)S(1)} %get-tuple-element.35), channel_id=1, source_target_pairs={{0,8},{2,10},{4,12},{6,14},{8,0},{10,2},{12,4},{14,6},{1,9},{3,11}... | collective-permute-start | bytes 49160 | tf_op jit(solution)/shard_map/ppermute | solution.py:488
  44.6 1.2 %collective-permute-start.25 = (f32[4,8,128]{2,1,0:T(8,128)S(1)}, f32[4,8,128]{2,1,0:T(8,128)S(1)}, u32[]{:S(2)}, u32[]{:S(2)}) collective-permute-start(f32[4,8,128]{2,1,0:T(8,128)S(1)} %get-tuple-element.36), channel_id=1, source_target_pairs={{0,12},{2,14},{4,8},{6,10},{8,4},{10,6},{12,0},{14,2},{1,13},{3,15... | collective-permute-start | bytes 49160 | tf_op jit(solution)/shard_map/ppermute | solution.py:488
  45.7 0.5 collective-permute-start.27
  46.2 1.5 %collective-permute-done.24.rest_2_ = f32[4,8,128]{2,1,0:T(8,128)S(1)} collective-permute-done((f32[4,8,128]{2,1,0:T(8,128)S(1)}, f32[4,8,128]{2,1,0:T(8,128)S(1)}, u32[]{:S(2)}, u32[]{:S(2)}) %collective-permute-start.24) | collective-permute-done | bytes 16416 | tf_op jit(solution)/shard_map/ppermute | solution.py:488
  47.7 2.4 %collective-permute-done.25.rest_3_ = f32[4,8,128]{2,1,0:T(8,128)S(1)} collective-permute-done((f32[4,8,128]{2,1,0:T(8,128)S(1)}, f32[4,8,128]{2,1,0:T(8,128)S(1)}, u32[]{:S(2)}, u32[]{:S(2)}) %collective-permute-start.25) | collective-permute-done | bytes 16416 | tf_op jit(solution)/shard_map/ppermute | solution.py:488
  50.1 1.2 %collective-permute-done.29.rest_7_ = f32[4,8,128]{2,1,0:T(8,128)S(1)} collective-permute-done((f32[4,8,128]{2,1,0:T(8,128)S(1)}, f32[4,8,128]{2,1,0:T(8,128)S(1)}, u32[]{:S(2)}, u32[]{:S(2)}) %collective-permute-start.29) | collective-permute-done | bytes 16416 | tf_op jit(solution)/shard_map/ppermute | solution.py:492
  51.3 1.2 %join_all.1 = f32[8,4,512]{2,1,0:T(4,128)} custom-call(s32[5]{0:T(128)S(1)} %stack.40.info, f32[4,8,128]{2,1,0:T(8,128)S(1)} %get-tuple-element.33.rest_0_, f32[4,8,128]{2,1,0:T(8,128)S(1)} %collective-permute-done.23.rest_1_, f32[4,8,128]{2,1,0:T(8,128)S(1)} %collective-permute-done.24.rest_2_, f32[4,8,128]{2,1,0:T(8,128)S(1)} %collective-permute-done.25.rest_3_, ...), custom_call_target="tpu_custom_call" | custom-call | tf_op jit(solution)/shard_map/join_all/pallas_call | solution.py:494
  (19 shorter events, 0.1 us)
Async XLA Ops:
  1.0 7.8 %collective-permute-start = (bf16[2,8,4,512]{3,2,1,0:T(4,128)(2,1)S(1)}, bf16[2,8,4,512]{3,2,1,0:T(4,128)(2,1)S(1)}, u32[]{:S(2)}, u32[]{:S(2)}) collective-permute-start(bf16[2,8,4,512]{3,2,1,0:T(4,128)(2,1)S(1)} %pad_maximum_fusion), channel_id=1, source_target_pairs={{0,1},{1,0},{2,3},{3,2},{4,5},{5,4},{6,7},{7,6},{8,9},{9,8},{10,11... | collective-permute-start | bytes 196616 | tf_op jit(solution)/shard_map/ppermute | solution.py:394
  10.9 5.7 %collective-permute-start.1 = (bf16[320,128]{1,0:T(8,128)(2,1)S(1)}, bf16[320,128]{1,0:T(8,128)(2,1)S(1)}, u32[]{:S(2)}, u32[]{:S(2)}) collective-permute-start(bf16[320,128]{1,0:T(8,128)(2,1)S(1)} %get-tuple-element.26), channel_id=1, source_target_pairs={{0,4},{2,6},{4,0},{6,2},{8,12},{10,14},{12,8},{14,10},{1,5},{3,7},... | collective-permute-start | bytes 245768 | tf_op jit(solution)/shard_map/ppermute | solution.py:453
  12.5 9.9 %collective-permute-start.2 = (bf16[320,128]{1,0:T(8,128)(2,1)S(1)}, bf16[320,128]{1,0:T(8,128)(2,1)S(1)}, u32[]{:S(2)}, u32[]{:S(2)}) collective-permute-start(bf16[320,128]{1,0:T(8,128)(2,1)S(1)} %get-tuple-element.27), channel_id=1, source_target_pairs={{0,8},{2,10},{4,12},{6,14},{8,0},{10,2},{12,4},{14,6},{1,9},{3,11}... | collective-permute-start | bytes 245768 | tf_op jit(solution)/shard_map/ppermute | solution.py:453
  15.1 7.3 %collective-permute-start.3 = (bf16[320,128]{1,0:T(8,128)(2,1)S(1)}, bf16[320,128]{1,0:T(8,128)(2,1)S(1)}, u32[]{:S(2)}, u32[]{:S(2)}) collective-permute-start(bf16[320,128]{1,0:T(8,128)(2,1)S(1)} %get-tuple-element.28), channel_id=1, source_target_pairs={{0,12},{2,14},{4,8},{6,10},{8,4},{10,6},{12,0},{14,2},{1,13},{3,15... | collective-permute-start | bytes 245768 | tf_op jit(solution)/shard_map/ppermute | solution.py:453
  15.4 9.7 %collective-permute-start.15 = (bf16[320,128]{1,0:T(8,128)(2,1)S(1)}, bf16[320,128]{1,0:T(8,128)(2,1)S(1)}, u32[]{:S(2)}, u32[]{:S(2)}) collective-permute-start(bf16[320,128]{1,0:T(8,128)(2,1)S(1)} %get-tuple-element.25.rest_0_), channel_id=1, source_target_pairs={{1,0},{0,1},{3,2},{2,3},{5,4},{4,5},{7,6},{6,7},{9,8},{8,9},{11,10... | collective-permute-start | bytes 245768 | tf_op jit(solution)/shard_map/ppermute | solution.py:454
  15.7 10.2 %collective-permute-start.8 = (bf16[328,128]{1,0:T(8,128)(2,1)S(1)}, bf16[328,128]{1,0:T(8,128)(2,1)S(1)}, u32[]{:S(2)}, u32[]{:S(2)}) collective-permute-start(bf16[328,128]{1,0:T(8,128)(2,1)S(1)} %get-tuple-element.30), channel_id=1, source_target_pairs={{0,4},{2,6},{4,0},{6,2},{8,12},{10,14},{12,8},{14,10},{1,5},{3,7},... | collective-permute-start | bytes 251912 | tf_op jit(solution)/shard_map/ppermute | solution.py:453
  16.6 10.3 %collective-permute-start.9 = (bf16[328,128]{1,0:T(8,128)(2,1)S(1)}, bf16[328,128]{1,0:T(8,128)(2,1)S(1)}, u32[]{:S(2)}, u32[]{:S(2)}) collective-permute-start(bf16[328,128]{1,0:T(8,128)(2,1)S(1)} %get-tuple-element.31), channel_id=1, source_target_pairs={{0,8},{2,10},{4,12},{6,14},{8,0},{10,2},{12,4},{14,6},{1,9},{3,11}... | collective-permute-start | bytes 251912 | tf_op jit(solution)/shard_map/ppermute | solution.py:453
  22.4 2.9 %collective-permute-start.4 = (bf16[320,128]{1,0:T(8,128)(2,1)S(1)}, bf16[320,128]{1,0:T(8,128)(2,1)S(1)}, u32[]{:S(2)}, u32[]{:S(2)}) collective-permute-start(bf16[320,128]{1,0:T(8,128)(2,1)S(1)} %get-tuple-element.25.rest_0_), channel_id=1, source_target_pairs={{0,2},{2,0},{4,6},{6,4},{8,10},{10,8},{12,14},{14,12},{1,3},{3,1},... | collective-permute-start | bytes 245768 | tf_op jit(solution)/shard_map/ppermute | solution.py:458
  22.4 6.8 %collective-permute-start.10 = (bf16[328,128]{1,0:T(8,128)(2,1)S(1)}, bf16[328,128]{1,0:T(8,128)(2,1)S(1)}, u32[]{:S(2)}, u32[]{:S(2)}) collective-permute-start(bf16[328,128]{1,0:T(8,128)(2,1)S(1)} %get-tuple-element.32), channel_id=1, source_target_pairs={{0,12},{2,14},{4,8},{6,10},{8,4},{10,6},{12,0},{14,2},{1,13},{3,15... | collective-permute-start | bytes 251912 | tf_op jit(solution)/shard_map/ppermute | solution.py:453
  25.1 4.1 %collective-permute-start.11 = (bf16[328,128]{1,0:T(8,128)(2,1)S(1)}, bf16[328,128]{1,0:T(8,128)(2,1)S(1)}, u32[]{:S(2)}, u32[]{:S(2)}) collective-permute-start(bf16[328,128]{1,0:T(8,128)(2,1)S(1)} %get-tuple-element.29.rest_8_), channel_id=1, source_target_pairs={{0,2},{2,0},{4,6},{6,4},{8,10},{10,8},{12,14},{14,12},{1,3},{3,1},... | collective-permute-start | bytes 251912 | tf_op jit(solution)/shard_map/ppermute | solution.py:458
  25.3 5.3 %collective-permute-start.16 = (bf16[320,128]{1,0:T(8,128)(2,1)S(1)}, bf16[320,128]{1,0:T(8,128)(2,1)S(1)}, u32[]{:S(2)}, u32[]{:S(2)}) collective-permute-start(bf16[320,128]{1,0:T(8,128)(2,1)S(1)} %collective-permute-done.1.rest_1_), channel_id=1, source_target_pairs={{1,0},{0,1},{3,2},{2,3},{5,4},{4,5},{7,6},{6,7},{9,8},{8,9},{11,10... | collective-permute-start | bytes 245768 | tf_op jit(solution)/shard_map/ppermute | solution.py:454
  25.8 4.8 %collective-permute-start.5 = (bf16[320,128]{1,0:T(8,128)(2,1)S(1)}, bf16[320,128]{1,0:T(8,128)(2,1)S(1)}, u32[]{:S(2)}, u32[]{:S(2)}) collective-permute-start(bf16[320,128]{1,0:T(8,128)(2,1)S(1)} %collective-permute-done.1.rest_1_), channel_id=1, source_target_pairs={{0,2},{2,0},{4,6},{6,4},{8,10},{10,8},{12,14},{14,12},{1,3},{3,1},... | collective-permute-start | bytes 245768 | tf_op jit(solution)/shard_map/ppermute | solution.py:458
  26.8 5.0 %collective-permute-start.17 = (bf16[320,128]{1,0:T(8,128)(2,1)S(1)}, bf16[320,128]{1,0:T(8,128)(2,1)S(1)}, u32[]{:S(2)}, u32[]{:S(2)}) collective-permute-start(bf16[320,128]{1,0:T(8,128)(2,1)S(1)} %collective-permute-done.2.rest_2_), channel_id=1, source_target_pairs={{1,0},{0,1},{3,2},{2,3},{5,4},{4,5},{7,6},{6,7},{9,8},{8,9},{11,10... | collective-permute-start | bytes 245768 | tf_op jit(solution)/shard_map/ppermute | solution.py:454
  29.2 2.7 %collective-permute-start.6 = (bf16[320,128]{1,0:T(8,128)(2,1)S(1)}, bf16[320,128]{1,0:T(8,128)(2,1)S(1)}, u32[]{:S(2)}, u32[]{:S(2)}) collective-permute-start(bf16[320,128]{1,0:T(8,128)(2,1)S(1)} %collective-permute-done.2.rest_2_), channel_id=1, source_target_pairs={{0,2},{2,0},{4,6},{6,4},{8,10},{10,8},{12,14},{14,12},{1,3},{3,1},... | collective-permute-start | bytes 245768 | tf_op jit(solution)/shard_map/ppermute | solution.py:458
  29.2 4.9 %collective-permute-start.18 = (bf16[320,128]{1,0:T(8,128)(2,1)S(1)}, bf16[320,128]{1,0:T(8,128)(2,1)S(1)}, u32[]{:S(2)}, u32[]{:S(2)}) collective-permute-start(bf16[320,128]{1,0:T(8,128)(2,1)S(1)} %collective-permute-done.3.rest_3_), channel_id=1, source_target_pairs={{1,0},{0,1},{3,2},{2,3},{5,4},{4,5},{7,6},{6,7},{9,8},{8,9},{11,10... | collective-permute-start | bytes 245768 | tf_op jit(solution)/shard_map/ppermute | solution.py:454
  30.6 4.0 %collective-permute-start.12 = (bf16[328,128]{1,0:T(8,128)(2,1)S(1)}, bf16[328,128]{1,0:T(8,128)(2,1)S(1)}, u32[]{:S(2)}, u32[]{:S(2)}) collective-permute-start(bf16[328,128]{1,0:T(8,128)(2,1)S(1)} %collective-permute-done.8.rest_9_), channel_id=1, source_target_pairs={{0,2},{2,0},{4,6},{6,4},{8,10},{10,8},{12,14},{14,12},{1,3},{3,1},... | collective-permute-start | bytes 251912 | tf_op jit(solution)/shard_map/ppermute | solution.py:458
  30.6 3.4 %collective-permute-start.7 = (bf16[320,128]{1,0:T(8,128)(2,1)S(1)}, bf16[320,128]{1,0:T(8,128)(2,1)S(1)}, u32[]{:S(2)}, u32[]{:S(2)}) collective-permute-start(bf16[320,128]{1,0:T(8,128)(2,1)S(1)} %collective-permute-done.3.rest_3_), channel_id=1, source_target_pairs={{0,2},{2,0},{4,6},{6,4},{8,10},{10,8},{12,14},{14,12},{1,3},{3,1},... | collective-permute-start | bytes 245768 | tf_op jit(solution)/shard_map/ppermute | solution.py:458
  31.8 2.7 %collective-permute-start.19 = (bf16[320,128]{1,0:T(8,128)(2,1)S(1)}, bf16[320,128]{1,0:T(8,128)(2,1)S(1)}, u32[]{:S(2)}, u32[]{:S(2)}) collective-permute-start(bf16[320,128]{1,0:T(8,128)(2,1)S(1)} %collective-permute-done.15.rest_16_), channel_id=1, source_target_pairs={{0,2},{2,0},{4,6},{6,4},{8,10},{10,8},{12,14},{14,12},{1,3},{3,1},... | collective-permute-start | bytes 245768 | tf_op jit(solution)/shard_map/ppermute | solution.py:458
  31.8 3.2 %collective-permute-start.13 = (bf16[328,128]{1,0:T(8,128)(2,1)S(1)}, bf16[328,128]{1,0:T(8,128)(2,1)S(1)}, u32[]{:S(2)}, u32[]{:S(2)}) collective-permute-start(bf16[328,128]{1,0:T(8,128)(2,1)S(1)} %collective-permute-done.9.rest_10_), channel_id=1, source_target_pairs={{0,2},{2,0},{4,6},{6,4},{8,10},{10,8},{12,14},{14,12},{1,3},{3,1},... | collective-permute-start | bytes 251912 | tf_op jit(solution)/shard_map/ppermute | solution.py:458
  34.0 1.3 %collective-permute-start.14 = (bf16[328,128]{1,0:T(8,128)(2,1)S(1)}, bf16[328,128]{1,0:T(8,128)(2,1)S(1)}, u32[]{:S(2)}, u32[]{:S(2)}) collective-permute-start(bf16[328,128]{1,0:T(8,128)(2,1)S(1)} %collective-permute-done.10.rest_11_), channel_id=1, source_target_pairs={{0,2},{2,0},{4,6},{6,4},{8,10},{10,8},{12,14},{14,12},{1,3},{3,1},... | collective-permute-start | bytes 251912 | tf_op jit(solution)/shard_map/ppermute | solution.py:458
  34.0 1.4 %collective-permute-start.20 = (bf16[320,128]{1,0:T(8,128)(2,1)S(1)}, bf16[320,128]{1,0:T(8,128)(2,1)S(1)}, u32[]{:S(2)}, u32[]{:S(2)}) collective-permute-start(bf16[320,128]{1,0:T(8,128)(2,1)S(1)} %collective-permute-done.16.rest_17_), channel_id=1, source_target_pairs={{0,2},{2,0},{4,6},{6,4},{8,10},{10,8},{12,14},{14,12},{1,3},{3,1},... | collective-permute-start | bytes 245768 | tf_op jit(solution)/shard_map/ppermute | solution.py:458
  34.6 1.3 %collective-permute-start.21 = (bf16[320,128]{1,0:T(8,128)(2,1)S(1)}, bf16[320,128]{1,0:T(8,128)(2,1)S(1)}, u32[]{:S(2)}, u32[]{:S(2)}) collective-permute-start(bf16[320,128]{1,0:T(8,128)(2,1)S(1)} %collective-permute-done.17.rest_18_), channel_id=1, source_target_pairs={{0,2},{2,0},{4,6},{6,4},{8,10},{10,8},{12,14},{14,12},{1,3},{3,1},... | collective-permute-start | bytes 245768 | tf_op jit(solution)/shard_map/ppermute | solution.py:458
  34.6 1.4 %collective-permute-start.22 = (bf16[320,128]{1,0:T(8,128)(2,1)S(1)}, bf16[320,128]{1,0:T(8,128)(2,1)S(1)}, u32[]{:S(2)}, u32[]{:S(2)}) collective-permute-start(bf16[320,128]{1,0:T(8,128)(2,1)S(1)} %collective-permute-done.18.rest_19_), channel_id=1, source_target_pairs={{0,2},{2,0},{4,6},{6,4},{8,10},{10,8},{12,14},{14,12},{1,3},{3,1},... | collective-permute-start | bytes 245768 | tf_op jit(solution)/shard_map/ppermute | solution.py:458
  41.3 4.5 %collective-permute-start.23 = (f32[4,8,128]{2,1,0:T(8,128)S(1)}, f32[4,8,128]{2,1,0:T(8,128)S(1)}, u32[]{:S(2)}, u32[]{:S(2)}) collective-permute-start(f32[4,8,128]{2,1,0:T(8,128)S(1)} %get-tuple-element.34), channel_id=1, source_target_pairs={{0,4},{2,6},{4,0},{6,2},{8,12},{10,14},{12,8},{14,10},{1,5},{3,7},... | collective-permute-start | bytes 49160 | tf_op jit(solution)/shard_map/ppermute | solution.py:488
  43.1 4.6 %collective-permute-start.24 = (f32[4,8,128]{2,1,0:T(8,128)S(1)}, f32[4,8,128]{2,1,0:T(8,128)S(1)}, u32[]{:S(2)}, u32[]{:S(2)}) collective-permute-start(f32[4,8,128]{2,1,0:T(8,128)S(1)} %get-tuple-element.35), channel_id=1, source_target_pairs={{0,8},{2,10},{4,12},{6,14},{8,0},{10,2},{12,4},{14,6},{1,9},{3,11}... | collective-permute-start | bytes 49160 | tf_op jit(solution)/shard_map/ppermute | solution.py:488
  44.6 5.5 %collective-permute-start.25 = (f32[4,8,128]{2,1,0:T(8,128)S(1)}, f32[4,8,128]{2,1,0:T(8,128)S(1)}, u32[]{:S(2)}, u32[]{:S(2)}) collective-permute-start(f32[4,8,128]{2,1,0:T(8,128)S(1)} %get-tuple-element.36), channel_id=1, source_target_pairs={{0,12},{2,14},{4,8},{6,10},{8,4},{10,6},{12,0},{14,2},{1,13},{3,15... | collective-permute-start | bytes 49160 | tf_op jit(solution)/shard_map/ppermute | solution.py:488
  45.7 4.4 %collective-permute-start.26 = (f32[4,8,128]{2,1,0:T(8,128)S(1)}, f32[4,8,128]{2,1,0:T(8,128)S(1)}, u32[]{:S(2)}, u32[]{:S(2)}) collective-permute-start(f32[4,8,128]{2,1,0:T(8,128)S(1)} %get-tuple-element.33.rest_0_), channel_id=1, source_target_pairs={{0,2},{2,0},{4,6},{6,4},{8,10},{10,8},{12,14},{14,12},{1,3},{3,1},... | collective-permute-start | bytes 49160 | tf_op jit(solution)/shard_map/ppermute | solution.py:492
  45.7 4.4 %collective-permute-start.27 = (f32[4,8,128]{2,1,0:T(8,128)S(1)}, f32[4,8,128]{2,1,0:T(8,128)S(1)}, u32[]{:S(2)}, u32[]{:S(2)}) collective-permute-start(f32[4,8,128]{2,1,0:T(8,128)S(1)} %collective-permute-done.23.rest_1_), channel_id=1, source_target_pairs={{0,2},{2,0},{4,6},{6,4},{8,10},{10,8},{12,14},{14,12},{1,3},{3,1},... | collective-permute-start | bytes 49160 | tf_op jit(solution)/shard_map/ppermute | solution.py:492
  47.7 2.4 %collective-permute-start.28 = (f32[4,8,128]{2,1,0:T(8,128)S(1)}, f32[4,8,128]{2,1,0:T(8,128)S(1)}, u32[]{:S(2)}, u32[]{:S(2)}) collective-permute-start(f32[4,8,128]{2,1,0:T(8,128)S(1)} %collective-permute-done.24.rest_2_), channel_id=1, source_target_pairs={{0,2},{2,0},{4,6},{6,4},{8,10},{10,8},{12,14},{14,12},{1,3},{3,1},... | collective-permute-start | bytes 49160 | tf_op jit(solution)/shard_map/ppermute | solution.py:492
  50.1 1.2 %collective-permute-start.29 = (f32[4,8,128]{2,1,0:T(8,128)S(1)}, f32[4,8,128]{2,1,0:T(8,128)S(1)}, u32[]{:S(2)}, u32[]{:S(2)}) collective-permute-start(f32[4,8,128]{2,1,0:T(8,128)S(1)} %collective-permute-done.25.rest_3_), channel_id=1, source_target_pairs={{0,2},{2,0},{4,6},{6,4},{8,10},{10,8},{12,14},{14,12},{1,3},{3,1},... | collective-permute-start | bytes 49160 | tf_op jit(solution)/shard_map/ppermute | solution.py:492

commit v10 on v9

--- a/solution.py
+++ b/solution.py
@@ -10,8 +10,7 @@
 SHIFT = 16
 LANES = 128
 SUBLANES = 8
-UNROLL = 16
-TAIL = 4
+UNROLL = 18
 
 SMEM = pl.BlockSpec(memory_space=pltpu.SMEM)
 VMEM = pl.BlockSpec(memory_space=pltpu.VMEM)
@@ -286,10 +285,9 @@
     for source in range(total):
         order[filled] = source
         filled = filled + scalars[source, 2 * vels]
-    for i in range(TAIL):
+    for i in range(UNROLL):
         order[filled + i] = total
-    trips = filled // UNROLL
-    tail_trips = (filled - trips * UNROLL + TAIL - 1) // TAIL
+    trips = (filled + UNROLL - 1) // UNROLL
 
     lane = lax.broadcasted_iota(jnp.int32, (rows, LANES), 1)
 
@@ -323,12 +321,7 @@
                 sums = step(t * UNROLL + i, sums)
             return sums
 
-        def tail_trip(t, sums):
-            for i in range(TAIL):
-                sums = step(trips * UNROLL + t * TAIL + i, sums)
-            return sums
-
-        return lax.fori_loop(0, tail_trips, tail_trip, lax.fori_loop(0, trips, trip, start))
+        return lax.fori_loop(0, trips, trip, start)
 
     zeros = main[total, 0, 0:rows]
     none = (zeros, zeros)

time: 52.7 us -> 52.9 us (level)
  no operation moved by 1% of the time
where the time goes in v10:
time: 52.9 us; the launch traced here: 52.7 us
  starting transfers between devices  25 us (47%)
  Pallas kernels  13.5 us (26%)
  waiting for transfers between devices  13.1 us (25%)
  local copies, waits for them, and re-layouts  0.99 us (2%)
    ppermute x6, starting transfers between devices, per_device(): lax.ppermute(sends[step * parts + p], 'expo', chunk_pairs(step, chunks, s...  11.5 us
    pallas_call x1, Pallas kernels, per_device(): pl.pallas_call(functools.partial(stack_kernel, groups, chunks, exposures,...  5.55 us
    pallas_call x1, Pallas kernels, per_device(): pl.pallas_call(functools.partial(inner_kernel, radius), out_shape=[jax.Sh...  4.65 us
    ppermute x3, starting transfers between devices, per_device(): lax.ppermute(pieces[step], 'expo', chunk_pairs(step, chunks, subs))  4.45 us
    ppermute x3, waiting for transfers between devices, per_device(): lax.ppermute(pieces[step], 'expo', chunk_pairs(step, chunks, subs))  3.85 us
    ppermute x4, waiting for transfers between devices, per_device(): blocks[parts][0][step] = lax.ppermute(blocks[0][0][step], 'strip', up)  3.75 us
    ppermute x6, waiting for transfers between devices, per_device(): lax.ppermute(sends[step * parts + p], 'expo', chunk_pairs(step, chunks, s...  3.34 us
    ppermute x4, starting transfers between devices, per_device(): blocks[parts][0][step] = lax.ppermute(blocks[0][0][step], 'strip', up)  3.26 us
  transfers between devices with their start and end apart: 30, of which 12 were waited for; matrix products, arithmetic and copies ran while one was open for 0% of the time, Pallas kernels for 9%

profile of v10, /device:TPU:0, one launch (start us, length us, event | category | flops | bytes accessed | tf_op | source)
XLA Modules:
  0.0 52.7 jit_solution(7331584525473346254)
XLA Ops:
  0.0 0.9 %dynamic-slice_bitcast_fusion = (bf16[1,8,4,512]{3,2,1,0:T(4,128)(2,1)S(1)}, bf16[1,8,4,512]{3,2,1,0:T(4,128)(2,1)S(1)}) fusion(bf16[8,32,512]{2,1,0:T(8,128)(2,1)} %inv_var_hbm.1, s32[]{:T(128)S(6)} %select_n.19, bf16[8,32,512]{2,1,0:T(8,128)(2,1)} %science_hbm.1), kind=kLoop, calls=%fused_computation.1 | loop fusion | bytes 131076 | tf_op jit(solution)/shard_map/stack | solution.py:383
  1.0 3.0 %collective-permute-start = (bf16[2,8,4,512]{3,2,1,0:T(4,128)(2,1)S(1)}, bf16[2,8,4,512]{3,2,1,0:T(4,128)(2,1)S(1)}, u32[]{:S(2)}, u32[]{:S(2)}) collective-permute-start(bf16[2,8,4,512]{3,2,1,0:T(4,128)(2,1)S(1)} %pad_maximum_fusion), channel_id=1, source_target_pairs={{0,1},{1,0},{2,3},{3,2},{4,5},{5,4},{6,7},{7,6},{8,9},{9,8},{10,11... | collective-permute-start | bytes 196616 | tf_op jit(solution)/shard_map/ppermute | solution.py:387
  4.0 0.1 stack.40.info
  4.1 4.6 %filter_inner.1 = (f32[4,512,128]{2,1,0:T(8,128)S(1)}, f32[4,128,128]{2,1,0:T(8,128)S(1)}, f32[8,128]{1,0:T(8,128)S(1)}, f32[8,24,128]{2,1,0:T(8,128)S(1)}) custom-call(bf16[8,32,512]{2,1,0:T(8,128)(2,1)} %science_hbm.1, bf16[8,32,512]{2,1,0:T(8,128)(2,1)} %inv_var_hbm.1, f32[8,9]{1,0:T(8,128)} %row_taps_hbm.1, f32[8,9]{1,0:T(8,128)} %col_taps_hbm.1, ...), custom_call_target="tpu_custom_call" | custom-call | flops 100000000 | bytes 4000000 | tf_op jit(solution)/shard_map/filter_inner/pallas_call | solution.py:395
  8.7 2.1 %filter_outer.1 = (bf16[320,128]{1,0:T(8,128)(2,1)S(1)}, bf16[328,128]{1,0:T(8,128)(2,1)S(1)}, bf16[320,128]{1,0:T(8,128)(2,1)S(1)}, bf16[328,128]{1,0:T(8,128)(...) custom-call(s32[5]{0:T(128)S(1)} %stack.40.info, ...), custom_call_target="tpu_custom_call" | custom-call | tf_op jit(solution)/shard_map/filter_outer/pallas_call | solution.py:425
  10.9 1.6 %collective-permute-start.1 = (bf16[320,128]{1,0:T(8,128)(2,1)S(1)}, bf16[320,128]{1,0:T(8,128)(2,1)S(1)}, u32[]{:S(2)}, u32[]{:S(2)}) collective-permute-start(bf16[320,128]{1,0:T(8,128)(2,1)S(1)} %get-tuple-element.26), channel_id=1, source_target_pairs={{0,4},{2,6},{4,0},{6,2},{8,12},{10,14},{12,8},{14,10},{1,5},{3,7},... | collective-permute-start | bytes 245768 | tf_op jit(solution)/shard_map/ppermute | solution.py:446
  12.5 2.6 %collective-permute-start.2 = (bf16[320,128]{1,0:T(8,128)(2,1)S(1)}, bf16[320,128]{1,0:T(8,128)(2,1)S(1)}, u32[]{:S(2)}, u32[]{:S(2)}) collective-permute-start(bf16[320,128]{1,0:T(8,128)(2,1)S(1)} %get-tuple-element.27), channel_id=1, source_target_pairs={{0,8},{2,10},{4,12},{6,14},{8,0},{10,2},{12,4},{14,6},{1,9},{3,11}... | collective-permute-start | bytes 245768 | tf_op jit(solution)/shard_map/ppermute | solution.py:446
  15.1 0.2 collective-permute-start.3
  15.4 0.3 collective-permute-start.15
  15.7 0.9 %collective-permute-start.8 = (bf16[328,128]{1,0:T(8,128)(2,1)S(1)}, bf16[328,128]{1,0:T(8,128)(2,1)S(1)}, u32[]{:S(2)}, u32[]{:S(2)}) collective-permute-start(bf16[328,128]{1,0:T(8,128)(2,1)S(1)} %get-tuple-element.30), channel_id=1, source_target_pairs={{0,4},{2,6},{4,0},{6,2},{8,12},{10,14},{12,8},{14,10},{1,5},{3,7},... | collective-permute-start | bytes 251912 | tf_op jit(solution)/shard_map/ppermute | solution.py:446
  16.6 3.5 %collective-permute-start.9 = (bf16[328,128]{1,0:T(8,128)(2,1)S(1)}, bf16[328,128]{1,0:T(8,128)(2,1)S(1)}, u32[]{:S(2)}, u32[]{:S(2)}) collective-permute-start(bf16[328,128]{1,0:T(8,128)(2,1)S(1)} %get-tuple-element.31), channel_id=1, source_target_pairs={{0,8},{2,10},{4,12},{6,14},{8,0},{10,2},{12,4},{14,6},{1,9},{3,11}... | collective-permute-start | bytes 251912 | tf_op jit(solution)/shard_map/ppermute | solution.py:446
  20.1 2.3 %collective-permute-done.2.rest_2_ = bf16[320,128]{1,0:T(8,128)(2,1)S(1)} collective-permute-done((bf16[320,128]{1,0:T(8,128)(2,1)S(1)}, bf16[320,128]{1,0:T(8,128)(2,1)S(1)}, u32[]{:S(2)}, u32[]{:S(2)}) %collective-permute-start.2) | collective-permute-done | bytes 81952 | tf_op jit(solution)/shard_map/ppermute | solution.py:446
  22.4 0.0 collective-permute-start.4
  22.4 0.0 collective-permute-done.3.rest_3_
  22.4 2.7 %collective-permute-start.10 = (bf16[328,128]{1,0:T(8,128)(2,1)S(1)}, bf16[328,128]{1,0:T(8,128)(2,1)S(1)}, u32[]{:S(2)}, u32[]{:S(2)}) collective-permute-start(bf16[328,128]{1,0:T(8,128)(2,1)S(1)} %get-tuple-element.32), channel_id=1, source_target_pairs={{0,12},{2,14},{4,8},{6,10},{8,4},{10,6},{12,0},{14,2},{1,13},{3,15... | collective-permute-start | bytes 251912 | tf_op jit(solution)/shard_map/ppermute | solution.py:446
  25.1 0.2 collective-permute-start.11
  25.3 0.0 collective-permute-done.4.rest_4_
  25.3 0.5 %collective-permute-start.16 = (bf16[320,128]{1,0:T(8,128)(2,1)S(1)}, bf16[320,128]{1,0:T(8,128)(2,1)S(1)}, u32[]{:S(2)}, u32[]{:S(2)}) collective-permute-start(bf16[320,128]{1,0:T(8,128)(2,1)S(1)} %collective-permute-done.1.rest_1_), channel_id=1, source_target_pairs={{1,0},{0,1},{3,2},{2,3},{5,4},{4,5},{7,6},{6,7},{9,8},{8,9},{11,10... | collective-permute-start | bytes 245768 | tf_op jit(solution)/shard_map/ppermute | solution.py:447
  25.8 0.0 collective-permute-done.8.rest_9_
  25.8 0.0 collective-permute-start.5
  25.9 1.0 %collective-permute-done.9.rest_10_ = bf16[328,128]{1,0:T(8,128)(2,1)S(1)} collective-permute-done((bf16[328,128]{1,0:T(8,128)(2,1)S(1)}, bf16[328,128]{1,0:T(8,128)(2,1)S(1)}, u32[]{:S(2)}, u32[]{:S(2)}) %collective-permute-start.9) | collective-permute-done | bytes 84000 | tf_op jit(solution)/shard_map/ppermute | solution.py:446
  26.8 2.3 %collective-permute-start.17 = (bf16[320,128]{1,0:T(8,128)(2,1)S(1)}, bf16[320,128]{1,0:T(8,128)(2,1)S(1)}, u32[]{:S(2)}, u32[]{:S(2)}) collective-permute-start(bf16[320,128]{1,0:T(8,128)(2,1)S(1)} %collective-permute-done.2.rest_2_), channel_id=1, source_target_pairs={{1,0},{0,1},{3,2},{2,3},{5,4},{4,5},{7,6},{6,7},{9,8},{8,9},{11,10... | collective-permute-start | bytes 245768 | tf_op jit(solution)/shard_map/ppermute | solution.py:447
  29.2 0.0 collective-permute-done.10.rest_11_
  29.2 0.0 collective-permute-start.6
  29.2 0.0 collective-permute-done.11.rest_12_
  29.2 0.1 collective-permute-start.18
  29.3 1.4 %collective-permute-done.16.rest_17_ = bf16[320,128]{1,0:T(8,128)(2,1)S(1)} collective-permute-done((bf16[320,128]{1,0:T(8,128)(2,1)S(1)}, bf16[320,128]{1,0:T(8,128)(2,1)S(1)}, u32[]{:S(2)}, u32[]{:S(2)}) %collective-permute-start.16) | collective-permute-done | bytes 81952 | tf_op jit(solution)/shard_map/ppermute | solution.py:447
  30.6 0.0 collective-permute-done.5.rest_5_
  30.6 0.5 collective-permute-start.7
  31.1 0.7 %collective-permute-done.17.rest_18_ = bf16[320,128]{1,0:T(8,128)(2,1)S(1)} collective-permute-done((bf16[320,128]{1,0:T(8,128)(2,1)S(1)}, bf16[320,128]{1,0:T(8,128)(2,1)S(1)}, u32[]{:S(2)}, u32[]{:S(2)}) %collective-permute-start.17) | collective-permute-done | bytes 81952 | tf_op jit(solution)/shard_map/ppermute | solution.py:447
  31.8 0.5 collective-permute-start.13
  32.4 1.7 %collective-permute-done.18.rest_19_ = bf16[320,128]{1,0:T(8,128)(2,1)S(1)} collective-permute-done((bf16[320,128]{1,0:T(8,128)(2,1)S(1)}, bf16[320,128]{1,0:T(8,128)(2,1)S(1)}, u32[]{:S(2)}, u32[]{:S(2)}) %collective-permute-start.18) | collective-permute-done | bytes 81952 | tf_op jit(solution)/shard_map/ppermute | solution.py:447
  34.0 0.5 collective-permute-start.20
  34.6 0.1 collective-permute-start.21
  34.6 0.4 collective-permute-start.22
  35.1 0.2 collective-permute-done.14.rest_15_
  35.3 0.2 collective-permute-done.20.rest_21_
  35.5 0.4 collective-permute-done.21.rest_22_
  35.8 0.2 collective-permute-done.22.rest_23_
  36.0 5.5 %stack_twice.1 = (f32[4,8,128]{2,1,0:T(8,128)S(1)}, f32[4,8,128]{2,1,0:T(8,128)S(1)}, f32[4,8,128]{2,1,0:T(8,128)S(1)}, f32[4,8,128]{2,1,0:T(8,128)S(1)}) custom-call(s32[5]{0:T(128)S(1)} %stack.40.info, bf16[320,128]{1,0:T(8,128)(2,1)S(1)} %get-tuple-element.25.rest_0_, bf16[320,128]{1,0:T(8,128)(2,1)S(1)} %collective-permute-done.1.rest_1_, ...), custom_call_target="tpu_custom_call" | custom-call | tf_op jit(solution)/shard_map/stack_twice/pallas_call | solution.py:459
  41.6 1.8 %collective-permute-start.23 = (f32[4,8,128]{2,1,0:T(8,128)S(1)}, f32[4,8,128]{2,1,0:T(8,128)S(1)}, u32[]{:S(2)}, u32[]{:S(2)}) collective-permute-start(f32[4,8,128]{2,1,0:T(8,128)S(1)} %get-tuple-element.34), channel_id=1, source_target_pairs={{0,4},{2,6},{4,0},{6,2},{8,12},{10,14},{12,8},{14,10},{1,5},{3,7},... | collective-permute-start | bytes 49160 | tf_op jit(solution)/shard_map/ppermute | solution.py:481
  43.3 1.5 %collective-permute-start.24 = (f32[4,8,128]{2,1,0:T(8,128)S(1)}, f32[4,8,128]{2,1,0:T(8,128)S(1)}, u32[]{:S(2)}, u32[]{:S(2)}) collective-permute-start(f32[4,8,128]{2,1,0:T(8,128)S(1)} %get-tuple-element.35), channel_id=1, source_target_pairs={{0,8},{2,10},{4,12},{6,14},{8,0},{10,2},{12,4},{14,6},{1,9},{3,11}... | collective-permute-start | bytes 49160 | tf_op jit(solution)/shard_map/ppermute | solution.py:481
  44.8 1.2 %collective-permute-start.25 = (f32[4,8,128]{2,1,0:T(8,128)S(1)}, f32[4,8,128]{2,1,0:T(8,128)S(1)}, u32[]{:S(2)}, u32[]{:S(2)}) collective-permute-start(f32[4,8,128]{2,1,0:T(8,128)S(1)} %get-tuple-element.36), channel_id=1, source_target_pairs={{0,12},{2,14},{4,8},{6,10},{8,4},{10,6},{12,0},{14,2},{1,13},{3,15... | collective-permute-start | bytes 49160 | tf_op jit(solution)/shard_map/ppermute | solution.py:481
  46.0 0.5 collective-permute-start.27
  46.5 1.5 %collective-permute-done.24.rest_2_ = f32[4,8,128]{2,1,0:T(8,128)S(1)} collective-permute-done((f32[4,8,128]{2,1,0:T(8,128)S(1)}, f32[4,8,128]{2,1,0:T(8,128)S(1)}, u32[]{:S(2)}, u32[]{:S(2)}) %collective-permute-start.24) | collective-permute-done | bytes 16416 | tf_op jit(solution)/shard_map/ppermute | solution.py:481
  48.0 2.4 %collective-permute-done.25.rest_3_ = f32[4,8,128]{2,1,0:T(8,128)S(1)} collective-permute-done((f32[4,8,128]{2,1,0:T(8,128)S(1)}, f32[4,8,128]{2,1,0:T(8,128)S(1)}, u32[]{:S(2)}, u32[]{:S(2)}) %collective-permute-start.25) | collective-permute-done | bytes 16416 | tf_op jit(solution)/shard_map/ppermute | solution.py:481
  50.4 1.2 %collective-permute-done.29.rest_7_ = f32[4,8,128]{2,1,0:T(8,128)S(1)} collective-permute-done((f32[4,8,128]{2,1,0:T(8,128)S(1)}, f32[4,8,128]{2,1,0:T(8,128)S(1)}, u32[]{:S(2)}, u32[]{:S(2)}) %collective-permute-start.29) | collective-permute-done | bytes 16416 | tf_op jit(solution)/shard_map/ppermute | solution.py:485
  51.6 1.2 %join_all.1 = f32[8,4,512]{2,1,0:T(4,128)} custom-call(s32[5]{0:T(128)S(1)} %stack.40.info, f32[4,8,128]{2,1,0:T(8,128)S(1)} %get-tuple-element.33.rest_0_, f32[4,8,128]{2,1,0:T(8,128)S(1)} %collective-permute-done.23.rest_1_, f32[4,8,128]{2,1,0:T(8,128)S(1)} %collective-permute-done.24.rest_2_, f32[4,8,128]{2,1,0:T(8,128)S(1)} %collective-permute-done.25.rest_3_, ...), custom_call_target="tpu_custom_call" | custom-call | tf_op jit(solution)/shard_map/join_all/pallas_call | solution.py:487
  (19 shorter events, 0.1 us)
Async XLA Ops:
  1.0 7.8 %collective-permute-start = (bf16[2,8,4,512]{3,2,1,0:T(4,128)(2,1)S(1)}, bf16[2,8,4,512]{3,2,1,0:T(4,128)(2,1)S(1)}, u32[]{:S(2)}, u32[]{:S(2)}) collective-permute-start(bf16[2,8,4,512]{3,2,1,0:T(4,128)(2,1)S(1)} %pad_maximum_fusion), channel_id=1, source_target_pairs={{0,1},{1,0},{2,3},{3,2},{4,5},{5,4},{6,7},{7,6},{8,9},{9,8},{10,11... | collective-permute-start | bytes 196616 | tf_op jit(solution)/shard_map/ppermute | solution.py:387
  10.9 5.7 %collective-permute-start.1 = (bf16[320,128]{1,0:T(8,128)(2,1)S(1)}, bf16[320,128]{1,0:T(8,128)(2,1)S(1)}, u32[]{:S(2)}, u32[]{:S(2)}) collective-permute-start(bf16[320,128]{1,0:T(8,128)(2,1)S(1)} %get-tuple-element.26), channel_id=1, source_target_pairs={{0,4},{2,6},{4,0},{6,2},{8,12},{10,14},{12,8},{14,10},{1,5},{3,7},... | collective-permute-start | bytes 245768 | tf_op jit(solution)/shard_map/ppermute | solution.py:446
  12.5 9.9 %collective-permute-start.2 = (bf16[320,128]{1,0:T(8,128)(2,1)S(1)}, bf16[320,128]{1,0:T(8,128)(2,1)S(1)}, u32[]{:S(2)}, u32[]{:S(2)}) collective-permute-start(bf16[320,128]{1,0:T(8,128)(2,1)S(1)} %get-tuple-element.27), channel_id=1, source_target_pairs={{0,8},{2,10},{4,12},{6,14},{8,0},{10,2},{12,4},{14,6},{1,9},{3,11}... | collective-permute-start | bytes 245768 | tf_op jit(solution)/shard_map/ppermute | solution.py:446
  15.1 7.3 %collective-permute-start.3 = (bf16[320,128]{1,0:T(8,128)(2,1)S(1)}, bf16[320,128]{1,0:T(8,128)(2,1)S(1)}, u32[]{:S(2)}, u32[]{:S(2)}) collective-permute-start(bf16[320,128]{1,0:T(8,128)(2,1)S(1)} %get-tuple-element.28), channel_id=1, source_target_pairs={{0,12},{2,14},{4,8},{6,10},{8,4},{10,6},{12,0},{14,2},{1,13},{3,15... | collective-permute-start | bytes 245768 | tf_op jit(solution)/shard_map/ppermute | solution.py:446
  15.4 9.7 %collective-permute-start.15 = (bf16[320,128]{1,0:T(8,128)(2,1)S(1)}, bf16[320,128]{1,0:T(8,128)(2,1)S(1)}, u32[]{:S(2)}, u32[]{:S(2)}) collective-permute-start(bf16[320,128]{1,0:T(8,128)(2,1)S(1)} %get-tuple-element.25.rest_0_), channel_id=1, source_target_pairs={{1,0},{0,1},{3,2},{2,3},{5,4},{4,5},{7,6},{6,7},{9,8},{8,9},{11,10... | collective-permute-start | bytes 245768 | tf_op jit(solution)/shard_map/ppermute | solution.py:447
  15.7 10.2 %collective-permute-start.8 = (bf16[328,128]{1,0:T(8,128)(2,1)S(1)}, bf16[328,128]{1,0:T(8,128)(2,1)S(1)}, u32[]{:S(2)}, u32[]{:S(2)}) collective-permute-start(bf16[328,128]{1,0:T(8,128)(2,1)S(1)} %get-tuple-element.30), channel_id=1, source_target_pairs={{0,4},{2,6},{4,0},{6,2},{8,12},{10,14},{12,8},{14,10},{1,5},{3,7},... | collective-permute-start | bytes 251912 | tf_op jit(solution)/shard_map/ppermute | solution.py:446
  16.6 10.3 %collective-permute-start.9 = (bf16[328,128]{1,0:T(8,128)(2,1)S(1)}, bf16[328,128]{1,0:T(8,128)(2,1)S(1)}, u32[]{:S(2)}, u32[]{:S(2)}) collective-permute-start(bf16[328,128]{1,0:T(8,128)(2,1)S(1)} %get-tuple-element.31), channel_id=1, source_target_pairs={{0,8},{2,10},{4,12},{6,14},{8,0},{10,2},{12,4},{14,6},{1,9},{3,11}... | collective-permute-start | bytes 251912 | tf_op jit(solution)/shard_map/ppermute | solution.py:446
  22.4 2.9 %collective-permute-start.4 = (bf16[320,128]{1,0:T(8,128)(2,1)S(1)}, bf16[320,128]{1,0:T(8,128)(2,1)S(1)}, u32[]{:S(2)}, u32[]{:S(2)}) collective-permute-start(bf16[320,128]{1,0:T(8,128)(2,1)S(1)} %get-tuple-element.25.rest_0_), channel_id=1, source_target_pairs={{0,2},{2,0},{4,6},{6,4},{8,10},{10,8},{12,14},{14,12},{1,3},{3,1},... | collective-permute-start | bytes 245768 | tf_op jit(solution)/shard_map/ppermute | solution.py:451
  22.4 6.8 %collective-permute-start.10 = (bf16[328,128]{1,0:T(8,128)(2,1)S(1)}, bf16[328,128]{1,0:T(8,128)(2,1)S(1)}, u32[]{:S(2)}, u32[]{:S(2)}) collective-permute-start(bf16[328,128]{1,0:T(8,128)(2,1)S(1)} %get-tuple-element.32), channel_id=1, source_target_pairs={{0,12},{2,14},{4,8},{6,10},{8,4},{10,6},{12,0},{14,2},{1,13},{3,15... | collective-permute-start | bytes 251912 | tf_op jit(solution)/shard_map/ppermute | solution.py:446
  25.1 4.1 %collective-permute-start.11 = (bf16[328,128]{1,0:T(8,128)(2,1)S(1)}, bf16[328,128]{1,0:T(8,128)(2,1)S(1)}, u32[]{:S(2)}, u32[]{:S(2)}) collective-permute-start(bf16[328,128]{1,0:T(8,128)(2,1)S(1)} %get-tuple-element.29.rest_8_), channel_id=1, source_target_pairs={{0,2},{2,0},{4,6},{6,4},{8,10},{10,8},{12,14},{14,12},{1,3},{3,1},... | collective-permute-start | bytes 251912 | tf_op jit(solution)/shard_map/ppermute | solution.py:451
  25.3 5.3 %collective-permute-start.16 = (bf16[320,128]{1,0:T(8,128)(2,1)S(1)}, bf16[320,128]{1,0:T(8,128)(2,1)S(1)}, u32[]{:S(2)}, u32[]{:S(2)}) collective-permute-start(bf16[320,128]{1,0:T(8,128)(2,1)S(1)} %collective-permute-done.1.rest_1_), channel_id=1, source_target_pairs={{1,0},{0,1},{3,2},{2,3},{5,4},{4,5},{7,6},{6,7},{9,8},{8,9},{11,10... | collective-permute-start | bytes 245768 | tf_op jit(solution)/shard_map/ppermute | solution.py:447
  25.8 4.8 %collective-permute-start.5 = (bf16[320,128]{1,0:T(8,128)(2,1)S(1)}, bf16[320,128]{1,0:T(8,128)(2,1)S(1)}, u32[]{:S(2)}, u32[]{:S(2)}) collective-permute-start(bf16[320,128]{1,0:T(8,128)(2,1)S(1)} %collective-permute-done.1.rest_1_), channel_id=1, source_target_pairs={{0,2},{2,0},{4,6},{6,4},{8,10},{10,8},{12,14},{14,12},{1,3},{3,1},... | collective-permute-start | bytes 245768 | tf_op jit(solution)/shard_map/ppermute | solution.py:451
  26.8 5.0 %collective-permute-start.17 = (bf16[320,128]{1,0:T(8,128)(2,1)S(1)}, bf16[320,128]{1,0:T(8,128)(2,1)S(1)}, u32[]{:S(2)}, u32[]{:S(2)}) collective-permute-start(bf16[320,128]{1,0:T(8,128)(2,1)S(1)} %collective-permute-done.2.rest_2_), channel_id=1, source_target_pairs={{1,0},{0,1},{3,2},{2,3},{5,4},{4,5},{7,6},{6,7},{9,8},{8,9},{11,10... | collective-permute-start | bytes 245768 | tf_op jit(solution)/shard_map/ppermute | solution.py:447
  29.2 2.7 %collective-permute-start.6 = (bf16[320,128]{1,0:T(8,128)(2,1)S(1)}, bf16[320,128]{1,0:T(8,128)(2,1)S(1)}, u32[]{:S(2)}, u32[]{:S(2)}) collective-permute-start(bf16[320,128]{1,0:T(8,128)(2,1)S(1)} %collective-permute-done.2.rest_2_), channel_id=1, source_target_pairs={{0,2},{2,0},{4,6},{6,4},{8,10},{10,8},{12,14},{14,12},{1,3},{3,1},... | collective-permute-start | bytes 245768 | tf_op jit(solution)/shard_map/ppermute | solution.py:451
  29.2 4.9 %collective-permute-start.18 = (bf16[320,128]{1,0:T(8,128)(2,1)S(1)}, bf16[320,128]{1,0:T(8,128)(2,1)S(1)}, u32[]{:S(2)}, u32[]{:S(2)}) collective-permute-start(bf16[320,128]{1,0:T(8,128)(2,1)S(1)} %collective-permute-done.3.rest_3_), channel_id=1, source_target_pairs={{1,0},{0,1},{3,2},{2,3},{5,4},{4,5},{7,6},{6,7},{9,8},{8,9},{11,10... | collective-permute-start | bytes 245768 | tf_op jit(solution)/shard_map/ppermute | solution.py:447
  30.6 4.0 %collective-permute-start.12 = (bf16[328,128]{1,0:T(8,128)(2,1)S(1)}, bf16[328,128]{1,0:T(8,128)(2,1)S(1)}, u32[]{:S(2)}, u32[]{:S(2)}) collective-permute-start(bf16[328,128]{1,0:T(8,128)(2,1)S(1)} %collective-permute-done.8.rest_9_), channel_id=1, source_target_pairs={{0,2},{2,0},{4,6},{6,4},{8,10},{10,8},{12,14},{14,12},{1,3},{3,1},... | collective-permute-start | bytes 251912 | tf_op jit(solution)/shard_map/ppermute | solution.py:451
  30.6 3.4 %collective-permute-start.7 = (bf16[320,128]{1,0:T(8,128)(2,1)S(1)}, bf16[320,128]{1,0:T(8,128)(2,1)S(1)}, u32[]{:S(2)}, u32[]{:S(2)}) collective-permute-start(bf16[320,128]{1,0:T(8,128)(2,1)S(1)} %collective-permute-done.3.rest_3_), channel_id=1, source_target_pairs={{0,2},{2,0},{4,6},{6,4},{8,10},{10,8},{12,14},{14,12},{1,3},{3,1},... | collective-permute-start | bytes 245768 | tf_op jit(solution)/shard_map/ppermute | solution.py:451
  31.8 2.7 %collective-permute-start.19 = (bf16[320,128]{1,0:T(8,128)(2,1)S(1)}, bf16[320,128]{1,0:T(8,128)(2,1)S(1)}, u32[]{:S(2)}, u32[]{:S(2)}) collective-permute-start(bf16[320,128]{1,0:T(8,128)(2,1)S(1)} %collective-permute-done.15.rest_16_), channel_id=1, source_target_pairs={{0,2},{2,0},{4,6},{6,4},{8,10},{10,8},{12,14},{14,12},{1,3},{3,1},... | collective-permute-start | bytes 245768 | tf_op jit(solution)/shard_map/ppermute | solution.py:451
  31.8 3.2 %collective-permute-start.13 = (bf16[328,128]{1,0:T(8,128)(2,1)S(1)}, bf16[328,128]{1,0:T(8,128)(2,1)S(1)}, u32[]{:S(2)}, u32[]{:S(2)}) collective-permute-start(bf16[328,128]{1,0:T(8,128)(2,1)S(1)} %collective-permute-done.9.rest_10_), channel_id=1, source_target_pairs={{0,2},{2,0},{4,6},{6,4},{8,10},{10,8},{12,14},{14,12},{1,3},{3,1},... | collective-permute-start | bytes 251912 | tf_op jit(solution)/shard_map/ppermute | solution.py:451
  34.0 1.3 %collective-permute-start.14 = (bf16[328,128]{1,0:T(8,128)(2,1)S(1)}, bf16[328,128]{1,0:T(8,128)(2,1)S(1)}, u32[]{:S(2)}, u32[]{:S(2)}) collective-permute-start(bf16[328,128]{1,0:T(8,128)(2,1)S(1)} %collective-permute-done.10.rest_11_), channel_id=1, source_target_pairs={{0,2},{2,0},{4,6},{6,4},{8,10},{10,8},{12,14},{14,12},{1,3},{3,1},... | collective-permute-start | bytes 251912 | tf_op jit(solution)/shard_map/ppermute | solution.py:451
  34.0 1.4 %collective-permute-start.20 = (bf16[320,128]{1,0:T(8,128)(2,1)S(1)}, bf16[320,128]{1,0:T(8,128)(2,1)S(1)}, u32[]{:S(2)}, u32[]{:S(2)}) collective-permute-start(bf16[320,128]{1,0:T(8,128)(2,1)S(1)} %collective-permute-done.16.rest_17_), channel_id=1, source_target_pairs={{0,2},{2,0},{4,6},{6,4},{8,10},{10,8},{12,14},{14,12},{1,3},{3,1},... | collective-permute-start | bytes 245768 | tf_op jit(solution)/shard_map/ppermute | solution.py:451
  34.6 1.3 %collective-permute-start.21 = (bf16[320,128]{1,0:T(8,128)(2,1)S(1)}, bf16[320,128]{1,0:T(8,128)(2,1)S(1)}, u32[]{:S(2)}, u32[]{:S(2)}) collective-permute-start(bf16[320,128]{1,0:T(8,128)(2,1)S(1)} %collective-permute-done.17.rest_18_), channel_id=1, source_target_pairs={{0,2},{2,0},{4,6},{6,4},{8,10},{10,8},{12,14},{14,12},{1,3},{3,1},... | collective-permute-start | bytes 245768 | tf_op jit(solution)/shard_map/ppermute | solution.py:451
  34.6 1.4 %collective-permute-start.22 = (bf16[320,128]{1,0:T(8,128)(2,1)S(1)}, bf16[320,128]{1,0:T(8,128)(2,1)S(1)}, u32[]{:S(2)}, u32[]{:S(2)}) collective-permute-start(bf16[320,128]{1,0:T(8,128)(2,1)S(1)} %collective-permute-done.18.rest_19_), channel_id=1, source_target_pairs={{0,2},{2,0},{4,6},{6,4},{8,10},{10,8},{12,14},{14,12},{1,3},{3,1},... | collective-permute-start | bytes 245768 | tf_op jit(solution)/shard_map/ppermute | solution.py:451
  41.6 4.5 %collective-permute-start.23 = (f32[4,8,128]{2,1,0:T(8,128)S(1)}, f32[4,8,128]{2,1,0:T(8,128)S(1)}, u32[]{:S(2)}, u32[]{:S(2)}) collective-permute-start(f32[4,8,128]{2,1,0:T(8,128)S(1)} %get-tuple-element.34), channel_id=1, source_target_pairs={{0,4},{2,6},{4,0},{6,2},{8,12},{10,14},{12,8},{14,10},{1,5},{3,7},... | collective-permute-start | bytes 49160 | tf_op jit(solution)/shard_map/ppermute | solution.py:481
  43.3 4.6 %collective-permute-start.24 = (f32[4,8,128]{2,1,0:T(8,128)S(1)}, f32[4,8,128]{2,1,0:T(8,128)S(1)}, u32[]{:S(2)}, u32[]{:S(2)}) collective-permute-start(f32[4,8,128]{2,1,0:T(8,128)S(1)} %get-tuple-element.35), channel_id=1, source_target_pairs={{0,8},{2,10},{4,12},{6,14},{8,0},{10,2},{12,4},{14,6},{1,9},{3,11}... | collective-permute-start | bytes 49160 | tf_op jit(solution)/shard_map/ppermute | solution.py:481
  44.8 5.5 %collective-permute-start.25 = (f32[4,8,128]{2,1,0:T(8,128)S(1)}, f32[4,8,128]{2,1,0:T(8,128)S(1)}, u32[]{:S(2)}, u32[]{:S(2)}) collective-permute-start(f32[4,8,128]{2,1,0:T(8,128)S(1)} %get-tuple-element.36), channel_id=1, source_target_pairs={{0,12},{2,14},{4,8},{6,10},{8,4},{10,6},{12,0},{14,2},{1,13},{3,15... | collective-permute-start | bytes 49160 | tf_op jit(solution)/shard_map/ppermute | solution.py:481
  46.0 4.4 %collective-permute-start.26 = (f32[4,8,128]{2,1,0:T(8,128)S(1)}, f32[4,8,128]{2,1,0:T(8,128)S(1)}, u32[]{:S(2)}, u32[]{:S(2)}) collective-permute-start(f32[4,8,128]{2,1,0:T(8,128)S(1)} %get-tuple-element.33.rest_0_), channel_id=1, source_target_pairs={{0,2},{2,0},{4,6},{6,4},{8,10},{10,8},{12,14},{14,12},{1,3},{3,1},... | collective-permute-start | bytes 49160 | tf_op jit(solution)/shard_map/ppermute | solution.py:485
  46.0 4.4 %collective-permute-start.27 = (f32[4,8,128]{2,1,0:T(8,128)S(1)}, f32[4,8,128]{2,1,0:T(8,128)S(1)}, u32[]{:S(2)}, u32[]{:S(2)}) collective-permute-start(f32[4,8,128]{2,1,0:T(8,128)S(1)} %collective-permute-done.23.rest_1_), channel_id=1, source_target_pairs={{0,2},{2,0},{4,6},{6,4},{8,10},{10,8},{12,14},{14,12},{1,3},{3,1},... | collective-permute-start | bytes 49160 | tf_op jit(solution)/shard_map/ppermute | solution.py:485
  48.0 2.4 %collective-permute-start.28 = (f32[4,8,128]{2,1,0:T(8,128)S(1)}, f32[4,8,128]{2,1,0:T(8,128)S(1)}, u32[]{:S(2)}, u32[]{:S(2)}) collective-permute-start(f32[4,8,128]{2,1,0:T(8,128)S(1)} %collective-permute-done.24.rest_2_), channel_id=1, source_target_pairs={{0,2},{2,0},{4,6},{6,4},{8,10},{10,8},{12,14},{14,12},{1,3},{3,1},... | collective-permute-start | bytes 49160 | tf_op jit(solution)/shard_map/ppermute | solution.py:485
  50.4 1.2 %collective-permute-start.29 = (f32[4,8,128]{2,1,0:T(8,128)S(1)}, f32[4,8,128]{2,1,0:T(8,128)S(1)}, u32[]{:S(2)}, u32[]{:S(2)}) collective-permute-start(f32[4,8,128]{2,1,0:T(8,128)S(1)} %collective-permute-done.25.rest_3_), channel_id=1, source_target_pairs={{0,2},{2,0},{4,6},{6,4},{8,10},{10,8},{12,14},{14,12},{1,3},{3,1},... | collective-permute-start | bytes 49160 | tf_op jit(solution)/shard_map/ppermute | solution.py:485

commit v11 on v10

--- a/solution.py
+++ b/solution.py
@@ -12,9 +12,16 @@
 SUBLANES = 8
 UNROLL = 18
 
-SMEM = pl.BlockSpec(memory_space=pltpu.SMEM)
 VMEM = pl.BlockSpec(memory_space=pltpu.VMEM)
 HBM = pl.BlockSpec(memory_space=pltpu.HBM)
+
+
+def whereabouts(subs, first_share):
+    strip, strips = lax.axis_index("strip"), lax.axis_size("strip")
+    me = lax.axis_index("expo")
+    chunk = lax.div(me, subs)
+    sub = lax.rem(me, subs)
+    return strip > 0, strip < strips - 1, chunk, sub, sub * first_share
 
 
 def partner(index, step, count):
@@ -179,7 +186,7 @@
 
 
 def outer_kernel(
-    radius, chunks, info, maps, edges, params, tap_rows, above, below, *rest
+    radius, chunks, subs, maps, edges, params, tap_rows, above, below, *rest
 ):
     exposures = params.shape[0]
     tiles = maps.shape[0]
@@ -187,7 +194,7 @@
     sends, (pixels, colpass, more, more_edges) = rest[: chunks * parts], rest[chunks * parts :]
     taps = 2 * radius + 1
     pad = SUBLANES
-    has_above, has_below, own = info[0] > 0, info[1] > 0, info[2]
+    has_above, has_below, own, _, _ = whereabouts(subs, 0)
 
     colpass[...] = jnp.zeros_like(colpass)
 
@@ -241,16 +248,16 @@
                 out[tail : tail + exposures] = params[...].astype(jnp.bfloat16)
 
 
-def stack_kernel(groups, chunks, exposures, rows, vels, info, *rest):
+def stack_kernel(groups, chunks, subs, exposures, rows, vels, *rest):
     parts = rows // SHIFT
     blocks = [rest[p * groups : (p + 1) * groups] for p in range(parts + 1)]
     rest = rest[(parts + 1) * groups :]
     outs = rest[:chunks]
     main, side, even, odd, whole_params, scalars, order, result, sem = rest[chunks:]
     windows = (even, odd)
-    own = info[2]
-    first_vel = info[4]
     share = result.shape[0]
+    _, has_below, own, _, first_vel = whereabouts(subs, share)
+    has_below = has_below.astype(jnp.float32)
     main_rows = exposures * 2 * SHIFT
     size = main_rows + exposures * SUBLANES
     total = groups * exposures
@@ -261,7 +268,6 @@
         )
     fetch = pltpu.make_async_copy(whole_params, scalars, sem)
     fetch.start()
-    has_below = info[1].astype(jnp.float32)
     for g in range(groups):
         for p in range(parts + 1):
             packed = blocks[p][g][main_rows:size]
@@ -347,10 +353,10 @@
         outs[step][...] = result[:, pl.ds(pl.multiple_of(to * block, block), block)]
 
 
-def join_kernel(chunks, subs, info, *rest):
+def join_kernel(chunks, subs, *rest):
     pieces = rest[: chunks * subs]
     out, held = rest[chunks * subs :]
-    own_chunk, own_sub = info[2], info[3]
+    _, _, own_chunk, own_sub, _ = whereabouts(subs, 0)
     share, rows = held.shape[2], out.shape[1]
     for u in range(subs):
         for step in range(chunks):
@@ -374,10 +380,6 @@
     share = vels // subs
     parts = rows // SHIFT
     strip = lax.axis_index("strip")
-    me = lax.axis_index("expo")
-    own_chunk = me // subs
-    own_sub = me % subs
-    info = jnp.stack([strip > 0, strip < strips - 1, own_chunk, own_sub, own_sub * share]).astype(jnp.int32)
 
     def rows_from(start):
         return jnp.stack([lax.dynamic_slice_in_dim(x, start, radius, 1) for x in (science, inv_var)])
@@ -423,9 +425,9 @@
         for p in range(parts)
     ]
     sends = pl.pallas_call(
-        functools.partial(outer_kernel, radius, chunks),
+        functools.partial(outer_kernel, radius, chunks, subs),
         out_shape=sent * chunks,
-        in_specs=[SMEM] + [VMEM] * 6,
+        in_specs=[VMEM] * 6,
         out_specs=[VMEM] * (chunks * parts),
         scratch_shapes=[
             pltpu.VMEM((2, 2 * radius, columns), jnp.float32),
@@ -435,7 +437,7 @@
         ],
         compiler_params=pltpu.CompilerParams(vmem_limit_bytes=8 << 20),
         name="filter_outer",
-    )(info, maps, edges, params, tap_rows, above, below)
+    )(maps, edges, params, tap_rows, above, below)
 
     blocks = [[[None] * chunks for _ in range(subs)] for _ in range(parts + 1)]
     up = [((i + 1) % strips, i) for i in range(strips)]
@@ -457,9 +459,9 @@
     piece = jax.ShapeDtypeStruct((share, block_rows, LANES), jnp.float32)
     total = groups * exposures
     pieces = pl.pallas_call(
-        functools.partial(stack_kernel, groups, chunks, exposures, rows, vels),
+        functools.partial(stack_kernel, groups, chunks, subs, exposures, rows, vels),
         out_shape=[piece] * chunks,
-        in_specs=[SMEM] + [VMEM] * ((parts + 1) * groups),
+        in_specs=[VMEM] * ((parts + 1) * groups),
         out_specs=[VMEM] * chunks,
         scratch_shapes=[
             pltpu.VMEM((total + 1, 2, reach, LANES), jnp.float32),
@@ -474,7 +476,7 @@
         ],
         compiler_params=pltpu.CompilerParams(vmem_limit_bytes=24 << 20),
         name="stack_twice",
-    )(info, *[block for part in blocks for block in part])
+    )(*[block for part in blocks for block in part])
 
     held = [pieces[0]]
     for step in range(1, chunks):
@@ -487,12 +489,12 @@
     likelihood = pl.pallas_call(
         functools.partial(join_kernel, chunks, subs),
         out_shape=jax.ShapeDtypeStruct((vels, out_rows, columns), jnp.float32),
-        in_specs=[SMEM] + [VMEM] * (chunks * subs),
+        in_specs=[VMEM] * (chunks * subs),
         out_specs=VMEM,
         scratch_shapes=[pltpu.VMEM((subs, chunks, share, block_rows, LANES), jnp.float32)],
         compiler_params=pltpu.CompilerParams(vmem_limit_bytes=2 << 20),
         name="join_all",
-    )(info, *[block for group in groups for block in group])
+    )(*[block for group in groups for block in group])
     return likelihood[None]
 
 

time: 52.9 us -> 51.3 us (0.970)
  Pallas kernels: 13.5 us -> 12 us
    pallas_call x2, Pallas kernels: 7.7 us -> 6.74 us  [the longest x1 5.12 us: per_device(): pl.pallas_call(functools.partial(stack_kernel, groups, chunks, subs, expo...]
    pallas_call x1, Pallas kernels: 1.19 us -> 0.66 us  [per_device(): pl.pallas_call(functools.partial(join_kernel, chunks, subs), out_shape=ja...]
where the time goes in v11:
time: 51.3 us; the launch traced here: 51.2 us
  starting transfers between devices  25 us (49%)
  waiting for transfers between devices  13.1 us (26%)
  Pallas kernels  12 us (23%)
  local copies, waits for them, and re-layouts  0.91 us (2%)
    ppermute x6, starting transfers between devices, per_device(): lax.ppermute(sends[step * parts + p], 'expo', chunk_pairs(step, chunks, s...  11.5 us
    pallas_call x1, Pallas kernels, per_device(): pl.pallas_call(functools.partial(stack_kernel, groups, chunks, subs, expo...  5.12 us
    pallas_call x1, Pallas kernels, per_device(): pl.pallas_call(functools.partial(inner_kernel, radius), out_shape=[jax.Sh...  4.65 us
    ppermute x3, starting transfers between devices, per_device(): lax.ppermute(pieces[step], 'expo', chunk_pairs(step, chunks, subs))  4.45 us
    ppermute x3, waiting for transfers between devices, per_device(): lax.ppermute(pieces[step], 'expo', chunk_pairs(step, chunks, subs))  3.85 us
    ppermute x4, waiting for transfers between devices, per_device(): blocks[parts][0][step] = lax.ppermute(blocks[0][0][step], 'strip', up)  3.75 us
    ppermute x6, waiting for transfers between devices, per_device(): lax.ppermute(sends[step * parts + p], 'expo', chunk_pairs(step, chunks, s...  3.34 us
    ppermute x4, starting transfers between devices, per_device(): blocks[parts][0][step] = lax.ppermute(blocks[0][0][step], 'strip', up)  3.26 us
  transfers between devices with their start and end apart: 30, of which 12 were waited for; matrix products, arithmetic and copies ran while one was open for 0% of the time, Pallas kernels for 9%

profile of v11, /device:TPU:0, one launch (start us, length us, event | category | flops | bytes accessed | tf_op | source)
XLA Modules:
  0.0 51.2 jit_solution(10653224291960368760)
XLA Ops:
  0.0 0.9 %dynamic-slice_bitcast_fusion = (bf16[1,8,4,512]{3,2,1,0:T(4,128)(2,1)S(1)}, bf16[1,8,4,512]{3,2,1,0:T(4,128)(2,1)S(1)}) fusion(bf16[8,32,512]{2,1,0:T(8,128)(2,1)} %inv_var_hbm.1, s32[]{:T(128)S(6)} %select_n.6, bf16[8,32,512]{2,1,0:T(8,128)(2,1)} %science_hbm.1), kind=kLoop, calls=%fused_computation.1 | loop fusion | bytes 131076 | tf_op jit(solution)/shard_map/stack | solution.py:385
  1.0 3.0 %collective-permute-start = (bf16[2,8,4,512]{3,2,1,0:T(4,128)(2,1)S(1)}, bf16[2,8,4,512]{3,2,1,0:T(4,128)(2,1)S(1)}, u32[]{:S(2)}, u32[]{:S(2)}) collective-permute-start(bf16[2,8,4,512]{3,2,1,0:T(4,128)(2,1)S(1)} %pad_maximum_fusion), channel_id=1, source_target_pairs={{0,1},{1,0},{2,3},{3,2},{4,5},{5,4},{6,7},{7,6},{8,9},{9,8},{10,11... | collective-permute-start | bytes 196616 | tf_op jit(solution)/shard_map/ppermute | solution.py:389
  4.0 4.6 %filter_inner.1 = (f32[4,512,128]{2,1,0:T(8,128)S(1)}, f32[4,128,128]{2,1,0:T(8,128)S(1)}, f32[8,128]{1,0:T(8,128)S(1)}, f32[8,24,128]{2,1,0:T(8,128)S(1)}) custom-call(bf16[8,32,512]{2,1,0:T(8,128)(2,1)} %science_hbm.1, bf16[8,32,512]{2,1,0:T(8,128)(2,1)} %inv_var_hbm.1, f32[8,9]{1,0:T(8,128)} %row_taps_hbm.1, f32[8,9]{1,0:T(8,128)} %col_taps_hbm.1, ...), custom_call_target="tpu_custom_call" | custom-call | flops 100000000 | bytes 4000000 | tf_op jit(solution)/shard_map/filter_inner/pallas_call | solution.py:397
  8.7 1.6 %filter_outer.1 = (bf16[320,128]{1,0:T(8,128)(2,1)S(1)}, bf16[328,128]{1,0:T(8,128)(2,1)S(1)}, bf16[320,128]{1,0:T(8,128)(2,1)S(1)}, bf16[328,128]{1,0:T(8,128)(...) custom-call(f32[4,512,128]{2,1,0:T(8,128)S(1)} %get-tuple-element.21, ...), custom_call_target="tpu_custom_call" | custom-call | tf_op jit(solution)/shard_map/filter_outer/pallas_call | solution.py:427
  10.3 1.6 %collective-permute-start.1 = (bf16[320,128]{1,0:T(8,128)(2,1)S(1)}, bf16[320,128]{1,0:T(8,128)(2,1)S(1)}, u32[]{:S(2)}, u32[]{:S(2)}) collective-permute-start(bf16[320,128]{1,0:T(8,128)(2,1)S(1)} %get-tuple-element.26), channel_id=1, source_target_pairs={{0,4},{2,6},{4,0},{6,2},{8,12},{10,14},{12,8},{14,10},{1,5},{3,7},... | collective-permute-start | bytes 245768 | tf_op jit(solution)/shard_map/ppermute | solution.py:448
  11.9 2.6 %collective-permute-start.2 = (bf16[320,128]{1,0:T(8,128)(2,1)S(1)}, bf16[320,128]{1,0:T(8,128)(2,1)S(1)}, u32[]{:S(2)}, u32[]{:S(2)}) collective-permute-start(bf16[320,128]{1,0:T(8,128)(2,1)S(1)} %get-tuple-element.27), channel_id=1, source_target_pairs={{0,8},{2,10},{4,12},{6,14},{8,0},{10,2},{12,4},{14,6},{1,9},{3,11}... | collective-permute-start | bytes 245768 | tf_op jit(solution)/shard_map/ppermute | solution.py:448
  14.5 0.2 collective-permute-start.3
  14.7 0.3 collective-permute-start.15
  15.1 0.9 %collective-permute-start.8 = (bf16[328,128]{1,0:T(8,128)(2,1)S(1)}, bf16[328,128]{1,0:T(8,128)(2,1)S(1)}, u32[]{:S(2)}, u32[]{:S(2)}) collective-permute-start(bf16[328,128]{1,0:T(8,128)(2,1)S(1)} %get-tuple-element.30), channel_id=1, source_target_pairs={{0,4},{2,6},{4,0},{6,2},{8,12},{10,14},{12,8},{14,10},{1,5},{3,7},... | collective-permute-start | bytes 251912 | tf_op jit(solution)/shard_map/ppermute | solution.py:448
  16.0 3.5 %collective-permute-start.9 = (bf16[328,128]{1,0:T(8,128)(2,1)S(1)}, bf16[328,128]{1,0:T(8,128)(2,1)S(1)}, u32[]{:S(2)}, u32[]{:S(2)}) collective-permute-start(bf16[328,128]{1,0:T(8,128)(2,1)S(1)} %get-tuple-element.31), channel_id=1, source_target_pairs={{0,8},{2,10},{4,12},{6,14},{8,0},{10,2},{12,4},{14,6},{1,9},{3,11}... | collective-permute-start | bytes 251912 | tf_op jit(solution)/shard_map/ppermute | solution.py:448
  19.4 2.3 %collective-permute-done.2.rest_2_ = bf16[320,128]{1,0:T(8,128)(2,1)S(1)} collective-permute-done((bf16[320,128]{1,0:T(8,128)(2,1)S(1)}, bf16[320,128]{1,0:T(8,128)(2,1)S(1)}, u32[]{:S(2)}, u32[]{:S(2)}) %collective-permute-start.2) | collective-permute-done | bytes 81952 | tf_op jit(solution)/shard_map/ppermute | solution.py:448
  21.8 0.0 collective-permute-start.4
  21.8 0.0 collective-permute-done.3.rest_3_
  21.8 2.7 %collective-permute-start.10 = (bf16[328,128]{1,0:T(8,128)(2,1)S(1)}, bf16[328,128]{1,0:T(8,128)(2,1)S(1)}, u32[]{:S(2)}, u32[]{:S(2)}) collective-permute-start(bf16[328,128]{1,0:T(8,128)(2,1)S(1)} %get-tuple-element.32), channel_id=1, source_target_pairs={{0,12},{2,14},{4,8},{6,10},{8,4},{10,6},{12,0},{14,2},{1,13},{3,15... | collective-permute-start | bytes 251912 | tf_op jit(solution)/shard_map/ppermute | solution.py:448
  24.5 0.2 collective-permute-start.11
  24.7 0.0 collective-permute-done.4.rest_4_
  24.7 0.5 %collective-permute-start.16 = (bf16[320,128]{1,0:T(8,128)(2,1)S(1)}, bf16[320,128]{1,0:T(8,128)(2,1)S(1)}, u32[]{:S(2)}, u32[]{:S(2)}) collective-permute-start(bf16[320,128]{1,0:T(8,128)(2,1)S(1)} %collective-permute-done.1.rest_1_), channel_id=1, source_target_pairs={{1,0},{0,1},{3,2},{2,3},{5,4},{4,5},{7,6},{6,7},{9,8},{8,9},{11,10... | collective-permute-start | bytes 245768 | tf_op jit(solution)/shard_map/ppermute | solution.py:449
  25.2 0.0 collective-permute-done.8.rest_9_
  25.2 0.0 collective-permute-start.5
  25.2 1.0 %collective-permute-done.9.rest_10_ = bf16[328,128]{1,0:T(8,128)(2,1)S(1)} collective-permute-done((bf16[328,128]{1,0:T(8,128)(2,1)S(1)}, bf16[328,128]{1,0:T(8,128)(2,1)S(1)}, u32[]{:S(2)}, u32[]{:S(2)}) %collective-permute-start.9) | collective-permute-done | bytes 84000 | tf_op jit(solution)/shard_map/ppermute | solution.py:448
  26.2 2.3 %collective-permute-start.17 = (bf16[320,128]{1,0:T(8,128)(2,1)S(1)}, bf16[320,128]{1,0:T(8,128)(2,1)S(1)}, u32[]{:S(2)}, u32[]{:S(2)}) collective-permute-start(bf16[320,128]{1,0:T(8,128)(2,1)S(1)} %collective-permute-done.2.rest_2_), channel_id=1, source_target_pairs={{1,0},{0,1},{3,2},{2,3},{5,4},{4,5},{7,6},{6,7},{9,8},{8,9},{11,10... | collective-permute-start | bytes 245768 | tf_op jit(solution)/shard_map/ppermute | solution.py:449
  28.6 0.0 collective-permute-done.10.rest_11_
  28.6 0.0 collective-permute-start.6
  28.6 0.0 collective-permute-done.11.rest_12_
  28.6 0.1 collective-permute-start.18
  28.6 1.4 %collective-permute-done.16.rest_17_ = bf16[320,128]{1,0:T(8,128)(2,1)S(1)} collective-permute-done((bf16[320,128]{1,0:T(8,128)(2,1)S(1)}, bf16[320,128]{1,0:T(8,128)(2,1)S(1)}, u32[]{:S(2)}, u32[]{:S(2)}) %collective-permute-start.16) | collective-permute-done | bytes 81952 | tf_op jit(solution)/shard_map/ppermute | solution.py:449
  30.0 0.0 collective-permute-done.5.rest_5_
  30.0 0.5 collective-permute-start.7
  30.5 0.7 %collective-permute-done.17.rest_18_ = bf16[320,128]{1,0:T(8,128)(2,1)S(1)} collective-permute-done((bf16[320,128]{1,0:T(8,128)(2,1)S(1)}, bf16[320,128]{1,0:T(8,128)(2,1)S(1)}, u32[]{:S(2)}, u32[]{:S(2)}) %collective-permute-start.17) | collective-permute-done | bytes 81952 | tf_op jit(solution)/shard_map/ppermute | solution.py:449
  31.2 0.0 collective-permute-start.19
  31.2 0.5 collective-permute-start.13
  31.7 1.7 %collective-permute-done.18.rest_19_ = bf16[320,128]{1,0:T(8,128)(2,1)S(1)} collective-permute-done((bf16[320,128]{1,0:T(8,128)(2,1)S(1)}, bf16[320,128]{1,0:T(8,128)(2,1)S(1)}, u32[]{:S(2)}, u32[]{:S(2)}) %collective-permute-start.18) | collective-permute-done | bytes 81952 | tf_op jit(solution)/shard_map/ppermute | solution.py:449
  33.4 0.5 collective-permute-start.20
  33.9 0.1 collective-permute-start.21
  34.0 0.4 collective-permute-start.22
  34.5 0.2 collective-permute-done.14.rest_15_
  34.7 0.2 collective-permute-done.20.rest_21_
  34.9 0.4 collective-permute-done.21.rest_22_
  35.2 0.2 collective-permute-done.22.rest_23_
  35.4 5.1 %stack_twice.1 = (f32[4,8,128]{2,1,0:T(8,128)S(1)}, f32[4,8,128]{2,1,0:T(8,128)S(1)}, f32[4,8,128]{2,1,0:T(8,128)S(1)}, f32[4,8,128]{2,1,0:T(8,128)S(1)}) custom-call(bf16[320,128]{1,0:T(8,128)(2,1)S(1)} %get-tuple-element.25.rest_0_, bf16[320,128]{1,0:T(8,128)(2,1)S(1)} %collective-permute-done.1.rest_1_, ...), custom_call_target="tpu_custom_call" | custom-call | tf_op jit(solution)/shard_map/stack_twice/pallas_call | solution.py:461
  40.5 1.8 %collective-permute-start.23 = (f32[4,8,128]{2,1,0:T(8,128)S(1)}, f32[4,8,128]{2,1,0:T(8,128)S(1)}, u32[]{:S(2)}, u32[]{:S(2)}) collective-permute-start(f32[4,8,128]{2,1,0:T(8,128)S(1)} %get-tuple-element.34), channel_id=1, source_target_pairs={{0,4},{2,6},{4,0},{6,2},{8,12},{10,14},{12,8},{14,10},{1,5},{3,7},... | collective-permute-start | bytes 49160 | tf_op jit(solution)/shard_map/ppermute | solution.py:483
  42.3 1.5 %collective-permute-start.24 = (f32[4,8,128]{2,1,0:T(8,128)S(1)}, f32[4,8,128]{2,1,0:T(8,128)S(1)}, u32[]{:S(2)}, u32[]{:S(2)}) collective-permute-start(f32[4,8,128]{2,1,0:T(8,128)S(1)} %get-tuple-element.35), channel_id=1, source_target_pairs={{0,8},{2,10},{4,12},{6,14},{8,0},{10,2},{12,4},{14,6},{1,9},{3,11}... | collective-permute-start | bytes 49160 | tf_op jit(solution)/shard_map/ppermute | solution.py:483
  43.8 1.2 %collective-permute-start.25 = (f32[4,8,128]{2,1,0:T(8,128)S(1)}, f32[4,8,128]{2,1,0:T(8,128)S(1)}, u32[]{:S(2)}, u32[]{:S(2)}) collective-permute-start(f32[4,8,128]{2,1,0:T(8,128)S(1)} %get-tuple-element.36), channel_id=1, source_target_pairs={{0,12},{2,14},{4,8},{6,10},{8,4},{10,6},{12,0},{14,2},{1,13},{3,15... | collective-permute-start | bytes 49160 | tf_op jit(solution)/shard_map/ppermute | solution.py:483
  45.0 0.5 collective-permute-start.27
  45.5 1.5 %collective-permute-done.24.rest_2_ = f32[4,8,128]{2,1,0:T(8,128)S(1)} collective-permute-done((f32[4,8,128]{2,1,0:T(8,128)S(1)}, f32[4,8,128]{2,1,0:T(8,128)S(1)}, u32[]{:S(2)}, u32[]{:S(2)}) %collective-permute-start.24) | collective-permute-done | bytes 16416 | tf_op jit(solution)/shard_map/ppermute | solution.py:483
  46.9 2.4 %collective-permute-done.25.rest_3_ = f32[4,8,128]{2,1,0:T(8,128)S(1)} collective-permute-done((f32[4,8,128]{2,1,0:T(8,128)S(1)}, f32[4,8,128]{2,1,0:T(8,128)S(1)}, u32[]{:S(2)}, u32[]{:S(2)}) %collective-permute-start.25) | collective-permute-done | bytes 16416 | tf_op jit(solution)/shard_map/ppermute | solution.py:483
  49.4 1.2 %collective-permute-done.29.rest_7_ = f32[4,8,128]{2,1,0:T(8,128)S(1)} collective-permute-done((f32[4,8,128]{2,1,0:T(8,128)S(1)}, f32[4,8,128]{2,1,0:T(8,128)S(1)}, u32[]{:S(2)}, u32[]{:S(2)}) %collective-permute-start.29) | collective-permute-done | bytes 16416 | tf_op jit(solution)/shard_map/ppermute | solution.py:487
  50.5 0.7 %join_all.1 = f32[8,4,512]{2,1,0:T(4,128)} custom-call(f32[4,8,128]{2,1,0:T(8,128)S(1)} %get-tuple-element.33.rest_0_, f32[4,8,128]{2,1,0:T(8,128)S(1)} %collective-permute-done.23.rest_1_, f32[4,8,128]{2,1,0:T(8,128)S(1)} %collective-permute-done.24.rest_2_, f32[4,8,128]{2,1,0:T(8,128)S(1)} %collective-permute-done.25.rest_3_, ...), custom_call_target="tpu_custom_call" | custom-call | tf_op jit(solution)/shard_map/join_all/pallas_call | solution.py:489
  (18 shorter events, 0.1 us)
Async XLA Ops:
  1.0 7.7 %collective-permute-start = (bf16[2,8,4,512]{3,2,1,0:T(4,128)(2,1)S(1)}, bf16[2,8,4,512]{3,2,1,0:T(4,128)(2,1)S(1)}, u32[]{:S(2)}, u32[]{:S(2)}) collective-permute-start(bf16[2,8,4,512]{3,2,1,0:T(4,128)(2,1)S(1)} %pad_maximum_fusion), channel_id=1, source_target_pairs={{0,1},{1,0},{2,3},{3,2},{4,5},{5,4},{6,7},{7,6},{8,9},{9,8},{10,11... | collective-permute-start | bytes 196616 | tf_op jit(solution)/shard_map/ppermute | solution.py:389
  10.3 5.7 %collective-permute-start.1 = (bf16[320,128]{1,0:T(8,128)(2,1)S(1)}, bf16[320,128]{1,0:T(8,128)(2,1)S(1)}, u32[]{:S(2)}, u32[]{:S(2)}) collective-permute-start(bf16[320,128]{1,0:T(8,128)(2,1)S(1)} %get-tuple-element.26), channel_id=1, source_target_pairs={{0,4},{2,6},{4,0},{6,2},{8,12},{10,14},{12,8},{14,10},{1,5},{3,7},... | collective-permute-start | bytes 245768 | tf_op jit(solution)/shard_map/ppermute | solution.py:448
  11.9 9.9 %collective-permute-start.2 = (bf16[320,128]{1,0:T(8,128)(2,1)S(1)}, bf16[320,128]{1,0:T(8,128)(2,1)S(1)}, u32[]{:S(2)}, u32[]{:S(2)}) collective-permute-start(bf16[320,128]{1,0:T(8,128)(2,1)S(1)} %get-tuple-element.27), channel_id=1, source_target_pairs={{0,8},{2,10},{4,12},{6,14},{8,0},{10,2},{12,4},{14,6},{1,9},{3,11}... | collective-permute-start | bytes 245768 | tf_op jit(solution)/shard_map/ppermute | solution.py:448
  14.5 7.3 %collective-permute-start.3 = (bf16[320,128]{1,0:T(8,128)(2,1)S(1)}, bf16[320,128]{1,0:T(8,128)(2,1)S(1)}, u32[]{:S(2)}, u32[]{:S(2)}) collective-permute-start(bf16[320,128]{1,0:T(8,128)(2,1)S(1)} %get-tuple-element.28), channel_id=1, source_target_pairs={{0,12},{2,14},{4,8},{6,10},{8,4},{10,6},{12,0},{14,2},{1,13},{3,15... | collective-permute-start | bytes 245768 | tf_op jit(solution)/shard_map/ppermute | solution.py:448
  14.7 9.7 %collective-permute-start.15 = (bf16[320,128]{1,0:T(8,128)(2,1)S(1)}, bf16[320,128]{1,0:T(8,128)(2,1)S(1)}, u32[]{:S(2)}, u32[]{:S(2)}) collective-permute-start(bf16[320,128]{1,0:T(8,128)(2,1)S(1)} %get-tuple-element.25.rest_0_), channel_id=1, source_target_pairs={{1,0},{0,1},{3,2},{2,3},{5,4},{4,5},{7,6},{6,7},{9,8},{8,9},{11,10... | collective-permute-start | bytes 245768 | tf_op jit(solution)/shard_map/ppermute | solution.py:449
  15.1 10.2 %collective-permute-start.8 = (bf16[328,128]{1,0:T(8,128)(2,1)S(1)}, bf16[328,128]{1,0:T(8,128)(2,1)S(1)}, u32[]{:S(2)}, u32[]{:S(2)}) collective-permute-start(bf16[328,128]{1,0:T(8,128)(2,1)S(1)} %get-tuple-element.30), channel_id=1, source_target_pairs={{0,4},{2,6},{4,0},{6,2},{8,12},{10,14},{12,8},{14,10},{1,5},{3,7},... | collective-permute-start | bytes 251912 | tf_op jit(solution)/shard_map/ppermute | solution.py:448
  16.0 10.3 %collective-permute-start.9 = (bf16[328,128]{1,0:T(8,128)(2,1)S(1)}, bf16[328,128]{1,0:T(8,128)(2,1)S(1)}, u32[]{:S(2)}, u32[]{:S(2)}) collective-permute-start(bf16[328,128]{1,0:T(8,128)(2,1)S(1)} %get-tuple-element.31), channel_id=1, source_target_pairs={{0,8},{2,10},{4,12},{6,14},{8,0},{10,2},{12,4},{14,6},{1,9},{3,11}... | collective-permute-start | bytes 251912 | tf_op jit(solution)/shard_map/ppermute | solution.py:448
  21.8 2.9 %collective-permute-start.4 = (bf16[320,128]{1,0:T(8,128)(2,1)S(1)}, bf16[320,128]{1,0:T(8,128)(2,1)S(1)}, u32[]{:S(2)}, u32[]{:S(2)}) collective-permute-start(bf16[320,128]{1,0:T(8,128)(2,1)S(1)} %get-tuple-element.25.rest_0_), channel_id=1, source_target_pairs={{0,2},{2,0},{4,6},{6,4},{8,10},{10,8},{12,14},{14,12},{1,3},{3,1},... | collective-permute-start | bytes 245768 | tf_op jit(solution)/shard_map/ppermute | solution.py:453
  21.8 6.8 %collective-permute-start.10 = (bf16[328,128]{1,0:T(8,128)(2,1)S(1)}, bf16[328,128]{1,0:T(8,128)(2,1)S(1)}, u32[]{:S(2)}, u32[]{:S(2)}) collective-permute-start(bf16[328,128]{1,0:T(8,128)(2,1)S(1)} %get-tuple-element.32), channel_id=1, source_target_pairs={{0,12},{2,14},{4,8},{6,10},{8,4},{10,6},{12,0},{14,2},{1,13},{3,15... | collective-permute-start | bytes 251912 | tf_op jit(solution)/shard_map/ppermute | solution.py:448
  24.5 4.1 %collective-permute-start.11 = (bf16[328,128]{1,0:T(8,128)(2,1)S(1)}, bf16[328,128]{1,0:T(8,128)(2,1)S(1)}, u32[]{:S(2)}, u32[]{:S(2)}) collective-permute-start(bf16[328,128]{1,0:T(8,128)(2,1)S(1)} %get-tuple-element.29.rest_8_), channel_id=1, source_target_pairs={{0,2},{2,0},{4,6},{6,4},{8,10},{10,8},{12,14},{14,12},{1,3},{3,1},... | collective-permute-start | bytes 251912 | tf_op jit(solution)/shard_map/ppermute | solution.py:453
  24.7 5.3 %collective-permute-start.16 = (bf16[320,128]{1,0:T(8,128)(2,1)S(1)}, bf16[320,128]{1,0:T(8,128)(2,1)S(1)}, u32[]{:S(2)}, u32[]{:S(2)}) collective-permute-start(bf16[320,128]{1,0:T(8,128)(2,1)S(1)} %collective-permute-done.1.rest_1_), channel_id=1, source_target_pairs={{1,0},{0,1},{3,2},{2,3},{5,4},{4,5},{7,6},{6,7},{9,8},{8,9},{11,10... | collective-permute-start | bytes 245768 | tf_op jit(solution)/shard_map/ppermute | solution.py:449
  25.2 4.8 %collective-permute-start.5 = (bf16[320,128]{1,0:T(8,128)(2,1)S(1)}, bf16[320,128]{1,0:T(8,128)(2,1)S(1)}, u32[]{:S(2)}, u32[]{:S(2)}) collective-permute-start(bf16[320,128]{1,0:T(8,128)(2,1)S(1)} %collective-permute-done.1.rest_1_), channel_id=1, source_target_pairs={{0,2},{2,0},{4,6},{6,4},{8,10},{10,8},{12,14},{14,12},{1,3},{3,1},... | collective-permute-start | bytes 245768 | tf_op jit(solution)/shard_map/ppermute | solution.py:453
  26.2 5.0 %collective-permute-start.17 = (bf16[320,128]{1,0:T(8,128)(2,1)S(1)}, bf16[320,128]{1,0:T(8,128)(2,1)S(1)}, u32[]{:S(2)}, u32[]{:S(2)}) collective-permute-start(bf16[320,128]{1,0:T(8,128)(2,1)S(1)} %collective-permute-done.2.rest_2_), channel_id=1, source_target_pairs={{1,0},{0,1},{3,2},{2,3},{5,4},{4,5},{7,6},{6,7},{9,8},{8,9},{11,10... | collective-permute-start | bytes 245768 | tf_op jit(solution)/shard_map/ppermute | solution.py:449
  28.6 2.7 %collective-permute-start.6 = (bf16[320,128]{1,0:T(8,128)(2,1)S(1)}, bf16[320,128]{1,0:T(8,128)(2,1)S(1)}, u32[]{:S(2)}, u32[]{:S(2)}) collective-permute-start(bf16[320,128]{1,0:T(8,128)(2,1)S(1)} %collective-permute-done.2.rest_2_), channel_id=1, source_target_pairs={{0,2},{2,0},{4,6},{6,4},{8,10},{10,8},{12,14},{14,12},{1,3},{3,1},... | collective-permute-start | bytes 245768 | tf_op jit(solution)/shard_map/ppermute | solution.py:453
  28.6 4.9 %collective-permute-start.18 = (bf16[320,128]{1,0:T(8,128)(2,1)S(1)}, bf16[320,128]{1,0:T(8,128)(2,1)S(1)}, u32[]{:S(2)}, u32[]{:S(2)}) collective-permute-start(bf16[320,128]{1,0:T(8,128)(2,1)S(1)} %collective-permute-done.3.rest_3_), channel_id=1, source_target_pairs={{1,0},{0,1},{3,2},{2,3},{5,4},{4,5},{7,6},{6,7},{9,8},{8,9},{11,10... | collective-permute-start | bytes 245768 | tf_op jit(solution)/shard_map/ppermute | solution.py:449
  30.0 4.0 %collective-permute-start.12 = (bf16[328,128]{1,0:T(8,128)(2,1)S(1)}, bf16[328,128]{1,0:T(8,128)(2,1)S(1)}, u32[]{:S(2)}, u32[]{:S(2)}) collective-permute-start(bf16[328,128]{1,0:T(8,128)(2,1)S(1)} %collective-permute-done.8.rest_9_), channel_id=1, source_target_pairs={{0,2},{2,0},{4,6},{6,4},{8,10},{10,8},{12,14},{14,12},{1,3},{3,1},... | collective-permute-start | bytes 251912 | tf_op jit(solution)/shard_map/ppermute | solution.py:453
  30.0 3.4 %collective-permute-start.7 = (bf16[320,128]{1,0:T(8,128)(2,1)S(1)}, bf16[320,128]{1,0:T(8,128)(2,1)S(1)}, u32[]{:S(2)}, u32[]{:S(2)}) collective-permute-start(bf16[320,128]{1,0:T(8,128)(2,1)S(1)} %collective-permute-done.3.rest_3_), channel_id=1, source_target_pairs={{0,2},{2,0},{4,6},{6,4},{8,10},{10,8},{12,14},{14,12},{1,3},{3,1},... | collective-permute-start | bytes 245768 | tf_op jit(solution)/shard_map/ppermute | solution.py:453
  31.2 2.7 %collective-permute-start.19 = (bf16[320,128]{1,0:T(8,128)(2,1)S(1)}, bf16[320,128]{1,0:T(8,128)(2,1)S(1)}, u32[]{:S(2)}, u32[]{:S(2)}) collective-permute-start(bf16[320,128]{1,0:T(8,128)(2,1)S(1)} %collective-permute-done.15.rest_16_), channel_id=1, source_target_pairs={{0,2},{2,0},{4,6},{6,4},{8,10},{10,8},{12,14},{14,12},{1,3},{3,1},... | collective-permute-start | bytes 245768 | tf_op jit(solution)/shard_map/ppermute | solution.py:453
  31.2 3.2 %collective-permute-start.13 = (bf16[328,128]{1,0:T(8,128)(2,1)S(1)}, bf16[328,128]{1,0:T(8,128)(2,1)S(1)}, u32[]{:S(2)}, u32[]{:S(2)}) collective-permute-start(bf16[328,128]{1,0:T(8,128)(2,1)S(1)} %collective-permute-done.9.rest_10_), channel_id=1, source_target_pairs={{0,2},{2,0},{4,6},{6,4},{8,10},{10,8},{12,14},{14,12},{1,3},{3,1},... | collective-permute-start | bytes 251912 | tf_op jit(solution)/shard_map/ppermute | solution.py:453
  33.4 1.3 %collective-permute-start.14 = (bf16[328,128]{1,0:T(8,128)(2,1)S(1)}, bf16[328,128]{1,0:T(8,128)(2,1)S(1)}, u32[]{:S(2)}, u32[]{:S(2)}) collective-permute-start(bf16[328,128]{1,0:T(8,128)(2,1)S(1)} %collective-permute-done.10.rest_11_), channel_id=1, source_target_pairs={{0,2},{2,0},{4,6},{6,4},{8,10},{10,8},{12,14},{14,12},{1,3},{3,1},... | collective-permute-start | bytes 251912 | tf_op jit(solution)/shard_map/ppermute | solution.py:453
  33.4 1.4 %collective-permute-start.20 = (bf16[320,128]{1,0:T(8,128)(2,1)S(1)}, bf16[320,128]{1,0:T(8,128)(2,1)S(1)}, u32[]{:S(2)}, u32[]{:S(2)}) collective-permute-start(bf16[320,128]{1,0:T(8,128)(2,1)S(1)} %collective-permute-done.16.rest_17_), channel_id=1, source_target_pairs={{0,2},{2,0},{4,6},{6,4},{8,10},{10,8},{12,14},{14,12},{1,3},{3,1},... | collective-permute-start | bytes 245768 | tf_op jit(solution)/shard_map/ppermute | solution.py:453
  33.9 1.3 %collective-permute-start.21 = (bf16[320,128]{1,0:T(8,128)(2,1)S(1)}, bf16[320,128]{1,0:T(8,128)(2,1)S(1)}, u32[]{:S(2)}, u32[]{:S(2)}) collective-permute-start(bf16[320,128]{1,0:T(8,128)(2,1)S(1)} %collective-permute-done.17.rest_18_), channel_id=1, source_target_pairs={{0,2},{2,0},{4,6},{6,4},{8,10},{10,8},{12,14},{14,12},{1,3},{3,1},... | collective-permute-start | bytes 245768 | tf_op jit(solution)/shard_map/ppermute | solution.py:453
  34.0 1.4 %collective-permute-start.22 = (bf16[320,128]{1,0:T(8,128)(2,1)S(1)}, bf16[320,128]{1,0:T(8,128)(2,1)S(1)}, u32[]{:S(2)}, u32[]{:S(2)}) collective-permute-start(bf16[320,128]{1,0:T(8,128)(2,1)S(1)} %collective-permute-done.18.rest_19_), channel_id=1, source_target_pairs={{0,2},{2,0},{4,6},{6,4},{8,10},{10,8},{12,14},{14,12},{1,3},{3,1},... | collective-permute-start | bytes 245768 | tf_op jit(solution)/shard_map/ppermute | solution.py:453
  40.5 4.5 %collective-permute-start.23 = (f32[4,8,128]{2,1,0:T(8,128)S(1)}, f32[4,8,128]{2,1,0:T(8,128)S(1)}, u32[]{:S(2)}, u32[]{:S(2)}) collective-permute-start(f32[4,8,128]{2,1,0:T(8,128)S(1)} %get-tuple-element.34), channel_id=1, source_target_pairs={{0,4},{2,6},{4,0},{6,2},{8,12},{10,14},{12,8},{14,10},{1,5},{3,7},... | collective-permute-start | bytes 49160 | tf_op jit(solution)/shard_map/ppermute | solution.py:483
  42.3 4.6 %collective-permute-start.24 = (f32[4,8,128]{2,1,0:T(8,128)S(1)}, f32[4,8,128]{2,1,0:T(8,128)S(1)}, u32[]{:S(2)}, u32[]{:S(2)}) collective-permute-start(f32[4,8,128]{2,1,0:T(8,128)S(1)} %get-tuple-element.35), channel_id=1, source_target_pairs={{0,8},{2,10},{4,12},{6,14},{8,0},{10,2},{12,4},{14,6},{1,9},{3,11}... | collective-permute-start | bytes 49160 | tf_op jit(solution)/shard_map/ppermute | solution.py:483
  43.8 5.5 %collective-permute-start.25 = (f32[4,8,128]{2,1,0:T(8,128)S(1)}, f32[4,8,128]{2,1,0:T(8,128)S(1)}, u32[]{:S(2)}, u32[]{:S(2)}) collective-permute-start(f32[4,8,128]{2,1,0:T(8,128)S(1)} %get-tuple-element.36), channel_id=1, source_target_pairs={{0,12},{2,14},{4,8},{6,10},{8,4},{10,6},{12,0},{14,2},{1,13},{3,15... | collective-permute-start | bytes 49160 | tf_op jit(solution)/shard_map/ppermute | solution.py:483
  45.0 4.4 %collective-permute-start.26 = (f32[4,8,128]{2,1,0:T(8,128)S(1)}, f32[4,8,128]{2,1,0:T(8,128)S(1)}, u32[]{:S(2)}, u32[]{:S(2)}) collective-permute-start(f32[4,8,128]{2,1,0:T(8,128)S(1)} %get-tuple-element.33.rest_0_), channel_id=1, source_target_pairs={{0,2},{2,0},{4,6},{6,4},{8,10},{10,8},{12,14},{14,12},{1,3},{3,1},... | collective-permute-start | bytes 49160 | tf_op jit(solution)/shard_map/ppermute | solution.py:487
  45.0 4.4 %collective-permute-start.27 = (f32[4,8,128]{2,1,0:T(8,128)S(1)}, f32[4,8,128]{2,1,0:T(8,128)S(1)}, u32[]{:S(2)}, u32[]{:S(2)}) collective-permute-start(f32[4,8,128]{2,1,0:T(8,128)S(1)} %collective-permute-done.23.rest_1_), channel_id=1, source_target_pairs={{0,2},{2,0},{4,6},{6,4},{8,10},{10,8},{12,14},{14,12},{1,3},{3,1},... | collective-permute-start | bytes 49160 | tf_op jit(solution)/shard_map/ppermute | solution.py:487
  46.9 2.4 %collective-permute-start.28 = (f32[4,8,128]{2,1,0:T(8,128)S(1)}, f32[4,8,128]{2,1,0:T(8,128)S(1)}, u32[]{:S(2)}, u32[]{:S(2)}) collective-permute-start(f32[4,8,128]{2,1,0:T(8,128)S(1)} %collective-permute-done.24.rest_2_), channel_id=1, source_target_pairs={{0,2},{2,0},{4,6},{6,4},{8,10},{10,8},{12,14},{14,12},{1,3},{3,1},... | collective-permute-start | bytes 49160 | tf_op jit(solution)/shard_map/ppermute | solution.py:487
  49.3 1.2 %collective-permute-start.29 = (f32[4,8,128]{2,1,0:T(8,128)S(1)}, f32[4,8,128]{2,1,0:T(8,128)S(1)}, u32[]{:S(2)}, u32[]{:S(2)}) collective-permute-start(f32[4,8,128]{2,1,0:T(8,128)S(1)} %collective-permute-done.25.rest_3_), channel_id=1, source_target_pairs={{0,2},{2,0},{4,6},{6,4},{8,10},{10,8},{12,14},{14,12},{1,3},{3,1},... | collective-permute-start | bytes 49160 | tf_op jit(solution)/shard_map/ppermute | solution.py:487
